TPU v7x, 128 devices: a whole 4x4x4 slice. The times are simulated.
128 devices in a mesh: ka: 16 (over z_lo, x, core), grid: 8 (over y, z_hi).
Axes of the slice: x: 4, y: 4, z: 4 (z_hi: 2, z_lo: 2; z = z_hi * 2 + z_lo), core: 2. Of those that a mesh axis runs over, the one named last changes fastest.
Arguments:
- orbitals: float32 [32, 3, 2, 64, 9216], P('ka', None, None, 'grid'), may hold values from -6 to 6
- partner_map: int32 [32], P('ka'), may hold values from 0 to 31, as said below
- wave_vectors: float32 [32, 3], P('ka'), may hold values from -0.5 to 0.5
- levels: float32 [32, 3], P('ka'), may hold values from 0.5 to 2
- potential: float32 [64, 9216], P('grid'), may hold values from 0 to 2
- perturbation: float32 [2, 64, 9216], P(None, 'grid'), may hold values from -0.5 to 1.5
- step_weights: int32 [4], replicated, may hold values from 2 to 12
Outputs:
- density: float32 [2, 64, 9216], P(None, 'grid')
Inputs may be any that keep to these rules, and one draw needn't show every extreme that they name: partner_map is a permutation; it maps the 2 k-points starting at j * 2 onto the 2 k-points starting at ((j + 8) mod (16)) * 2, in an order of its own for each j.
All inputs are finite; a program needn't handle non-finite values.
Results may differ from a plain program's by a relative error of at most 0.00007.
Values sent between devices are 32-bit elements; how exact they have to be, the bound alone decides.
No kernel may reach another device: no remote copies, remote signals or barrier semaphores. Data moves between devices by JAX's collectives and lax.ppermute only.
A program may use at most 192 MiB of HBM per device.

v0:
```python
import jax
import jax.numpy as jnp
from jax import lax
from jax.sharding import PartitionSpec as P

NX = 96
ITERS = 4


def from_behind(value, axis, by):
    peers = lax.axis_size(axis)
    return lax.ppermute(value, axis, [(i, (i + by) % peers) for i in range(peers)])


def extended(value, sides, width):
    for axis, dim in sides:
        peers, length = (lax.axis_size(axis), value.shape[dim])
        up = [(i, (i + 1) % peers) for i in range(peers)]
        down = [(j, i) for i, j in up]
        last = lax.slice_in_dim(value, length - width, length, axis=dim)
        initial = lax.slice_in_dim(value, 0, width, axis=dim)
        before = lax.ppermute(last, axis, up)
        after = lax.ppermute(initial, axis, down)
        value = jnp.concatenate([before, value, after], axis=dim)
    return value


def shift_x(field, offset, columns, width):
    main = jnp.roll(field, -offset, -1)
    if offset > 0:
        wrapped = jnp.roll(field, width - offset, -1)
        outside = columns + offset >= width
    else:
        wrapped = jnp.roll(field, -offset - width, -1)
        outside = columns + offset < 0
    return jnp.where(outside, wrapped, main)


def derivatives(component, columns):
    middle = component[:, :, 2:-2]
    above_one = component[:, :, 3:-1]
    below_one = component[:, :, 1:-3]
    above_two = component[:, :, 4:]
    below_two = component[:, :, :-4]
    x_plus_one = shift_x(middle, 1, columns, NX)
    x_minus_one = shift_x(middle, -1, columns, NX)
    x_plus_two = shift_x(middle, 2, columns, NX)
    x_minus_two = shift_x(middle, -2, columns, NX)
    y_plus_one = jnp.roll(middle, -NX, -1)
    y_minus_one = jnp.roll(middle, NX, -1)
    y_plus_two = jnp.roll(middle, -2 * NX, -1)
    y_minus_two = jnp.roll(middle, 2 * NX, -1)
    second_x = (
        16.0 * (x_plus_one + x_minus_one) - (x_plus_two + x_minus_two) - 30.0 * middle
    ) / 12.0
    second_y = (
        16.0 * (y_plus_one + y_minus_one) - (y_plus_two + y_minus_two) - 30.0 * middle
    ) / 12.0
    second_z = (16.0 * (above_one + below_one) - (above_two + below_two) - 30.0 * middle) / 12.0
    first_x = (8.0 * (x_plus_one - x_minus_one) - (x_plus_two - x_minus_two)) / 12.0
    first_y = (8.0 * (y_plus_one - y_minus_one) - (y_plus_two - y_minus_two)) / 12.0
    first_z = (8.0 * (above_one - below_one) - (above_two - below_two)) / 12.0
    return (middle, second_x + second_y + second_z, (first_x, first_y, first_z))


def apply_operator(padded, wave_vectors, levels, potential_mid, columns):
    real_mid, lap_real, firsts_real = derivatives(padded[:, :, 0], columns)
    imag_mid, lap_imag, firsts_imag = derivatives(padded[:, :, 1], columns)
    wave_x = wave_vectors[:, 0][:, None, None, None]
    wave_y = wave_vectors[:, 1][:, None, None, None]
    wave_z = wave_vectors[:, 2][:, None, None, None]
    grad_real = wave_x * firsts_real[0] + wave_y * firsts_real[1] + wave_z * firsts_real[2]
    grad_imag = wave_x * firsts_imag[0] + wave_y * firsts_imag[1] + wave_z * firsts_imag[2]
    square = wave_x * wave_x + wave_y * wave_y + wave_z * wave_z
    total_pot = potential_mid[None, None] + levels[:, :, None, None]
    out_real = -0.5 * (lap_real - 2.0 * grad_imag - square * real_mid) + total_pot * real_mid
    out_imag = -0.5 * (lap_imag + 2.0 * grad_real - square * imag_mid) + total_pot * imag_mid
    return jnp.stack([out_real, out_imag], 2)


def on_device(orbitals, partner_map, wave_vectors, levels, potential, perturbation, step_weights):
    kpoints_local = orbitals.shape[0]
    planes = orbitals.shape[3]
    cells_xy = orbitals.shape[4]
    highest = lax.Precision.HIGHEST
    columns = jnp.arange(cells_xy, dtype=jnp.int32) % NX
    arrived = from_behind(orbitals, "ka", lax.axis_size("ka") // 2)
    matched = jnp.take(arrived, partner_map % kpoints_local, axis=0)
    own_real = orbitals[:, :, 0]
    own_imag = orbitals[:, :, 1]
    mate_real = matched[:, :, 0]
    mate_imag = matched[:, :, 1]
    pert_real = perturbation[0]
    pert_imag = perturbation[1]
    w_real = pert_real * own_real - pert_imag * own_imag
    w_imag = pert_real * own_imag + pert_imag * own_real
    part_real = jnp.einsum("kmzc,knzc->kmn", mate_real, w_real, precision=highest) + jnp.einsum(
        "kmzc,knzc->kmn", mate_imag, w_imag, precision=highest
    )
    part_imag = jnp.einsum("kmzc,knzc->kmn", mate_real, w_imag, precision=highest) - jnp.einsum(
        "kmzc,knzc->kmn", mate_imag, w_real, precision=highest
    )
    summed_real, summed_imag = lax.psum((part_real, part_imag), "grid")
    ncells = planes * lax.axis_size("grid") * cells_xy
    prod_real = summed_real / ncells
    prod_imag = summed_imag / ncells
    proj_real = jnp.einsum("kmn,kmzc->knzc", prod_real, mate_real, precision=highest) - jnp.einsum(
        "kmn,kmzc->knzc", prod_imag, mate_imag, precision=highest
    )
    proj_imag = jnp.einsum("kmn,kmzc->knzc", prod_imag, mate_real, precision=highest) + jnp.einsum(
        "kmn,kmzc->knzc", prod_real, mate_imag, precision=highest
    )
    right = jnp.stack([-(w_real - proj_real), -(w_imag - proj_imag)], 2)
    weights = step_weights.astype(jnp.float32) / 100.0
    solution = weights[0] * right
    for count in range(1, ITERS):
        padded = extended(solution, (("grid", 3),), 2)
        image = apply_operator(padded, wave_vectors, levels, potential, columns)
        solution = solution + weights[count] * (right - image)
    sol_real = solution[:, :, 0]
    sol_imag = solution[:, :, 1]
    dens_real = jnp.sum(own_real * sol_real + own_imag * sol_imag, axis=(0, 1))
    dens_imag = jnp.sum(own_real * sol_imag - own_imag * sol_real, axis=(0, 1))
    stacked = jnp.stack([dens_real, dens_imag], 0)
    kpoints_all = kpoints_local * lax.axis_size("ka")
    total = lax.psum(stacked, "ka")
    return total / kpoints_all


def solution(mesh):
    return jax.shard_map(
        on_device,
        mesh=mesh,
        in_specs=(
            P("ka", None, None, "grid", None),
            P("ka"),
            P("ka", None),
            P("ka", None),
            P("grid", None),
            P(None, "grid", None),
            P(),
        ),
        out_specs=P(None, "grid", None),
        check_vma=False,
    )
```

profile of v0, /device:TPU:1, one launch (start us, length us, event | category | flops | bytes accessed | tf_op | source)
XLA Modules:
  0.0 690.4 jit_solution(14541296557504057893)
XLA Ops:
  6.5 2.5 collective-permute-start
  12.1 2.4 fusion.26
  14.6 71.0 %collective-permute-done = f32[2,3,2,8,9216]{4,3,2,1,0:T(8,128)} collective-permute-done((f32[2,3,2,8,9216]{4,3,2,1,0:T(8,128)}, f32[2,3,2,8,9216]{4,3,2,1,0:T(8,128)}, u32[]{:S(2)}, u32[]{:S(2)}) %collective-permute-start) | collective-permute-done | bytes 3538976 | tf_op jit(solution)/shard_map/ppermute | solution.py:12
  85.5 4.5 gather_fusion
  90.1 4.9 copy_select_fusion
  95.0 11.0 %fusion.57 = f32[2,3,3]{2,1,0:T(4,128)S(1)} fusion(f32[2,3,8,9216]{3,2,1,0:T(8,128)S(1)} %get-tuple-element.21, f32[2,3,2,8,9216]{4,1,3,0,2:T(4,128)S(1)} %copy_select_fusion), kind=kOutput, calls=%fused_computation.151 | convolution fusion | flops 15925248 | bytes 4128840 | tf_op jit(solution)/shard_map/kmzc,knzc->kmn/dot_general | solution.py:100
  106.0 11.2 %fusion.60 = f32[2,3,3]{2,1,0:T(4,128)S(1)} fusion(f32[2,3,8,9216]{3,2,1,0:T(8,128)S(1)} %get-tuple-element.22, f32[2,3,2,8,9216]{4,1,3,0,2:T(4,128)S(1)} %copy_select_fusion), kind=kOutput, calls=%fused_computation.152 | convolution fusion | flops 15925248 | bytes 4128840 | tf_op jit(solution)/shard_map/kmzc,knzc->kmn/dot_general | solution.py:97
  117.2 11.2 %fusion.66 = f32[2,3,3]{2,1,0:T(4,128)S(1)} fusion(f32[2,3,3]{2,1,0:T(4,128)S(1)} %fusion.57, f32[2,3,8,9216]{3,2,1,0:T(8,128)S(1)} %get-tuple-element.22, f32[2,3,2,8,9216]{4,1,3,0,2:T(4,128)S(1)} %copy_select_fusion), kind=kOutput, calls=%fused_computation.154 | convolution fusion | flops 15925266 | bytes 4132936 | tf_op jit(solution)/shard_map/kmzc,knzc->kmn/dot_general | solution.py:100
  128.4 10.2 %fusion.69 = f32[2,3,3]{2,1,0:T(4,128)S(1)} fusion(f32[2,3,3]{2,1,0:T(4,128)S(1)} %fusion.60, f32[2,3,8,9216]{3,2,1,0:T(8,128)S(1)} %get-tuple-element.21, f32[2,3,2,8,9216]{4,1,3,0,2:T(4,128)S(1)} %copy_select_fusion), kind=kOutput, calls=%fused_computation.155 | convolution fusion | flops 15925266 | bytes 4132936 | tf_op jit(solution)/shard_map/kmzc,knzc->kmn/dot_general | solution.py:97
  138.6 21.7 %all-reduce = (f32[2,3,3]{2,1,0:T(4,128)S(1)}, f32[2,3,3]{2,1,0:T(4,128)S(1)}) all-reduce(f32[2,3,3]{2,1,0:T(4,128)S(1)} %fusion.69, f32[2,3,3]{2,1,0:T(4,128)S(1)} %fusion.66), channel_id=1, replica_groups=mesh['ka'=16,'grid'=8] {'grid'}, use_global_device_ids=true, to_apply=%region_0.1 | all-reduce | flops 36 | bytes 288 | tf_op jit(solution)/shard_map/psum | solution.py:103
  160.4 6.5 fusion.52
  166.9 5.0 fusion.51
  171.9 5.1 fusion.50
  177.0 5.2 fusion.53
  182.2 4.6 fusion.34
  188.5 3.0 collective-permute-start.1
  192.9 35.4 %collective-permute-done.2 = f32[2,3,2,2,9216]{4,3,2,1,0:T(2,128)S(1)} collective-permute-done((f32[2,3,2,2,9216]{4,3,2,1,0:T(2,128)S(1)}, f32[2,3,2,2,9216]{4,3,2,1,0:T(2,128)S(1)}, u32[]{:S(2)}, u32[]{:S(2)}) %collective-permute-start.2) | collective-permute-done | bytes 884768 | tf_op jit(solution)/shard_map/ppermute | solution.py:23
  238.6 2.4 fusion.160
  241.0 2.5 fusion.164
  244.1 2.4 fusion.147
  246.4 2.4 fusion.158
  248.8 2.4 fusion.144
  251.2 2.4 fusion.143
  253.7 2.5 fusion.156
  256.1 2.5 fusion.155
  258.6 2.4 fusion.162
  261.0 2.4 fusion.152
  263.4 2.4 fusion.151
  265.9 19.9 %fusion.17 = f32[2,3,1,8,9216]{4,3,1,0,2:T(8,128)S(1)} fusion(f32[2,3,12,9216]{3,2,1,0:T(8,128)S(1)} %get-tuple-element.20, f32[2,3,12,9216]{3,2,1,0:T(8,128)S(1)} %get-tuple-element.19, f32[2,3,8,9024]{3,2,1,0:T(8,128)} %get-tuple-element.168, f32[2,3,8,192]{3,2,1,0:T(8,128)} %get-tuple-element.170, f32[2,3,8,192]{3,2,1,0:T(8,128)} %get-tuple-element.169, ...), kind=kLoop, calls=%fused_computation.40 | loop fusion | flops 33619968 | bytes 60493880 | tf_op jit(solution)/shard_map/stack | solution.py:78
  285.8 19.9 %fusion.15 = f32[2,3,1,8,9216]{4,3,1,0,2:T(8,128)S(1)} fusion(f32[2,3,12,9216]{3,2,1,0:T(8,128)S(1)} %get-tuple-element.19, f32[2,3,12,9216]{3,2,1,0:T(8,128)S(1)} %get-tuple-element.20, f32[2,3,8,9024]{3,2,1,0:T(8,128)} %get-tuple-element.168, f32[2,3,8,192]{3,2,1,0:T(8,128)} %get-tuple-element.170, f32[2,3,8,192]{3,2,1,0:T(8,128)} %get-tuple-element.169, ...), kind=kLoop, calls=%fused_computation.38 | loop fusion | flops 33619968 | bytes 60493880 | tf_op jit(solution)/shard_map/stack | solution.py:78
  308.2 3.7 collective-permute-start.4
  311.9 35.4 %collective-permute-done.4 = f32[2,3,2,2,9216]{4,3,2,1,0:T(2,128)S(1)} collective-permute-done((f32[2,3,2,2,9216]{4,3,2,1,0:T(2,128)S(1)}, f32[2,3,2,2,9216]{4,3,2,1,0:T(2,128)S(1)}, u32[]{:S(2)}, u32[]{:S(2)}) %collective-permute-start.4) | collective-permute-done | bytes 884768 | tf_op jit(solution)/shard_map/ppermute | solution.py:23
  359.0 2.4 fusion.135
  361.4 2.4 fusion.139
  365.6 2.5 fusion.122
  368.1 2.5 fusion.133
  370.6 2.4 fusion.119
  372.9 2.5 fusion.118
  375.4 2.5 fusion.131
  377.9 2.4 fusion.130
  380.3 2.4 fusion.137
  382.7 2.4 fusion.127
  385.1 2.4 fusion.126
  387.5 20.6 %fusion.21 = f32[2,3,1,8,9216]{4,3,1,0,2:T(8,128)} fusion(f32[2,3,12,9216]{3,2,1,0:T(8,128)S(1)} %get-tuple-element.18, f32[2,3,12,9216]{3,2,1,0:T(8,128)S(1)} %get-tuple-element.17, f32[2,3,8,9024]{3,2,1,0:T(8,128)} %get-tuple-element.118, f32[2,3,8,192]{3,2,1,0:T(8,128)} %get-tuple-element.120, f32[2,3,8,192]{3,2,1,0:T(8,128)} %get-tuple-element.119, ...), kind=kLoop, calls=%fused_computation.44 | loop fusion | flops 33619968 | bytes 60493880 | tf_op jit(solution)/shard_map/stack | solution.py:78
  408.1 20.7 %fusion.19 = f32[2,3,1,8,9216]{4,3,1,0,2:T(8,128)} fusion(f32[2,3,12,9216]{3,2,1,0:T(8,128)S(1)} %get-tuple-element.17, f32[2,3,12,9216]{3,2,1,0:T(8,128)S(1)} %get-tuple-element.18, f32[2,3,8,9024]{3,2,1,0:T(8,128)} %get-tuple-element.118, f32[2,3,8,192]{3,2,1,0:T(8,128)} %get-tuple-element.120, f32[2,3,8,192]{3,2,1,0:T(8,128)} %get-tuple-element.119, ...), kind=kLoop, calls=%fused_computation.42 | loop fusion | flops 33619968 | bytes 60493880 | tf_op jit(solution)/shard_map/stack | solution.py:78
  428.8 4.4 fusion.3
  433.9 4.1 collective-permute-start.6
  438.0 36.8 %collective-permute-done.6 = f32[2,3,2,2,9216]{4,3,2,1,0:T(2,128)S(1)} collective-permute-done((f32[2,3,2,2,9216]{4,3,2,1,0:T(2,128)S(1)}, f32[2,3,2,2,9216]{4,3,2,1,0:T(2,128)S(1)}, u32[]{:S(2)}, u32[]{:S(2)}) %collective-permute-start.6) | collective-permute-done | bytes 884768 | tf_op jit(solution)/shard_map/ppermute | solution.py:23
  486.2 2.4 fusion.110
  488.6 2.4 fusion.114
  492.9 2.5 fusion.97
  495.3 2.5 fusion.108
  497.8 2.5 fusion.94
  500.3 2.4 fusion.93
  502.6 2.4 fusion.106
  505.0 2.4 fusion.105
  507.4 2.5 fusion.112
  509.9 2.4 fusion.102
  512.3 2.4 fusion.101
  514.7 20.7 %fusion.25 = f32[2,3,1,8,9216]{4,3,1,0,2:T(8,128)} fusion(f32[2,3,12,9216]{3,2,1,0:T(8,128)S(1)} %get-tuple-element.16, f32[2,3,12,9216]{3,2,1,0:T(8,128)S(1)} %get-tuple-element.15, f32[2,3,8,9024]{3,2,1,0:T(8,128)} %get-tuple-element.68, f32[2,3,8,192]{3,2,1,0:T(8,128)} %get-tuple-element.70, f32[2,3,8,192]{3,2,1,0:T(8,128)} %get-tuple-element.69, ...), kind=kLoop, calls=%fused_computation.48 | loop fusion | flops 33619968 | bytes 60493880 | tf_op jit(solution)/shard_map/stack | solution.py:78
  535.4 20.7 %fusion.23 = f32[2,3,1,8,9216]{4,3,1,0,2:T(8,128)} fusion(f32[2,3,12,9216]{3,2,1,0:T(8,128)S(1)} %get-tuple-element.15, f32[2,3,12,9216]{3,2,1,0:T(8,128)S(1)} %get-tuple-element.16, f32[2,3,8,9024]{3,2,1,0:T(8,128)} %get-tuple-element.68, f32[2,3,8,192]{3,2,1,0:T(8,128)} %get-tuple-element.70, f32[2,3,8,192]{3,2,1,0:T(8,128)} %get-tuple-element.69, ...), kind=kLoop, calls=%fused_computation.46 | loop fusion | flops 33619968 | bytes 60493880 | tf_op jit(solution)/shard_map/stack | solution.py:78
  556.1 6.7 fusion.5
  564.4 116.8 %all-reduce.3.cloned.1.call-done = f32[2,8,9216]{2,1,0:T(8,128)} async-done(((f32[2,8,9216]{2,1,0:T(8,128)}), f32[2,8,9216]{2,1,0:T(8,128)}) %all-reduce.3.cloned.1.call-update) | async-done | bytes 589840 | tf_op jit(solution)/shard_map/psum | solution.py:126
  681.2 1.9 broadcast_multiply_fusion.1
  (88 shorter events, 48.6 us)
Async XLA Ops:
  6.5 674.6 %all-reduce.3.cloned.1.call-start = ((), (), s32[]{:S(2)}) async-start(), calls=%async_computation | async-start | bytes 1179648 | tf_op jit(solution)/shard_map/psum | solution.py:126
  6.5 79.0 %collective-permute-start = (f32[2,3,2,8,9216]{4,3,2,1,0:T(8,128)}, f32[2,3,2,8,9216]{4,3,2,1,0:T(8,128)}, u32[]{:S(2)}, u32[]{:S(2)}) collective-permute-start(f32[2,3,2,8,9216]{4,3,2,1,0:T(8,128)} %param.7), channel_id=1, source_target_pairs={{0,64},{8,72},{16,80},{24,88},{32,96},{40,104},{48,112},{56,120},{... | collective-permute-start | bytes 10616840 | tf_op jit(solution)/shard_map/ppermute | solution.py:12
  95.0 33.5 %copy-start = (f32[2,3,2,8,9216]{4,1,3,0,2:T(4,128)}, f32[2,3,2,8,9216]{4,1,3,0,2:T(4,128)S(1)}, u32[]{:S(2)}) copy-start(f32[2,3,2,8,9216]{4,1,3,0,2:T(4,128)S(1)} %copy_select_fusion) | copy-start | bytes 10616836
  160.4 6.5 copy-start.1
  188.3 3.2 copy-start.6
  188.4 39.9 %collective-permute-start.2 = (f32[2,3,2,2,9216]{4,3,2,1,0:T(2,128)S(1)}, f32[2,3,2,2,9216]{4,3,2,1,0:T(2,128)S(1)}, u32[]{:S(2)}, u32[]{:S(2)}) collective-permute-start(f32[2,3,2,2,9216]{4,3,2,1,0:T(2,128)S(1)} %copy.56), channel_id=1, source_target_pairs={{1,0},{2,1},{3,2},{4,3},{5,4},{6,5},{7,6},{0,7},{9,8},{10,9},{11,1... | collective-permute-start | bytes 2654216 | tf_op jit(solution)/shard_map/ppermute | solution.py:23
  188.5 39.8 %collective-permute-start.1 = (f32[2,3,2,2,9216]{4,3,2,1,0:T(2,128)S(1)}, f32[2,3,2,2,9216]{4,3,2,1,0:T(2,128)S(1)}, u32[]{:S(2)}, u32[]{:S(2)}) collective-permute-start(f32[2,3,2,2,9216]{4,3,2,1,0:T(2,128)S(1)} %copy.55), channel_id=1, source_target_pairs={{0,1},{1,2},{2,3},{3,4},{4,5},{5,6},{6,7},{7,0},{8,9},{9,10},{10,1... | collective-permute-start | bytes 2654216 | tf_op jit(solution)/shard_map/ppermute | solution.py:22
  244.0 21.8 %copy-start.2 = (f32[2,3,8,9214]{3,2,1,0:T(8,128)}, f32[2,3,8,9214]{3,2,1,0:T(8,128)S(1)}, u32[]{:S(2)}) copy-start(f32[2,3,8,9214]{3,2,1,0:T(8,128)S(1)} %get-tuple-element.136) | copy-start | bytes 5307268
  263.4 2.4 copy-start.4
  263.4 2.4 copy-start.5
  308.2 39.1 %collective-permute-start.4 = (f32[2,3,2,2,9216]{4,3,2,1,0:T(2,128)S(1)}, f32[2,3,2,2,9216]{4,3,2,1,0:T(2,128)S(1)}, u32[]{:S(2)}, u32[]{:S(2)}) collective-permute-start(f32[2,3,2,2,9216]{4,3,2,1,0:T(2,128)S(1)} %copy.60), channel_id=1, source_target_pairs={{1,0},{2,1},{3,2},{4,3},{5,4},{6,5},{7,6},{0,7},{9,8},{10,9},{11,1... | collective-permute-start | bytes 2654216 | tf_op jit(solution)/shard_map/ppermute | solution.py:23
  311.9 36.6 %collective-permute-start.3 = (f32[2,3,2,2,9216]{4,3,2,1,0:T(2,128)S(1)}, f32[2,3,2,2,9216]{4,3,2,1,0:T(2,128)S(1)}, u32[]{:S(2)}, u32[]{:S(2)}) collective-permute-start(f32[2,3,2,2,9216]{4,3,2,1,0:T(2,128)S(1)} %copy.59), channel_id=1, source_target_pairs={{0,1},{1,2},{2,3},{3,4},{4,5},{5,6},{6,7},{7,0},{8,9},{9,10},{10,1... | collective-permute-start | bytes 2654216 | tf_op jit(solution)/shard_map/ppermute | solution.py:22
  433.9 40.9 %collective-permute-start.6 = (f32[2,3,2,2,9216]{4,3,2,1,0:T(2,128)S(1)}, f32[2,3,2,2,9216]{4,3,2,1,0:T(2,128)S(1)}, u32[]{:S(2)}, u32[]{:S(2)}) collective-permute-start(f32[2,3,2,2,9216]{4,3,2,1,0:T(2,128)S(1)} %copy.64), channel_id=1, source_target_pairs={{1,0},{2,1},{3,2},{4,3},{5,4},{6,5},{7,6},{0,7},{9,8},{10,9},{11,1... | collective-permute-start | bytes 2654216 | tf_op jit(solution)/shard_map/ppermute | solution.py:23
  438.0 37.8 %collective-permute-start.5 = (f32[2,3,2,2,9216]{4,3,2,1,0:T(2,128)S(1)}, f32[2,3,2,2,9216]{4,3,2,1,0:T(2,128)S(1)}, u32[]{:S(2)}, u32[]{:S(2)}) collective-permute-start(f32[2,3,2,2,9216]{4,3,2,1,0:T(2,128)S(1)} %copy.63), channel_id=1, source_target_pairs={{0,1},{1,2},{2,3},{3,4},{4,5},{5,6},{6,7},{7,0},{8,9},{9,10},{10,1... | collective-permute-start | bytes 2654216 | tf_op jit(solution)/shard_map/ppermute | solution.py:22
  556.1 6.7 copy-start.3
Sparse Core Ops, SparseCore 0:
  564.5 116.6 all-reduce.2
where the time goes:
time: 702 us; the launch traced here: 690 us
  waiting for transfers between devices  298 us (42%)
  other arithmetic  159 us (23%)
  local copies, waits for them, and re-layouts  119 us (17%)
  matrix products  65.4 us (9%)
  blocking collectives  21.7 us (3%)
  between operations  14.2 us (2%)
  starting transfers between devices  13.3 us (2%)
    another operation x6, other arithmetic, apply_operator(): return jnp.stack([out_real, out_imag], 2)  123 us
    psum x1, waiting for transfers between devices, on_device(): total = lax.psum(stacked, 'ka')  117 us
    ppermute x3, waiting for transfers between devices, extended(): after = lax.ppermute(initial, axis, down)  108 us
    ppermute x1, waiting for transfers between devices, from_behind(): lax.ppermute(value, axis, [(i, (i + by) % peers) for i in range(peers)])  71 us
    slice x24, local copies, waits for them, and re-layouts, shift_x(): wrapped = jnp.roll(field, width - offset, -1)  37.3 us
    slice x24, local copies, waits for them, and re-layouts, shift_x(): main = jnp.roll(field, -offset, -1)  34.4 us
    psum x1, blocking collectives, on_device(): summed_real, summed_imag = lax.psum((part_real, part_imag), 'grid')  21.7 us
    slice x12, local copies, waits for them, and re-layouts, derivatives(): y_plus_one = jnp.roll(middle, -NX, -1)  18.7 us
  transfers between devices with their start and end apart: 8, of which 7 were waited for; matrix products, arithmetic and copies ran while one was open for 1% of the time, Pallas kernels for 0%

commit v1 on v0

v1 whole, which is shorter than its diff:
```python
import functools

import jax
import jax.numpy as jnp
from jax import lax
from jax.experimental import pallas as pl
from jax.experimental.pallas import tpu as pltpu
from jax.sharding import Mesh
from jax.sharding import PartitionSpec as P

NX = 96
ITERS = 4
ROWS = 24
CHUNK = ROWS * NX
GROUP = 4 * NX
F32 = jnp.float32
ZAX = ("zl", "zh")
PIECE = CHUNK // 2


def z_perm(to):
    index = lambda z: (z & 1) * 2 + (z >> 1)
    return [(index(z), index(to(z))) for z in range(4)]


def z_xor(value, m):
    return lax.ppermute(value, ZAX, z_perm(lambda z: z ^ m))


def z_ring(value, by):
    return lax.ppermute(value, ZAX, z_perm(lambda z: (z + by) % 4))


def y_ring(value, by):
    return lax.ppermute(value, "y", [(i, (i + by) % 4) for i in range(4)])


def lane_ids():
    return lax.broadcasted_iota(jnp.int32, (8, 128), 1)


def unpack_rows(a, b, c, lanes):
    r0 = a
    r1 = jnp.where(lanes < 32, pltpu.roll(a, 32, 1), pltpu.roll(b, 32, 1))
    r2 = jnp.where(lanes < 64, pltpu.roll(b, 64, 1), pltpu.roll(c, 64, 1))
    r3 = pltpu.roll(c, 96, 1)
    return r0, r1, r2, r3


def pack_rows(r0, r1, r2, r3, lanes):
    r1s = pltpu.roll(r1, 96, 1)
    r2s = pltpu.roll(r2, 64, 1)
    r3s = pltpu.roll(r3, 32, 1)
    return (
        jnp.where(lanes < 96, r0, r1s),
        jnp.where(lanes < 64, r1s, r2s),
        jnp.where(lanes < 32, r2s, r3s),
    )


def wrap_x(value, lanes):
    return jnp.where(
        lanes < 96, value, jnp.where(lanes < 112, pltpu.roll(value, 96, 1), pltpu.roll(value, 32, 1))
    )


def perturbed(field, pert_r, pert_i):
    re, im = field
    return pert_r * re - pert_i * im, pert_r * im + pert_i * re


def products_kernel(slot_ref, o0, o1, o2, o3, p0, p1, out_ref, acc_ref):
    step = pl.program_id(0)

    @pl.when(step == 0)
    def _():
        acc_ref[...] = jnp.zeros_like(acc_ref)

    slabs = (((o0, o1), p0), ((o2, o3), p1))
    for k in range(4):
        block, kk = k // 2, k % 2
        slot = slot_ref[k]
        acc = [acc_ref[k * 18 + i] for i in range(18)]
        for pair, pert in slabs:
            own, mate = pair[block], pair[1 - block]
            for v in range(3):
                at = pl.ds(v * 128, 128)
                pr, pi = pert[1, :, at], pert[2, :, at]
                w = [perturbed((own[kk, n, 0, :, at], own[kk, n, 1, :, at]), pr, pi) for n in range(3)]
                for m in range(3):
                    mr, mi = mate[slot, m, 0, :, at], mate[slot, m, 1, :, at]
                    for n in range(3):
                        i = (m * 3 + n) * 2
                        acc[i] = acc[i] + (mr * w[n][0] + mi * w[n][1])
                        acc[i + 1] = acc[i + 1] + (mr * w[n][1] - mi * w[n][0])
        for i in range(18):
            acc_ref[k * 18 + i] = acc[i]

    @pl.when(step == pl.num_programs(0) - 1)
    def _():
        for i in range(72):
            out_ref[pl.ds(i, 1), :] = jnp.sum(acc_ref[i], axis=0, keepdims=True)


def orbital_specs():
    block = pl.BlockSpec((2, 3, 2, 8, GROUP), lambda i: (0, 0, 0, 0, i))
    pert = pl.BlockSpec((3, 8, GROUP), lambda i: (0, 0, i))
    return [block] * 4 + [pert] * 2


def products(slots, fields, perts):
    return pl.pallas_call(
        products_kernel,
        grid=(CHUNK // GROUP,),
        in_specs=[pl.BlockSpec(memory_space=pltpu.SMEM)] + orbital_specs(),
        out_specs=pl.BlockSpec((72, 128), lambda i: (0, 0)),
        out_shape=jax.ShapeDtypeStruct((72, 128), F32),
        scratch_shapes=[pltpu.VMEM((72, 8, 128), F32)],
        cost_estimate=pl.CostEstimate(flops=20_000_000, bytes_accessed=4_000_000, transcendentals=0),
        name="products",
    )(slots, *fields, *perts)


def right_kernel(ncells, slot_ref, half_ref, s0, s1, s2, s3, o0, o1, o2, o3, p0, p1, r_ref, orb_ref, v_ref, prod_ref):
    @pl.when(pl.program_id(0) == 0)
    def _():
        total = (s0[...] + s1[...]) + (s2[...] + s3[...])
        ones = jnp.full((128, 128), 1.0, F32)
        prod_ref[...] = jnp.dot(total, ones, precision=lax.Precision.HIGHEST, preferred_element_type=F32) / ncells

    lanes = lane_ids()
    half = half_ref[0]
    slabs = (((o0, o1), p0, half), ((o2, o3), p1, 1 - half))
    for pair, pert, z in slabs:
        planes = pl.ds(pl.multiple_of(z * 8, 8), 8)
        rows = unpack_rows(*[pert[0, :, pl.ds(v * 128, 128)] for v in range(3)], lanes)
        for j in range(4):
            v_ref[j, planes, :] = rows[j]
        for k in range(4):
            block, kk = k // 2, k % 2
            slot = slot_ref[k]
            own, mate = pair[block], pair[1 - block]
            right = [[[], []] for _ in range(3)]
            for v in range(3):
                at = pl.ds(v * 128, 128)
                pr, pi = pert[1, :, at], pert[2, :, at]
                mates = [(mate[slot, m, 0, :, at], mate[slot, m, 1, :, at]) for m in range(3)]
                for n in range(3):
                    wr, wi = perturbed((own[kk, n, 0, :, at], own[kk, n, 1, :, at]), pr, pi)
                    gr, gi = -wr, -wi
                    for m in range(3):
                        row = k * 18 + (m * 3 + n) * 2
                        qr = prod_ref[pl.ds(row, 1), :]
                        qi = prod_ref[pl.ds(row + 1, 1), :]
                        mr, mi = mates[m]
                        gr = gr + (qr * mr - qi * mi)
                        gi = gi + (qi * mr + qr * mi)
                    right[n][0].append(gr)
                    right[n][1].append(gi)
            for n in range(3):
                for c in range(2):
                    rows = unpack_rows(*right[n][c], lanes)
                    orb = unpack_rows(*[own[kk, n, c, :, pl.ds(v * 128, 128)] for v in range(3)], lanes)
                    for j in range(4):
                        r_ref[k * 3 + n, c, j, planes, :] = wrap_x(rows[j], lanes)
                        orb_ref[k * 3 + n, c, j, planes, :] = orb[j]


def right_sides(ncells, slots, half, sums, fields, perts):
    smem = pl.BlockSpec(memory_space=pltpu.SMEM)
    whole = pl.BlockSpec((72, 128), lambda i: (0, 0))
    rows = pl.BlockSpec((12, 2, 4, 16, 128), lambda i: (0, 0, i, 0, 0))
    shape = jax.ShapeDtypeStruct((12, 2, ROWS, 16, 128), F32)
    return pl.pallas_call(
        functools.partial(right_kernel, ncells),
        grid=(CHUNK // GROUP,),
        in_specs=[smem, smem] + [whole] * 4 + orbital_specs(),
        out_specs=[rows, rows, pl.BlockSpec((4, 16, 128), lambda i: (i, 0, 0))],
        out_shape=[shape, shape, jax.ShapeDtypeStruct((ROWS, 16, 128), F32)],
        scratch_shapes=[pltpu.VMEM((72, 128), F32)],
        cost_estimate=pl.CostEstimate(flops=20_000_000, bytes_accessed=14_000_000, transcendentals=0),
        name="right_sides",
    )(slots, half, *sums, *fields, *perts)


def step_kernel(last, coef_ref, u_ref, r_ref, v_ref, zm, zp, ym, yp, *refs):
    if last:
        orb_ref, out_ref, dens_ref, pad = refs
    else:
        out_ref, pad = refs
    kn = pl.program_id(0)
    coef = [coef_ref[kn * 16 + i] for i in range(9)]
    diag, minus_wt, wt, c1, c2, kx, ky, kz, scale = coef
    for c in range(2):
        pad[c, 2:26, 8:24, :] = u_ref[0, c] * scale
        pad[c, 2:26, 6:8, :] = zm[0, c] * scale
        pad[c, 2:26, 24:26, :] = zp[0, c] * scale
        pad[c, 0:2, 8:24, :] = ym[0, c] * scale
        pad[c, 26:28, 8:24, :] = yp[0, c] * scale
    lanes = lax.broadcasted_iota(jnp.int32, (16, 128), 1)

    if last:
        @pl.when(kn == 0)
        def _():
            dens_ref[...] = jnp.zeros_like(dens_ref)

    def row(r, carry):
        cells, first, second, grad = [], [], [], []
        for c in range(2):
            u = pad[c, r + 2, 8:24, :]
            xp1, xm1 = pltpu.roll(u, 127, 1), pltpu.roll(u, 1, 1)
            xp2, xm2 = pltpu.roll(u, 126, 1), pltpu.roll(u, 2, 1)
            yp1, ym1 = pad[c, r + 3, 8:24, :], pad[c, r + 1, 8:24, :]
            yp2, ym2 = pad[c, r + 4, 8:24, :], pad[c, r, 8:24, :]
            zp1, zm1 = pad[c, r + 2, 9:25, :], pad[c, r + 2, 7:23, :]
            zp2, zm2 = pad[c, r + 2, 10:26, :], pad[c, r + 2, 6:22, :]
            cells.append(u)
            first.append((xp1 + xm1) + (yp1 + ym1) + (zp1 + zm1))
            second.append((xp2 + xm2) + (yp2 + ym2) + (zp2 + zm2))
            gx = (xp1 - xm1) - 0.125 * (xp2 - xm2)
            gy = (yp1 - ym1) - 0.125 * (yp2 - ym2)
            gz = (zp1 - zm1) - 0.125 * (zp2 - zm2)
            grad.append(kx * gx + ky * gy + kz * gz)
        center = diag + minus_wt * v_ref[r]
        new = []
        for c in range(2):
            value = center * cells[c] + wt * r_ref[0, c, r] + (c1 * first[c] + c2 * second[c])
            value = value - grad[1] if c == 0 else value + grad[0]
            new.append(value)
        if last:
            orb_r, orb_i = orb_ref[0, 0, r], orb_ref[0, 1, r]
            dens_ref[0, r] += orb_r * new[0] + orb_i * new[1]
            dens_ref[1, r] += orb_r * new[1] - orb_i * new[0]
        else:
            for c in range(2):
                wrapped = jnp.where(
                    lanes < 96,
                    new[c],
                    jnp.where(lanes < 112, pltpu.roll(new[c], 96, 1), pltpu.roll(new[c], 32, 1)),
                )
                out_ref[0, c, r] = wrapped
        return carry

    lax.fori_loop(0, ROWS, row, 0, unroll=2)

    if last:
        @pl.when(kn == pl.num_programs(0) - 1)
        def _():
            ids = lane_ids()
            for c in range(2):
                for z in range(2):
                    for g in range(6):
                        rows = [dens_ref[c, 4 * g + j, 8 * z : 8 * z + 8, :] * (1.0 / 32.0) for j in range(4)]
                        packed = pack_rows(*rows, ids)
                        for v in range(3):
                            at = (g % 3) * GROUP + v * 128
                            out_ref[(c * 2 + g // 3) * 2 + z, :, at : at + 128] = packed[v]


def richardson_step(coef, u, right, pot, halos, orb=None):
    last = orb is not None
    field = pl.BlockSpec((1, 2, ROWS, 16, 128), lambda i: (i, 0, 0, 0, 0))
    zspec = pl.BlockSpec((1, 2, ROWS, 2, 128), lambda i: (i, 0, 0, 0, 0))
    yspec = pl.BlockSpec((1, 2, 2, 16, 128), lambda i: ((i + 6) % 12, 0, 0, 0, 0))
    vspec = pl.BlockSpec((ROWS, 16, 128), lambda i: (0, 0, 0))
    scratch = [pltpu.VMEM((2, ROWS + 4, 32, 128), F32)]
    if last:
        out_spec = pl.BlockSpec((8, 8, PIECE), lambda i: (0, 0, 0))
        out_shape = jax.ShapeDtypeStruct((8, 8, PIECE), F32)
        scratch = [pltpu.VMEM((2, ROWS, 16, 128), F32)] + scratch
    else:
        out_spec, out_shape = field, jax.ShapeDtypeStruct((12, 2, ROWS, 16, 128), F32)
    return pl.pallas_call(
        functools.partial(step_kernel, last),
        grid=(12,),
        in_specs=[pl.BlockSpec(memory_space=pltpu.SMEM), field, field, vspec, zspec, zspec, yspec, yspec]
        + ([field] if last else []),
        out_specs=out_spec,
        out_shape=out_shape,
        scratch_shapes=scratch,
        cost_estimate=pl.CostEstimate(flops=40_000_000, bytes_accessed=16_000_000, transcendentals=0),
        name="last_step" if last else "step",
    )(coef, u, right, pot, *halos, *([orb] if last else []))


def assemble_kernel(pos_ref, b0, b1, b2, b3, out_ref):
    x, z = pos_ref[0], pos_ref[1]
    for d, block in enumerate((b0, b1, b2, b3)):
        part = x ^ d
        for m in range(4):
            q = z ^ m
            at = pl.multiple_of(q * CHUNK + (part & 1) * PIECE, 128)
            out_ref[part >> 1, :, pl.ds(at, PIECE)] = block[m]


def assemble(pos, blocks):
    return pl.pallas_call(
        assemble_kernel,
        in_specs=[pl.BlockSpec(memory_space=pltpu.SMEM)] + [pl.BlockSpec(memory_space=pltpu.VMEM)] * 4,
        out_specs=pl.BlockSpec(memory_space=pltpu.VMEM),
        out_shape=jax.ShapeDtypeStruct((2, 8, 4 * CHUNK), F32),
        name="assemble",
    )(pos, *blocks)


def exchange(field):
    zm = y_ring(field[:, :, :, 14:16, :], 1)
    zp = y_ring(field[:, :, :, 0:2, :], 3)
    ym = z_ring(field[:, :, ROWS - 2 :], 1)
    yp = z_ring(field[:, :, :2], 3)
    return zm, zp, ym, yp


def on_device(orbitals, partner_map, wave_vectors, levels, potential, perturbation, step_weights):
    zl, zh = lax.axis_index("zl"), lax.axis_index("zh")
    x, core = lax.axis_index("x"), lax.axis_index("c")
    z = zh * 2 + zl
    ncells = 64 * 4 * CHUNK

    def chunk(array, q):
        return lax.dynamic_slice_in_dim(array, q * CHUNK, CHUNK, axis=array.ndim - 1)

    pots = jnp.concatenate([potential[None], perturbation], 0)
    moved = [z_xor(chunk(orbitals, z ^ m), m) for m in (1, 2, 3)]
    fields = [chunk(orbitals, z)] + moved
    perts = [chunk(pots, z), z_xor(chunk(pots, z ^ 3), 3)]
    slot = (partner_map % 2).astype(F32)
    mine = jnp.concatenate([wave_vectors, levels, slot[:, None], jnp.zeros((2, 1), F32)], 1)
    other = z_xor(mine, 1)
    both = jnp.concatenate([mine, other], 0)
    slots = both[:, 6].astype(jnp.int32)

    weights = step_weights.astype(F32) / 100.0
    wave = jnp.repeat(both[:, :3], 3, axis=0)
    level = both[:, 3:6].reshape(12)
    square = wave[:, 0] * wave[:, 0] + wave[:, 1] * wave[:, 1] + wave[:, 2] * wave[:, 2]
    base = 3.75 + 0.5 * square + level

    def coefficients(count):
        wt = weights[count]
        one = jnp.ones((12,), F32)
        scale = weights[0] if count == 1 else jnp.float32(1.0)
        cols = [
            1.0 - wt * base,
            -wt * one,
            wt * one,
            (wt * 2.0 / 3.0) * one,
            (-wt / 24.0) * one,
            (wt * 2.0 / 3.0) * wave[:, 0],
            (wt * 2.0 / 3.0) * wave[:, 1],
            (wt * 2.0 / 3.0) * wave[:, 2],
            scale * one,
        ]
        cols += [jnp.zeros((12,), F32)] * 7
        return jnp.stack(cols, 1).reshape(-1)

    part = products(slots, fields, perts)

    def swapped(value):
        return jnp.concatenate([value[36:], value[:36]], 0)

    part = part + swapped(z_xor(part, 1)) + z_xor(part, 2) + swapped(z_xor(part, 3))
    sums = [part] + [y_ring(part, by) for by in (1, 2, 3)]
    right, orb, pot = right_sides(float(ncells), slots, zh[None].astype(jnp.int32), sums, fields, perts)
    u = right
    for count in range(1, ITERS):
        halos = exchange(u)
        u = richardson_step(coefficients(count), u, right, pot, halos, orb if count == ITERS - 1 else None)

    me = x * 2 + core
    piece = lax.dynamic_index_in_dim(u, me, 0, keepdims=False)
    for m in range(1, 8):
        send = lax.dynamic_index_in_dim(u, me ^ m, 0, keepdims=False)
        piece = piece + lax.ppermute(send, ("x", "c"), [(i, i ^ m) for i in range(8)])
    got = [piece]
    for m in (1, 2, 3):
        pairs = []
        for zz in range(4):
            to = zz ^ m
            c = to >> 1
            index = lambda w: (w & 1) * 4 + c * 2 + (w >> 1)
            pairs.append((index(zz), index(to)))
        got.append(lax.ppermute(piece, ("zl", "c", "zh"), pairs))
    slab = jnp.stack(got)
    same = core == zh
    blocks = []
    for d in range(4):
        index = lambda xx, c, h: xx * 4 + c * 2 + h
        across = lax.ppermute(slab, ("x", "c", "zh"), [(index(i, h, h), index(i ^ d, 1 - h, h)) for i in range(4) for h in range(2)])
        straight = slab
        if d:
            straight = lax.ppermute(slab, ("x", "c", "zh"), [(index(i, h, h), index(i ^ d, h, h)) for i in range(4) for h in range(2)])
        blocks.append(jnp.where(same, straight, across))
    return assemble(jnp.stack([x, z]).astype(jnp.int32), blocks)


def solution(mesh):
    fine = Mesh(mesh.devices.reshape(2, 4, 2, 4, 2), ("zl", "x", "c", "y", "zh"))
    ka, grid = ("zl", "x", "c"), ("y", "zh")
    return jax.shard_map(
        on_device,
        mesh=fine,
        in_specs=(
            P(ka, None, None, grid, None),
            P(ka),
            P(ka, None),
            P(ka, None),
            P(grid, None),
            P(None, grid, None),
            P(),
        ),
        out_specs=P(None, grid, None),
        check_vma=False,
    )
```

time: 702 us -> 308 us (0.44); the launches traced: 690 us -> 307 us
  waiting for transfers between devices: 298 us -> 59.5 us
  other arithmetic: 159 us -> 13.1 us
  Pallas kernels: 0 us -> 111 us
  matrix products: 65.4 us -> 0 us
  local copies, waits for them, and re-layouts: 119 us -> 58.9 us
  starting transfers between devices: 13.3 us -> 60.2 us
  blocking collectives: 21.7 us -> 0 us
  between operations: 14.2 us -> 4.15 us
    another operation x8 -> x2, other arithmetic: 128 us -> 0.68 us  [the longest x1 0.67 us: on_device(): return assemble(jnp.stack([x, z]).astype(jnp.int32), blocks)]
    ppermute x7 -> x40, waiting for transfers between devices: 181 us -> 59.5 us  [the longest x8 40 us: z_xor(): return lax.ppermute(value, ZAX, z_perm(lambda z: z ^ m))]
    psum x1 -> x0, waiting for transfers between devices: 117 us -> none  [on_device(): total = lax.psum(stacked, 'ka')]
    pallas_call x0 -> x6, Pallas kernels: none -> 111 us  [the longest x3 80.9 us: richardson_step(): pl.pallas_call(functools.partial(step_kernel, last), grid=(12,), in_specs...]
    slice x82 -> x11, local copies, waits for them, and re-layouts: 112 us -> 12.9 us  [the longest x3 8.53 us: exchange(): zp = y_ring(field[:, :, :, 0:2, :], 3)]
    dot_general x8 -> x0, matrix products: 65.4 us -> none  [the longest x1 11.2 us: on_device(): jnp.einsum('kmzc,knzc->kmn', mate_real, w_imag, precision=highest)]
    ppermute x7 -> x40, starting transfers between devices: 13.3 us -> 60.2 us  [the longest x7 15.6 us: on_device(): lax.ppermute(send, ('x', 'c'), [(i, i ^ m) for i in range(8)])]
    psum x1 -> x0, blocking collectives: 21.7 us -> none  [on_device(): summed_real, summed_imag = lax.psum((part_real, part_imag), 'grid')]
  transfers between devices with their start and end apart: 8 -> 40, of which waited for: 7 -> 9; matrix products, arithmetic and copies ran while one was open for 1% -> 16% of each run, Pallas kernels for 0% -> 0%
where the time goes in v1:
time: 308 us; the launch traced here: 307 us
  Pallas kernels  111 us (36%)
  starting transfers between devices  60.2 us (20%)
  waiting for transfers between devices  59.5 us (19%)
  local copies, waits for them, and re-layouts  58.9 us (19%)
  other arithmetic  13.1 us (4%)
  between operations  4.15 us (1%)
    pallas_call x3, Pallas kernels, richardson_step(): pl.pallas_call(functools.partial(step_kernel, last), grid=(12,), in_specs...  80.9 us
    ppermute x8, waiting for transfers between devices, z_xor(): return lax.ppermute(value, ZAX, z_perm(lambda z: z ^ m))  40 us
    pallas_call x1, Pallas kernels, right_sides(): pl.pallas_call(functools.partial(right_kernel, ncells), grid=(CHUNK // GR...  22.8 us
    ppermute x4, waiting for transfers between devices, on_device(): lax.ppermute(slab, ('x', 'c', 'zh'), [(index(i, h, h), index(i ^ d, 1 - h...  16.7 us
    ppermute x7, starting transfers between devices, on_device(): lax.ppermute(send, ('x', 'c'), [(i, i ^ m) for i in range(8)])  15.6 us
    ppermute x9, starting transfers between devices, y_ring(): return lax.ppermute(value, 'y', [(i, (i + by) % 4) for i in range(4)])  13.3 us
    ppermute x8, starting transfers between devices, z_xor(): return lax.ppermute(value, ZAX, z_perm(lambda z: z ^ m))  12.3 us
    another operation x13, local copies, waits for them, and re-layouts, coefficients(): return jnp.stack(cols, 1).reshape(-1)  11.2 us
  transfers between devices with their start and end apart: 40, of which 9 were waited for; matrix products, arithmetic and copies ran while one was open for 16% of the time, Pallas kernels for 0%

profile of v1, /device:TPU:1, one launch (start us, length us, event | category | flops | bytes accessed | tf_op | source)
XLA Modules:
  0.0 306.9 jit_solution(10760748413231493574)
XLA Ops:
  0.0 3.6 %constant_dynamic-slice_fusion = (f32[2,3,2,8,2304]{4,3,2,1,0:T(8,128)S(1)}, f32[2,3,2,8,2304]{4,3,2,1,0:T(8,128)}, f32[2,3,2,8,2304]{4,3,2,1,0:T(8,128)}, f32[2,3,2,8,2304]{4,3,2,1,0:T(8,128)}) fusion(f32[2,3,2,8,9216]{4,3,2,1,0:T(8,128)} %param.7, s32[]{:T(128)S(6)} %select_n.71, s32[]{:T(128)S(6)} %select_n.69, s32[]{:T(128)S(6)} %select_n.68, ...), kind=kLoop, calls=%fused_computation.28 | loop fusion | bytes 7077904 | tf_op jit(solution)/shard_map/dynamic_slice | solution.py:321
  3.6 2.5 collective-permute-start.1
  6.1 3.3 %collective-permute-start.2 = (f32[2,3,2,8,2304]{4,3,2,1,0:T(8,128)}, f32[2,3,2,8,2304]{4,3,2,1,0:T(8,128)S(1)}, u32[]{:S(2)}, u32[]{:S(2)}) collective-permute-start(f32[2,3,2,8,2304]{4,3,2,1,0:T(8,128)} %get-tuple-element.28), channel_id=1, source_target_pairs={{0,1},{64,65},{1,0},{65,64},{2,3},{66,67},{3,2},{67,66},{4,5},{68,... | collective-permute-start | bytes 2654216 | tf_op jit(solution)/shard_map/ppermute | solution.py:27
  10.7 1.8 fusion
  12.5 2.7 collective-permute-start.4
  15.2 29.4 %collective-permute-done = f32[2,8]{1,0:T(2,128)S(1)} collective-permute-done((f32[2,8]{1,0:T(2,128)S(1)}, f32[2,8]{1,0:T(2,128)S(1)}, u32[]{:S(2)}, u32[]{:S(2)}) %collective-permute-start) | collective-permute-done | bytes 96 | tf_op jit(solution)/shard_map/ppermute | solution.py:27
  45.5 8.7 %collective-permute-done.4.p1 = f32[3,8,2304]{2,1,0:T(8,128)S(1)} collective-permute-done((f32[3,8,2304]{2,1,0:T(8,128)S(1)}, f32[3,8,2304]{2,1,0:T(8,128)S(1)}, u32[]{:S(2)}, u32[]{:S(2)}) %collective-permute-start.4) | collective-permute-done | bytes 221216 | tf_op jit(solution)/shard_map/ppermute | solution.py:27
  55.9 5.4 %products.1 = f32[72,128]{1,0:T(8,128)} custom-call(s32[4]{0:T(128)} %convert_reduce_fusion.slot_ref, f32[2,3,2,8,2304]{4,3,2,1,0:T(8,128)} %get-tuple-element.27.o0, f32[2,3,2,8,2304]{4,3,2,1,0:T(8,128)} %copy-done, f32[2,3,2,8,2304]{4,3,2,1,0:T(8,128)} %copy-done.1, f32[2,3,2,8,2304]{4,3,2,1,0:T(8,128)} %copy-done.2, f32[3,8,2304]{2,1,0:T(8,128)} %get-tuple-element.30.p0, ...), custom_call_target="tpu_custom_call" | custom-call | flops 20000000 | bytes 4000000 | tf_op jit(solution)/shard_map/products/pallas_call | solution.py:112
  62.0 1.5 collective-permute-start.6
  63.4 2.4 collective-permute-start.7
  65.8 1.8 collective-permute-done.7
  68.4 1.4 collective-permute-start.8
  69.8 2.6 collective-permute-start.9
  77.3 22.8 %right_sides.1 = (f32[12,2,24,16,128]{4,3,2,1,0:T(8,128)}, f32[12,2,24,16,128]{4,3,2,1,0:T(8,128)}, f32[24,16,128]{2,1,0:T(8,128)}) custom-call(s32[4]{0:T(128)} %convert_reduce_fusion.slot_ref, s32[1]{0:T(128)} %bitcast.7.half_ref, f32[72,128]{1,0:T(8,128)} %copy-done.13, f32[72,128]{1,0:T(8,128)} %copy-done.14, f32[72,128]{1,0:T(8,128)} %copy-done.15, ...), custom_call_target="tpu_custom_call" | custom-call | flops 20000000 | bytes 14000000 | tf_op jit(solution)/shard_map/right_sides/pallas_call | solution.py:174
  100.1 2.8 fusion.18
  103.4 2.3 collective-permute-start.12
  105.7 1.2 fusion.17
  107.2 2.5 collective-permute-start.14
  110.6 1.9 broadcast_multiply_fusion
  112.5 1.3 copy.46
  116.5 1.2 mul.150.clone
  118.9 1.3 stack.92
  120.8 1.5 stack.93
  122.3 1.3 reshape.23.coef_ref
  124.8 30.1 %step.2.u_ref = f32[12,2,24,16,128]{4,3,2,1,0:T(8,128)} custom-call(f32[192]{0:T(256)} %reshape.23.coef_ref, f32[12,2,24,16,128]{4,3,2,1,0:T(8,128)} %get-tuple-element.8.u_ref.r_ref, f32[12,2,24,16,128]{4,3,2,1,0:T(8,128)} %get-tuple-element.8.u_ref.r_ref, f32[24,16,128]{2,1,0:T(8,128)} %get-tuple-element.9.v_ref, f32[12,2,24,2,128]{4,3,2,1,0:T(2,128)} %copy-done.6, ...), custom_call_target="tpu_custom_call" | custom-call | flops 40000000 | bytes 16000000 | tf_op jit(solution)/shard_map/step/pallas_call | solution.py:273
  154.9 2.8 fusion.16
  157.9 2.7 collective-permute-start.16
  160.5 1.2 fusion.15
  161.8 2.7 collective-permute-start.18
  165.0 2.4 multiply_subtract_fusion.1
  167.4 1.3 copy.39
  168.7 1.3 copy.42
  170.0 1.3 copy.43
  171.3 1.4 copy.44
  173.2 1.1 mul.145.clone
  176.2 1.5 stack.88
  177.7 1.4 reshape.22.coef_ref
  180.8 30.1 %step.3.u_ref = f32[12,2,24,16,128]{4,3,2,1,0:T(8,128)} custom-call(f32[192]{0:T(256)} %reshape.22.coef_ref, f32[12,2,24,16,128]{4,3,2,1,0:T(8,128)} %step.2.u_ref, f32[12,2,24,16,128]{4,3,2,1,0:T(8,128)} %get-tuple-element.8.u_ref.r_ref, f32[24,16,128]{2,1,0:T(8,128)} %get-tuple-element.9.v_ref, f32[12,2,24,2,128]{4,3,2,1,0:T(2,128)} %copy-done.8, ...), custom_call_target="tpu_custom_call" | custom-call | flops 40000000 | bytes 16000000 | tf_op jit(solution)/shard_map/step/pallas_call | solution.py:273
  210.9 2.8 fusion.14
  213.9 2.7 collective-permute-start.20
  216.5 1.2 fusion.13
  217.8 2.7 collective-permute-start.22
  221.1 1.3 copy.32
  222.4 1.3 copy.35
  223.7 1.3 copy.36
  225.0 1.3 copy.37
  226.9 1.2 mul.136.clone
  229.3 1.5 stack.84
  230.8 1.4 reshape.21.coef_ref
  233.3 20.6 %last_step.1 = f32[8,8,1152]{2,1,0:T(8,128)} custom-call(f32[192]{0:T(256)} %reshape.21.coef_ref, f32[12,2,24,16,128]{4,3,2,1,0:T(8,128)} %step.3.u_ref, f32[12,2,24,16,128]{4,3,2,1,0:T(8,128)} %get-tuple-element.8.u_ref.r_ref, f32[24,16,128]{2,1,0:T(8,128)} %get-tuple-element.9.v_ref, f32[12,2,24,2,128]{4,3,2,1,0:T(2,128)} %copy-done.4, ...), custom_call_target="tpu_custom_call" | custom-call | flops 40000000 | bytes 16000000 | tf_op jit(solution)/shard_map/last_step/pallas_call | solution.py:273
  254.8 10.1 %collective-permute-start.29 = (f32[8,1152]{1,0:T(8,128)S(1)}, f32[8,1152]{1,0:T(8,128)S(1)}, u32[]{:S(2)}, u32[]{:S(2)}) collective-permute-start(f32[8,1152]{1,0:T(8,128)S(1)} %get-tuple-element.32), channel_id=1, source_target_pairs={{0,56},{8,48},{16,40},{24,32},{32,24},{40,16},{48,8},{56,0},{1,57}... | collective-permute-start | bytes 110600 | tf_op jit(solution)/shard_map/ppermute | solution.py:374
  265.8 2.4 collective-permute-start.26
  268.6 1.5 collective-permute-start.24
  270.4 1.7 collective-permute-done.25
  273.5 1.6 collective-permute-start.32
  275.2 1.3 collective-permute-start.31
  278.2 1.3 collective-permute-start.35
  280.2 1.3 collective-permute-start.33
  282.1 1.3 collective-permute-start.37
  284.1 6.6 %collective-permute-done.35 = f32[4,8,1152]{2,1,0:T(8,128)S(1)} collective-permute-done((f32[4,8,1152]{2,1,0:T(8,128)S(1)}, f32[4,8,1152]{2,1,0:T(8,128)S(1)}, u32[]{:S(2)}, u32[]{:S(2)}) %collective-permute-start.35) | collective-permute-done | bytes 147488 | tf_op jit(solution)/shard_map/ppermute | solution.py:389
  290.7 1.3 collective-permute-start.39
  292.7 5.8 %collective-permute-done.37 = f32[4,8,1152]{2,1,0:T(8,128)S(1)} collective-permute-done((f32[4,8,1152]{2,1,0:T(8,128)S(1)}, f32[4,8,1152]{2,1,0:T(8,128)S(1)}, u32[]{:S(2)}, u32[]{:S(2)}) %collective-permute-start.37) | collective-permute-done | bytes 147488 | tf_op jit(solution)/shard_map/ppermute | solution.py:389
  299.8 4.4 %collective-permute-done.39 = f32[4,8,1152]{2,1,0:T(8,128)S(1)} collective-permute-done((f32[4,8,1152]{2,1,0:T(8,128)S(1)}, f32[4,8,1152]{2,1,0:T(8,128)S(1)}, u32[]{:S(2)}, u32[]{:S(2)}) %collective-permute-start.39) | collective-permute-done | bytes 147488 | tf_op jit(solution)/shard_map/ppermute | solution.py:389
  304.9 2.0 assemble.1
  (131 shorter events, 32.6 us)
Async XLA Ops:
  0.0 9.4 %copy-start.19 = (s32[2]{0:T(128)S(1)}, s32[2]{0:T(128)}, u32[]{:S(2)}) copy-start(s32[2]{0:T(128)} %param.8) | copy-start | bytes 28
  0.0 10.6 %copy-start.17 = (f32[2,3]{1,0:T(2,128)S(1)}, f32[2,3]{1,0:T(2,128)}, u32[]{:S(2)}) copy-start(f32[2,3]{1,0:T(2,128)} %param.10) | copy-start | bytes 76
  0.0 10.6 %copy-start.18 = (f32[2,3]{1,0:T(2,128)S(1)}, f32[2,3]{1,0:T(2,128)}, u32[]{:S(2)}) copy-start(f32[2,3]{1,0:T(2,128)} %param.9) | copy-start | bytes 76
  3.6 50.6 %collective-permute-start.1 = (f32[2,3,2,8,2304]{4,3,2,1,0:T(8,128)}, f32[2,3,2,8,2304]{4,3,2,1,0:T(8,128)S(1)}, u32[]{:S(2)}, u32[]{:S(2)}) collective-permute-start(f32[2,3,2,8,2304]{4,3,2,1,0:T(8,128)} %get-tuple-element.26), channel_id=1, source_target_pairs={{0,64},{64,0},{1,65},{65,1},{2,66},{66,2},{3,67},{67,3},{4,68},{68... | collective-permute-start | bytes 2654216 | tf_op jit(solution)/shard_map/ppermute | solution.py:27
  6.1 48.2 %collective-permute-start.2 = (f32[2,3,2,8,2304]{4,3,2,1,0:T(8,128)}, f32[2,3,2,8,2304]{4,3,2,1,0:T(8,128)S(1)}, u32[]{:S(2)}, u32[]{:S(2)}) collective-permute-start(f32[2,3,2,8,2304]{4,3,2,1,0:T(8,128)} %get-tuple-element.28), channel_id=1, source_target_pairs={{0,1},{64,65},{1,0},{65,64},{2,3},{66,67},{3,2},{67,66},{4,5},{68,... | collective-permute-start | bytes 2654216 | tf_op jit(solution)/shard_map/ppermute | solution.py:27
  9.4 44.9 %collective-permute-start.3 = (f32[2,3,2,8,2304]{4,3,2,1,0:T(8,128)S(1)}, f32[2,3,2,8,2304]{4,3,2,1,0:T(8,128)S(1)}, u32[]{:S(2)}, u32[]{:S(2)}) collective-permute-start(f32[2,3,2,8,2304]{4,3,2,1,0:T(8,128)S(1)} %get-tuple-element.25), channel_id=1, source_target_pairs={{0,65},{64,1},{1,64},{65,0},{2,67},{66,3},{3,66},{67,2},{4,69},{68... | collective-permute-start | bytes 2654216 | tf_op jit(solution)/shard_map/ppermute | solution.py:27
  10.7 33.9 %collective-permute-start = (f32[2,8]{1,0:T(2,128)S(1)}, f32[2,8]{1,0:T(2,128)S(1)}, u32[]{:S(2)}, u32[]{:S(2)}) collective-permute-start(f32[2,8]{1,0:T(2,128)S(1)} %pad_maximum_fusion.2), channel_id=1, source_target_pairs={{0,64},{64,0},{1,65},{65,1},{2,66},{66,2},{3,67},{67,3},{4,68},{68... | collective-permute-start | bytes 200 | tf_op jit(solution)/shard_map/ppermute | solution.py:27
  12.5 41.7 %collective-permute-start.4 = (f32[3,8,2304]{2,1,0:T(8,128)S(1)}, f32[3,8,2304]{2,1,0:T(8,128)S(1)}, u32[]{:S(2)}, u32[]{:S(2)}) collective-permute-start(f32[3,8,2304]{2,1,0:T(8,128)S(1)} %get-tuple-element.29), channel_id=1, source_target_pairs={{0,65},{64,1},{1,64},{65,0},{2,67},{66,3},{3,66},{67,2},{4,69},{68... | collective-permute-start | bytes 663560 | tf_op jit(solution)/shard_map/ppermute | solution.py:27
  54.2 0.7 copy-start.3
  54.2 1.0 copy-start
  54.3 1.3 copy-start.1
  54.9 1.0 copy-start.2
  61.3 4.5 %collective-permute-start.5 = (f32[72,128]{1,0:T(8,128)}, f32[72,128]{1,0:T(8,128)S(1)}, u32[]{:S(2)}, u32[]{:S(2)}) collective-permute-start(f32[72,128]{1,0:T(8,128)} %products.1), channel_id=1, source_target_pairs={{0,64},{64,0},{1,65},{65,1},{2,66},{66,2},{3,67},{67,3},{4,68},{68... | collective-permute-start | bytes 110600 | tf_op jit(solution)/shard_map/ppermute | solution.py:27
  62.0 5.7 %collective-permute-start.6 = (f32[72,128]{1,0:T(8,128)}, f32[72,128]{1,0:T(8,128)S(1)}, u32[]{:S(2)}, u32[]{:S(2)}) collective-permute-start(f32[72,128]{1,0:T(8,128)} %products.1), channel_id=1, source_target_pairs={{0,1},{64,65},{1,0},{65,64},{2,3},{66,67},{3,2},{67,66},{4,5},{68,... | collective-permute-start | bytes 110600 | tf_op jit(solution)/shard_map/ppermute | solution.py:27
  63.4 4.2 %collective-permute-start.7 = (f32[72,128]{1,0:T(8,128)}, f32[72,128]{1,0:T(8,128)S(1)}, u32[]{:S(2)}, u32[]{:S(2)}) collective-permute-start(f32[72,128]{1,0:T(8,128)} %products.1), channel_id=1, source_target_pairs={{0,65},{64,1},{1,64},{65,0},{2,67},{66,3},{3,66},{67,2},{4,69},{68... | collective-permute-start | bytes 110600 | tf_op jit(solution)/shard_map/ppermute | solution.py:27
  68.4 8.2 %copy-start.13 = (f32[72,128]{1,0:T(8,128)}, f32[72,128]{1,0:T(8,128)S(1)}, u32[]{:S(2)}) copy-start(f32[72,128]{1,0:T(8,128)S(1)} %fusion.3.s0) | copy-start | bytes 110596
  68.4 8.1 %collective-permute-start.8 = (f32[72,128]{1,0:T(8,128)S(1)}, f32[72,128]{1,0:T(8,128)S(1)}, u32[]{:S(2)}, u32[]{:S(2)}) collective-permute-start(f32[72,128]{1,0:T(8,128)S(1)} %fusion.3.s0), channel_id=1, source_target_pairs={{0,2},{2,4},{4,6},{6,0},{1,3},{3,5},{5,7},{7,1},{8,10},{10,12},{12... | collective-permute-start | bytes 110600 | tf_op jit(solution)/shard_map/ppermute | solution.py:35
  69.8 6.8 %collective-permute-start.9 = (f32[72,128]{1,0:T(8,128)S(1)}, f32[72,128]{1,0:T(8,128)S(1)}, u32[]{:S(2)}, u32[]{:S(2)}) collective-permute-start(f32[72,128]{1,0:T(8,128)S(1)} %fusion.3.s0), channel_id=1, source_target_pairs={{0,4},{2,6},{4,0},{6,2},{1,5},{3,7},{5,1},{7,3},{8,12},{10,14},{12... | collective-permute-start | bytes 110600 | tf_op jit(solution)/shard_map/ppermute | solution.py:35
  72.4 4.2 %collective-permute-start.10 = (f32[72,128]{1,0:T(8,128)S(1)}, f32[72,128]{1,0:T(8,128)S(1)}, u32[]{:S(2)}, u32[]{:S(2)}) collective-permute-start(f32[72,128]{1,0:T(8,128)S(1)} %fusion.3.s0), channel_id=1, source_target_pairs={{0,6},{2,0},{4,2},{6,4},{1,7},{3,1},{5,3},{7,5},{8,14},{10,8},{12,... | collective-permute-start | bytes 110600 | tf_op jit(solution)/shard_map/ppermute | solution.py:35
  76.6 0.6 copy-start.14
  76.6 0.6 copy-start.15
  76.6 0.6 copy-start.16
  102.9 20.7 %collective-permute-start.11 = (f32[12,2,24,2,128]{4,3,2,1,0:T(2,128)S(1)}, f32[12,2,24,2,128]{4,3,2,1,0:T(2,128)S(1)}, u32[]{:S(2)}, u32[]{:S(2)}) collective-permute-start(f32[12,2,24,2,128]{4,3,2,1,0:T(2,128)S(1)} %get-tuple-element.24), channel_id=1, source_target_pairs={{0,2},{2,4},{4,6},{6,0},{1,3},{3,5},{5,7},{7,1},{8,10},{10,12},{12... | collective-permute-start | bytes 1769480 | tf_op jit(solution)/shard_map/ppermute | solution.py:35
  103.4 20.3 %collective-permute-start.12 = (f32[12,2,24,2,128]{4,3,2,1,0:T(2,128)S(1)}, f32[12,2,24,2,128]{4,3,2,1,0:T(2,128)S(1)}, u32[]{:S(2)}, u32[]{:S(2)}) collective-permute-start(f32[12,2,24,2,128]{4,3,2,1,0:T(2,128)S(1)} %get-tuple-element.23), channel_id=1, source_target_pairs={{0,6},{2,0},{4,2},{6,4},{1,7},{3,1},{5,3},{7,5},{8,14},{10,8},{12,... | collective-permute-start | bytes 1769480 | tf_op jit(solution)/shard_map/ppermute | solution.py:35
  106.9 16.8 %collective-permute-start.13 = (f32[12,2,2,16,128]{4,3,2,1,0:T(8,128)S(1)}, f32[12,2,2,16,128]{4,3,2,1,0:T(8,128)S(1)}, u32[]{:S(2)}, u32[]{:S(2)}) collective-permute-start(f32[12,2,2,16,128]{4,3,2,1,0:T(8,128)S(1)} %get-tuple-element.22), channel_id=1, source_target_pairs={{0,64},{64,1},{1,65},{65,0},{2,66},{66,3},{3,67},{67,2},{4,68},{68... | collective-permute-start | bytes 1179656 | tf_op jit(solution)/shard_map/ppermute | solution.py:31
  107.2 16.4 %collective-permute-start.14 = (f32[12,2,2,16,128]{4,3,2,1,0:T(8,128)S(1)}, f32[12,2,2,16,128]{4,3,2,1,0:T(8,128)}, u32[]{:S(2)}, u32[]{:S(2)}) collective-permute-start(f32[12,2,2,16,128]{4,3,2,1,0:T(8,128)S(1)} %get-tuple-element.21), channel_id=1, source_target_pairs={{0,65},{64,0},{1,64},{65,1},{2,67},{66,2},{3,66},{67,3},{4,69},{68... | collective-permute-start | bytes 1179656 | tf_op jit(solution)/shard_map/ppermute | solution.py:31
  123.6 0.7 copy-start.11
  123.6 0.9 copy-start.6
  123.7 1.1 copy-start.7
  157.8 21.3 %collective-permute-start.15 = (f32[12,2,24,2,128]{4,3,2,1,0:T(2,128)S(1)}, f32[12,2,24,2,128]{4,3,2,1,0:T(2,128)S(1)}, u32[]{:S(2)}, u32[]{:S(2)}) collective-permute-start(f32[12,2,24,2,128]{4,3,2,1,0:T(2,128)S(1)} %get-tuple-element.20), channel_id=1, source_target_pairs={{0,2},{2,4},{4,6},{6,0},{1,3},{3,5},{5,7},{7,1},{8,10},{10,12},{12... | collective-permute-start | bytes 1769480 | tf_op jit(solution)/shard_map/ppermute | solution.py:35
  157.9 21.2 %collective-permute-start.16 = (f32[12,2,24,2,128]{4,3,2,1,0:T(2,128)S(1)}, f32[12,2,24,2,128]{4,3,2,1,0:T(2,128)S(1)}, u32[]{:S(2)}, u32[]{:S(2)}) collective-permute-start(f32[12,2,24,2,128]{4,3,2,1,0:T(2,128)S(1)} %get-tuple-element.19), channel_id=1, source_target_pairs={{0,6},{2,0},{4,2},{6,4},{1,7},{3,1},{5,3},{7,5},{8,14},{10,8},{12,... | collective-permute-start | bytes 1769480 | tf_op jit(solution)/shard_map/ppermute | solution.py:35
  161.7 17.3 %collective-permute-start.17 = (f32[12,2,2,16,128]{4,3,2,1,0:T(8,128)S(1)}, f32[12,2,2,16,128]{4,3,2,1,0:T(8,128)S(1)}, u32[]{:S(2)}, u32[]{:S(2)}) collective-permute-start(f32[12,2,2,16,128]{4,3,2,1,0:T(8,128)S(1)} %get-tuple-element.18), channel_id=1, source_target_pairs={{0,64},{64,1},{1,65},{65,0},{2,66},{66,3},{3,67},{67,2},{4,68},{68... | collective-permute-start | bytes 1179656 | tf_op jit(solution)/shard_map/ppermute | solution.py:31
  161.8 17.3 %collective-permute-start.18 = (f32[12,2,2,16,128]{4,3,2,1,0:T(8,128)S(1)}, f32[12,2,2,16,128]{4,3,2,1,0:T(8,128)}, u32[]{:S(2)}, u32[]{:S(2)}) collective-permute-start(f32[12,2,2,16,128]{4,3,2,1,0:T(8,128)S(1)} %get-tuple-element.17), channel_id=1, source_target_pairs={{0,65},{64,0},{1,64},{65,1},{2,67},{66,2},{3,66},{67,3},{4,69},{68... | collective-permute-start | bytes 1179656 | tf_op jit(solution)/shard_map/ppermute | solution.py:31
  179.0 0.7 copy-start.12
  179.1 0.9 copy-start.8
  180.0 0.8 copy-start.9
  213.8 18.4 %collective-permute-start.19 = (f32[12,2,24,2,128]{4,3,2,1,0:T(2,128)S(1)}, f32[12,2,24,2,128]{4,3,2,1,0:T(2,128)S(1)}, u32[]{:S(2)}, u32[]{:S(2)}) collective-permute-start(f32[12,2,24,2,128]{4,3,2,1,0:T(2,128)S(1)} %get-tuple-element.16), channel_id=1, source_target_pairs={{0,2},{2,4},{4,6},{6,0},{1,3},{3,5},{5,7},{7,1},{8,10},{10,12},{12... | collective-permute-start | bytes 1769480 | tf_op jit(solution)/shard_map/ppermute | solution.py:35
  213.9 18.3 %collective-permute-start.20 = (f32[12,2,24,2,128]{4,3,2,1,0:T(2,128)S(1)}, f32[12,2,24,2,128]{4,3,2,1,0:T(2,128)S(1)}, u32[]{:S(2)}, u32[]{:S(2)}) collective-permute-start(f32[12,2,24,2,128]{4,3,2,1,0:T(2,128)S(1)} %get-tuple-element.15), channel_id=1, source_target_pairs={{0,6},{2,0},{4,2},{6,4},{1,7},{3,1},{5,3},{7,5},{8,14},{10,8},{12,... | collective-permute-start | bytes 1769480 | tf_op jit(solution)/shard_map/ppermute | solution.py:35
  217.7 14.5 %collective-permute-start.21 = (f32[12,2,2,16,128]{4,3,2,1,0:T(8,128)S(1)}, f32[12,2,2,16,128]{4,3,2,1,0:T(8,128)S(1)}, u32[]{:S(2)}, u32[]{:S(2)}) collective-permute-start(f32[12,2,2,16,128]{4,3,2,1,0:T(8,128)S(1)} %get-tuple-element.14), channel_id=1, source_target_pairs={{0,64},{64,1},{1,65},{65,0},{2,66},{66,3},{3,67},{67,2},{4,68},{68... | collective-permute-start | bytes 1179656 | tf_op jit(solution)/shard_map/ppermute | solution.py:31
  217.8 14.4 %collective-permute-start.22 = (f32[12,2,2,16,128]{4,3,2,1,0:T(8,128)S(1)}, f32[12,2,2,16,128]{4,3,2,1,0:T(8,128)}, u32[]{:S(2)}, u32[]{:S(2)}) collective-permute-start(f32[12,2,2,16,128]{4,3,2,1,0:T(8,128)S(1)} %get-tuple-element.13), channel_id=1, source_target_pairs={{0,65},{64,0},{1,64},{65,1},{2,67},{66,2},{3,66},{67,3},{4,69},{68... | collective-permute-start | bytes 1179656 | tf_op jit(solution)/shard_map/ppermute | solution.py:31
  232.2 0.8 copy-start.10
  232.2 0.9 copy-start.4
  232.2 1.1 copy-start.5
  254.8 13.8 %collective-permute-start.29 = (f32[8,1152]{1,0:T(8,128)S(1)}, f32[8,1152]{1,0:T(8,128)S(1)}, u32[]{:S(2)}, u32[]{:S(2)}) collective-permute-start(f32[8,1152]{1,0:T(8,128)S(1)} %get-tuple-element.32), channel_id=1, source_target_pairs={{0,56},{8,48},{16,40},{24,32},{32,24},{40,16},{48,8},{56,0},{1,57}... | collective-permute-start | bytes 110600 | tf_op jit(solution)/shard_map/ppermute | solution.py:374
  264.9 5.2 %collective-permute-start.28 = (f32[8,1152]{1,0:T(8,128)S(1)}, f32[8,1152]{1,0:T(8,128)S(1)}, u32[]{:S(2)}, u32[]{:S(2)}) collective-permute-start(f32[8,1152]{1,0:T(8,128)S(1)} %get-tuple-element.33), channel_id=1, source_target_pairs={{0,48},{8,56},{16,32},{24,40},{32,16},{40,24},{48,0},{56,8},{1,49}... | collective-permute-start | bytes 110600 | tf_op jit(solution)/shard_map/ppermute | solution.py:374
  265.1 5.3 %collective-permute-start.27 = (f32[8,1152]{1,0:T(8,128)S(1)}, f32[8,1152]{1,0:T(8,128)S(1)}, u32[]{:S(2)}, u32[]{:S(2)}) collective-permute-start(f32[8,1152]{1,0:T(8,128)S(1)} %get-tuple-element.34), channel_id=1, source_target_pairs={{0,40},{8,32},{16,56},{24,48},{32,8},{40,0},{48,24},{56,16},{1,41}... | collective-permute-start | bytes 110600 | tf_op jit(solution)/shard_map/ppermute | solution.py:374
  265.8 4.6 %collective-permute-start.26 = (f32[8,1152]{1,0:T(8,128)S(1)}, f32[8,1152]{1,0:T(8,128)S(1)}, u32[]{:S(2)}, u32[]{:S(2)}) collective-permute-start(f32[8,1152]{1,0:T(8,128)S(1)} %get-tuple-element.35), channel_id=1, source_target_pairs={{0,32},{8,40},{16,48},{24,56},{32,0},{40,8},{48,16},{56,24},{1,33}... | collective-permute-start | bytes 110600 | tf_op jit(solution)/shard_map/ppermute | solution.py:374
  268.2 3.9 %collective-permute-start.25 = (f32[8,1152]{1,0:T(8,128)S(1)}, f32[8,1152]{1,0:T(8,128)S(1)}, u32[]{:S(2)}, u32[]{:S(2)}) collective-permute-start(f32[8,1152]{1,0:T(8,128)S(1)} %get-tuple-element.36), channel_id=1, source_target_pairs={{0,24},{8,16},{16,8},{24,0},{32,56},{40,48},{48,40},{56,32},{1,25}... | collective-permute-start | bytes 110600 | tf_op jit(solution)/shard_map/ppermute | solution.py:374
  268.6 4.1 %collective-permute-start.24 = (f32[8,1152]{1,0:T(8,128)S(1)}, f32[8,1152]{1,0:T(8,128)S(1)}, u32[]{:S(2)}, u32[]{:S(2)}) collective-permute-start(f32[8,1152]{1,0:T(8,128)S(1)} %get-tuple-element.37), channel_id=1, source_target_pairs={{0,16},{8,24},{16,0},{24,8},{32,48},{40,56},{48,32},{56,40},{1,17}... | collective-permute-start | bytes 110600 | tf_op jit(solution)/shard_map/ppermute | solution.py:374
  270.1 2.6 collective-permute-start.23
  273.5 3.6 %collective-permute-start.32 = (f32[8,1152]{1,0:T(8,128)S(1)}, f32[8,1152]{1,0:T(8,128)S(1)}, u32[]{:S(2)}, u32[]{:S(2)}) collective-permute-start(f32[8,1152]{1,0:T(8,128)S(1)} %fusion.9), channel_id=1, source_target_pairs={{8,73},{72,9},{1,64},{65,0},{10,75},{74,11},{3,66},{67,2},{12,77},... | collective-permute-start | bytes 110600 | tf_op jit(solution)/shard_map/ppermute | solution.py:383
  275.2 2.3 collective-permute-start.31
  276.5 1.0 collective-permute-start.30
  277.5 5.9 %collective-permute-start.34 = (f32[4,8,1152]{2,1,0:T(8,128)S(1)}, f32[4,8,1152]{2,1,0:T(8,128)S(1)}, u32[]{:S(2)}, u32[]{:S(2)}) collective-permute-start(f32[4,8,1152]{2,1,0:T(8,128)S(1)} %pad_maximum_fusion), channel_id=1, source_target_pairs={{0,16},{9,25},{16,0},{25,9},{32,48},{41,57},{48,32},{57,41},{2,18}... | collective-permute-start | bytes 442376 | tf_op jit(solution)/shard_map/ppermute | solution.py:392
  278.2 12.5 %collective-permute-start.35 = (f32[4,8,1152]{2,1,0:T(8,128)S(1)}, f32[4,8,1152]{2,1,0:T(8,128)S(1)}, u32[]{:S(2)}, u32[]{:S(2)}) collective-permute-start(f32[4,8,1152]{2,1,0:T(8,128)S(1)} %pad_maximum_fusion), channel_id=1, source_target_pairs={{0,24},{9,17},{16,8},{25,1},{32,56},{41,49},{48,40},{57,33},{2,26}... | collective-permute-start | bytes 442376 | tf_op jit(solution)/shard_map/ppermute | solution.py:389
  280.2 18.9 %collective-permute-start.33 = (f32[4,8,1152]{2,1,0:T(8,128)S(1)}, f32[4,8,1152]{2,1,0:T(8,128)S(1)}, u32[]{:S(2)}, u32[]{:S(2)}) collective-permute-start(f32[4,8,1152]{2,1,0:T(8,128)S(1)} %pad_maximum_fusion), channel_id=1, source_target_pairs={{0,8},{9,1},{16,24},{25,17},{32,40},{41,33},{48,56},{57,49},{2,10}... | collective-permute-start | bytes 442376 | tf_op jit(solution)/shard_map/ppermute | solution.py:389
  281.5 11.2 %collective-permute-start.36 = (f32[4,8,1152]{2,1,0:T(8,128)S(1)}, f32[4,8,1152]{2,1,0:T(8,128)S(1)}, u32[]{:S(2)}, u32[]{:S(2)}) collective-permute-start(f32[4,8,1152]{2,1,0:T(8,128)S(1)} %pad_maximum_fusion), channel_id=1, source_target_pairs={{0,32},{9,41},{16,48},{25,57},{32,0},{41,9},{48,16},{57,25},{2,34}... | collective-permute-start | bytes 442376 | tf_op jit(solution)/shard_map/ppermute | solution.py:392
  282.1 16.3 %collective-permute-start.37 = (f32[4,8,1152]{2,1,0:T(8,128)S(1)}, f32[4,8,1152]{2,1,0:T(8,128)S(1)}, u32[]{:S(2)}, u32[]{:S(2)}) collective-permute-start(f32[4,8,1152]{2,1,0:T(8,128)S(1)} %pad_maximum_fusion), channel_id=1, source_target_pairs={{0,40},{9,33},{16,56},{25,49},{32,8},{41,1},{48,24},{57,17},{2,42}... | collective-permute-start | bytes 442376 | tf_op jit(solution)/shard_map/ppermute | solution.py:389
  283.5 16.3 %collective-permute-start.38 = (f32[4,8,1152]{2,1,0:T(8,128)S(1)}, f32[4,8,1152]{2,1,0:T(8,128)S(1)}, u32[]{:S(2)}, u32[]{:S(2)}) collective-permute-start(f32[4,8,1152]{2,1,0:T(8,128)S(1)} %pad_maximum_fusion), channel_id=1, source_target_pairs={{0,48},{9,57},{16,32},{25,41},{32,16},{41,25},{48,0},{57,9},{2,50}... | collective-permute-start | bytes 442376 | tf_op jit(solution)/shard_map/ppermute | solution.py:392
  290.7 13.5 %collective-permute-start.39 = (f32[4,8,1152]{2,1,0:T(8,128)S(1)}, f32[4,8,1152]{2,1,0:T(8,128)S(1)}, u32[]{:S(2)}, u32[]{:S(2)}) collective-permute-start(f32[4,8,1152]{2,1,0:T(8,128)S(1)} %pad_maximum_fusion), channel_id=1, source_target_pairs={{0,56},{9,49},{16,40},{25,33},{32,24},{41,17},{48,8},{57,1},{2,58}... | collective-permute-start | bytes 442376 | tf_op jit(solution)/shard_map/ppermute | solution.py:389

commit v2 on v1

v2 whole, which is shorter than its diff:
```python
import functools

import jax
import jax.numpy as jnp
import numpy as np
from jax import lax
from jax.experimental import pallas as pl
from jax.experimental.pallas import tpu as pltpu
from jax.sharding import Mesh
from jax.sharding import PartitionSpec as P

NX = 96
ITERS = 4
ROWS = 24
CHUNK = ROWS * NX
GROUP = 4 * NX
F32 = jnp.float32
ZAX = ("zl", "zh")
PIECE = CHUNK // 2


def z_perm(to):
    index = lambda z: (z & 1) * 2 + (z >> 1)
    return [(index(z), index(to(z))) for z in range(4)]


def z_xor(value, m):
    return lax.ppermute(value, ZAX, z_perm(lambda z: z ^ m))


def z_ring(value, by):
    return lax.ppermute(value, ZAX, z_perm(lambda z: (z + by) % 4))


def y_ring(value, by):
    return lax.ppermute(value, "y", [(i, (i + by) % 4) for i in range(4)])


def lane_ids():
    return lax.broadcasted_iota(jnp.int32, (8, 128), 1)


def unpack_rows(a, b, c, lanes):
    r0 = a
    r1 = jnp.where(lanes < 32, pltpu.roll(a, 32, 1), pltpu.roll(b, 32, 1))
    r2 = jnp.where(lanes < 64, pltpu.roll(b, 64, 1), pltpu.roll(c, 64, 1))
    r3 = pltpu.roll(c, 96, 1)
    return r0, r1, r2, r3


def pack_rows(r0, r1, r2, r3, lanes):
    r1s = pltpu.roll(r1, 96, 1)
    r2s = pltpu.roll(r2, 64, 1)
    r3s = pltpu.roll(r3, 32, 1)
    return (
        jnp.where(lanes < 96, r0, r1s),
        jnp.where(lanes < 64, r1s, r2s),
        jnp.where(lanes < 32, r2s, r3s),
    )


def in_vmem(shape):
    return pltpu.VMEM(shape, F32)


def call(kernel, name, args, outs, scratch=(), scalars=0, aliases=None, flops=10_000_000, limit=8):
    specs = [pl.BlockSpec(memory_space=pltpu.SMEM)] * scalars
    specs += [pl.BlockSpec(memory_space=pltpu.VMEM)] * (len(args) - scalars)
    args = list(args[:scalars]) + [pltpu.with_memory_space_constraint(a, pltpu.VMEM) for a in args[scalars:]]
    return pl.pallas_call(
        kernel,
        in_specs=specs,
        out_specs=[pl.BlockSpec(memory_space=pltpu.VMEM)] * len(outs),
        out_shape=[in_vmem(o) for o in outs],
        scratch_shapes=list(scratch),
        input_output_aliases=aliases or {},
        compiler_params=pltpu.CompilerParams(vmem_limit_bytes=limit * 2**20),
        cost_estimate=pl.CostEstimate(flops=flops, bytes_accessed=10_000_000, transcendentals=0),
        name=name,
    )(*args)


def lanes_at(group, v):
    return pl.ds(pl.multiple_of(group * GROUP + v * 128, 128), 128)


def perturbed(field, pert_r, pert_i):
    re, im = field
    return pert_r * re - pert_i * im, pert_r * im + pert_i * re


def products_kernel(slot_ref, o0, o1, o2, o3, p0, p1, out_ref):
    slabs = (((o0, o1), p0), ((o2, o3), p1))
    for k in range(4):
        block, kk = k // 2, k % 2
        slot = slot_ref[k]

        def body(g, acc, block=block, kk=kk, slot=slot):
            acc = list(acc)
            for pair, pert in slabs:
                own, mate = pair[block], pair[1 - block]
                for v in range(3):
                    at = lanes_at(g, v)
                    pr, pi = pert[1, :, at], pert[2, :, at]
                    w = [perturbed((own[kk, n, 0, :, at], own[kk, n, 1, :, at]), pr, pi) for n in range(3)]
                    for m in range(3):
                        mr, mi = mate[slot, m, 0, :, at], mate[slot, m, 1, :, at]
                        for n in range(3):
                            i = (m * 3 + n) * 2
                            acc[i] = acc[i] + (mr * w[n][0] + mi * w[n][1])
                            acc[i + 1] = acc[i + 1] + (mr * w[n][1] - mi * w[n][0])
            return tuple(acc)

        acc = lax.fori_loop(0, CHUNK // GROUP, body, (jnp.zeros((8, 128), F32),) * 18)
        for i in range(18):
            out_ref[pl.ds(k * 18 + i, 1), :] = jnp.sum(acc[i], axis=0, keepdims=True)


def products(slots, fields, perts):
    return call(products_kernel, "products", (slots, *fields, *perts), [(72, 128)], scalars=1, flops=20_000_000)[0]


def rows_at(kn, c, r):
    return ((kn * 2 + c) * ROWS + r) * 16


def orbital_rows_kernel(half_ref, o0, o1, o2, o3, p0, p1, orb_ref, v_ref):
    lanes = lane_ids()
    half = half_ref[0]

    def body(g, carry):
        for pair, pert, z in (((o0, o1), p0, half), ((o2, o3), p1, 1 - half)):
            rows = unpack_rows(*[pert[0, :, lanes_at(g, v)] for v in range(3)], lanes)
            for j in range(4):
                v_ref[pl.ds(pl.multiple_of((4 * g + j) * 16 + 8 * z, 8), 8), :] = rows[j]
            for k in range(4):
                for n in range(3):
                    for c in range(2):
                        rows = unpack_rows(*[pair[k // 2][k % 2, n, c, :, lanes_at(g, v)] for v in range(3)], lanes)
                        for j in range(4):
                            at = pl.multiple_of(rows_at(k * 3 + n, c, 4 * g + j) + 8 * z, 8)
                            orb_ref[pl.ds(at, 8), :] = rows[j]
        return carry

    lax.fori_loop(0, CHUNK // GROUP, body, 0)


def orbital_rows(half, fields, perts):
    outs = [(24 * ROWS * 16, 128), (ROWS * 16, 128)]
    return call(orbital_rows_kernel, "orbital_rows", (half, *fields, *perts), outs, scalars=1)


ZHALO, YHALO = (48 * ROWS, 128), (24 * 32, 128)


def cut_halos(u_ref, kn, zdn, zup, ydn, yup):
    for c in range(2):
        base = rows_at(kn, c, 0)
        for p in range(2):
            to = pl.ds(pl.multiple_of(((kn * 2 + c) * 2 + p) * ROWS, 8), ROWS)
            zdn[to, :] = u_ref[pl.ds(base + p, ROWS, stride=16), :]
            zup[to, :] = u_ref[pl.ds(base + 14 + p, ROWS, stride=16), :]
        to = pl.ds(pl.multiple_of((kn * 2 + c) * 32, 8), 32)
        ydn[to, :] = u_ref[pl.ds(pl.multiple_of(base, 8), 32), :]
        yup[to, :] = u_ref[pl.ds(pl.multiple_of(base + 22 * 16, 8), 32), :]


def exchange(zdn, zup, ydn, yup):
    return y_ring(zup, 1), y_ring(zdn, 3), z_ring(yup, 1), z_ring(ydn, 3)


def right_kernel(ncells, slot_ref, half_ref, s0, s1, s2, s3, o0, o1, o2, o3, p0, p1, r_ref, zdn, zup, ydn, yup, prod_ref):
    total = (s0[...] + s1[...]) + (s2[...] + s3[...])
    ones = jnp.full((128, 128), 1.0, F32)
    prod_ref[...] = jnp.dot(total, ones, precision=lax.Precision.HIGHEST, preferred_element_type=F32) / ncells
    lanes = lane_ids()
    half = half_ref[0]
    slabs = (((o0, o1), p0, half), ((o2, o3), p1, 1 - half))
    for k in range(4):
        block, kk = k // 2, k % 2
        slot = slot_ref[k]

        def body(g, carry, k=k, block=block, kk=kk, slot=slot):
            for pair, pert, z in slabs:
                own, mate = pair[block], pair[1 - block]
                right = [[[], []] for _ in range(3)]
                for v in range(3):
                    at = lanes_at(g, v)
                    pr, pi = pert[1, :, at], pert[2, :, at]
                    mates = [(mate[slot, m, 0, :, at], mate[slot, m, 1, :, at]) for m in range(3)]
                    for n in range(3):
                        wr, wi = perturbed((own[kk, n, 0, :, at], own[kk, n, 1, :, at]), pr, pi)
                        gr, gi = -wr, -wi
                        for m in range(3):
                            row = k * 18 + (m * 3 + n) * 2
                            qr = prod_ref[pl.ds(row, 1), :]
                            qi = prod_ref[pl.ds(row + 1, 1), :]
                            mr, mi = mates[m]
                            gr = gr + (qr * mr - qi * mi)
                            gi = gi + (qi * mr + qr * mi)
                        right[n][0].append(gr)
                        right[n][1].append(gi)
                for n in range(3):
                    for c in range(2):
                        rows = unpack_rows(*right[n][c], lanes)
                        for j in range(4):
                            at = pl.multiple_of(rows_at(k * 3 + n, c, 4 * g + j) + 8 * z, 8)
                            r_ref[pl.ds(at, 8), :] = rows[j]
            return carry

        lax.fori_loop(0, CHUNK // GROUP, body, 0)

    def cut(kn, carry):
        cut_halos(r_ref, kn, zdn, zup, ydn, yup)
        return carry

    lax.fori_loop(0, 12, cut, 0)


def right_sides(ncells, slots, half, sums, fields, perts):
    return call(
        functools.partial(right_kernel, ncells),
        "right_sides",
        (slots, half, *sums, *fields, *perts),
        [(24 * ROWS * 16, 128), ZHALO, ZHALO, YHALO, YHALO],
        scratch=[pltpu.VMEM((72, 128), F32)],
        scalars=2,
        flops=20_000_000,
    )


def x_matrix():
    m = np.zeros((128, 256), np.float32)
    for i in range(NX):
        for s, lap, grad in ((1, 16, 8), (-1, 16, -8), (2, -1, -1), (-2, -1, 1)):
            m[(i + s) % NX, i] += lap
            m[(i + s) % NX, 128 + i] += grad
    return np.concatenate([m, m], 0)


def scalars_of(count, par_ref, w_ref, kn):
    k, n = kn // 3, kn % 3
    kx, ky, kz = par_ref[k * 8], par_ref[k * 8 + 1], par_ref[k * 8 + 2]
    base = 3.75 + 0.5 * (kx * kx + ky * ky + kz * kz) + par_ref[k * 8 + 3 + n]
    wt = w_ref[count]
    scale = w_ref[0] if count == 1 else jnp.float32(1.0)
    return kx, ky, kz, base, wt, scale


def step_kernel(count, par_ref, w_ref, u_ref, r_ref, v_ref, m_ref, *refs):
    last = count == ITERS - 1
    if last:
        orb_ref, out_ref, pad, flat = refs
        out_ref[...] = jnp.zeros_like(out_ref)
    else:
        out_ref, pad, flat = refs
    pad[...] = jnp.zeros_like(pad)

    def orbital(kn, carry):
        kx, ky, kz, base, wt, scale = scalars_of(count, par_ref, w_ref, kn)
        whole = pl.ds(pl.multiple_of(rows_at(kn, 0, 0), 8), 48 * 16)
        u2 = u_ref[whole, :] * scale
        hi = u2.astype(jnp.bfloat16)
        lo = (u2 - hi.astype(F32)).astype(jnp.bfloat16)
        flat[...] = jnp.dot(jnp.concatenate([hi, lo], 1), m_ref[...], preferred_element_type=F32)
        for c in range(2):
            for r in range(ROWS):
                pad[c, r + 2, 8:24, :] = u2[(c * ROWS + r) * 16 : (c * ROWS + r + 1) * 16]
        lap = wt / 24.0
        gx, gy, gz = wt * kx / 12.0, wt * ky * (2.0 / 3.0), wt * kz * (2.0 / 3.0)
        keep = 1.0 - wt * base

        def row(r, carry):
            cells, second, grad = [], [], []
            for c in range(2):
                at = pl.multiple_of((c * ROWS + r) * 16, 16)
                yp1, ym1 = pad[c, r + 3, 8:24, :], pad[c, r + 1, 8:24, :]
                yp2, ym2 = pad[c, r + 4, 8:24, :], pad[c, r, 8:24, :]
                zp1, zm1 = pad[c, r + 2, 9:25, :], pad[c, r + 2, 7:23, :]
                zp2, zm2 = pad[c, r + 2, 10:26, :], pad[c, r + 2, 6:22, :]
                cells.append(pad[c, r + 2, 8:24, :])
                one = (yp1 + ym1) + (zp1 + zm1)
                two = (yp2 + ym2) + (zp2 + zm2)
                second.append(flat[pl.ds(at, 16), 0:128] + (16.0 * one - two))
                dy = (yp1 - ym1) - 0.125 * (yp2 - ym2)
                dz = (zp1 - zm1) - 0.125 * (zp2 - zm2)
                grad.append(gx * flat[pl.ds(at, 16), 128:256] + (gy * dy + gz * dz))
            center = keep - wt * v_ref[pl.ds(pl.multiple_of(r * 16, 16), 16), :]
            new = []
            for c in range(2):
                at = pl.multiple_of(rows_at(kn, c, r), 16)
                value = (center * cells[c] + wt * r_ref[pl.ds(at, 16), :]) + lap * second[c]
                new.append(value - grad[1] if c == 0 else value + grad[0])
            if last:
                orb_r = orb_ref[pl.ds(pl.multiple_of(rows_at(kn, 0, r), 16), 16), :]
                orb_i = orb_ref[pl.ds(pl.multiple_of(rows_at(kn, 1, r), 16), 16), :]
                out_ref[pl.ds(pl.multiple_of(r * 16, 16), 16), :] += orb_r * new[0] + orb_i * new[1]
                out_ref[pl.ds(pl.multiple_of((ROWS + r) * 16, 16), 16), :] += orb_r * new[1] - orb_i * new[0]
            else:
                for c in range(2):
                    out_ref[pl.ds(pl.multiple_of(rows_at(kn, c, r), 16), 16), :] = new[c]
            return carry

        lax.fori_loop(0, ROWS, row, 0)
        return carry

    lax.fori_loop(0, 12, orbital, 0)


def inner_step(count, par, weights, u, right, pot, matrix, orb):
    last = count == ITERS - 1
    return call(
        functools.partial(step_kernel, count),
        "last_step" if last else "step",
        (par, weights, u, right, pot, matrix) + ((orb,) if last else ()),
        [(2 * ROWS * 16, 128) if last else (24 * ROWS * 16, 128)],
        scratch=[pltpu.VMEM((2, ROWS + 4, 32, 128), F32), pltpu.VMEM((2 * ROWS * 16, 256), F32)],
        scalars=2,
        flops=60_000_000,
    )[0]


def face_terms(lap, g, beyond1, beyond2, sign):
    first = [lap * (16.0 * beyond1[c] - beyond2[c]) for c in range(2)]
    grad1 = [(sign * g) * (beyond1[c] - 0.125 * beyond2[c]) for c in range(2)]
    second = [-lap * beyond1[c] for c in range(2)]
    grad2 = [(-0.125 * sign * g) * beyond1[c] for c in range(2)]
    return (
        (first[0] - grad1[1], first[1] + grad1[0]),
        (second[0] - grad2[1], second[1] + grad2[0]),
    )


def faces(count, par_ref, w_ref, kn, zm, zp, ym, yp, add):
    kx, ky, kz, base, wt, scale = scalars_of(count, par_ref, w_ref, kn)
    ws = wt * scale
    lap = ws / 24.0
    gy, gz = ws * ky * (2.0 / 3.0), ws * kz * (2.0 / 3.0)

    def plane(ref, p):
        return [ref[pl.ds(pl.multiple_of(((kn * 2 + c) * 2 + p) * ROWS, 8), ROWS), :] for c in range(2)]

    from_z = (kn + 6) % 12

    def line(ref, r):
        return [ref[pl.ds(pl.multiple_of(((from_z * 2 + c) * 2 + r) * 16, 8), 16), :] for c in range(2)]

    for ref, near, far, sign, cells in ((zm, 1, 0, -1.0, (0, 1)), (zp, 0, 1, 1.0, (15, 14))):
        terms = face_terms(lap, gz, plane(ref, near), plane(ref, far), sign)
        for cell, term in zip(cells, terms):
            add([pl.ds(rows_at(kn, c, 0) + cell, ROWS, stride=16) for c in range(2)],
                [pl.ds(c * ROWS * 16 + cell, ROWS, stride=16) for c in range(2)], term)
    for ref, near, far, sign, cells in ((ym, 1, 0, -1.0, (0, 1)), (yp, 0, 1, 1.0, (23, 22))):
        terms = face_terms(lap, gy, line(ref, near), line(ref, far), sign)
        for cell, term in zip(cells, terms):
            add([pl.ds(pl.multiple_of(rows_at(kn, c, cell), 16), 16) for c in range(2)],
                [pl.ds((c * ROWS + cell) * 16, 16) for c in range(2)], term)


def faces_kernel(count, par_ref, w_ref, u_in, zm, zp, ym, yp, u_ref, zdn, zup, ydn, yup):
    def orbital(kn, carry):
        def add(at, _, term):
            for c in range(2):
                u_ref[at[c], :] = u_ref[at[c], :] + term[c]

        faces(count, par_ref, w_ref, kn, zm, zp, ym, yp, add)
        cut_halos(u_ref, kn, zdn, zup, ydn, yup)
        return carry

    lax.fori_loop(0, 12, orbital, 0)


def add_faces(count, par, weights, u, halos):
    return call(
        functools.partial(faces_kernel, count),
        "faces",
        (par, weights, u, *halos),
        [(24 * ROWS * 16, 128), ZHALO, ZHALO, YHALO, YHALO],
        scalars=2,
        aliases={2: 0},
    )


def density_kernel(par_ref, w_ref, d_in, zm, zp, ym, yp, orb_ref, out_ref, d_ref):
    d_ref[...] = d_in[...]

    def orbital(kn, carry):
        def add(at, to, term):
            orb_r, orb_i = orb_ref[at[0], :], orb_ref[at[1], :]
            d_ref[to[0], :] = d_ref[to[0], :] + (orb_r * term[0] + orb_i * term[1])
            d_ref[to[1], :] = d_ref[to[1], :] + (orb_r * term[1] - orb_i * term[0])

        faces(ITERS - 1, par_ref, w_ref, kn, zm, zp, ym, yp, add)
        return carry

    lax.fori_loop(0, 12, orbital, 0)
    ids = lane_ids()
    for c in range(2):
        for z in range(2):
            for g in range(6):
                rows = [d_ref[pl.ds((c * ROWS + 4 * g + j) * 16 + 8 * z, 8), :] * (1.0 / 32.0) for j in range(4)]
                packed = pack_rows(*rows, ids)
                for v in range(3):
                    at = (g % 3) * GROUP + v * 128
                    out_ref[(c * 2 + g // 3) * 2 + z, :, at : at + 128] = packed[v]


def density_pieces(par, weights, dens, halos, orb):
    return call(
        density_kernel,
        "density",
        (par, weights, dens, *halos, orb),
        [(8, 8, PIECE)],
        scratch=[pltpu.VMEM((2 * ROWS * 16, 128), F32)],
        scalars=2,
    )[0]


def assemble_kernel(pos_ref, b0, b1, b2, b3, out_ref):
    x, z = pos_ref[0], pos_ref[1]
    for d, block in enumerate((b0, b1, b2, b3)):
        part = x ^ d
        for m in range(4):
            q = z ^ m
            at = pl.multiple_of(q * CHUNK + (part & 1) * PIECE, 128)
            out_ref[part >> 1, :, pl.ds(at, PIECE)] = block[m]


def assemble(pos, blocks):
    return pl.pallas_call(
        assemble_kernel,
        in_specs=[pl.BlockSpec(memory_space=pltpu.SMEM)] + [pl.BlockSpec(memory_space=pltpu.VMEM)] * 4,
        out_specs=pl.BlockSpec(memory_space=pltpu.VMEM),
        out_shape=jax.ShapeDtypeStruct((2, 8, 4 * CHUNK), F32),
        name="assemble",
    )(pos, *blocks)


def on_device(orbitals, partner_map, wave_vectors, levels, potential, perturbation, step_weights):
    zl, zh = lax.axis_index("zl"), lax.axis_index("zh")
    x, core = lax.axis_index("x"), lax.axis_index("c")
    z = zh * 2 + zl
    ncells = 64 * 4 * CHUNK

    def chunk(array, q):
        return lax.dynamic_slice_in_dim(array, q * CHUNK, CHUNK, axis=array.ndim - 1)

    pots = jnp.concatenate([potential[None], perturbation], 0)
    moved = [z_xor(chunk(orbitals, z ^ m), m) for m in (1, 2, 3)]
    fields = [chunk(orbitals, z)] + moved
    perts = [chunk(pots, z), z_xor(chunk(pots, z ^ 3), 3)]
    slot = (partner_map % 2).astype(F32)
    mine = jnp.concatenate([wave_vectors, levels, slot[:, None], jnp.zeros((2, 1), F32)], 1)
    other = z_xor(mine, 1)
    both = jnp.concatenate([mine, other], 0)
    slots = both[:, 6].astype(jnp.int32)

    weights = step_weights.astype(F32) / 100.0
    par = both.reshape(32)
    half = zh[None].astype(jnp.int32)
    matrix = jnp.asarray(x_matrix(), jnp.bfloat16)

    part = products(slots, fields, perts)
    orb, pot = orbital_rows(half, fields, perts)

    def swapped(value):
        return jnp.concatenate([value[36:], value[:36]], 0)

    part = part + swapped(z_xor(part, 1)) + z_xor(part, 2) + swapped(z_xor(part, 3))
    sums = [part] + [y_ring(part, by) for by in (1, 2, 3)]
    right, *cut = right_sides(float(ncells), slots, half, sums, fields, perts)
    u = right
    for count in range(1, ITERS):
        halos = exchange(*cut)
        u = inner_step(count, par, weights, u, right, pot, matrix, orb)
        if count < ITERS - 1:
            u, *cut = add_faces(count, par, weights, u, halos)
    u = density_pieces(par, weights, u, halos, orb)

    me = x * 2 + core
    piece = lax.dynamic_index_in_dim(u, me, 0, keepdims=False)
    for m in range(1, 8):
        send = lax.dynamic_index_in_dim(u, me ^ m, 0, keepdims=False)
        piece = piece + lax.ppermute(send, ("x", "c"), [(i, i ^ m) for i in range(8)])
    got = [piece]
    for m in (1, 2, 3):
        pairs = []
        for zz in range(4):
            to = zz ^ m
            c = to >> 1
            index = lambda w: (w & 1) * 4 + c * 2 + (w >> 1)
            pairs.append((index(zz), index(to)))
        got.append(lax.ppermute(piece, ("zl", "c", "zh"), pairs))
    slab = jnp.stack(got)
    same = core == zh
    blocks = []
    for d in range(4):
        index = lambda xx, c, h: xx * 4 + c * 2 + h
        across = lax.ppermute(slab, ("x", "c", "zh"), [(index(i, h, h), index(i ^ d, 1 - h, h)) for i in range(4) for h in range(2)])
        straight = slab
        if d:
            straight = lax.ppermute(slab, ("x", "c", "zh"), [(index(i, h, h), index(i ^ d, h, h)) for i in range(4) for h in range(2)])
        blocks.append(jnp.where(same, straight, across))
    return assemble(jnp.stack([x, z]).astype(jnp.int32), blocks)


def solution(mesh):
    fine = Mesh(mesh.devices.reshape(2, 4, 2, 4, 2), ("zl", "x", "c", "y", "zh"))
    ka, grid = ("zl", "x", "c"), ("y", "zh")
    return jax.shard_map(
        on_device,
        mesh=fine,
        in_specs=(
            P(ka, None, None, grid, None),
            P(ka),
            P(ka, None),
            P(ka, None),
            P(grid, None),
            P(None, grid, None),
            P(),
        ),
        out_specs=P(None, grid, None),
        check_vma=False,
    )
```

time: 308 us -> 209 us (0.68)
  Pallas kernels: 111 us -> 55.6 us
  local copies, waits for them, and re-layouts: 58.9 us -> 23.2 us
  other arithmetic: 13.1 us -> 5.34 us
  between operations: 4.15 us -> 0.47 us
    pallas_call x5 -> x9, Pallas kernels: 109 us -> 53.6 us  [call(): pl.pallas_call(kernel, in_specs=specs, out_specs=[pl.BlockSpec(memory_spa...]
    mul x12 -> x0, local copies, waits for them, and re-layouts: 13.5 us -> none  [the longest x3 3.58 us: coefficients(): wt * base]
    slice x9 -> x0, local copies, waits for them, and re-layouts: 12.9 us -> none  [the longest x3 8.53 us: exchange(): zp = y_ring(field[:, :, :, 0:2, :], 3)]
    unnamed x40 -> x44, local copies, waits for them, and re-layouts: 6.23 us -> 18.8 us
    another operation x18 -> x1, local copies, waits for them, and re-layouts: 12.4 us -> 0.01 us  [the longest x13 11.2 us: coefficients(): return jnp.stack(cols, 1).reshape(-1)]
    reshape x5 -> x1, local copies, waits for them, and re-layouts: 4.7 us -> 0.08 us  [on_device(): par = both.reshape(32)]
    ppermute x4, waiting for transfers between devices: 16.7 us -> 12.4 us  [on_device(): lax.ppermute(slab, ('x', 'c', 'zh'), [(index(i, h, h), index(i ^ d, 1 - h...]
    sub x3 -> x0, local copies, waits for them, and re-layouts: 3.97 us -> none  [coefficients(): 1.0 - wt * base]
  transfers between devices with their start and end apart: 40 -> 40, of which waited for: 9 -> 13; matrix products, arithmetic and copies ran while one was open for 16% -> 3% of each run, Pallas kernels for 0% -> 17%
where the time goes in v2:
time: 209 us
  starting transfers between devices  62.5 us (30%)
  waiting for transfers between devices  61.7 us (30%)
  Pallas kernels  55.6 us (27%)
  local copies, waits for them, and re-layouts  23.2 us (11%)
  other arithmetic  5.34 us (3%)
    pallas_call x9, Pallas kernels, call(): pl.pallas_call(kernel, in_specs=specs, out_specs=[pl.BlockSpec(memory_spa...  53.6 us
    ppermute x8, waiting for transfers between devices, z_xor(): return lax.ppermute(value, ZAX, z_perm(lambda z: z ^ m))  41.3 us
    unnamed x44, local copies, waits for them, and re-layouts  18.8 us
    ppermute x7, starting transfers between devices, on_device(): lax.ppermute(send, ('x', 'c'), [(i, i ^ m) for i in range(8)])  16.3 us
    ppermute x9, starting transfers between devices, y_ring(): return lax.ppermute(value, 'y', [(i, (i + by) % 4) for i in range(4)])  12.5 us
    ppermute x8, starting transfers between devices, z_xor(): return lax.ppermute(value, ZAX, z_perm(lambda z: z ^ m))  12.5 us
    ppermute x4, waiting for transfers between devices, on_device(): lax.ppermute(slab, ('x', 'c', 'zh'), [(index(i, h, h), index(i ^ d, 1 - h...  12.4 us
    ppermute x6, starting transfers between devices, z_ring(): return lax.ppermute(value, ZAX, z_perm(lambda z: (z + by) % 4))  8.03 us
  transfers between devices with their start and end apart: 40, of which 13 were waited for; matrix products, arithmetic and copies ran while one was open for 3% of the time, Pallas kernels for 17%

profile of v2, /device:TPU:1, one launch (start us, length us, event | category | flops | bytes accessed | tf_op | source)
XLA Modules:
  0.0 208.8 jit_solution(14352523583579956391)
XLA Ops:
  0.0 3.5 %constant_dynamic-slice_fusion = (f32[2,3,2,8,2304]{4,3,2,1,0:T(8,128)}, f32[2,3,2,8,2304]{4,3,2,1,0:T(8,128)}, f32[2,3,2,8,2304]{4,3,2,1,0:T(8,128)S(1)}, f32[2,3,2,8,2304]{4,3,2,1,0:T(8,128)}) fusion(f32[2,3,2,8,9216]{4,3,2,1,0:T(8,128)} %param.8, s32[]{:T(128)S(6)} %select_n.71, s32[]{:T(128)S(6)} %select_n.69, s32[]{:T(128)S(6)} %select_n.68, ...), kind=kLoop, calls=%fused_computation.28 | loop fusion | bytes 7077904 | tf_op jit(solution)/shard_map/dynamic_slice | solution.py:446
  3.6 2.5 %collective-permute-start.1 = (f32[2,3,2,8,2304]{4,3,2,1,0:T(8,128)}, f32[2,3,2,8,2304]{4,3,2,1,0:T(8,128)S(1)}, u32[]{:S(2)}, u32[]{:S(2)}) collective-permute-start(f32[2,3,2,8,2304]{4,3,2,1,0:T(8,128)} %get-tuple-element.40), channel_id=1, source_target_pairs={{0,64},{64,0},{1,65},{65,1},{2,66},{66,2},{3,67},{67,3},{4,68},{68... | collective-permute-start | bytes 2654216 | tf_op jit(solution)/shard_map/ppermute | solution.py:28
  6.0 3.3 %collective-permute-start.2 = (f32[2,3,2,8,2304]{4,3,2,1,0:T(8,128)}, f32[2,3,2,8,2304]{4,3,2,1,0:T(8,128)S(1)}, u32[]{:S(2)}, u32[]{:S(2)}) collective-permute-start(f32[2,3,2,8,2304]{4,3,2,1,0:T(8,128)} %get-tuple-element.42), channel_id=1, source_target_pairs={{0,1},{64,65},{1,0},{65,64},{2,3},{66,67},{3,2},{67,66},{4,5},{68,... | collective-permute-start | bytes 2654216 | tf_op jit(solution)/shard_map/ppermute | solution.py:28
  9.8 0.7 copy.12
  10.7 1.1 fusion
  11.8 2.8 %collective-permute-start.4 = (f32[3,8,2304]{2,1,0:T(8,128)S(1)}, f32[3,8,2304]{2,1,0:T(8,128)S(1)}, u32[]{:S(2)}, u32[]{:S(2)}) collective-permute-start(f32[3,8,2304]{2,1,0:T(8,128)S(1)} %get-tuple-element.43), channel_id=1, source_target_pairs={{0,65},{64,1},{1,64},{65,0},{2,67},{66,3},{3,66},{67,2},{4,69},{68... | collective-permute-start | bytes 663560 | tf_op jit(solution)/shard_map/ppermute | solution.py:28
  14.6 30.0 %collective-permute-done = f32[2,8]{1,0:T(2,128)S(1)} collective-permute-done((f32[2,8]{1,0:T(2,128)S(1)}, f32[2,8]{1,0:T(2,128)S(1)}, u32[]{:S(2)}, u32[]{:S(2)}) %collective-permute-start) | collective-permute-done | bytes 96 | tf_op jit(solution)/shard_map/ppermute | solution.py:28
  44.9 9.5 %collective-permute-done.4.p1 = f32[3,8,2304]{2,1,0:T(8,128)S(1)} collective-permute-done((f32[3,8,2304]{2,1,0:T(8,128)S(1)}, f32[3,8,2304]{2,1,0:T(8,128)S(1)}, u32[]{:S(2)}, u32[]{:S(2)}) %collective-permute-start.4) | collective-permute-done | bytes 221216 | tf_op jit(solution)/shard_map/ppermute | solution.py:28
  54.4 2.5 %products.1 = f32[72,128]{1,0:T(8,128)S(1)} custom-call(s32[4]{0:T(128)S(1)} %convert_reduce_fusion.slot_ref, f32[2,3,2,8,2304]{4,3,2,1,0:T(8,128)S(1)} %get-tuple-element.41.o0, f32[2,3,2,8,2304]{4,3,2,1,0:T(8,128)S(1)} %collective-permute-done.1.o1, f32[2,3,2,8,2304]{4,3,2,1,0:T(8,128)S(1)} %collective-permute-done.2.o2, ...), custom_call_target="tpu_custom_call" | custom-call | flops 20000000 | bytes 10000000 | tf_op jit(solution)/shard_map/products/pallas_call | solution.py:70
  57.3 3.6 %collective-permute-start.6 = (f32[72,128]{1,0:T(8,128)S(1)}, f32[72,128]{1,0:T(8,128)S(1)}, u32[]{:S(2)}, u32[]{:S(2)}) collective-permute-start(f32[72,128]{1,0:T(8,128)S(1)} %products.1), channel_id=1, source_target_pairs={{0,1},{64,65},{1,0},{65,64},{2,3},{66,67},{3,2},{67,66},{4,5},{68,... | collective-permute-start | bytes 110600 | tf_op jit(solution)/shard_map/ppermute | solution.py:28
  61.1 1.6 collective-permute-done.6
  62.6 2.8 %collective-permute-start.10 = (f32[72,128]{1,0:T(8,128)S(1)}, f32[72,128]{1,0:T(8,128)S(1)}, u32[]{:S(2)}, u32[]{:S(2)}) collective-permute-start(f32[72,128]{1,0:T(8,128)S(1)} %fusion.3.s0), channel_id=1, source_target_pairs={{0,6},{2,0},{4,2},{6,4},{1,7},{3,1},{5,3},{7,5},{8,14},{10,8},{12,... | collective-permute-start | bytes 110600 | tf_op jit(solution)/shard_map/ppermute | solution.py:36
  65.5 1.6 collective-permute-start.9
  67.1 2.4 %collective-permute-done.8.s1 = f32[72,128]{1,0:T(8,128)S(1)} collective-permute-done((f32[72,128]{1,0:T(8,128)S(1)}, f32[72,128]{1,0:T(8,128)S(1)}, u32[]{:S(2)}, u32[]{:S(2)}) %collective-permute-start.8) | collective-permute-done | bytes 36896 | tf_op jit(solution)/shard_map/ppermute | solution.py:36
  69.9 6.3 %right_sides.1 = (f32[9216,128]{1,0:T(8,128)S(1)}, f32[1152,128]{1,0:T(8,128)}, f32[1152,128]{1,0:T(8,128)}, f32[768,128]{1,0:T(8,128)}, f32[768,128]{1,0:T(8,128)}) custom-call(s32[4]{0:T(128)S(1)} %convert_reduce_fusion.slot_ref, s32[1]{0:T(128)} %bitcast.3.half_ref, f32[72,128]{1,0:T(8,128)S(1)} %fusion.3.s0, f32[72,128]{1,0:T(8,128)S(1)} %collective-permute-done.8.s1, ...), custom_call_target="tpu_custom_call" | custom-call | flops 20000000 | bytes 10000000 | tf_op jit(solution)/shard_map/right_sides/pallas_call | solution.py:70
  76.1 2.2 %copy-done = f32[9216,128]{1,0:T(8,128)} copy-done((f32[9216,128]{1,0:T(8,128)}, f32[9216,128]{1,0:T(8,128)S(1)}, u32[]{:S(2)}) %copy-start) | copy-done | bytes 4718616
  78.5 2.5 %collective-permute-start.12 = (f32[1152,128]{1,0:T(8,128)}, f32[1152,128]{1,0:T(8,128)}, u32[]{:S(2)}, u32[]{:S(2)}) collective-permute-start(f32[1152,128]{1,0:T(8,128)} %get-tuple-element.25), channel_id=1, source_target_pairs={{0,6},{2,0},{4,2},{6,4},{1,7},{3,1},{5,3},{7,5},{8,14},{10,8},{12,... | collective-permute-start | bytes 1769480 | tf_op jit(solution)/shard_map/ppermute | solution.py:36
  81.5 2.2 %collective-permute-start.14 = (f32[768,128]{1,0:T(8,128)}, f32[768,128]{1,0:T(8,128)}, u32[]{:S(2)}, u32[]{:S(2)}) collective-permute-start(f32[768,128]{1,0:T(8,128)} %get-tuple-element.27), channel_id=1, source_target_pairs={{0,65},{64,0},{1,64},{65,1},{2,67},{66,2},{3,66},{67,3},{4,69},{68... | collective-permute-start | bytes 1179656 | tf_op jit(solution)/shard_map/ppermute | solution.py:32
  83.8 0.9 copy-done.9
  84.7 0.9 copy-done.11
  85.6 2.0 orbital_rows.1
  87.7 2.2 %copy-done.6 = f32[9216,128]{1,0:T(8,128)} copy-done((f32[9216,128]{1,0:T(8,128)}, f32[9216,128]{1,0:T(8,128)S(1)}, u32[]{:S(2)}) %copy-start.6) | copy-done | bytes 4718616
  89.9 2.4 %copy-done.1 = f32[9216,128]{1,0:T(8,128)S(1)} copy-done((f32[9216,128]{1,0:T(8,128)S(1)}, f32[9216,128]{1,0:T(8,128)}, u32[]{:S(2)}) %copy-start.1) | copy-done | bytes 4718616
  92.3 0.9 copy-done.14
  93.2 11.0 %step.2.u_in = f32[9216,128]{1,0:T(8,128)S(1)} custom-call(f32[32]{0:T(128)S(1)} %reshape.4.par_ref, f32[4]{0:T(128)S(1)} %convert_multiply_fusion.w_ref, f32[9216,128]{1,0:T(8,128)S(1)} %copy-done.1, f32[9216,128]{1,0:T(8,128)S(1)} %copy-done.1, f32[384,128]{1,0:T(8,128)S(1)} %get-tuple-element.23.v_ref, bf16[256,256]{1,0:T(8,128)(2,1)S(1)} %copy-done.14), custom_call_target="tpu_custom_call" | custom-call | flops 60000000 | bytes 10000000 | tf_op jit(solution)/shard_map/step/pallas_call | solution.py:70
  104.2 3.1 %faces.2 = (f32[9216,128]{1,0:T(8,128)S(1)}, f32[1152,128]{1,0:T(8,128)S(1)}, f32[1152,128]{1,0:T(8,128)S(1)}, f32[768,128]{1,0:T(8,128)S(1)}, f32[768,128]{1,0:T(8,128)S(1)}) custom-call(f32[32]{0:T(128)S(1)} %reshape.4.par_ref, f32[4]{0:T(128)S(1)} %convert_multiply_fusion.w_ref, f32[9216,128]{1,0:T(8,128)S(1)} %step.2.u_in, ...), custom_call_target="tpu_custom_call", output_to_operand_aliasing={{0}: (2, {})} | custom-call | flops 10000000 | bytes 10000000 | tf_op jit(solution)/shard_map/faces/pallas_call | solution.py:70
  107.4 2.7 %collective-permute-start.16 = (f32[1152,128]{1,0:T(8,128)S(1)}, f32[1152,128]{1,0:T(8,128)S(1)}, u32[]{:S(2)}, u32[]{:S(2)}) collective-permute-start(f32[1152,128]{1,0:T(8,128)S(1)} %get-tuple-element.30), channel_id=1, source_target_pairs={{0,6},{2,0},{4,2},{6,4},{1,7},{3,1},{5,3},{7,5},{8,14},{10,8},{12,... | collective-permute-start | bytes 1769480 | tf_op jit(solution)/shard_map/ppermute | solution.py:36
  110.0 2.7 %collective-permute-start.18 = (f32[768,128]{1,0:T(8,128)S(1)}, f32[768,128]{1,0:T(8,128)S(1)}, u32[]{:S(2)}, u32[]{:S(2)}) collective-permute-start(f32[768,128]{1,0:T(8,128)S(1)} %get-tuple-element.32), channel_id=1, source_target_pairs={{0,65},{64,0},{1,64},{65,1},{2,67},{66,2},{3,66},{67,3},{4,69},{68... | collective-permute-start | bytes 1179656 | tf_op jit(solution)/shard_map/ppermute | solution.py:32
  112.7 10.9 %step.3.u_in = f32[9216,128]{1,0:T(8,128)S(1)} custom-call(f32[32]{0:T(128)S(1)} %reshape.4.par_ref, f32[4]{0:T(128)S(1)} %convert_multiply_fusion.w_ref, f32[9216,128]{1,0:T(8,128)S(1)} %get-tuple-element.28.u_ref, f32[9216,128]{1,0:T(8,128)S(1)} %copy-done.2, f32[384,128]{1,0:T(8,128)S(1)} %get-tuple-element.23.v_ref, bf16[256,256]{1,0:T(8,128)(2,1)S(1)} %copy-done.15), custom_call_target="tpu_custom_call" | custom-call | flops 60000000 | bytes 10000000 | tf_op jit(solution)/shard_map/step/pallas_call | solution.py:70
  123.7 3.1 %faces.3 = (f32[9216,128]{1,0:T(8,128)S(1)}, f32[1152,128]{1,0:T(8,128)S(1)}, f32[1152,128]{1,0:T(8,128)}, f32[768,128]{1,0:T(8,128)}, f32[768,128]{1,0:T(8,128)}) custom-call(f32[32]{0:T(128)S(1)} %reshape.4.par_ref, f32[4]{0:T(128)S(1)} %convert_multiply_fusion.w_ref, f32[9216,128]{1,0:T(8,128)S(1)} %step.3.u_in, ...), custom_call_target="tpu_custom_call", output_to_operand_aliasing={{0}: (2, {})} | custom-call | flops 10000000 | bytes 10000000 | tf_op jit(solution)/shard_map/faces/pallas_call | solution.py:70
  126.8 2.2 %copy-done.4 = f32[9216,128]{1,0:T(8,128)} copy-done((f32[9216,128]{1,0:T(8,128)}, f32[9216,128]{1,0:T(8,128)S(1)}, u32[]{:S(2)}) %copy-start.4) | copy-done | bytes 4718616
  129.1 2.7 %collective-permute-start.20 = (f32[1152,128]{1,0:T(8,128)S(1)}, f32[1152,128]{1,0:T(8,128)S(1)}, u32[]{:S(2)}, u32[]{:S(2)}) collective-permute-start(f32[1152,128]{1,0:T(8,128)S(1)} %get-tuple-element.36), channel_id=1, source_target_pairs={{0,6},{2,0},{4,2},{6,4},{1,7},{3,1},{5,3},{7,5},{8,14},{10,8},{12,... | collective-permute-start | bytes 1769480 | tf_op jit(solution)/shard_map/ppermute | solution.py:36
  131.7 2.7 %collective-permute-start.22 = (f32[768,128]{1,0:T(8,128)}, f32[768,128]{1,0:T(8,128)S(1)}, u32[]{:S(2)}, u32[]{:S(2)}) collective-permute-start(f32[768,128]{1,0:T(8,128)} %get-tuple-element.38), channel_id=1, source_target_pairs={{0,65},{64,0},{1,64},{65,1},{2,67},{66,2},{3,66},{67,3},{4,69},{68... | collective-permute-start | bytes 1179656 | tf_op jit(solution)/shard_map/ppermute | solution.py:32
  134.4 2.3 %copy-done.3 = f32[9216,128]{1,0:T(8,128)S(1)} copy-done((f32[9216,128]{1,0:T(8,128)S(1)}, f32[9216,128]{1,0:T(8,128)}, u32[]{:S(2)}) %copy-start.3) | copy-done | bytes 4718616
  136.8 2.3 %copy-done.5 = f32[9216,128]{1,0:T(8,128)S(1)} copy-done((f32[9216,128]{1,0:T(8,128)S(1)}, f32[9216,128]{1,0:T(8,128)}, u32[]{:S(2)}) %copy-start.5) | copy-done | bytes 4718616
  139.1 2.3 %copy-done.7 = f32[9216,128]{1,0:T(8,128)S(1)} copy-done((f32[9216,128]{1,0:T(8,128)S(1)}, f32[9216,128]{1,0:T(8,128)}, u32[]{:S(2)}) %copy-start.7) | copy-done | bytes 4718616
  141.4 12.5 %last_step.1.d_in = f32[768,128]{1,0:T(8,128)S(1)} custom-call(f32[32]{0:T(128)S(1)} %reshape.4.par_ref, f32[4]{0:T(128)S(1)} %convert_multiply_fusion.w_ref, f32[9216,128]{1,0:T(8,128)S(1)} %copy-done.5, f32[9216,128]{1,0:T(8,128)S(1)} %copy-done.3, f32[384,128]{1,0:T(8,128)S(1)} %copy-done.13, bf16[256,256]{1,0:T(8,128)(2,1)S(1)} %copy-done.15, ...), custom_call_target="tpu_custom_call" | custom-call | flops 60000000 | bytes 10000000 | tf_op jit(solution)/shard_map/last_step/pallas_call | solution.py:70
  154.0 2.2 %density.1 = f32[8,8,1152]{2,1,0:T(8,128)S(1)} custom-call(f32[32]{0:T(128)S(1)} %reshape.4.par_ref, f32[4]{0:T(128)S(1)} %convert_multiply_fusion.w_ref, f32[768,128]{1,0:T(8,128)S(1)} %last_step.1.d_in, f32[1152,128]{1,0:T(8,128)S(1)} %collective-permute-done.19.zm, f32[1152,128]{1,0:T(8,128)S(1)} %collective-permute-done.20.zp, ...), custom_call_target="tpu_custom_call" | custom-call | flops 10000000 | bytes 10000000 | tf_op jit(solution)/shard_map/density/pallas_call | solution.py:70
  156.2 8.4 %collective-permute-start.23 = (f32[8,1152]{1,0:T(8,128)S(1)}, f32[8,1152]{1,0:T(8,128)S(1)}, u32[]{:S(2)}, u32[]{:S(2)}) collective-permute-start(f32[8,1152]{1,0:T(8,128)S(1)} %get-tuple-element.45), channel_id=1, source_target_pairs={{0,8},{8,0},{16,24},{24,16},{32,40},{40,32},{48,56},{56,48},{1,9},... | collective-permute-start | bytes 110600 | tf_op jit(solution)/shard_map/ppermute | solution.py:484
  164.6 1.2 collective-permute-start.24
  166.4 2.7 %collective-permute-start.26 = (f32[8,1152]{1,0:T(8,128)S(1)}, f32[8,1152]{1,0:T(8,128)S(1)}, u32[]{:S(2)}, u32[]{:S(2)}) collective-permute-start(f32[8,1152]{1,0:T(8,128)S(1)} %get-tuple-element.49), channel_id=1, source_target_pairs={{0,32},{8,40},{16,48},{24,56},{32,0},{40,8},{48,16},{56,24},{1,33}... | collective-permute-start | bytes 110600 | tf_op jit(solution)/shard_map/ppermute | solution.py:484
  169.6 2.5 %collective-permute-start.28 = (f32[8,1152]{1,0:T(8,128)S(1)}, f32[8,1152]{1,0:T(8,128)S(1)}, u32[]{:S(2)}, u32[]{:S(2)}) collective-permute-start(f32[8,1152]{1,0:T(8,128)S(1)} %get-tuple-element.47), channel_id=1, source_target_pairs={{0,48},{8,56},{16,32},{24,40},{32,16},{40,24},{48,0},{56,8},{1,49}... | collective-permute-start | bytes 110600 | tf_op jit(solution)/shard_map/ppermute | solution.py:484
  172.6 1.6 collective-permute-done.27
  174.2 0.8 collective-permute-done.28
  175.0 1.8 collective-permute-done.29
  176.8 0.7 collective-permute-start.30
  177.5 4.0 %collective-permute-start.31 = (f32[8,1152]{1,0:T(8,128)S(1)}, f32[8,1152]{1,0:T(8,128)S(1)}, u32[]{:S(2)}, u32[]{:S(2)}) collective-permute-start(f32[8,1152]{1,0:T(8,128)S(1)} %fusion.9), channel_id=1, source_target_pairs={{8,9},{72,73},{1,0},{65,64},{10,11},{74,75},{3,2},{67,66},{12,13},... | collective-permute-start | bytes 110600 | tf_op jit(solution)/shard_map/ppermute | solution.py:493
  181.5 1.3 collective-permute-start.32
  182.8 1.0 collective-permute-done.32
  183.9 0.7 collective-permute-start.38
  184.6 1.3 collective-permute-start.39
  186.5 0.7 collective-permute-start.36
  187.1 1.3 collective-permute-start.37
  188.4 0.7 collective-permute-start.34
  189.1 1.3 collective-permute-start.35
  190.4 7.6 %collective-permute-done.39 = f32[4,8,1152]{2,1,0:T(8,128)S(1)} collective-permute-done((f32[4,8,1152]{2,1,0:T(8,128)S(1)}, f32[4,8,1152]{2,1,0:T(8,128)S(1)}, u32[]{:S(2)}, u32[]{:S(2)}) %collective-permute-start.39) | collective-permute-done | bytes 147488 | tf_op jit(solution)/shard_map/ppermute | solution.py:499
  198.1 1.3 collective-permute-start.33
  199.4 0.7 broadcast_select_fusion.b3
  200.0 2.9 %collective-permute-done.37 = f32[4,8,1152]{2,1,0:T(8,128)S(1)} collective-permute-done((f32[4,8,1152]{2,1,0:T(8,128)S(1)}, f32[4,8,1152]{2,1,0:T(8,128)S(1)}, u32[]{:S(2)}, u32[]{:S(2)}) %collective-permute-start.37) | collective-permute-done | bytes 147488 | tf_op jit(solution)/shard_map/ppermute | solution.py:499
  203.0 0.7 broadcast_select_fusion.1.b2
  203.7 1.8 collective-permute-done.33
  205.4 0.7 broadcast_select_fusion.3.b0
  206.1 0.7 broadcast_select_fusion.2.b1
  206.8 2.0 assemble.1
  (92 shorter events, 5.0 us)
Async XLA Ops:
  0.0 9.3 %copy-start.18 = (s32[2]{0:T(128)S(1)}, s32[2]{0:T(128)}, u32[]{:S(2)}) copy-start(s32[2]{0:T(128)} %param.9) | copy-start | bytes 28
  0.0 10.6 %copy-start.17 = (f32[2,3]{1,0:T(2,128)S(1)}, f32[2,3]{1,0:T(2,128)}, u32[]{:S(2)}) copy-start(f32[2,3]{1,0:T(2,128)} %param.10) | copy-start | bytes 76
  0.0 10.6 %copy-start.16 = (f32[2,3]{1,0:T(2,128)S(1)}, f32[2,3]{1,0:T(2,128)}, u32[]{:S(2)}) copy-start(f32[2,3]{1,0:T(2,128)} %param.11) | copy-start | bytes 76
  3.6 50.9 %collective-permute-start.1 = (f32[2,3,2,8,2304]{4,3,2,1,0:T(8,128)}, f32[2,3,2,8,2304]{4,3,2,1,0:T(8,128)S(1)}, u32[]{:S(2)}, u32[]{:S(2)}) collective-permute-start(f32[2,3,2,8,2304]{4,3,2,1,0:T(8,128)} %get-tuple-element.40), channel_id=1, source_target_pairs={{0,64},{64,0},{1,65},{65,1},{2,66},{66,2},{3,67},{67,3},{4,68},{68... | collective-permute-start | bytes 2654216 | tf_op jit(solution)/shard_map/ppermute | solution.py:28
  6.0 48.4 %collective-permute-start.2 = (f32[2,3,2,8,2304]{4,3,2,1,0:T(8,128)}, f32[2,3,2,8,2304]{4,3,2,1,0:T(8,128)S(1)}, u32[]{:S(2)}, u32[]{:S(2)}) collective-permute-start(f32[2,3,2,8,2304]{4,3,2,1,0:T(8,128)} %get-tuple-element.42), channel_id=1, source_target_pairs={{0,1},{64,65},{1,0},{65,64},{2,3},{66,67},{3,2},{67,66},{4,5},{68,... | collective-permute-start | bytes 2654216 | tf_op jit(solution)/shard_map/ppermute | solution.py:28
  9.3 45.1 %collective-permute-start.3 = (f32[2,3,2,8,2304]{4,3,2,1,0:T(8,128)}, f32[2,3,2,8,2304]{4,3,2,1,0:T(8,128)S(1)}, u32[]{:S(2)}, u32[]{:S(2)}) collective-permute-start(f32[2,3,2,8,2304]{4,3,2,1,0:T(8,128)} %get-tuple-element.39), channel_id=1, source_target_pairs={{0,65},{64,1},{1,64},{65,0},{2,67},{66,3},{3,66},{67,2},{4,69},{68... | collective-permute-start | bytes 2654216 | tf_op jit(solution)/shard_map/ppermute | solution.py:28
  10.7 33.9 %collective-permute-start = (f32[2,8]{1,0:T(2,128)S(1)}, f32[2,8]{1,0:T(2,128)S(1)}, u32[]{:S(2)}, u32[]{:S(2)}) collective-permute-start(f32[2,8]{1,0:T(2,128)S(1)} %pad_maximum_fusion.2), channel_id=1, source_target_pairs={{0,64},{64,0},{1,65},{65,1},{2,66},{66,2},{3,67},{67,3},{4,68},{68... | collective-permute-start | bytes 200 | tf_op jit(solution)/shard_map/ppermute | solution.py:28
  10.7 73.0 %copy-start.19 = (s32[4]{0:T(128)S(1)}, s32[4]{0:T(128)}, u32[]{:S(2)}) copy-start(s32[4]{0:T(128)} %param.14) | copy-start | bytes 52
  11.8 64.3 %copy-start.8 = (f32[3,8,2304]{2,1,0:T(8,128)}, f32[3,8,2304]{2,1,0:T(8,128)S(1)}, u32[]{:S(2)}) copy-start(f32[3,8,2304]{2,1,0:T(8,128)S(1)} %get-tuple-element.44.p0) | copy-start | bytes 663556
  11.8 42.6 %collective-permute-start.4 = (f32[3,8,2304]{2,1,0:T(8,128)S(1)}, f32[3,8,2304]{2,1,0:T(8,128)S(1)}, u32[]{:S(2)}, u32[]{:S(2)}) collective-permute-start(f32[3,8,2304]{2,1,0:T(8,128)S(1)} %get-tuple-element.43), channel_id=1, source_target_pairs={{0,65},{64,1},{1,64},{65,0},{2,67},{66,3},{3,66},{67,2},{4,69},{68... | collective-permute-start | bytes 663560 | tf_op jit(solution)/shard_map/ppermute | solution.py:28
  54.4 23.9 %copy-start.10 = (f32[3,8,2304]{2,1,0:T(8,128)}, f32[3,8,2304]{2,1,0:T(8,128)S(1)}, u32[]{:S(2)}) copy-start(f32[3,8,2304]{2,1,0:T(8,128)S(1)} %collective-permute-done.4.p1) | copy-start | bytes 663556
  57.0 4.1 %collective-permute-start.7 = (f32[72,128]{1,0:T(8,128)S(1)}, f32[72,128]{1,0:T(8,128)S(1)}, u32[]{:S(2)}, u32[]{:S(2)}) collective-permute-start(f32[72,128]{1,0:T(8,128)S(1)} %products.1), channel_id=1, source_target_pairs={{0,65},{64,1},{1,64},{65,0},{2,67},{66,3},{3,66},{67,2},{4,69},{68... | collective-permute-start | bytes 110600 | tf_op jit(solution)/shard_map/ppermute | solution.py:28
  57.3 3.7 %collective-permute-start.5 = (f32[72,128]{1,0:T(8,128)S(1)}, f32[72,128]{1,0:T(8,128)S(1)}, u32[]{:S(2)}, u32[]{:S(2)}) collective-permute-start(f32[72,128]{1,0:T(8,128)S(1)} %products.1), channel_id=1, source_target_pairs={{0,64},{64,0},{1,65},{65,1},{2,66},{66,2},{3,67},{67,3},{4,68},{68... | collective-permute-start | bytes 110600 | tf_op jit(solution)/shard_map/ppermute | solution.py:28
  57.3 5.3 %collective-permute-start.6 = (f32[72,128]{1,0:T(8,128)S(1)}, f32[72,128]{1,0:T(8,128)S(1)}, u32[]{:S(2)}, u32[]{:S(2)}) collective-permute-start(f32[72,128]{1,0:T(8,128)S(1)} %products.1), channel_id=1, source_target_pairs={{0,1},{64,65},{1,0},{65,64},{2,3},{66,67},{3,2},{67,66},{4,5},{68,... | collective-permute-start | bytes 110600 | tf_op jit(solution)/shard_map/ppermute | solution.py:28
  62.6 4.5 %collective-permute-start.10 = (f32[72,128]{1,0:T(8,128)S(1)}, f32[72,128]{1,0:T(8,128)S(1)}, u32[]{:S(2)}, u32[]{:S(2)}) collective-permute-start(f32[72,128]{1,0:T(8,128)S(1)} %fusion.3.s0), channel_id=1, source_target_pairs={{0,6},{2,0},{4,2},{6,4},{1,7},{3,1},{5,3},{7,5},{8,14},{10,8},{12,... | collective-permute-start | bytes 110600 | tf_op jit(solution)/shard_map/ppermute | solution.py:36
  65.5 4.0 %collective-permute-start.8 = (f32[72,128]{1,0:T(8,128)S(1)}, f32[72,128]{1,0:T(8,128)S(1)}, u32[]{:S(2)}, u32[]{:S(2)}) collective-permute-start(f32[72,128]{1,0:T(8,128)S(1)} %fusion.3.s0), channel_id=1, source_target_pairs={{0,2},{2,4},{4,6},{6,0},{1,3},{3,5},{5,7},{7,1},{8,10},{10,12},{12... | collective-permute-start | bytes 110600 | tf_op jit(solution)/shard_map/ppermute | solution.py:36
  65.5 4.4 %collective-permute-start.9 = (f32[72,128]{1,0:T(8,128)S(1)}, f32[72,128]{1,0:T(8,128)S(1)}, u32[]{:S(2)}, u32[]{:S(2)}) collective-permute-start(f32[72,128]{1,0:T(8,128)S(1)} %fusion.3.s0), channel_id=1, source_target_pairs={{0,4},{2,6},{4,0},{6,2},{1,5},{3,7},{5,1},{7,3},{8,12},{10,14},{12... | collective-permute-start | bytes 110600 | tf_op jit(solution)/shard_map/ppermute | solution.py:36
  76.1 2.2 %copy-start = (f32[9216,128]{1,0:T(8,128)}, f32[9216,128]{1,0:T(8,128)S(1)}, u32[]{:S(2)}) copy-start(f32[9216,128]{1,0:T(8,128)S(1)} %get-tuple-element.22.u_ref.r_ref) | copy-start | bytes 14155780
  78.3 25.9 %collective-permute-start.11 = (f32[1152,128]{1,0:T(8,128)}, f32[1152,128]{1,0:T(8,128)}, u32[]{:S(2)}, u32[]{:S(2)}) collective-permute-start(f32[1152,128]{1,0:T(8,128)} %get-tuple-element.24), channel_id=1, source_target_pairs={{0,2},{2,4},{4,6},{6,0},{1,3},{3,5},{5,7},{7,1},{8,10},{10,12},{12... | collective-permute-start | bytes 1769480 | tf_op jit(solution)/shard_map/ppermute | solution.py:36
  78.5 25.7 %collective-permute-start.12 = (f32[1152,128]{1,0:T(8,128)}, f32[1152,128]{1,0:T(8,128)}, u32[]{:S(2)}, u32[]{:S(2)}) collective-permute-start(f32[1152,128]{1,0:T(8,128)} %get-tuple-element.25), channel_id=1, source_target_pairs={{0,6},{2,0},{4,2},{6,4},{1,7},{3,1},{5,3},{7,5},{8,14},{10,8},{12,... | collective-permute-start | bytes 1769480 | tf_op jit(solution)/shard_map/ppermute | solution.py:36
  81.0 23.2 %collective-permute-start.13 = (f32[768,128]{1,0:T(8,128)}, f32[768,128]{1,0:T(8,128)}, u32[]{:S(2)}, u32[]{:S(2)}) collective-permute-start(f32[768,128]{1,0:T(8,128)} %get-tuple-element.26), channel_id=1, source_target_pairs={{0,64},{64,1},{1,65},{65,0},{2,66},{66,3},{3,67},{67,2},{4,68},{68... | collective-permute-start | bytes 1179656 | tf_op jit(solution)/shard_map/ppermute | solution.py:32
  81.5 22.7 %collective-permute-start.14 = (f32[768,128]{1,0:T(8,128)}, f32[768,128]{1,0:T(8,128)}, u32[]{:S(2)}, u32[]{:S(2)}) collective-permute-start(f32[768,128]{1,0:T(8,128)} %get-tuple-element.27), channel_id=1, source_target_pairs={{0,65},{64,0},{1,64},{65,1},{2,67},{66,2},{3,66},{67,3},{4,69},{68... | collective-permute-start | bytes 1179656 | tf_op jit(solution)/shard_map/ppermute | solution.py:32
  83.8 0.9 copy-start.9
  84.7 0.9 copy-start.11
  87.7 2.2 %copy-start.6 = (f32[9216,128]{1,0:T(8,128)}, f32[9216,128]{1,0:T(8,128)S(1)}, u32[]{:S(2)}) copy-start(f32[9216,128]{1,0:T(8,128)S(1)} %get-tuple-element.34.refs_0_.orb_ref) | copy-start | bytes 14155780
  89.8 22.9 %copy-start.12 = (f32[384,128]{1,0:T(8,128)}, f32[384,128]{1,0:T(8,128)S(1)}, u32[]{:S(2)}) copy-start(f32[384,128]{1,0:T(8,128)S(1)} %get-tuple-element.23.v_ref) | copy-start | bytes 589828
  89.8 2.4 %copy-start.1 = (f32[9216,128]{1,0:T(8,128)S(1)}, f32[9216,128]{1,0:T(8,128)}, u32[]{:S(2)}) copy-start(f32[9216,128]{1,0:T(8,128)} %copy-done) | copy-start | bytes 14155780
  92.3 0.9 copy-start.14
  104.1 8.6 %copy-start.2 = (f32[9216,128]{1,0:T(8,128)S(1)}, f32[9216,128]{1,0:T(8,128)}, u32[]{:S(2)}) copy-start(f32[9216,128]{1,0:T(8,128)} %copy-done) | copy-start | bytes 14155780
  104.1 8.6 %copy-start.15 = (bf16[256,256]{1,0:T(8,128)(2,1)S(1)}, bf16[256,256]{1,0:T(8,128)(2,1)}, u32[]{:S(2)}) copy-start(bf16[256,256]{1,0:T(8,128)(2,1)} %constant.74.clone.m_ref) | copy-start | bytes 393220
  107.3 16.4 %collective-permute-start.15 = (f32[1152,128]{1,0:T(8,128)S(1)}, f32[1152,128]{1,0:T(8,128)S(1)}, u32[]{:S(2)}, u32[]{:S(2)}) collective-permute-start(f32[1152,128]{1,0:T(8,128)S(1)} %get-tuple-element.29), channel_id=1, source_target_pairs={{0,2},{2,4},{4,6},{6,0},{1,3},{3,5},{5,7},{7,1},{8,10},{10,12},{12... | collective-permute-start | bytes 1769480 | tf_op jit(solution)/shard_map/ppermute | solution.py:36
  107.4 16.3 %collective-permute-start.16 = (f32[1152,128]{1,0:T(8,128)S(1)}, f32[1152,128]{1,0:T(8,128)S(1)}, u32[]{:S(2)}, u32[]{:S(2)}) collective-permute-start(f32[1152,128]{1,0:T(8,128)S(1)} %get-tuple-element.30), channel_id=1, source_target_pairs={{0,6},{2,0},{4,2},{6,4},{1,7},{3,1},{5,3},{7,5},{8,14},{10,8},{12,... | collective-permute-start | bytes 1769480 | tf_op jit(solution)/shard_map/ppermute | solution.py:36
  110.0 13.6 %collective-permute-start.17 = (f32[768,128]{1,0:T(8,128)S(1)}, f32[768,128]{1,0:T(8,128)S(1)}, u32[]{:S(2)}, u32[]{:S(2)}) collective-permute-start(f32[768,128]{1,0:T(8,128)S(1)} %get-tuple-element.31), channel_id=1, source_target_pairs={{0,64},{64,1},{1,65},{65,0},{2,66},{66,3},{3,67},{67,2},{4,68},{68... | collective-permute-start | bytes 1179656 | tf_op jit(solution)/shard_map/ppermute | solution.py:32
  110.0 13.6 %collective-permute-start.18 = (f32[768,128]{1,0:T(8,128)S(1)}, f32[768,128]{1,0:T(8,128)S(1)}, u32[]{:S(2)}, u32[]{:S(2)}) collective-permute-start(f32[768,128]{1,0:T(8,128)S(1)} %get-tuple-element.32), channel_id=1, source_target_pairs={{0,65},{64,0},{1,64},{65,1},{2,67},{66,2},{3,66},{67,3},{4,69},{68... | collective-permute-start | bytes 1179656 | tf_op jit(solution)/shard_map/ppermute | solution.py:32
  123.6 10.8 %copy-start.13 = (f32[384,128]{1,0:T(8,128)S(1)}, f32[384,128]{1,0:T(8,128)}, u32[]{:S(2)}) copy-start(f32[384,128]{1,0:T(8,128)} %copy-done.12) | copy-start | bytes 589828
  123.7 30.3 %slice-start = ((s8[4718592]{0:T(1024)(128)(4,1)}), s8[524288]{0:T(1024)(128)(4,1)S(1)}, s32[]{:S(2)}) async-start(s8[4718592]{0:T(1024)(128)(4,1)} %bitcast.38), calls=%async_computation | async-start | bytes 1048576
  126.8 2.2 %copy-start.4 = (f32[9216,128]{1,0:T(8,128)}, f32[9216,128]{1,0:T(8,128)S(1)}, u32[]{:S(2)}) copy-start(f32[9216,128]{1,0:T(8,128)S(1)} %get-tuple-element.33.u_ref) | copy-start | bytes 14155780
  129.1 24.9 %collective-permute-start.19 = (f32[1152,128]{1,0:T(8,128)}, f32[1152,128]{1,0:T(8,128)S(1)}, u32[]{:S(2)}, u32[]{:S(2)}) collective-permute-start(f32[1152,128]{1,0:T(8,128)} %get-tuple-element.35), channel_id=1, source_target_pairs={{0,2},{2,4},{4,6},{6,0},{1,3},{3,5},{5,7},{7,1},{8,10},{10,12},{12... | collective-permute-start | bytes 1769480 | tf_op jit(solution)/shard_map/ppermute | solution.py:36
  129.1 24.9 %collective-permute-start.20 = (f32[1152,128]{1,0:T(8,128)S(1)}, f32[1152,128]{1,0:T(8,128)S(1)}, u32[]{:S(2)}, u32[]{:S(2)}) collective-permute-start(f32[1152,128]{1,0:T(8,128)S(1)} %get-tuple-element.36), channel_id=1, source_target_pairs={{0,6},{2,0},{4,2},{6,4},{1,7},{3,1},{5,3},{7,5},{8,14},{10,8},{12,... | collective-permute-start | bytes 1769480 | tf_op jit(solution)/shard_map/ppermute | solution.py:36
  131.7 22.2 %collective-permute-start.21 = (f32[768,128]{1,0:T(8,128)}, f32[768,128]{1,0:T(8,128)S(1)}, u32[]{:S(2)}, u32[]{:S(2)}) collective-permute-start(f32[768,128]{1,0:T(8,128)} %get-tuple-element.37), channel_id=1, source_target_pairs={{0,64},{64,1},{1,65},{65,0},{2,66},{66,3},{3,67},{67,2},{4,68},{68... | collective-permute-start | bytes 1179656 | tf_op jit(solution)/shard_map/ppermute | solution.py:32
  131.7 22.2 %collective-permute-start.22 = (f32[768,128]{1,0:T(8,128)}, f32[768,128]{1,0:T(8,128)S(1)}, u32[]{:S(2)}, u32[]{:S(2)}) collective-permute-start(f32[768,128]{1,0:T(8,128)} %get-tuple-element.38), channel_id=1, source_target_pairs={{0,65},{64,0},{1,64},{65,1},{2,67},{66,2},{3,66},{67,3},{4,69},{68... | collective-permute-start | bytes 1179656 | tf_op jit(solution)/shard_map/ppermute | solution.py:32
  134.4 2.3 %copy-start.3 = (f32[9216,128]{1,0:T(8,128)S(1)}, f32[9216,128]{1,0:T(8,128)}, u32[]{:S(2)}) copy-start(f32[9216,128]{1,0:T(8,128)} %copy-done) | copy-start | bytes 14155780
  136.8 2.3 %copy-start.5 = (f32[9216,128]{1,0:T(8,128)S(1)}, f32[9216,128]{1,0:T(8,128)}, u32[]{:S(2)}) copy-start(f32[9216,128]{1,0:T(8,128)} %copy-done.4) | copy-start | bytes 14155780
  139.1 2.3 %copy-start.7 = (f32[9216,128]{1,0:T(8,128)S(1)}, f32[9216,128]{1,0:T(8,128)}, u32[]{:S(2)}) copy-start(f32[9216,128]{1,0:T(8,128)} %copy-done.6) | copy-start | bytes 14155780
  141.4 12.5 %slice-start.1 = ((s8[4718592]{0:T(1024)(128)(4,1)}), s8[4194304]{0:T(1024)(128)(4,1)S(1)}, s32[]{:S(2)}) async-start(s8[4718592]{0:T(1024)(128)(4,1)} %bitcast.38), calls=%async_computation.1 | async-start | bytes 8388608
  156.2 13.4 %collective-permute-start.23 = (f32[8,1152]{1,0:T(8,128)S(1)}, f32[8,1152]{1,0:T(8,128)S(1)}, u32[]{:S(2)}, u32[]{:S(2)}) collective-permute-start(f32[8,1152]{1,0:T(8,128)S(1)} %get-tuple-element.45), channel_id=1, source_target_pairs={{0,8},{8,0},{16,24},{24,16},{32,40},{40,32},{48,56},{56,48},{1,9},... | collective-permute-start | bytes 110600 | tf_op jit(solution)/shard_map/ppermute | solution.py:484
  164.6 7.5 %collective-permute-start.24 = (f32[8,1152]{1,0:T(8,128)S(1)}, f32[8,1152]{1,0:T(8,128)S(1)}, u32[]{:S(2)}, u32[]{:S(2)}) collective-permute-start(f32[8,1152]{1,0:T(8,128)S(1)} %get-tuple-element.51), channel_id=1, source_target_pairs={{0,16},{8,24},{16,0},{24,8},{32,48},{40,56},{48,32},{56,40},{1,17}... | collective-permute-start | bytes 110600 | tf_op jit(solution)/shard_map/ppermute | solution.py:484
  165.8 6.7 %collective-permute-start.25 = (f32[8,1152]{1,0:T(8,128)S(1)}, f32[8,1152]{1,0:T(8,128)S(1)}, u32[]{:S(2)}, u32[]{:S(2)}) collective-permute-start(f32[8,1152]{1,0:T(8,128)S(1)} %get-tuple-element.50), channel_id=1, source_target_pairs={{0,24},{8,16},{16,8},{24,0},{32,56},{40,48},{48,40},{56,32},{1,25}... | collective-permute-start | bytes 110600 | tf_op jit(solution)/shard_map/ppermute | solution.py:484
  166.4 6.2 %collective-permute-start.26 = (f32[8,1152]{1,0:T(8,128)S(1)}, f32[8,1152]{1,0:T(8,128)S(1)}, u32[]{:S(2)}, u32[]{:S(2)}) collective-permute-start(f32[8,1152]{1,0:T(8,128)S(1)} %get-tuple-element.49), channel_id=1, source_target_pairs={{0,32},{8,40},{16,48},{24,56},{32,0},{40,8},{48,16},{56,24},{1,33}... | collective-permute-start | bytes 110600 | tf_op jit(solution)/shard_map/ppermute | solution.py:484
  169.1 5.1 %collective-permute-start.27 = (f32[8,1152]{1,0:T(8,128)S(1)}, f32[8,1152]{1,0:T(8,128)S(1)}, u32[]{:S(2)}, u32[]{:S(2)}) collective-permute-start(f32[8,1152]{1,0:T(8,128)S(1)} %get-tuple-element.48), channel_id=1, source_target_pairs={{0,40},{8,32},{16,56},{24,48},{32,8},{40,0},{48,24},{56,16},{1,41}... | collective-permute-start | bytes 110600 | tf_op jit(solution)/shard_map/ppermute | solution.py:484
  169.6 5.3 %collective-permute-start.28 = (f32[8,1152]{1,0:T(8,128)S(1)}, f32[8,1152]{1,0:T(8,128)S(1)}, u32[]{:S(2)}, u32[]{:S(2)}) collective-permute-start(f32[8,1152]{1,0:T(8,128)S(1)} %get-tuple-element.47), channel_id=1, source_target_pairs={{0,48},{8,56},{16,32},{24,40},{32,16},{40,24},{48,0},{56,8},{1,49}... | collective-permute-start | bytes 110600 | tf_op jit(solution)/shard_map/ppermute | solution.py:484
  172.1 4.7 %collective-permute-start.29 = (f32[8,1152]{1,0:T(8,128)S(1)}, f32[8,1152]{1,0:T(8,128)S(1)}, u32[]{:S(2)}, u32[]{:S(2)}) collective-permute-start(f32[8,1152]{1,0:T(8,128)S(1)} %get-tuple-element.46), channel_id=1, source_target_pairs={{0,56},{8,48},{16,40},{24,32},{32,24},{40,16},{48,8},{56,0},{1,57}... | collective-permute-start | bytes 110600 | tf_op jit(solution)/shard_map/ppermute | solution.py:484
  176.8 6.0 %collective-permute-start.30 = (f32[8,1152]{1,0:T(8,128)S(1)}, f32[8,1152]{1,0:T(8,128)S(1)}, u32[]{:S(2)}, u32[]{:S(2)}) collective-permute-start(f32[8,1152]{1,0:T(8,128)S(1)} %fusion.9), channel_id=1, source_target_pairs={{0,64},{64,0},{9,73},{73,9},{2,66},{66,2},{11,75},{75,11},{4,68},{... | collective-permute-start | bytes 110600 | tf_op jit(solution)/shard_map/ppermute | solution.py:493
  177.5 5.4 %collective-permute-start.31 = (f32[8,1152]{1,0:T(8,128)S(1)}, f32[8,1152]{1,0:T(8,128)S(1)}, u32[]{:S(2)}, u32[]{:S(2)}) collective-permute-start(f32[8,1152]{1,0:T(8,128)S(1)} %fusion.9), channel_id=1, source_target_pairs={{8,9},{72,73},{1,0},{65,64},{10,11},{74,75},{3,2},{67,66},{12,13},... | collective-permute-start | bytes 110600 | tf_op jit(solution)/shard_map/ppermute | solution.py:493
  181.5 2.3 %collective-permute-start.32 = (f32[8,1152]{1,0:T(8,128)S(1)}, f32[8,1152]{1,0:T(8,128)S(1)}, u32[]{:S(2)}, u32[]{:S(2)}) collective-permute-start(f32[8,1152]{1,0:T(8,128)S(1)} %fusion.9), channel_id=1, source_target_pairs={{8,73},{72,9},{1,64},{65,0},{10,75},{74,11},{3,66},{67,2},{12,77},... | collective-permute-start | bytes 110600 | tf_op jit(solution)/shard_map/ppermute | solution.py:493
  183.9 5.2 %collective-permute-start.38 = (f32[4,8,1152]{2,1,0:T(8,128)S(1)}, f32[4,8,1152]{2,1,0:T(8,128)S(1)}, u32[]{:S(2)}, u32[]{:S(2)}) collective-permute-start(f32[4,8,1152]{2,1,0:T(8,128)S(1)} %pad_maximum_fusion), channel_id=1, source_target_pairs={{0,48},{9,57},{16,32},{25,41},{32,16},{41,25},{48,0},{57,9},{2,50}... | collective-permute-start | bytes 442376 | tf_op jit(solution)/shard_map/ppermute | solution.py:502
  184.6 13.5 %collective-permute-start.39 = (f32[4,8,1152]{2,1,0:T(8,128)S(1)}, f32[4,8,1152]{2,1,0:T(8,128)S(1)}, u32[]{:S(2)}, u32[]{:S(2)}) collective-permute-start(f32[4,8,1152]{2,1,0:T(8,128)S(1)} %pad_maximum_fusion), channel_id=1, source_target_pairs={{0,56},{9,49},{16,40},{25,33},{32,24},{41,17},{48,8},{57,1},{2,58}... | collective-permute-start | bytes 442376 | tf_op jit(solution)/shard_map/ppermute | solution.py:499
  186.5 13.6 %collective-permute-start.36 = (f32[4,8,1152]{2,1,0:T(8,128)S(1)}, f32[4,8,1152]{2,1,0:T(8,128)S(1)}, u32[]{:S(2)}, u32[]{:S(2)}) collective-permute-start(f32[4,8,1152]{2,1,0:T(8,128)S(1)} %pad_maximum_fusion), channel_id=1, source_target_pairs={{0,32},{9,41},{16,48},{25,57},{32,0},{41,9},{48,16},{57,25},{2,34}... | collective-permute-start | bytes 442376 | tf_op jit(solution)/shard_map/ppermute | solution.py:502
  187.1 15.8 %collective-permute-start.37 = (f32[4,8,1152]{2,1,0:T(8,128)S(1)}, f32[4,8,1152]{2,1,0:T(8,128)S(1)}, u32[]{:S(2)}, u32[]{:S(2)}) collective-permute-start(f32[4,8,1152]{2,1,0:T(8,128)S(1)} %pad_maximum_fusion), channel_id=1, source_target_pairs={{0,40},{9,33},{16,56},{25,49},{32,8},{41,1},{48,24},{57,17},{2,42}... | collective-permute-start | bytes 442376 | tf_op jit(solution)/shard_map/ppermute | solution.py:499
  188.4 17.7 %collective-permute-start.34 = (f32[4,8,1152]{2,1,0:T(8,128)S(1)}, f32[4,8,1152]{2,1,0:T(8,128)S(1)}, u32[]{:S(2)}, u32[]{:S(2)}) collective-permute-start(f32[4,8,1152]{2,1,0:T(8,128)S(1)} %pad_maximum_fusion), channel_id=1, source_target_pairs={{0,16},{9,25},{16,0},{25,9},{32,48},{41,57},{48,32},{57,41},{2,18}... | collective-permute-start | bytes 442376 | tf_op jit(solution)/shard_map/ppermute | solution.py:502
  189.1 17.0 %collective-permute-start.35 = (f32[4,8,1152]{2,1,0:T(8,128)S(1)}, f32[4,8,1152]{2,1,0:T(8,128)S(1)}, u32[]{:S(2)}, u32[]{:S(2)}) collective-permute-start(f32[4,8,1152]{2,1,0:T(8,128)S(1)} %pad_maximum_fusion), channel_id=1, source_target_pairs={{0,24},{9,17},{16,8},{25,1},{32,56},{41,49},{48,40},{57,33},{2,26}... | collective-permute-start | bytes 442376 | tf_op jit(solution)/shard_map/ppermute | solution.py:499
  198.1 7.4 %collective-permute-start.33 = (f32[4,8,1152]{2,1,0:T(8,128)S(1)}, f32[4,8,1152]{2,1,0:T(8,128)S(1)}, u32[]{:S(2)}, u32[]{:S(2)}) collective-permute-start(f32[4,8,1152]{2,1,0:T(8,128)S(1)} %pad_maximum_fusion), channel_id=1, source_target_pairs={{0,8},{9,1},{16,24},{25,17},{32,40},{41,33},{48,56},{57,49},{2,10}... | collective-permute-start | bytes 442376 | tf_op jit(solution)/shard_map/ppermute | solution.py:499

commit v3 on v2

v3 whole, which is shorter than its diff:
```python
import functools

import jax
import jax.numpy as jnp
import numpy as np
from jax import lax
from jax.experimental import pallas as pl
from jax.experimental.pallas import tpu as pltpu
from jax.sharding import Mesh
from jax.sharding import PartitionSpec as P

NX = 96
ITERS = 4
ROWS = 24
CHUNK = ROWS * NX
GROUP = 4 * NX
F32 = jnp.float32
ZAX = ("zl", "zh")


def z_perm(to):
    index = lambda z: (z & 1) * 2 + (z >> 1)
    return [(index(z), index(to(z))) for z in range(4)]


def z_xor(value, m):
    return lax.ppermute(value, ZAX, z_perm(lambda z: z ^ m))


def y_xor(value, m):
    return lax.ppermute(value, "y", [(i, i ^ m) for i in range(4)])


def lane_ids():
    return lax.broadcasted_iota(jnp.int32, (8, 128), 1)


def unpack_rows(a, b, c, lanes):
    r0 = a
    r1 = jnp.where(lanes < 32, pltpu.roll(a, 32, 1), pltpu.roll(b, 32, 1))
    r2 = jnp.where(lanes < 64, pltpu.roll(b, 64, 1), pltpu.roll(c, 64, 1))
    r3 = pltpu.roll(c, 96, 1)
    return r0, r1, r2, r3


def pack_rows(r0, r1, r2, r3, lanes):
    r1s = pltpu.roll(r1, 96, 1)
    r2s = pltpu.roll(r2, 64, 1)
    r3s = pltpu.roll(r3, 32, 1)
    return (
        jnp.where(lanes < 96, r0, r1s),
        jnp.where(lanes < 64, r1s, r2s),
        jnp.where(lanes < 32, r2s, r3s),
    )


def in_vmem(shape):
    return pltpu.VMEM(shape, F32)


def call(kernel, name, args, outs, scratch=(), scalars=0, aliases=None, flops=10_000_000, limit=8):
    specs = [pl.BlockSpec(memory_space=pltpu.SMEM)] * scalars
    specs += [pl.BlockSpec(memory_space=pltpu.VMEM)] * (len(args) - scalars)
    args = list(args[:scalars]) + [pltpu.with_memory_space_constraint(a, pltpu.VMEM) for a in args[scalars:]]
    return pl.pallas_call(
        kernel,
        in_specs=specs,
        out_specs=[pl.BlockSpec(memory_space=pltpu.VMEM)] * len(outs),
        out_shape=[in_vmem(o) for o in outs],
        scratch_shapes=list(scratch),
        input_output_aliases=aliases or {},
        compiler_params=pltpu.CompilerParams(vmem_limit_bytes=limit * 2**20),
        cost_estimate=pl.CostEstimate(flops=flops, bytes_accessed=10_000_000, transcendentals=0),
        name=name,
    )(*args)


def lanes_at(group, v):
    return pl.ds(pl.multiple_of(group * GROUP + v * 128, 128), 128)


def perturbed(field, pert_r, pert_i):
    re, im = field
    return pert_r * re - pert_i * im, pert_r * im + pert_i * re


def products_kernel(slot_ref, o0, o1, o2, o3, p0, p1, out_ref):
    slabs = (((o0, o1), p0), ((o2, o3), p1))
    for k in range(4):
        block, kk = k // 2, k % 2
        slot = slot_ref[k]

        def body(g, acc, block=block, kk=kk, slot=slot):
            acc = list(acc)
            for pair, pert in slabs:
                own, mate = pair[block], pair[1 - block]
                for v in range(3):
                    at = lanes_at(g, v)
                    pr, pi = pert[1, :, at], pert[2, :, at]
                    w = [perturbed((own[kk, n, 0, :, at], own[kk, n, 1, :, at]), pr, pi) for n in range(3)]
                    for m in range(3):
                        mr, mi = mate[slot, m, 0, :, at], mate[slot, m, 1, :, at]
                        for n in range(3):
                            i = (m * 3 + n) * 2
                            acc[i] = acc[i] + (mr * w[n][0] + mi * w[n][1])
                            acc[i + 1] = acc[i + 1] + (mr * w[n][1] - mi * w[n][0])
            return tuple(acc)

        acc = lax.fori_loop(0, CHUNK // GROUP, body, (jnp.zeros((8, 128), F32),) * 18)
        for i in range(18):
            out_ref[pl.ds(k * 18 + i, 1), :] = jnp.sum(acc[i], axis=0, keepdims=True)


def products(slots, fields, perts):
    return call(products_kernel, "products", (slots, *fields, *perts), [(72, 128)], scalars=1, flops=20_000_000)[0]


TALL, DEEP = ROWS + 4, 32
FIELD = (24, TALL, DEEP, 128)
ORBITALS = (24 * ROWS * 16, 128)


def rows_at(kn, c, r):
    return ((kn * 2 + c) * ROWS + r) * 16


def orbital_rows_kernel(pos_ref, o0, o1, o2, o3, p0, p1, orb_ref, v_ref):
    lanes = lane_ids()
    half = pos_ref[0]

    def body(g, carry):
        for pair, pert, z in (((o0, o1), p0, half), ((o2, o3), p1, 1 - half)):
            rows = unpack_rows(*[pert[0, :, lanes_at(g, v)] for v in range(3)], lanes)
            for j in range(4):
                v_ref[pl.ds(pl.multiple_of((4 * g + j) * 16 + 8 * z, 8), 8), :] = rows[j]
            for k in range(4):
                for n in range(3):
                    for c in range(2):
                        rows = unpack_rows(*[pair[k // 2][k % 2, n, c, :, lanes_at(g, v)] for v in range(3)], lanes)
                        for j in range(4):
                            at = pl.multiple_of(rows_at(k * 3 + n, c, 4 * g + j) + 8 * z, 8)
                            orb_ref[pl.ds(at, 8), :] = rows[j]
        return carry

    lax.fori_loop(0, CHUNK // GROUP, body, 0)


def orbital_rows(pos, fields, perts):
    return call(orbital_rows_kernel, "orbital_rows", (pos, *fields, *perts), [ORBITALS, (ROWS * 16, 128)], scalars=1)


ZHALO, YHALO = (48 * ROWS, 128), (24 * 32, 128)


def field_rows(kn, c, r, plane):
    return ((kn * 2 + c) * TALL + r + 2) * DEEP + 8 + plane


def clear_margin(u_ref):
    def body(i, carry):
        for r in (0, 1, TALL - 2, TALL - 1):
            u_ref[i, r] = jnp.zeros((DEEP, 128), F32)
        for r in range(2, TALL - 2):
            u_ref[i, r, 0:8] = jnp.zeros((8, 128), F32)
            u_ref[i, r, 24:32] = jnp.zeros((8, 128), F32)
        return carry

    lax.fori_loop(0, 24, body, 0)


def near_face(parity, size):
    return (1 - parity) * (size - 2)


def cut_planes(flat, pos_ref, kn, za, zb):
    up = near_face(pos_ref[4] & 1, 16)
    for ref, first in ((za, up), (zb, 14 - up)):
        for c in range(2):
            for p in range(2):
                to = pl.ds(pl.multiple_of(((kn * 2 + c) * 2 + p) * ROWS, 8), ROWS)
                ref[to, :] = flat[pl.ds(field_rows(kn, c, 0, first + p), ROWS, stride=DEEP), :]


def cut_rows(u_ref, pos_ref, kn, ya, yb):
    up = near_face(pos_ref[1] & 1, ROWS)
    for ref, first in ((ya, up), (yb, ROWS - 2 - up)):
        for c in range(2):
            i = kn * 2 + c
            for p in range(2):
                to = pl.ds(pl.multiple_of((i * 2 + p) * 16, 8), 16)
                ref[to, :] = u_ref[i, 2 + first + p, 8:24, :]


def exchange(za, zb, ya, yb):
    return y_xor(za, 1), y_xor(zb, 3), z_xor(ya, 1), z_xor(yb, 3)


def right_kernel(ncells, slot_ref, pos_ref, s0, s1, s2, s3, o0, o1, o2, o3, p0, p1, r_ref, za, zb, ya, yb, prod_ref):
    total = (s0[...] + s1[...]) + (s2[...] + s3[...])
    ones = jnp.full((128, 128), 1.0, F32)
    prod_ref[...] = jnp.dot(total, ones, precision=lax.Precision.HIGHEST, preferred_element_type=F32) / ncells
    clear_margin(r_ref)
    lanes = lane_ids()
    half = pos_ref[0]
    slabs = (((o0, o1), p0, half), ((o2, o3), p1, 1 - half))
    for k in range(4):
        block, kk = k // 2, k % 2
        slot = slot_ref[k]

        def body(g, carry, k=k, block=block, kk=kk, slot=slot):
            for pair, pert, z in slabs:
                own, mate = pair[block], pair[1 - block]
                right = [[[], []] for _ in range(3)]
                for v in range(3):
                    at = lanes_at(g, v)
                    pr, pi = pert[1, :, at], pert[2, :, at]
                    mates = [(mate[slot, m, 0, :, at], mate[slot, m, 1, :, at]) for m in range(3)]
                    for n in range(3):
                        wr, wi = perturbed((own[kk, n, 0, :, at], own[kk, n, 1, :, at]), pr, pi)
                        gr, gi = -wr, -wi
                        for m in range(3):
                            row = k * 18 + (m * 3 + n) * 2
                            qr = prod_ref[pl.ds(row, 1), :]
                            qi = prod_ref[pl.ds(row + 1, 1), :]
                            mr, mi = mates[m]
                            gr = gr + (qr * mr - qi * mi)
                            gi = gi + (qi * mr + qr * mi)
                        right[n][0].append(gr)
                        right[n][1].append(gi)
                for n in range(3):
                    for c in range(2):
                        rows = unpack_rows(*right[n][c], lanes)
                        for j in range(4):
                            planes = pl.ds(pl.multiple_of(8 + 8 * z, 8), 8)
                            r_ref[(k * 3 + n) * 2 + c, 2 + 4 * g + j, planes, :] = rows[j]
            return carry

        lax.fori_loop(0, CHUNK // GROUP, body, 0)

    flat = r_ref.reshape(24 * TALL * DEEP, 128)

    def cut(kn, carry):
        cut_planes(flat, pos_ref, kn, za, zb)
        cut_rows(r_ref, pos_ref, kn, ya, yb)
        return carry

    lax.fori_loop(0, 12, cut, 0)


def right_sides(ncells, slots, pos, sums, fields, perts):
    return call(
        functools.partial(right_kernel, ncells),
        "right_sides",
        (slots, pos, *sums, *fields, *perts),
        [FIELD, ZHALO, ZHALO, YHALO, YHALO],
        scratch=[pltpu.VMEM((72, 128), F32)],
        scalars=2,
        flops=20_000_000,
    )


def x_matrix():
    m = np.zeros((128, 256), np.float32)
    for i in range(NX):
        for s, lap, grad in ((1, 16, 8), (-1, 16, -8), (2, -1, -1), (-2, -1, 1)):
            m[(i + s) % NX, i] += lap
            m[(i + s) % NX, 128 + i] += grad
    return np.concatenate([m, m], 0)


def scalars_of(count, par_ref, w_ref, kn):
    k, n = kn // 3, kn % 3
    kx, ky, kz = par_ref[k * 8], par_ref[k * 8 + 1], par_ref[k * 8 + 2]
    base = 3.75 + 0.5 * (kx * kx + ky * ky + kz * kz) + par_ref[k * 8 + 3 + n]
    wt = w_ref[count]
    scale = w_ref[0] if count == 1 else jnp.float32(1.0)
    return kx, ky, kz, base, wt, scale


def step_kernel(count, par_ref, w_ref, *refs):
    last, first = count == ITERS - 1, count == 1
    if first:
        r_ref, v_ref, m_ref, *refs = refs
        u_ref = r_ref
    else:
        u_ref, r_ref, v_ref, m_ref, *refs = refs
    if last:
        orb_ref, out_ref, *flats = refs
        out_ref[...] = jnp.zeros_like(out_ref)
    else:
        out_ref, *flats = refs

    def along_x(kn, g, flat):
        cells = [u_ref[kn * 2 + c, 2 + 8 * g : 10 + 8 * g, 8:24, :].reshape(128, 128) for c in range(2)]
        u2 = jnp.concatenate(cells, 0)
        hi = u2.astype(jnp.bfloat16)
        lo = (u2 - hi.astype(F32)).astype(jnp.bfloat16)
        flat[...] = jnp.dot(jnp.concatenate([hi, lo], 1), m_ref[...], preferred_element_type=F32)

    def rows_of(kn, g, flat, coef):
        lap, gx, gy, gz, keep, pull, wt = coef
        for r in range(8 * g, 8 * g + 8):
            cells, second, grad = [], [], []
            for c in range(2):
                i = kn * 2 + c
                at = slice((c * 8 + r - 8 * g) * 16, (c * 8 + r - 8 * g + 1) * 16)
                yp1, ym1 = u_ref[i, r + 3, 8:24, :], u_ref[i, r + 1, 8:24, :]
                yp2, ym2 = u_ref[i, r + 4, 8:24, :], u_ref[i, r, 8:24, :]
                zp1, zm1 = u_ref[i, r + 2, 9:25, :], u_ref[i, r + 2, 7:23, :]
                zp2, zm2 = u_ref[i, r + 2, 10:26, :], u_ref[i, r + 2, 6:22, :]
                cells.append(u_ref[i, r + 2, 8:24, :])
                one = (yp1 + ym1) + (zp1 + zm1)
                two = (yp2 + ym2) + (zp2 + zm2)
                second.append(flat[at, 0:128] + (16.0 * one - two))
                dy = (yp1 - ym1) - 0.125 * (yp2 - ym2)
                dz = (zp1 - zm1) - 0.125 * (zp2 - zm2)
                grad.append(gx * flat[at, 128:256] + (gy * dy + gz * dz))
            center = keep - pull * v_ref[16 * r : 16 * r + 16, :]
            new = []
            for c in range(2):
                i = kn * 2 + c
                value = center * cells[c] + lap * second[c]
                if not first:
                    value = value + wt * r_ref[i, r + 2, 8:24, :]
                new.append(value - grad[1] if c == 0 else value + grad[0])
            if last:
                orb_r = orb_ref[pl.ds(pl.multiple_of(rows_at(kn, 0, r), 16), 16), :]
                orb_i = orb_ref[pl.ds(pl.multiple_of(rows_at(kn, 1, r), 16), 16), :]
                out_ref[16 * r : 16 * r + 16, :] += orb_r * new[0] + orb_i * new[1]
                out_ref[16 * (ROWS + r) : 16 * (ROWS + r) + 16, :] += orb_r * new[1] - orb_i * new[0]
            else:
                for c in range(2):
                    out_ref[pl.ds(pl.multiple_of(rows_at(kn, c, r), 16), 16), :] = new[c]

    along_x(0, 0, flats[0])

    def orbital(kn, carry):
        kx, ky, kz, base, wt, scale = scalars_of(count, par_ref, w_ref, kn)
        ws = wt * scale
        keep = scale - ws * base
        if first:
            keep = keep + wt
        coef = (ws / 24.0, ws * kx / 12.0, ws * ky * (2.0 / 3.0), ws * kz * (2.0 / 3.0), keep, ws, wt)
        ahead = jnp.minimum(kn + 1, 11)
        for g in range(3):
            along_x(kn if g < 2 else ahead, (g + 1) % 3, flats[(g + 1) % 3])
            rows_of(kn, g, flats[g], coef)
        return carry

    lax.fori_loop(0, 12, orbital, 0)


def inner_step(count, par, weights, u, right, pot, matrix, orb):
    last = count == ITERS - 1
    return call(
        functools.partial(step_kernel, count),
        "last_step" if last else "step",
        (par, weights) + ((u,) if count > 1 else ()) + (right, pot, matrix) + ((orb,) if last else ()),
        [(2 * ROWS * 16, 128) if last else ORBITALS],
        scratch=[pltpu.VMEM((256, 256), F32)] * 3,
        scalars=2,
        flops=60_000_000,
    )[0]


def face_terms(lap, g, beyond1, beyond2):
    first = [lap * (16.0 * beyond1[c] - beyond2[c]) for c in range(2)]
    grad1 = [g * (beyond1[c] - 0.125 * beyond2[c]) for c in range(2)]
    second = [-lap * beyond1[c] for c in range(2)]
    grad2 = [(-0.125 * g) * beyond1[c] for c in range(2)]
    return (
        (first[0] - grad1[1], first[1] + grad1[0]),
        (second[0] - grad2[1], second[1] + grad2[0]),
    )


def faces(count, par_ref, w_ref, pos_ref, kn, za, zb, ya, yb, add_plane, add_row):
    kx, ky, kz, base, wt, scale = scalars_of(count, par_ref, w_ref, kn)
    ws = wt * scale
    lap = ws / 24.0
    gy, gz = ws * ky * (2.0 / 3.0), ws * kz * (2.0 / 3.0)
    from_z = (kn + 6) % 12

    def plane(ref, p):
        return [ref[pl.ds(pl.multiple_of(((kn * 2 + c) * 2 + p) * ROWS, 8), ROWS), :] for c in range(2)]

    def line(ref, r):
        return [ref[pl.ds(pl.multiple_of(((from_z * 2 + c) * 2 + r) * 16, 8), 16), :] for c in range(2)]

    def side(ref, layer, size, g, below, add):
        sign = (1 - 2 * below).astype(F32)
        first = (1 - below) * (size - 1)
        terms = face_terms(lap, sign * g, layer(ref, below), layer(ref, 1 - below))
        add(first, terms[0])
        add(first + 2 * below - 1, terms[1])

    odd = pos_ref[1] & 1
    side(ya, line, ROWS, gy, odd, add_row)
    side(yb, line, ROWS, gy, 1 - odd, add_row)
    odd = pos_ref[4] & 1
    side(za, plane, 16, gz, odd, add_plane)
    side(zb, plane, 16, gz, 1 - odd, add_plane)


def faces_kernel(count, par_ref, w_ref, pos_ref, u_in, za_in, zb_in, ya_in, yb_in, u_ref, za, zb, ya, yb):
    clear_margin(u_ref)
    flat = u_ref.reshape(24 * TALL * DEEP, 128)

    def orbital(kn, carry):
        for c in range(2):
            for r in range(ROWS):
                u_ref[kn * 2 + c, r + 2, 8:24, :] = u_in[pl.ds(pl.multiple_of(rows_at(kn, c, r), 16), 16), :]

        def add_plane(p, term):
            for c in range(2):
                at = pl.ds(field_rows(kn, c, 0, p), ROWS, stride=DEEP)
                flat[at, :] = flat[at, :] + term[c]

        def add_row(r, term):
            for c in range(2):
                u_ref[kn * 2 + c, r + 2, 8:24, :] = u_ref[kn * 2 + c, r + 2, 8:24, :] + term[c]

        faces(count, par_ref, w_ref, pos_ref, kn, za_in, zb_in, ya_in, yb_in, add_plane, add_row)
        cut_planes(flat, pos_ref, kn, za, zb)
        cut_rows(u_ref, pos_ref, kn, ya, yb)
        return carry

    lax.fori_loop(0, 12, orbital, 0)


def add_faces(count, par, weights, pos, u, halos):
    return call(
        functools.partial(faces_kernel, count),
        "faces",
        (par, weights, pos, u, *halos),
        [FIELD, ZHALO, ZHALO, YHALO, YHALO],
        scalars=3,
    )


def density_kernel(par_ref, w_ref, pos_ref, d_in, za, zb, ya, yb, orb_ref, keep_ref, send_ref, d_ref):
    d_ref[...] = d_in[...]

    def orbital(kn, carry):
        def add(at, to, term):
            orb_r, orb_i = orb_ref[at[0], :], orb_ref[at[1], :]
            d_ref[to[0], :] = d_ref[to[0], :] + (orb_r * term[0] + orb_i * term[1])
            d_ref[to[1], :] = d_ref[to[1], :] + (orb_r * term[1] - orb_i * term[0])

        def add_plane(p, term):
            add(
                [pl.ds(rows_at(kn, c, 0) + p, ROWS, stride=16) for c in range(2)],
                [pl.ds(c * ROWS * 16 + p, ROWS, stride=16) for c in range(2)],
                term,
            )

        def add_row(r, term):
            add(
                [pl.ds(pl.multiple_of(rows_at(kn, c, r), 16), 16) for c in range(2)],
                [pl.ds(pl.multiple_of((c * ROWS + r) * 16, 16), 16) for c in range(2)],
                term,
            )

        faces(ITERS - 1, par_ref, w_ref, pos_ref, kn, za, zb, ya, yb, add_plane, add_row)
        return carry

    lax.fori_loop(0, 12, orbital, 0)
    ids = lane_ids()
    core = pos_ref[3]
    for ref, c in ((send_ref, 1 - core), (keep_ref, core)):
        for z in range(2):
            for g in range(6):
                rows = [
                    d_ref[pl.ds(pl.multiple_of((c * ROWS + 4 * g + j) * 16 + 8 * z, 8), 8), :] * (1.0 / 32.0)
                    for j in range(4)
                ]
                packed = pack_rows(*rows, ids)
                for v in range(3):
                    at = g * GROUP + v * 128
                    ref[z, :, at : at + 128] = packed[v]


TILE = (2, 8, CHUNK)


def tile_density(par, weights, pos, dens, halos, orb):
    return call(
        density_kernel,
        "density",
        (par, weights, pos, dens, *halos, orb),
        [TILE, TILE],
        scratch=[pltpu.VMEM((2 * ROWS * 16, 128), F32)],
        scalars=3,
    )


def pair_kernel(a, b, out):
    out[...] = a[...] + b[...]


def split_kernel(pos_ref, s0, s1, s2, s3, mine, other):
    half = pos_ref[0]
    mine[...] = (s0[half] + s1[half]) + (s2[half] + s3[half])
    half = 1 - half
    other[...] = (s0[half] + s1[half]) + (s2[half] + s3[half])


def place_kernel(pos_ref, t0, t1, t2, t3, out_ref):
    z = pos_ref[1]
    for m, tile in enumerate((t0, t1, t2, t3)):
        out_ref[:, pl.ds(pl.multiple_of((z ^ m) * CHUNK, 128), CHUNK)] = tile[...]


def both_kernel(pos_ref, mine, other, out_ref):
    core = pos_ref[3]
    out_ref[core] = mine[...]
    out_ref[1 - core] = other[...]


def both_components(pos, mine, other):
    return pl.pallas_call(
        both_kernel,
        in_specs=[pl.BlockSpec(memory_space=pltpu.SMEM)] + [pl.BlockSpec(memory_space=pltpu.VMEM)] * 2,
        out_specs=pl.BlockSpec(memory_space=pltpu.VMEM),
        out_shape=jax.ShapeDtypeStruct((2, 8, 4 * CHUNK), F32),
        compiler_params=pltpu.CompilerParams(vmem_limit_bytes=8 * 2**20),
        name="both_components",
    )(pos, mine, other)


def on_device(orbitals, partner_map, wave_vectors, levels, potential, perturbation, step_weights):
    zl, zh = lax.axis_index("zl"), lax.axis_index("zh")
    z = zh * 2 + zl
    pos = jnp.stack([zh, z, lax.axis_index("x"), lax.axis_index("c"), lax.axis_index("y")]).astype(jnp.int32)
    ncells = 64 * 4 * CHUNK

    def chunk(array, q):
        return lax.dynamic_slice_in_dim(array, q * CHUNK, CHUNK, axis=array.ndim - 1)

    fields = [None] * 4
    for m in (1, 3, 2):
        part = chunk(orbitals, z ^ m)
        fields[m] = z_xor(part, m)
        orbitals, part = lax.optimization_barrier((orbitals, part))
    partner_map, wave_vectors, levels, potential, perturbation, step_weights, part = lax.optimization_barrier(
        (partner_map, wave_vectors, levels, potential, perturbation, step_weights, part)
    )
    pots = jnp.concatenate([potential[None], perturbation], 0)
    perts = [chunk(pots, z), z_xor(chunk(pots, z ^ 3), 3)]
    slot = (partner_map % 2).astype(F32)
    mine = jnp.concatenate([wave_vectors, levels, slot[:, None], jnp.zeros((2, 1), F32)], 1)
    weights = step_weights.astype(F32) / 100.0
    both = jnp.concatenate([mine, z_xor(mine, 1)], 0)
    slots = both[:, 6].astype(jnp.int32)
    par = both.reshape(32)
    matrix = jnp.asarray(x_matrix(), jnp.bfloat16)
    pos, slots, par, weights, orbitals = lax.optimization_barrier((pos, slots, par, weights, orbitals))
    fields[0] = chunk(orbitals, z)
    pos, slots, par, weights, fields, perts = lax.optimization_barrier((pos, slots, par, weights, fields, perts))

    part = products(slots, fields, perts)
    orb, pot = orbital_rows(pos, fields, perts)

    def swapped(value):
        return jnp.concatenate([value[36:], value[:36]], 0)

    part = part + swapped(z_xor(part, 1)) + z_xor(part, 2) + swapped(z_xor(part, 3))
    sums = [part] + [y_xor(part, m) for m in (1, 2, 3)]
    orb, pot, sums = lax.optimization_barrier((orb, pot, sums))
    right, *cut = right_sides(float(ncells), slots, pos, sums, fields, perts)
    u = right
    for count in range(1, ITERS):
        halos = exchange(*cut)
        u = inner_step(count, par, weights, u, right, pot, matrix, orb)
        if count < ITERS - 1:
            u, *cut = add_faces(count, par, weights, pos, u, halos)
    keep, send = tile_density(par, weights, pos, u, halos, orb)

    def other_core(value):
        return lax.ppermute(value, "c", [(0, 1), (1, 0)])

    chip = call(pair_kernel, "pair", (keep, other_core(send)), [TILE])[0]
    parts = [chip] + [lax.ppermute(chip, "x", [(i, i ^ m) for i in range(4)]) for m in (1, 2, 3)]
    same, cross = call(split_kernel, "split", (pos, *parts), [(8, CHUNK)] * 2, scalars=1)
    tiles = [same, z_xor(same, 1), z_xor(cross, 2), z_xor(cross, 3)]
    slab = call(place_kernel, "place", (pos, *tiles), [(8, 4 * CHUNK)], scalars=1)[0]
    return both_components(pos, slab, other_core(slab))


def solution(mesh):
    fine = Mesh(mesh.devices.reshape(2, 4, 2, 4, 2), ("zl", "x", "c", "y", "zh"))
    ka, grid = ("zl", "x", "c"), ("y", "zh")
    return jax.shard_map(
        on_device,
        mesh=fine,
        in_specs=(
            P(ka, None, None, grid, None),
            P(ka),
            P(ka, None),
            P(ka, None),
            P(grid, None),
            P(None, grid, None),
            P(),
        ),
        out_specs=P(None, grid, None),
        check_vma=False,
    )
```

time: 209 us -> 159 us (0.76)
  local copies, waits for them, and re-layouts: 23.2 us -> 4.83 us
  starting transfers between devices: 62.5 us -> 44.5 us
  waiting for transfers between devices: 61.7 us -> 52.5 us
  Pallas kernels: 55.6 us -> 51.9 us
    ppermute x32 -> x14, starting transfers between devices: 50.1 us -> 24.5 us  [the longest x2 10.9 us: other_core(): return lax.ppermute(value, 'c', [(0, 1), (1, 0)])]
    unnamed x44 -> x16, local copies, waits for them, and re-layouts: 18.8 us -> 1.53 us
    ppermute x32 -> x14, waiting for transfers between devices: 20.4 us -> 9.22 us  [the longest x3 6.55 us: on_device(): lax.ppermute(chip, 'x', [(i, i ^ m) for i in range(4)])]
    ppermute x8 -> x17, starting transfers between devices: 12.5 us -> 20.1 us  [z_xor(): return lax.ppermute(value, ZAX, z_perm(lambda z: z ^ m))]
    pallas_call x9 -> x12, Pallas kernels: 53.6 us -> 50.5 us  [call(): pl.pallas_call(kernel, in_specs=specs, out_specs=[pl.BlockSpec(memory_spa...]
    select_n x4 -> x0, other arithmetic: 2.72 us -> none  [on_device(): blocks.append(jnp.where(same, straight, across))]
    ppermute x8 -> x17, waiting for transfers between devices: 41.3 us -> 43.3 us  [z_xor(): return lax.ppermute(value, ZAX, z_perm(lambda z: z ^ m))]
  transfers between devices with their start and end apart: 40 -> 31, of which waited for: 13 -> 12; matrix products, arithmetic and copies ran while one was open for 3% -> 4% of each run, Pallas kernels for 17% -> 17%
where the time goes in v3:
time: 159 us
  waiting for transfers between devices  52.5 us (33%)
  Pallas kernels  51.9 us (33%)
  starting transfers between devices  44.5 us (28%)
  other arithmetic  5.07 us (3%)
  local copies, waits for them, and re-layouts  4.83 us (3%)
    pallas_call x12, Pallas kernels, call(): pl.pallas_call(kernel, in_specs=specs, out_specs=[pl.BlockSpec(memory_spa...  50.5 us
    ppermute x17, waiting for transfers between devices, z_xor(): return lax.ppermute(value, ZAX, z_perm(lambda z: z ^ m))  43.3 us
    ppermute x17, starting transfers between devices, z_xor(): return lax.ppermute(value, ZAX, z_perm(lambda z: z ^ m))  20.1 us
    ppermute x2, starting transfers between devices, other_core(): return lax.ppermute(value, 'c', [(0, 1), (1, 0)])  10.9 us
    ppermute x9, starting transfers between devices, y_xor(): return lax.ppermute(value, 'y', [(i, i ^ m) for i in range(4)])  10.3 us
    ppermute x3, waiting for transfers between devices, on_device(): lax.ppermute(chip, 'x', [(i, i ^ m) for i in range(4)])  6.55 us
    ppermute x3, starting transfers between devices, on_device(): lax.ppermute(chip, 'x', [(i, i ^ m) for i in range(4)])  3.33 us
  transfers between devices with their start and end apart: 31, of which 12 were waited for; matrix products, arithmetic and copies ran while one was open for 4% of the time, Pallas kernels for 17%

profile of v3, /device:TPU:1, one launch (start us, length us, event | category | flops | bytes accessed | tf_op | source)
XLA Modules:
  0.0 159.1 jit_solution(13877063548028668451)
XLA Ops:
  0.0 0.8 fusion.5
  0.8 0.1 copy.10
  0.9 0.6 copy-done.7
  1.5 0.8 pad_maximum_fusion.1
  2.3 2.5 %collective-permute-start = (f32[2,8]{1,0:T(2,128)S(1)}, f32[2,8]{1,0:T(2,128)}, u32[]{:S(2)}, u32[]{:S(2)}) collective-permute-start(f32[2,8]{1,0:T(2,128)S(1)} %pad_maximum_fusion.1), channel_id=1, source_target_pairs={{0,64},{64,0},{1,65},{65,1},{2,66},{66,2},{3,67},{67,3},{4,68},{68... | collective-permute-start | bytes 200 | tf_op jit(solution)/shard_map/ppermute | solution.py:27
  4.7 1.0 constant_dynamic-slice_fusion.3
  5.8 1.0 constant_dynamic-slice_fusion.2
  6.7 3.5 %collective-permute-start.3 = (f32[2,3,2,8,2304]{4,3,2,1,0:T(8,128)}, f32[2,3,2,8,2304]{4,3,2,1,0:T(8,128)}, u32[]{:S(2)}, u32[]{:S(2)}) collective-permute-start(f32[2,3,2,8,2304]{4,3,2,1,0:T(8,128)} %constant_dynamic-slice_fusion.2), channel_id=1, source_target_pairs={{0,65},{64,1},{1,64},{65,0},{2,67},{66,3},{3,66},{67,2},{4,69},{68... | collective-permute-start | bytes 2654216 | tf_op jit(solution)/shard_map/ppermute | solution.py:27
  10.3 1.0 constant_dynamic-slice_fusion.1
  11.3 1.9 %fusion = (f32[3,8,2304]{2,1,0:T(8,128)}, f32[3,8,2304]{2,1,0:T(8,128)}) fusion(s32[]{:T(128)S(6)} %select_n.23, f32[2,8,9216]{2,1,0:T(8,128)} %param.13, f32[1,8,9216]{2,1,0:T(8,128)} %bitcast.8, s32[]{:T(128)S(6)} %select_n.25), kind=kLoop, calls=%fused_computation.4 | loop fusion | flops 110592 | bytes 1327112 | tf_op jit(solution)/shard_map/concatenate | solution.py:548
  13.2 1.9 %collective-permute-start.4 = (f32[3,8,2304]{2,1,0:T(8,128)}, f32[3,8,2304]{2,1,0:T(8,128)}, u32[]{:S(2)}, u32[]{:S(2)}) collective-permute-start(f32[3,8,2304]{2,1,0:T(8,128)} %get-tuple-element.107), channel_id=1, source_target_pairs={{0,65},{64,1},{1,64},{65,0},{2,67},{66,3},{3,66},{67,2},{4,69},{68... | collective-permute-start | bytes 663560 | tf_op jit(solution)/shard_map/ppermute | solution.py:27
  15.1 0.7 convert_multiply_fusion.w_ref
  15.7 0.1 stack.23.pos_ref
  15.8 0.8 pad_maximum_fusion
  16.6 0.1 reshape.4.par_ref
  16.7 0.2 convert_reduce_fusion.slot_ref
  16.9 0.1 constant_dynamic-slice_fusion.o0
  16.9 36.2 %collective-permute-done.4.p1 = f32[3,8,2304]{2,1,0:T(8,128)} collective-permute-done((f32[3,8,2304]{2,1,0:T(8,128)}, f32[3,8,2304]{2,1,0:T(8,128)}, u32[]{:S(2)}, u32[]{:S(2)}) %collective-permute-start.4) | collective-permute-done | bytes 221216 | tf_op jit(solution)/shard_map/ppermute | solution.py:27
  53.1 0.9 copy-done.2
  54.0 3.7 %products.1 = f32[72,128]{1,0:T(8,128)S(1)} custom-call(s32[4]{0:T(128)S(1)} %convert_reduce_fusion.slot_ref, f32[2,3,2,8,2304]{4,3,2,1,0:T(8,128)S(1)} %constant_dynamic-slice_fusion.o0, f32[2,3,2,8,2304]{4,3,2,1,0:T(8,128)} %collective-permute-done.1.o1, f32[2,3,2,8,2304]{4,3,2,1,0:T(8,128)} %collective-permute-done.2.o2, ...), custom_call_target="tpu_custom_call" | custom-call | flops 20000000 | bytes 10000000 | tf_op jit(solution)/shard_map/products/pallas_call | solution.py:65
  57.8 2.5 %collective-permute-start.7 = (f32[72,128]{1,0:T(8,128)S(1)}, f32[72,128]{1,0:T(8,128)S(1)}, u32[]{:S(2)}, u32[]{:S(2)}) collective-permute-start(f32[72,128]{1,0:T(8,128)S(1)} %products.1), channel_id=1, source_target_pairs={{0,65},{64,1},{1,64},{65,0},{2,67},{66,3},{3,66},{67,2},{4,69},{68... | collective-permute-start | bytes 110600 | tf_op jit(solution)/shard_map/ppermute | solution.py:27
  60.3 0.9 collective-permute-start.5
  61.1 0.8 collective-permute-done.7
  61.9 1.2 collective-permute-done.5
  63.1 1.5 collective-permute-done.6
  64.6 2.8 %collective-permute-start.10 = (f32[72,128]{1,0:T(8,128)S(1)}, f32[72,128]{1,0:T(8,128)S(1)}, u32[]{:S(2)}, u32[]{:S(2)}) collective-permute-start(f32[72,128]{1,0:T(8,128)S(1)} %fusion.3.s0), channel_id=1, source_target_pairs={{0,6},{2,4},{4,2},{6,0},{1,7},{3,5},{5,3},{7,1},{8,14},{10,12},{12... | collective-permute-start | bytes 110600 | tf_op jit(solution)/shard_map/ppermute | solution.py:31
  67.4 0.3 collective-permute-start.9
  67.7 0.3 collective-permute-start.8
  68.1 3.8 %orbital_rows.1 = (f32[9216,128]{1,0:T(8,128)S(1)}, f32[384,128]{1,0:T(8,128)S(1)}) custom-call(s32[5]{0:T(128)S(1)} %stack.23.pos_ref, f32[2,3,2,8,2304]{4,3,2,1,0:T(8,128)S(1)} %constant_dynamic-slice_fusion.o0, f32[2,3,2,8,2304]{4,3,2,1,0:T(8,128)} %collective-permute-done.1.o1, f32[2,3,2,8,2304]{4,3,2,1,0:T(8,128)} %collective-permute-done.2.o2, ...), custom_call_target="tpu_custom_call" | custom-call | flops 10000000 | bytes 10000000 | tf_op jit(solution)/shard_map/orbital_rows/pallas_call | solution.py:65
  71.9 7.3 %right_sides.1 = (f32[24,28,32,128]{3,2,1,0:T(8,128)S(1)}, f32[1152,128]{1,0:T(8,128)S(1)}, f32[1152,128]{1,0:T(8,128)S(1)}, f32[768,128]{1,0:T(8,128)S(1)}, f32[768,128]{1,0:T(8,128)S(1)}) custom-call(s32[4]{0:T(128)S(1)} %convert_reduce_fusion.slot_ref, s32[5]{0:T(128)S(1)} %stack.23.pos_ref, f32[72,128]{1,0:T(8,128)S(1)} %fusion.3.s0, ...), custom_call_target="tpu_custom_call" | custom-call | flops 20000000 | bytes 10000000 | tf_op jit(solution)/shard_map/right_sides/pallas_call | solution.py:65
  79.1 1.2 collective-permute-start.11
  80.4 1.9 %collective-permute-start.12 = (f32[1152,128]{1,0:T(8,128)S(1)}, f32[1152,128]{1,0:T(8,128)S(1)}, u32[]{:S(2)}, u32[]{:S(2)}) collective-permute-start(f32[1152,128]{1,0:T(8,128)S(1)} %get-tuple-element.89), channel_id=1, source_target_pairs={{0,6},{2,4},{4,2},{6,0},{1,7},{3,5},{5,3},{7,1},{8,14},{10,12},{12... | collective-permute-start | bytes 1769480 | tf_op jit(solution)/shard_map/ppermute | solution.py:31
  82.3 1.9 %collective-permute-start.14 = (f32[768,128]{1,0:T(8,128)S(1)}, f32[768,128]{1,0:T(8,128)S(1)}, u32[]{:S(2)}, u32[]{:S(2)}) collective-permute-start(f32[768,128]{1,0:T(8,128)S(1)} %get-tuple-element.91), channel_id=1, source_target_pairs={{0,65},{64,1},{1,64},{65,0},{2,67},{66,3},{3,66},{67,2},{4,69},{68... | collective-permute-start | bytes 1179656 | tf_op jit(solution)/shard_map/ppermute | solution.py:27
  84.2 7.2 %step.2.u_in = f32[9216,128]{1,0:T(8,128)S(1)} custom-call(f32[32]{0:T(128)S(1)} %reshape.4.par_ref, f32[4]{0:T(128)S(1)} %convert_multiply_fusion.w_ref, f32[24,28,32,128]{3,2,1,0:T(8,128)S(1)} %get-tuple-element.86.refs_0_.refs_1_, f32[384,128]{1,0:T(8,128)S(1)} %get-tuple-element.87.refs_1_.refs_2_, bf16[256,256]{1,0:T(8,128)(2,1)S(1)} %copy-done.4), custom_call_target="tpu_custom_call" | custom-call | flops 60000000 | bytes 10000000 | tf_op jit(solution)/shard_map/step/pallas_call | solution.py:65
  91.4 0.4 collective-permute-done.12.zb_in
  91.8 4.6 %faces.2 = (f32[24,28,32,128]{3,2,1,0:T(8,128)S(1)}, f32[1152,128]{1,0:T(8,128)S(1)}, f32[1152,128]{1,0:T(8,128)S(1)}, f32[768,128]{1,0:T(8,128)S(1)}, f32[768,128]{1,0:T(8,128)S(1)}) custom-call(f32[32]{0:T(128)S(1)} %reshape.4.par_ref, f32[4]{0:T(128)S(1)} %convert_multiply_fusion.w_ref, s32[5]{0:T(128)S(1)} %stack.23.pos_ref, f32[9216,128]{1,0:T(8,128)S(1)} %step.2.u_in, ...), custom_call_target="tpu_custom_call" | custom-call | flops 10000000 | bytes 10000000 | tf_op jit(solution)/shard_map/faces/pallas_call | solution.py:65
  96.4 0.1 collective-permute-start.15
  96.5 2.0 %collective-permute-start.16 = (f32[1152,128]{1,0:T(8,128)S(1)}, f32[1152,128]{1,0:T(8,128)S(1)}, u32[]{:S(2)}, u32[]{:S(2)}) collective-permute-start(f32[1152,128]{1,0:T(8,128)S(1)} %get-tuple-element.94), channel_id=1, source_target_pairs={{0,6},{2,4},{4,2},{6,0},{1,7},{3,5},{5,3},{7,1},{8,14},{10,12},{12... | collective-permute-start | bytes 1769480 | tf_op jit(solution)/shard_map/ppermute | solution.py:31
  98.5 1.7 %collective-permute-start.18 = (f32[768,128]{1,0:T(8,128)S(1)}, f32[768,128]{1,0:T(8,128)S(1)}, u32[]{:S(2)}, u32[]{:S(2)}) collective-permute-start(f32[768,128]{1,0:T(8,128)S(1)} %get-tuple-element.96), channel_id=1, source_target_pairs={{0,65},{64,1},{1,64},{65,0},{2,67},{66,3},{3,66},{67,2},{4,69},{68... | collective-permute-start | bytes 1179656 | tf_op jit(solution)/shard_map/ppermute | solution.py:27
  100.2 7.6 %step.3.u_in = f32[9216,128]{1,0:T(8,128)S(1)} custom-call(f32[32]{0:T(128)S(1)} %reshape.4.par_ref, f32[4]{0:T(128)S(1)} %convert_multiply_fusion.w_ref, f32[24,28,32,128]{3,2,1,0:T(8,128)S(1)} %get-tuple-element.92.refs_0_, f32[24,28,32,128]{3,2,1,0:T(8,128)S(1)} %get-tuple-element.86.refs_0_.refs_1_, f32[384,128]{1,0:T(8,128)S(1)} %get-tuple-element.87.refs_1_.refs_2_, ...), custom_call_target="tpu_custom_call" | custom-call | flops 60000000 | bytes 10000000 | tf_op jit(solution)/shard_map/step/pallas_call | solution.py:65
  107.9 4.6 %faces.3 = (f32[24,28,32,128]{3,2,1,0:T(8,128)S(1)}, f32[1152,128]{1,0:T(8,128)S(1)}, f32[1152,128]{1,0:T(8,128)S(1)}, f32[768,128]{1,0:T(8,128)S(1)}, f32[768,128]{1,0:T(8,128)S(1)}) custom-call(f32[32]{0:T(128)S(1)} %reshape.4.par_ref, f32[4]{0:T(128)S(1)} %convert_multiply_fusion.w_ref, s32[5]{0:T(128)S(1)} %stack.23.pos_ref, f32[9216,128]{1,0:T(8,128)S(1)} %step.3.u_in, ...), custom_call_target="tpu_custom_call" | custom-call | flops 10000000 | bytes 10000000 | tf_op jit(solution)/shard_map/faces/pallas_call | solution.py:65
  112.4 0.9 collective-permute-start.19
  113.3 0.7 collective-permute-start.20
  114.0 1.8 %collective-permute-start.22 = (f32[768,128]{1,0:T(8,128)S(1)}, f32[768,128]{1,0:T(8,128)S(1)}, u32[]{:S(2)}, u32[]{:S(2)}) collective-permute-start(f32[768,128]{1,0:T(8,128)S(1)} %get-tuple-element.102), channel_id=1, source_target_pairs={{0,65},{64,1},{1,64},{65,0},{2,67},{66,3},{3,66},{67,2},{4,69},{68... | collective-permute-start | bytes 1179656 | tf_op jit(solution)/shard_map/ppermute | solution.py:27
  115.8 8.2 %last_step.1.d_in = f32[768,128]{1,0:T(8,128)S(1)} custom-call(f32[32]{0:T(128)S(1)} %reshape.4.par_ref, f32[4]{0:T(128)S(1)} %convert_multiply_fusion.w_ref, f32[24,28,32,128]{3,2,1,0:T(8,128)S(1)} %get-tuple-element.97.refs_0_, f32[24,28,32,128]{3,2,1,0:T(8,128)S(1)} %get-tuple-element.86.refs_0_.refs_1_, ...), custom_call_target="tpu_custom_call" | custom-call | flops 60000000 | bytes 10000000 | tf_op jit(solution)/shard_map/last_step/pallas_call | solution.py:65
  124.0 2.5 %density.1 = (f32[2,8,2304]{2,1,0:T(8,128)S(1)}, f32[2,8,2304]{2,1,0:T(8,128)S(1)}) custom-call(f32[32]{0:T(128)S(1)} %reshape.4.par_ref, f32[4]{0:T(128)S(1)} %convert_multiply_fusion.w_ref, s32[5]{0:T(128)S(1)} %stack.23.pos_ref, f32[768,128]{1,0:T(8,128)S(1)} %last_step.1.d_in, f32[1152,128]{1,0:T(8,128)S(1)} %collective-permute-done.19.za, ...), custom_call_target="tpu_custom_call" | custom-call | flops 10000000 | bytes 10000000 | tf_op jit(solution)/shard_map/density/pallas_call | solution.py:65
  126.6 7.8 %collective-permute-start.23 = (f32[2,8,2304]{2,1,0:T(8,128)S(1)}, f32[2,8,2304]{2,1,0:T(8,128)S(1)}, u32[]{:S(2)}, u32[]{:S(2)}) collective-permute-start(f32[2,8,2304]{2,1,0:T(8,128)S(1)} %get-tuple-element.104), channel_id=1, source_target_pairs={{0,8},{8,0},{1,9},{9,1},{2,10},{10,2},{3,11},{11,3},{4,12},{12,4},... | collective-permute-start | bytes 442376 | tf_op jit(solution)/shard_map/ppermute | solution.py:580
  134.4 1.0 collective-permute-done.23.b
  135.4 2.6 %collective-permute-start.26 = (f32[2,8,2304]{2,1,0:T(8,128)S(1)}, f32[2,8,2304]{2,1,0:T(8,128)S(1)}, u32[]{:S(2)}, u32[]{:S(2)}) collective-permute-start(f32[2,8,2304]{2,1,0:T(8,128)S(1)} %pair.1.s0), channel_id=1, source_target_pairs={{0,48},{16,32},{32,16},{48,0},{1,49},{17,33},{33,17},{49,1},{2,50}... | collective-permute-start | bytes 442376 | tf_op jit(solution)/shard_map/ppermute | solution.py:583
  138.0 0.5 collective-permute-start.25
  138.5 0.3 collective-permute-start.24
  138.8 5.3 %collective-permute-done.26.s3 = f32[2,8,2304]{2,1,0:T(8,128)S(1)} collective-permute-done((f32[2,8,2304]{2,1,0:T(8,128)S(1)}, f32[2,8,2304]{2,1,0:T(8,128)S(1)}, u32[]{:S(2)}, u32[]{:S(2)}) %collective-permute-start.26) | collective-permute-done | bytes 147488 | tf_op jit(solution)/shard_map/ppermute | solution.py:583
  144.1 0.3 collective-permute-done.25.s2
  144.3 1.0 collective-permute-done.24.s1
  145.3 0.6 split.1
  145.9 0.3 collective-permute-start.27
  146.2 1.7 %collective-permute-start.29 = (f32[8,2304]{1,0:T(8,128)S(1)}, f32[8,2304]{1,0:T(8,128)S(1)}, u32[]{:S(2)}, u32[]{:S(2)}) collective-permute-start(f32[8,2304]{1,0:T(8,128)S(1)} %get-tuple-element.106), channel_id=1, source_target_pairs={{0,65},{64,1},{1,64},{65,0},{2,67},{66,3},{3,66},{67,2},{4,69},{68... | collective-permute-start | bytes 221192 | tf_op jit(solution)/shard_map/ppermute | solution.py:27
  147.9 1.4 collective-permute-start.28
  149.2 1.4 collective-permute-done.29.t3
  150.6 2.3 %collective-permute-done.28.t2 = f32[8,2304]{1,0:T(8,128)S(1)} collective-permute-done((f32[8,2304]{1,0:T(8,128)S(1)}, f32[8,2304]{1,0:T(8,128)S(1)}, u32[]{:S(2)}, u32[]{:S(2)}) %collective-permute-start.28) | collective-permute-done | bytes 73760 | tf_op jit(solution)/shard_map/ppermute | solution.py:27
  152.9 0.6 place.1.mine
  153.4 3.0 %collective-permute-start.30 = (f32[8,9216]{1,0:T(8,128)S(1)}, f32[8,9216]{1,0:T(8,128)S(1)}, u32[]{:S(2)}, u32[]{:S(2)}) collective-permute-start(f32[8,9216]{1,0:T(8,128)S(1)} %place.1.mine), channel_id=1, source_target_pairs={{0,8},{8,0},{1,9},{9,1},{2,10},{10,2},{3,11},{11,3},{4,12},{12,4},... | collective-permute-start | bytes 884744 | tf_op jit(solution)/shard_map/ppermute | solution.py:580
  156.5 1.2 collective-permute-done.30.other
  157.7 1.4 both_components.1
  (44 shorter events, 0.2 us)
Async XLA Ops:
  0.0 4.7 %copy-start = (f32[2,3,2,8,9216]{4,3,2,1,0:T(8,128)S(1)}, f32[2,3,2,8,9216]{4,3,2,1,0:T(8,128)}, u32[]{:S(2)}) copy-start(f32[2,3,2,8,9216]{4,3,2,1,0:T(8,128)} %param.8) | copy-start | bytes 10616836
  0.0 15.8 %copy-start.5 = (f32[2,3]{1,0:T(2,128)S(1)}, f32[2,3]{1,0:T(2,128)}, u32[]{:S(2)}) copy-start(f32[2,3]{1,0:T(2,128)} %param.11) | copy-start | bytes 76
  0.9 14.8 %copy-start.6 = (f32[2,1]{1,0:T(2,128)}, f32[2,1]{1,0:T(2,128)S(1)}, u32[]{:S(2)}) copy-start(f32[2,1]{1,0:T(2,128)S(1)} %copy.10) | copy-start | bytes 28
  0.9 0.6 copy-start.7
  2.3 13.5 %collective-permute-start = (f32[2,8]{1,0:T(2,128)S(1)}, f32[2,8]{1,0:T(2,128)}, u32[]{:S(2)}, u32[]{:S(2)}) collective-permute-start(f32[2,8]{1,0:T(2,128)S(1)} %pad_maximum_fusion.1), channel_id=1, source_target_pairs={{0,64},{64,0},{1,65},{65,1},{2,66},{66,2},{3,67},{67,3},{4,68},{68... | collective-permute-start | bytes 200 | tf_op jit(solution)/shard_map/ppermute | solution.py:27
  5.7 47.4 %collective-permute-start.1 = (f32[2,3,2,8,2304]{4,3,2,1,0:T(8,128)}, f32[2,3,2,8,2304]{4,3,2,1,0:T(8,128)}, u32[]{:S(2)}, u32[]{:S(2)}) collective-permute-start(f32[2,3,2,8,2304]{4,3,2,1,0:T(8,128)} %constant_dynamic-slice_fusion.3), channel_id=1, source_target_pairs={{0,64},{64,0},{1,65},{65,1},{2,66},{66,2},{3,67},{67,3},{4,68},{68... | collective-permute-start | bytes 2654216 | tf_op jit(solution)/shard_map/ppermute | solution.py:27
  6.7 46.4 %collective-permute-start.3 = (f32[2,3,2,8,2304]{4,3,2,1,0:T(8,128)}, f32[2,3,2,8,2304]{4,3,2,1,0:T(8,128)}, u32[]{:S(2)}, u32[]{:S(2)}) collective-permute-start(f32[2,3,2,8,2304]{4,3,2,1,0:T(8,128)} %constant_dynamic-slice_fusion.2), channel_id=1, source_target_pairs={{0,65},{64,1},{1,64},{65,0},{2,67},{66,3},{3,66},{67,2},{4,69},{68... | collective-permute-start | bytes 2654216 | tf_op jit(solution)/shard_map/ppermute | solution.py:27
  11.3 41.8 %collective-permute-start.2 = (f32[2,3,2,8,2304]{4,3,2,1,0:T(8,128)}, f32[2,3,2,8,2304]{4,3,2,1,0:T(8,128)}, u32[]{:S(2)}, u32[]{:S(2)}) collective-permute-start(f32[2,3,2,8,2304]{4,3,2,1,0:T(8,128)} %constant_dynamic-slice_fusion.1), channel_id=1, source_target_pairs={{0,1},{64,65},{1,0},{65,64},{2,3},{66,67},{3,2},{67,66},{4,5},{68,... | collective-permute-start | bytes 2654216 | tf_op jit(solution)/shard_map/ppermute | solution.py:27
  13.2 39.9 %collective-permute-start.4 = (f32[3,8,2304]{2,1,0:T(8,128)}, f32[3,8,2304]{2,1,0:T(8,128)}, u32[]{:S(2)}, u32[]{:S(2)}) collective-permute-start(f32[3,8,2304]{2,1,0:T(8,128)} %get-tuple-element.107), channel_id=1, source_target_pairs={{0,65},{64,1},{1,64},{65,0},{2,67},{66,3},{3,66},{67,2},{4,69},{68... | collective-permute-start | bytes 663560 | tf_op jit(solution)/shard_map/ppermute | solution.py:27
  16.7 51.4 %copy-start.3 = (f32[3,8,2304]{2,1,0:T(8,128)S(1)}, f32[3,8,2304]{2,1,0:T(8,128)}, u32[]{:S(2)}) copy-start(f32[3,8,2304]{2,1,0:T(8,128)} %get-tuple-element.78.p0) | copy-start | bytes 663556
  53.1 0.9 copy-start.2
  57.8 26.4 %copy-start.4 = (bf16[256,256]{1,0:T(8,128)(2,1)S(1)}, bf16[256,256]{1,0:T(8,128)(2,1)}, u32[]{:S(2)}) copy-start(bf16[256,256]{1,0:T(8,128)(2,1)} %constant.49.clone.refs_2_.refs_3_) | copy-start | bytes 393220
  57.8 4.1 %collective-permute-start.7 = (f32[72,128]{1,0:T(8,128)S(1)}, f32[72,128]{1,0:T(8,128)S(1)}, u32[]{:S(2)}, u32[]{:S(2)}) collective-permute-start(f32[72,128]{1,0:T(8,128)S(1)} %products.1), channel_id=1, source_target_pairs={{0,65},{64,1},{1,64},{65,0},{2,67},{66,3},{3,66},{67,2},{4,69},{68... | collective-permute-start | bytes 110600 | tf_op jit(solution)/shard_map/ppermute | solution.py:27
  60.2 4.3 %collective-permute-start.6 = (f32[72,128]{1,0:T(8,128)S(1)}, f32[72,128]{1,0:T(8,128)S(1)}, u32[]{:S(2)}, u32[]{:S(2)}) collective-permute-start(f32[72,128]{1,0:T(8,128)S(1)} %products.1), channel_id=1, source_target_pairs={{0,1},{64,65},{1,0},{65,64},{2,3},{66,67},{3,2},{67,66},{4,5},{68,... | collective-permute-start | bytes 110600 | tf_op jit(solution)/shard_map/ppermute | solution.py:27
  60.3 2.8 %collective-permute-start.5 = (f32[72,128]{1,0:T(8,128)S(1)}, f32[72,128]{1,0:T(8,128)S(1)}, u32[]{:S(2)}, u32[]{:S(2)}) collective-permute-start(f32[72,128]{1,0:T(8,128)S(1)} %products.1), channel_id=1, source_target_pairs={{0,64},{64,0},{1,65},{65,1},{2,66},{66,2},{3,67},{67,3},{4,68},{68... | collective-permute-start | bytes 110600 | tf_op jit(solution)/shard_map/ppermute | solution.py:27
  64.6 7.3 %collective-permute-start.10 = (f32[72,128]{1,0:T(8,128)S(1)}, f32[72,128]{1,0:T(8,128)S(1)}, u32[]{:S(2)}, u32[]{:S(2)}) collective-permute-start(f32[72,128]{1,0:T(8,128)S(1)} %fusion.3.s0), channel_id=1, source_target_pairs={{0,6},{2,4},{4,2},{6,0},{1,7},{3,5},{5,3},{7,1},{8,14},{10,12},{12... | collective-permute-start | bytes 110600 | tf_op jit(solution)/shard_map/ppermute | solution.py:31
  67.4 4.5 %collective-permute-start.9 = (f32[72,128]{1,0:T(8,128)S(1)}, f32[72,128]{1,0:T(8,128)S(1)}, u32[]{:S(2)}, u32[]{:S(2)}) collective-permute-start(f32[72,128]{1,0:T(8,128)S(1)} %fusion.3.s0), channel_id=1, source_target_pairs={{0,4},{2,6},{4,0},{6,2},{1,5},{3,7},{5,1},{7,3},{8,12},{10,14},{12... | collective-permute-start | bytes 110600 | tf_op jit(solution)/shard_map/ppermute | solution.py:31
  67.7 4.1 %collective-permute-start.8 = (f32[72,128]{1,0:T(8,128)S(1)}, f32[72,128]{1,0:T(8,128)S(1)}, u32[]{:S(2)}, u32[]{:S(2)}) collective-permute-start(f32[72,128]{1,0:T(8,128)S(1)} %fusion.3.s0), channel_id=1, source_target_pairs={{0,2},{2,0},{4,6},{6,4},{1,3},{3,1},{5,7},{7,5},{8,10},{10,8},{12,... | collective-permute-start | bytes 110600 | tf_op jit(solution)/shard_map/ppermute | solution.py:31
  79.1 12.2 %collective-permute-start.11 = (f32[1152,128]{1,0:T(8,128)S(1)}, f32[1152,128]{1,0:T(8,128)S(1)}, u32[]{:S(2)}, u32[]{:S(2)}) collective-permute-start(f32[1152,128]{1,0:T(8,128)S(1)} %get-tuple-element.88), channel_id=1, source_target_pairs={{0,2},{2,0},{4,6},{6,4},{1,3},{3,1},{5,7},{7,5},{8,10},{10,8},{12,... | collective-permute-start | bytes 1769480 | tf_op jit(solution)/shard_map/ppermute | solution.py:31
  80.4 11.5 %collective-permute-start.12 = (f32[1152,128]{1,0:T(8,128)S(1)}, f32[1152,128]{1,0:T(8,128)S(1)}, u32[]{:S(2)}, u32[]{:S(2)}) collective-permute-start(f32[1152,128]{1,0:T(8,128)S(1)} %get-tuple-element.89), channel_id=1, source_target_pairs={{0,6},{2,4},{4,2},{6,0},{1,7},{3,5},{5,3},{7,1},{8,14},{10,12},{12... | collective-permute-start | bytes 1769480 | tf_op jit(solution)/shard_map/ppermute | solution.py:31
  82.3 9.1 %collective-permute-start.13 = (f32[768,128]{1,0:T(8,128)S(1)}, f32[768,128]{1,0:T(8,128)S(1)}, u32[]{:S(2)}, u32[]{:S(2)}) collective-permute-start(f32[768,128]{1,0:T(8,128)S(1)} %get-tuple-element.90), channel_id=1, source_target_pairs={{0,64},{64,0},{1,65},{65,1},{2,66},{66,2},{3,67},{67,3},{4,68},{68... | collective-permute-start | bytes 1179656 | tf_op jit(solution)/shard_map/ppermute | solution.py:27
  82.3 9.1 %collective-permute-start.14 = (f32[768,128]{1,0:T(8,128)S(1)}, f32[768,128]{1,0:T(8,128)S(1)}, u32[]{:S(2)}, u32[]{:S(2)}) collective-permute-start(f32[768,128]{1,0:T(8,128)S(1)} %get-tuple-element.91), channel_id=1, source_target_pairs={{0,65},{64,1},{1,64},{65,0},{2,67},{66,3},{3,66},{67,2},{4,69},{68... | collective-permute-start | bytes 1179656 | tf_op jit(solution)/shard_map/ppermute | solution.py:27
  96.4 11.4 %collective-permute-start.15 = (f32[1152,128]{1,0:T(8,128)S(1)}, f32[1152,128]{1,0:T(8,128)S(1)}, u32[]{:S(2)}, u32[]{:S(2)}) collective-permute-start(f32[1152,128]{1,0:T(8,128)S(1)} %get-tuple-element.93), channel_id=1, source_target_pairs={{0,2},{2,0},{4,6},{6,4},{1,3},{3,1},{5,7},{7,5},{8,10},{10,8},{12,... | collective-permute-start | bytes 1769480 | tf_op jit(solution)/shard_map/ppermute | solution.py:31
  96.5 11.4 %collective-permute-start.16 = (f32[1152,128]{1,0:T(8,128)S(1)}, f32[1152,128]{1,0:T(8,128)S(1)}, u32[]{:S(2)}, u32[]{:S(2)}) collective-permute-start(f32[1152,128]{1,0:T(8,128)S(1)} %get-tuple-element.94), channel_id=1, source_target_pairs={{0,6},{2,4},{4,2},{6,0},{1,7},{3,5},{5,3},{7,1},{8,14},{10,12},{12... | collective-permute-start | bytes 1769480 | tf_op jit(solution)/shard_map/ppermute | solution.py:31
  98.5 9.3 %collective-permute-start.17 = (f32[768,128]{1,0:T(8,128)S(1)}, f32[768,128]{1,0:T(8,128)S(1)}, u32[]{:S(2)}, u32[]{:S(2)}) collective-permute-start(f32[768,128]{1,0:T(8,128)S(1)} %get-tuple-element.95), channel_id=1, source_target_pairs={{0,64},{64,0},{1,65},{65,1},{2,66},{66,2},{3,67},{67,3},{4,68},{68... | collective-permute-start | bytes 1179656 | tf_op jit(solution)/shard_map/ppermute | solution.py:27
  98.5 9.3 %collective-permute-start.18 = (f32[768,128]{1,0:T(8,128)S(1)}, f32[768,128]{1,0:T(8,128)S(1)}, u32[]{:S(2)}, u32[]{:S(2)}) collective-permute-start(f32[768,128]{1,0:T(8,128)S(1)} %get-tuple-element.96), channel_id=1, source_target_pairs={{0,65},{64,1},{1,64},{65,0},{2,67},{66,3},{3,66},{67,2},{4,69},{68... | collective-permute-start | bytes 1179656 | tf_op jit(solution)/shard_map/ppermute | solution.py:27
  112.4 11.6 %collective-permute-start.19 = (f32[1152,128]{1,0:T(8,128)S(1)}, f32[1152,128]{1,0:T(8,128)S(1)}, u32[]{:S(2)}, u32[]{:S(2)}) collective-permute-start(f32[1152,128]{1,0:T(8,128)S(1)} %get-tuple-element.99), channel_id=1, source_target_pairs={{0,2},{2,0},{4,6},{6,4},{1,3},{3,1},{5,7},{7,5},{8,10},{10,8},{12,... | collective-permute-start | bytes 1769480 | tf_op jit(solution)/shard_map/ppermute | solution.py:31
  113.3 10.7 %collective-permute-start.20 = (f32[1152,128]{1,0:T(8,128)S(1)}, f32[1152,128]{1,0:T(8,128)S(1)}, u32[]{:S(2)}, u32[]{:S(2)}) collective-permute-start(f32[1152,128]{1,0:T(8,128)S(1)} %get-tuple-element.100), channel_id=1, source_target_pairs={{0,6},{2,4},{4,2},{6,0},{1,7},{3,5},{5,3},{7,1},{8,14},{10,12},{12... | collective-permute-start | bytes 1769480 | tf_op jit(solution)/shard_map/ppermute | solution.py:31
  114.0 10.0 %collective-permute-start.21 = (f32[768,128]{1,0:T(8,128)S(1)}, f32[768,128]{1,0:T(8,128)S(1)}, u32[]{:S(2)}, u32[]{:S(2)}) collective-permute-start(f32[768,128]{1,0:T(8,128)S(1)} %get-tuple-element.101), channel_id=1, source_target_pairs={{0,64},{64,0},{1,65},{65,1},{2,66},{66,2},{3,67},{67,3},{4,68},{68... | collective-permute-start | bytes 1179656 | tf_op jit(solution)/shard_map/ppermute | solution.py:27
  114.0 10.0 %collective-permute-start.22 = (f32[768,128]{1,0:T(8,128)S(1)}, f32[768,128]{1,0:T(8,128)S(1)}, u32[]{:S(2)}, u32[]{:S(2)}) collective-permute-start(f32[768,128]{1,0:T(8,128)S(1)} %get-tuple-element.102), channel_id=1, source_target_pairs={{0,65},{64,1},{1,64},{65,0},{2,67},{66,3},{3,66},{67,2},{4,69},{68... | collective-permute-start | bytes 1179656 | tf_op jit(solution)/shard_map/ppermute | solution.py:27
  115.8 43.3 %copy-start.1 = (f32[2,3,2,8,9216]{4,3,2,1,0:T(8,128)S(1)}, f32[2,3,2,8,9216]{4,3,2,1,0:T(8,128)}, u32[]{:S(2)}) copy-start(f32[2,3,2,8,9216]{4,3,2,1,0:T(8,128)} %param.8) | copy-start | bytes 10616836
  126.6 8.8 %collective-permute-start.23 = (f32[2,8,2304]{2,1,0:T(8,128)S(1)}, f32[2,8,2304]{2,1,0:T(8,128)S(1)}, u32[]{:S(2)}, u32[]{:S(2)}) collective-permute-start(f32[2,8,2304]{2,1,0:T(8,128)S(1)} %get-tuple-element.104), channel_id=1, source_target_pairs={{0,8},{8,0},{1,9},{9,1},{2,10},{10,2},{3,11},{11,3},{4,12},{12,4},... | collective-permute-start | bytes 442376 | tf_op jit(solution)/shard_map/ppermute | solution.py:580
  135.4 8.7 %collective-permute-start.26 = (f32[2,8,2304]{2,1,0:T(8,128)S(1)}, f32[2,8,2304]{2,1,0:T(8,128)S(1)}, u32[]{:S(2)}, u32[]{:S(2)}) collective-permute-start(f32[2,8,2304]{2,1,0:T(8,128)S(1)} %pair.1.s0), channel_id=1, source_target_pairs={{0,48},{16,32},{32,16},{48,0},{1,49},{17,33},{33,17},{49,1},{2,50}... | collective-permute-start | bytes 442376 | tf_op jit(solution)/shard_map/ppermute | solution.py:583
  138.0 6.4 %collective-permute-start.25 = (f32[2,8,2304]{2,1,0:T(8,128)S(1)}, f32[2,8,2304]{2,1,0:T(8,128)S(1)}, u32[]{:S(2)}, u32[]{:S(2)}) collective-permute-start(f32[2,8,2304]{2,1,0:T(8,128)S(1)} %pair.1.s0), channel_id=1, source_target_pairs={{0,32},{16,48},{32,0},{48,16},{1,33},{17,49},{33,1},{49,17},{2,34}... | collective-permute-start | bytes 442376 | tf_op jit(solution)/shard_map/ppermute | solution.py:583
  138.5 6.8 %collective-permute-start.24 = (f32[2,8,2304]{2,1,0:T(8,128)S(1)}, f32[2,8,2304]{2,1,0:T(8,128)S(1)}, u32[]{:S(2)}, u32[]{:S(2)}) collective-permute-start(f32[2,8,2304]{2,1,0:T(8,128)S(1)} %pair.1.s0), channel_id=1, source_target_pairs={{0,16},{16,0},{32,48},{48,32},{1,17},{17,1},{33,49},{49,33},{2,18}... | collective-permute-start | bytes 442376 | tf_op jit(solution)/shard_map/ppermute | solution.py:583
  145.9 3.3 %collective-permute-start.27 = (f32[8,2304]{1,0:T(8,128)S(1)}, f32[8,2304]{1,0:T(8,128)S(1)}, u32[]{:S(2)}, u32[]{:S(2)}) collective-permute-start(f32[8,2304]{1,0:T(8,128)S(1)} %get-tuple-element.105.t0), channel_id=1, source_target_pairs={{0,64},{64,0},{1,65},{65,1},{2,66},{66,2},{3,67},{67,3},{4,68},{68... | collective-permute-start | bytes 221192 | tf_op jit(solution)/shard_map/ppermute | solution.py:27
  146.2 4.4 %collective-permute-start.29 = (f32[8,2304]{1,0:T(8,128)S(1)}, f32[8,2304]{1,0:T(8,128)S(1)}, u32[]{:S(2)}, u32[]{:S(2)}) collective-permute-start(f32[8,2304]{1,0:T(8,128)S(1)} %get-tuple-element.106), channel_id=1, source_target_pairs={{0,65},{64,1},{1,64},{65,0},{2,67},{66,3},{3,66},{67,2},{4,69},{68... | collective-permute-start | bytes 221192 | tf_op jit(solution)/shard_map/ppermute | solution.py:27
  147.9 5.0 %collective-permute-start.28 = (f32[8,2304]{1,0:T(8,128)S(1)}, f32[8,2304]{1,0:T(8,128)S(1)}, u32[]{:S(2)}, u32[]{:S(2)}) collective-permute-start(f32[8,2304]{1,0:T(8,128)S(1)} %get-tuple-element.106), channel_id=1, source_target_pairs={{0,1},{64,65},{1,0},{65,64},{2,3},{66,67},{3,2},{67,66},{4,5},{68,... | collective-permute-start | bytes 221192 | tf_op jit(solution)/shard_map/ppermute | solution.py:27
  153.4 4.2 %collective-permute-start.30 = (f32[8,9216]{1,0:T(8,128)S(1)}, f32[8,9216]{1,0:T(8,128)S(1)}, u32[]{:S(2)}, u32[]{:S(2)}) collective-permute-start(f32[8,9216]{1,0:T(8,128)S(1)} %place.1.mine), channel_id=1, source_target_pairs={{0,8},{8,0},{1,9},{9,1},{2,10},{10,2},{3,11},{11,3},{4,12},{12,4},... | collective-permute-start | bytes 884744 | tf_op jit(solution)/shard_map/ppermute | solution.py:580

commit v4 on v3

--- a/solution.py
+++ b/solution.py
@@ -9,6 +9,7 @@
 from jax.sharding import Mesh
 from jax.sharding import PartitionSpec as P
 
+
 NX = 96
 ITERS = 4
 ROWS = 24
@@ -27,6 +28,10 @@
     return lax.ppermute(value, ZAX, z_perm(lambda z: z ^ m))
 
 
+def other_core(value):
+    return lax.ppermute(value, "c", [(0, 1), (1, 0)])
+
+
 def y_xor(value, m):
     return lax.ppermute(value, "y", [(i, i ^ m) for i in range(4)])
 
@@ -36,11 +41,10 @@
 
 
 def unpack_rows(a, b, c, lanes):
-    r0 = a
-    r1 = jnp.where(lanes < 32, pltpu.roll(a, 32, 1), pltpu.roll(b, 32, 1))
-    r2 = jnp.where(lanes < 64, pltpu.roll(b, 64, 1), pltpu.roll(c, 64, 1))
+    r1 = pltpu.roll(jnp.where(lanes < 96, b, a), 32, 1)
+    r2 = pltpu.roll(jnp.where(lanes < 64, c, b), 64, 1)
     r3 = pltpu.roll(c, 96, 1)
-    return r0, r1, r2, r3
+    return a, r1, r2, r3
 
 
 def pack_rows(r0, r1, r2, r3, lanes):
@@ -58,7 +62,7 @@
     return pltpu.VMEM(shape, F32)
 
 
-def call(kernel, name, args, outs, scratch=(), scalars=0, aliases=None, flops=10_000_000, limit=8):
+def call(kernel, args, outs, scratch=(), scalars=0, aliases=None, flops=10_000_000, limit=8):
     specs = [pl.BlockSpec(memory_space=pltpu.SMEM)] * scalars
     specs += [pl.BlockSpec(memory_space=pltpu.VMEM)] * (len(args) - scalars)
     args = list(args[:scalars]) + [pltpu.with_memory_space_constraint(a, pltpu.VMEM) for a in args[scalars:]]
@@ -71,12 +75,90 @@
         input_output_aliases=aliases or {},
         compiler_params=pltpu.CompilerParams(vmem_limit_bytes=limit * 2**20),
         cost_estimate=pl.CostEstimate(flops=flops, bytes_accessed=10_000_000, transcendentals=0),
-        name=name,
     )(*args)
 
 
-def lanes_at(group, v):
-    return pl.ds(pl.multiple_of(group * GROUP + v * 128, 128), 128)
+def lanes_at(group, v, base=0):
+    return pl.ds(pl.multiple_of(base + group * GROUP + v * 128, 128), 128)
+
+
+HALF = CHUNK // 2
+IN_HBM = pl.BlockSpec(memory_space=pltpu.HBM)
+
+
+def rows_of_chunk(ref, z, extra=0, width=CHUNK):
+    index = (slice(None),) * (len(ref.shape) - 1) + (pl.ds(pl.multiple_of(z * CHUNK + extra, 128), width),)
+    return ref.at[index]
+
+
+def cut_near_kernel(pos_ref, orb, pert, wave, level, partner, send3, send1, small, mine, wave_s, level_s, partner_s, sems):
+    z, core = pos_ref[1], pos_ref[3]
+    moves = [
+        (wave, wave_s),
+        (level, level_s),
+        (partner, partner_s),
+        (rows_of_chunk(pert, z ^ 3, core * HALF, HALF), small.at[:, :, pl.ds(0, HALF)]),
+        (rows_of_chunk(orb, z ^ 3), send3),
+        (rows_of_chunk(orb, z ^ 1), send1),
+    ]
+    copies = [pltpu.make_async_copy(source, target, sems.at[i]) for i, (source, target) in enumerate(moves)]
+    for copy in copies:
+        copy.start()
+    rows = lax.broadcasted_iota(jnp.int32, (8, 128), 0)
+    cols = lax.broadcasted_iota(jnp.int32, (8, 128), 1)
+    out = jnp.zeros((8, 128), F32)
+    for copy in copies[:3]:
+        copy.wait()
+    for k in range(2):
+        values = [wave_s[k, d] for d in range(3)] + [level_s[k, n] for n in range(3)]
+        values.append((partner_s[k] & 1).astype(F32))
+        for j, value in enumerate(values):
+            out = jnp.where((rows == k) & (cols == j), value, out)
+    mine[...] = out
+    small[0, :, HALF:] = out
+    small[1, :, HALF:] = out
+    for copy in copies[3:]:
+        copy.wait()
+
+
+def cut_near(pos, orbitals, perturbation, wave, level, partner_map):
+    chunk = orbitals.shape[:-1] + (CHUNK,)
+    return pl.pallas_call(
+        cut_near_kernel,
+        in_specs=[pl.BlockSpec(memory_space=pltpu.SMEM)] + [IN_HBM] * 5,
+        out_specs=[pl.BlockSpec(memory_space=pltpu.VMEM)] * 4,
+        out_shape=[in_vmem(chunk), in_vmem(chunk), in_vmem((2, 8, HALF + 128)), in_vmem((8, 128))],
+        scratch_shapes=[
+            pltpu.SMEM((2, 3), F32),
+            pltpu.SMEM((2, 3), F32),
+            pltpu.SMEM((2,), jnp.int32),
+            pltpu.SemaphoreType.DMA((6,)),
+        ],
+        compiler_params=pltpu.CompilerParams(vmem_limit_bytes=4 * 2**20),
+        name="cut_near",
+    )(pos, *[pltpu.with_memory_space_constraint(a, pltpu.HBM) for a in (orbitals, perturbation, wave, level, partner_map)])
+
+
+def cut_far_kernel(pos_ref, orb, pot, after, send2, pot_send, sems):
+    z = pos_ref[1]
+    moves = ((rows_of_chunk(orb, z ^ 2), send2), (rows_of_chunk(pot, z ^ 3), pot_send))
+    copies = [pltpu.make_async_copy(source, target, sems.at[i]) for i, (source, target) in enumerate(moves)]
+    for copy in copies:
+        copy.start()
+    for copy in copies:
+        copy.wait()
+
+
+def cut_far(pos, orbitals, potential, after):
+    return pl.pallas_call(
+        cut_far_kernel,
+        in_specs=[pl.BlockSpec(memory_space=pltpu.SMEM), IN_HBM, IN_HBM, pl.BlockSpec(memory_space=pl.ANY)],
+        out_specs=[pl.BlockSpec(memory_space=pltpu.VMEM)] * 2,
+        out_shape=[in_vmem(orbitals.shape[:-1] + (CHUNK,)), in_vmem((8, CHUNK))],
+        scratch_shapes=[pltpu.SemaphoreType.DMA((2,))],
+        compiler_params=pltpu.CompilerParams(vmem_limit_bytes=4 * 2**20),
+        name="cut_far",
+    )(pos, *[pltpu.with_memory_space_constraint(a, pltpu.HBM) for a in (orbitals, potential)], after)
 
 
 def perturbed(field, pert_r, pert_i):
@@ -84,35 +166,59 @@
     return pert_r * re - pert_i * im, pert_r * im + pert_i * re
 
 
-def products_kernel(slot_ref, o0, o1, o2, o3, p0, p1, out_ref):
-    slabs = (((o0, o1), p0), ((o2, o3), p1))
+def join_halves(pos_ref, got, swap, joined):
+    core = pos_ref[3]
+    joined[:, :, pl.ds(pl.multiple_of(core * HALF, 128), HALF)] = got[:, :, :HALF]
+    joined[:, :, pl.ds(pl.multiple_of((1 - core) * HALF, 128), HALF)] = swap[:, :, :HALF]
+
+
+def products_kernel(near, pos_ref, slot_ref, o0, o1, *refs):
+    if near:
+        pert, out_ref = refs
+        base = pos_ref[1] * CHUNK
+    else:
+        got, swap, near_ref, out_ref, pert = refs
+        join_halves(pos_ref, got, swap, pert)
+        base = 0
+    pair, bases = (o0, o1), (base, 0)
     for k in range(4):
         block, kk = k // 2, k % 2
         slot = slot_ref[k]
 
         def body(g, acc, block=block, kk=kk, slot=slot):
             acc = list(acc)
-            for pair, pert in slabs:
-                own, mate = pair[block], pair[1 - block]
-                for v in range(3):
-                    at = lanes_at(g, v)
-                    pr, pi = pert[1, :, at], pert[2, :, at]
-                    w = [perturbed((own[kk, n, 0, :, at], own[kk, n, 1, :, at]), pr, pi) for n in range(3)]
-                    for m in range(3):
-                        mr, mi = mate[slot, m, 0, :, at], mate[slot, m, 1, :, at]
-                        for n in range(3):
-                            i = (m * 3 + n) * 2
-                            acc[i] = acc[i] + (mr * w[n][0] + mi * w[n][1])
-                            acc[i + 1] = acc[i + 1] + (mr * w[n][1] - mi * w[n][0])
+            own, mate = pair[block], pair[1 - block]
+            for v in range(3):
+                at, mate_at, pert_at = (lanes_at(g, v, start) for start in (bases[block], bases[1 - block], base))
+                pr, pi = pert[0, :, pert_at], pert[1, :, pert_at]
+                w = [perturbed((own[kk, n, 0, :, at], own[kk, n, 1, :, at]), pr, pi) for n in range(3)]
+                for m in range(3):
+                    mr, mi = mate[slot, m, 0, :, mate_at], mate[slot, m, 1, :, mate_at]
+                    for n in range(3):
+                        i = (m * 3 + n) * 2
+                        acc[i] = acc[i] + (mr * w[n][0] + mi * w[n][1])
+                        acc[i + 1] = acc[i + 1] + (mr * w[n][1] - mi * w[n][0])
             return tuple(acc)
 
         acc = lax.fori_loop(0, CHUNK // GROUP, body, (jnp.zeros((8, 128), F32),) * 18)
         for i in range(18):
-            out_ref[pl.ds(k * 18 + i, 1), :] = jnp.sum(acc[i], axis=0, keepdims=True)
-
-
-def products(slots, fields, perts):
-    return call(products_kernel, "products", (slots, *fields, *perts), [(72, 128)], scalars=1, flops=20_000_000)[0]
+            at = pl.ds(block * 40 + kk * 18 + i, 1)
+            value = jnp.sum(acc[i], axis=0, keepdims=True)
+            out_ref[at, :] = value if near else near_ref[at, :] + value
+    for block in range(2):
+        out_ref[block * 40 + 36 : block * 40 + 40, :] = jnp.zeros((4, 128), F32)
+
+
+def products(pos, slots, o0, o1, *pert):
+    near = len(pert) == 1
+    return call(
+        functools.partial(products_kernel, near),
+        (pos, slots, o0, o1, *pert),
+        [(80, 128)],
+        scratch=() if near else [pltpu.VMEM((2, 8, CHUNK), F32)],
+        scalars=2,
+        flops=20_000_000,
+    )[0]
 
 
 TALL, DEEP = ROWS + 4, 32
@@ -124,19 +230,21 @@
     return ((kn * 2 + c) * ROWS + r) * 16
 
 
-def orbital_rows_kernel(pos_ref, o0, o1, o2, o3, p0, p1, orb_ref, v_ref):
+def orbital_rows_kernel(pos_ref, o0, o1, o2, o3, pot, pot1, orb_ref, v_ref):
     lanes = lane_ids()
     half = pos_ref[0]
 
     def body(g, carry):
-        for pair, pert, z in (((o0, o1), p0, half), ((o2, o3), p1, 1 - half)):
-            rows = unpack_rows(*[pert[0, :, lanes_at(g, v)] for v in range(3)], lanes)
+        for pair, pot_ref, z, base in (((o0, o1), pot, half, pos_ref[1] * CHUNK), ((o2, o3), pot1, 1 - half, 0)):
+            rows = unpack_rows(*[pot_ref[:, lanes_at(g, v, base)] for v in range(3)], lanes)
             for j in range(4):
                 v_ref[pl.ds(pl.multiple_of((4 * g + j) * 16 + 8 * z, 8), 8), :] = rows[j]
             for k in range(4):
+                start = base if k < 2 else 0
                 for n in range(3):
                     for c in range(2):
-                        rows = unpack_rows(*[pair[k // 2][k % 2, n, c, :, lanes_at(g, v)] for v in range(3)], lanes)
+                        cells = [pair[k // 2][k % 2, n, c, :, lanes_at(g, v, start)] for v in range(3)]
+                        rows = unpack_rows(*cells, lanes)
                         for j in range(4):
                             at = pl.multiple_of(rows_at(k * 3 + n, c, 4 * g + j) + 8 * z, 8)
                             orb_ref[pl.ds(at, 8), :] = rows[j]
@@ -145,8 +253,8 @@
     lax.fori_loop(0, CHUNK // GROUP, body, 0)
 
 
-def orbital_rows(pos, fields, perts):
-    return call(orbital_rows_kernel, "orbital_rows", (pos, *fields, *perts), [ORBITALS, (ROWS * 16, 128)], scalars=1)
+def orbital_rows(pos, fields, pots):
+    return call(orbital_rows_kernel, (pos, *fields, *pots), [ORBITALS, (ROWS * 16, 128)], scalars=1)
 
 
 ZHALO, YHALO = (48 * ROWS, 128), (24 * 32, 128)
@@ -156,16 +264,13 @@
     return ((kn * 2 + c) * TALL + r + 2) * DEEP + 8 + plane
 
 
-def clear_margin(u_ref):
-    def body(i, carry):
+def clear_margin(u_ref, kn):
+    for i in (kn * 2, kn * 2 + 1):
         for r in (0, 1, TALL - 2, TALL - 1):
             u_ref[i, r] = jnp.zeros((DEEP, 128), F32)
         for r in range(2, TALL - 2):
             u_ref[i, r, 0:8] = jnp.zeros((8, 128), F32)
             u_ref[i, r, 24:32] = jnp.zeros((8, 128), F32)
-        return carry
-
-    lax.fori_loop(0, 24, body, 0)
 
 
 def near_face(parity, size):
@@ -195,31 +300,32 @@
     return y_xor(za, 1), y_xor(zb, 3), z_xor(ya, 1), z_xor(yb, 3)
 
 
-def right_kernel(ncells, slot_ref, pos_ref, s0, s1, s2, s3, o0, o1, o2, o3, p0, p1, r_ref, za, zb, ya, yb, prod_ref):
+def right_kernel(ncells, slot_ref, pos_ref, s0, s1, s2, s3, o0, o1, o2, o3, pert0, got, swap, r_ref, za, zb, ya, yb, prod_ref, pert1):
+    join_halves(pos_ref, got, swap, pert1)
     total = (s0[...] + s1[...]) + (s2[...] + s3[...])
     ones = jnp.full((128, 128), 1.0, F32)
     prod_ref[...] = jnp.dot(total, ones, precision=lax.Precision.HIGHEST, preferred_element_type=F32) / ncells
-    clear_margin(r_ref)
     lanes = lane_ids()
     half = pos_ref[0]
-    slabs = (((o0, o1), p0, half), ((o2, o3), p1, 1 - half))
+    slabs = (((o0, o1), pert0, half, pos_ref[1] * CHUNK), ((o2, o3), pert1, 1 - half, 0))
     for k in range(4):
         block, kk = k // 2, k % 2
         slot = slot_ref[k]
 
         def body(g, carry, k=k, block=block, kk=kk, slot=slot):
-            for pair, pert, z in slabs:
+            for pair, pert, z, base in slabs:
                 own, mate = pair[block], pair[1 - block]
+                own_base, mate_base = (base, 0) if block == 0 else (0, base)
                 right = [[[], []] for _ in range(3)]
                 for v in range(3):
-                    at = lanes_at(g, v)
-                    pr, pi = pert[1, :, at], pert[2, :, at]
-                    mates = [(mate[slot, m, 0, :, at], mate[slot, m, 1, :, at]) for m in range(3)]
+                    at, mate_at, pert_at = (lanes_at(g, v, start) for start in (own_base, mate_base, base))
+                    pr, pi = pert[0, :, pert_at], pert[1, :, pert_at]
+                    mates = [(mate[slot, m, 0, :, mate_at], mate[slot, m, 1, :, mate_at]) for m in range(3)]
                     for n in range(3):
                         wr, wi = perturbed((own[kk, n, 0, :, at], own[kk, n, 1, :, at]), pr, pi)
                         gr, gi = -wr, -wi
                         for m in range(3):
-                            row = k * 18 + (m * 3 + n) * 2
+                            row = block * 40 + kk * 18 + (m * 3 + n) * 2
                             qr = prod_ref[pl.ds(row, 1), :]
                             qi = prod_ref[pl.ds(row + 1, 1), :]
                             mr, mi = mates[m]
@@ -240,6 +346,7 @@
     flat = r_ref.reshape(24 * TALL * DEEP, 128)
 
     def cut(kn, carry):
+        clear_margin(r_ref, kn)
         cut_planes(flat, pos_ref, kn, za, zb)
         cut_rows(r_ref, pos_ref, kn, ya, yb)
         return carry
@@ -250,10 +357,9 @@
 def right_sides(ncells, slots, pos, sums, fields, perts):
     return call(
         functools.partial(right_kernel, ncells),
-        "right_sides",
         (slots, pos, *sums, *fields, *perts),
         [FIELD, ZHALO, ZHALO, YHALO, YHALO],
-        scratch=[pltpu.VMEM((72, 128), F32)],
+        scratch=[pltpu.VMEM((80, 128), F32), pltpu.VMEM((2, 8, CHUNK), F32)],
         scalars=2,
         flops=20_000_000,
     )
@@ -270,8 +376,8 @@
 
 def scalars_of(count, par_ref, w_ref, kn):
     k, n = kn // 3, kn % 3
-    kx, ky, kz = par_ref[k * 8], par_ref[k * 8 + 1], par_ref[k * 8 + 2]
-    base = 3.75 + 0.5 * (kx * kx + ky * ky + kz * kz) + par_ref[k * 8 + 3 + n]
+    kx, ky, kz = par_ref[k, 0], par_ref[k, 1], par_ref[k, 2]
+    base = 3.75 + 0.5 * (kx * kx + ky * ky + kz * kz) + par_ref[k, 3 + n]
     wt = w_ref[count]
     scale = w_ref[0] if count == 1 else jnp.float32(1.0)
     return kx, ky, kz, base, wt, scale
@@ -354,7 +460,6 @@
     last = count == ITERS - 1
     return call(
         functools.partial(step_kernel, count),
-        "last_step" if last else "step",
         (par, weights) + ((u,) if count > 1 else ()) + (right, pot, matrix) + ((orb,) if last else ()),
         [(2 * ROWS * 16, 128) if last else ORBITALS],
         scratch=[pltpu.VMEM((256, 256), F32)] * 3,
@@ -375,7 +480,7 @@
 
 
 def faces(count, par_ref, w_ref, pos_ref, kn, za, zb, ya, yb, add_plane, add_row):
-    kx, ky, kz, base, wt, scale = scalars_of(count, par_ref, w_ref, kn)
+    _, ky, kz, _, wt, scale = scalars_of(count, par_ref, w_ref, kn)
     ws = wt * scale
     lap = ws / 24.0
     gy, gz = ws * ky * (2.0 / 3.0), ws * kz * (2.0 / 3.0)
@@ -387,41 +492,43 @@
     def line(ref, r):
         return [ref[pl.ds(pl.multiple_of(((from_z * 2 + c) * 2 + r) * 16, 8), 16), :] for c in range(2)]
 
-    def side(ref, layer, size, g, below, add):
+    def side(ref, layer, size, g, below, add, which):
         sign = (1 - 2 * below).astype(F32)
         first = (1 - below) * (size - 1)
         terms = face_terms(lap, sign * g, layer(ref, below), layer(ref, 1 - below))
-        add(first, terms[0])
-        add(first + 2 * below - 1, terms[1])
+        add(first, terms[0], which, 1 - below)
+        add(first + 2 * below - 1, terms[1], which, below)
 
     odd = pos_ref[1] & 1
-    side(ya, line, ROWS, gy, odd, add_row)
-    side(yb, line, ROWS, gy, 1 - odd, add_row)
+    side(ya, line, ROWS, gy, odd, add_row, 0)
+    side(yb, line, ROWS, gy, 1 - odd, add_row, 1)
     odd = pos_ref[4] & 1
-    side(za, plane, 16, gz, odd, add_plane)
-    side(zb, plane, 16, gz, 1 - odd, add_plane)
+    side(za, plane, 16, gz, odd, add_plane, 0)
+    side(zb, plane, 16, gz, 1 - odd, add_plane, 1)
 
 
 def faces_kernel(count, par_ref, w_ref, pos_ref, u_in, za_in, zb_in, ya_in, yb_in, u_ref, za, zb, ya, yb):
-    clear_margin(u_ref)
     flat = u_ref.reshape(24 * TALL * DEEP, 128)
 
     def orbital(kn, carry):
+        clear_margin(u_ref, kn)
         for c in range(2):
             for r in range(ROWS):
                 u_ref[kn * 2 + c, r + 2, 8:24, :] = u_in[pl.ds(pl.multiple_of(rows_at(kn, c, r), 16), 16), :]
 
-        def add_plane(p, term):
+        def add_plane(p, term, which, place):
             for c in range(2):
                 at = pl.ds(field_rows(kn, c, 0, p), ROWS, stride=DEEP)
-                flat[at, :] = flat[at, :] + term[c]
-
-        def add_row(r, term):
+                value = flat[at, :] + term[c]
+                flat[at, :] = value
+                to = pl.ds(pl.multiple_of(((kn * 2 + c) * 2 + place) * ROWS, 8), ROWS)
+                (za, zb)[which][to, :] = value
+
+        def add_row(r, term, which, place):
             for c in range(2):
                 u_ref[kn * 2 + c, r + 2, 8:24, :] = u_ref[kn * 2 + c, r + 2, 8:24, :] + term[c]
 
         faces(count, par_ref, w_ref, pos_ref, kn, za_in, zb_in, ya_in, yb_in, add_plane, add_row)
-        cut_planes(flat, pos_ref, kn, za, zb)
         cut_rows(u_ref, pos_ref, kn, ya, yb)
         return carry
 
@@ -431,7 +538,6 @@
 def add_faces(count, par, weights, pos, u, halos):
     return call(
         functools.partial(faces_kernel, count),
-        "faces",
         (par, weights, pos, u, *halos),
         [FIELD, ZHALO, ZHALO, YHALO, YHALO],
         scalars=3,
@@ -447,14 +553,14 @@
             d_ref[to[0], :] = d_ref[to[0], :] + (orb_r * term[0] + orb_i * term[1])
             d_ref[to[1], :] = d_ref[to[1], :] + (orb_r * term[1] - orb_i * term[0])
 
-        def add_plane(p, term):
+        def add_plane(p, term, which, place):
             add(
                 [pl.ds(rows_at(kn, c, 0) + p, ROWS, stride=16) for c in range(2)],
                 [pl.ds(c * ROWS * 16 + p, ROWS, stride=16) for c in range(2)],
                 term,
             )
 
-        def add_row(r, term):
+        def add_row(r, term, which, place):
             add(
                 [pl.ds(pl.multiple_of(rows_at(kn, c, r), 16), 16) for c in range(2)],
                 [pl.ds(pl.multiple_of((c * ROWS + r) * 16, 16), 16) for c in range(2)],
@@ -486,7 +592,6 @@
 def tile_density(par, weights, pos, dens, halos, orb):
     return call(
         density_kernel,
-        "density",
         (par, weights, pos, dens, *halos, orb),
         [TILE, TILE],
         scratch=[pltpu.VMEM((2 * ROWS * 16, 128), F32)],
@@ -528,62 +633,50 @@
     )(pos, mine, other)
 
 
-def on_device(orbitals, partner_map, wave_vectors, levels, potential, perturbation, step_weights):
+def program(orbitals, partner_map, wave_vectors, levels, potential, perturbation, step_weights):
     zl, zh = lax.axis_index("zl"), lax.axis_index("zh")
     z = zh * 2 + zl
     pos = jnp.stack([zh, z, lax.axis_index("x"), lax.axis_index("c"), lax.axis_index("y")]).astype(jnp.int32)
     ncells = 64 * 4 * CHUNK
-
-    def chunk(array, q):
-        return lax.dynamic_slice_in_dim(array, q * CHUNK, CHUNK, axis=array.ndim - 1)
-
-    fields = [None] * 4
-    for m in (1, 3, 2):
-        part = chunk(orbitals, z ^ m)
-        fields[m] = z_xor(part, m)
-        orbitals, part = lax.optimization_barrier((orbitals, part))
-    partner_map, wave_vectors, levels, potential, perturbation, step_weights, part = lax.optimization_barrier(
-        (partner_map, wave_vectors, levels, potential, perturbation, step_weights, part)
-    )
-    pots = jnp.concatenate([potential[None], perturbation], 0)
-    perts = [chunk(pots, z), z_xor(chunk(pots, z ^ 3), 3)]
-    slot = (partner_map % 2).astype(F32)
-    mine = jnp.concatenate([wave_vectors, levels, slot[:, None], jnp.zeros((2, 1), F32)], 1)
+    matrix = jnp.asarray(x_matrix(), jnp.bfloat16)
+
+    send3, send1, small, mine = cut_near(pos, orbitals, perturbation, wave_vectors, levels, partner_map)
+    got = z_xor(small, 3)
+    o3 = z_xor(send3, 3)
+    o1 = z_xor(send1, 1)
+    send2, pot_send = cut_far(pos, orbitals, potential, send1)
+    o2 = z_xor(send2, 2)
+    pot1 = z_xor(pot_send, 3)
+    swap = other_core(got)
+    par = jnp.concatenate([mine[:2, :8], got[0, :2, HALF : HALF + 8]], 0)
+    slots = par[:, 6].astype(jnp.int32)
     weights = step_weights.astype(F32) / 100.0
-    both = jnp.concatenate([mine, z_xor(mine, 1)], 0)
-    slots = both[:, 6].astype(jnp.int32)
-    par = both.reshape(32)
-    matrix = jnp.asarray(x_matrix(), jnp.bfloat16)
-    pos, slots, par, weights, orbitals = lax.optimization_barrier((pos, slots, par, weights, orbitals))
-    fields[0] = chunk(orbitals, z)
-    pos, slots, par, weights, fields, perts = lax.optimization_barrier((pos, slots, par, weights, fields, perts))
-
-    part = products(slots, fields, perts)
-    orb, pot = orbital_rows(pos, fields, perts)
+
+    fields, pert = [orbitals, o1, o2, o3], (perturbation, got, swap)
+    part = products(pos, slots, orbitals, o1, perturbation)
+    part = products(pos, slots, o2, o3, got, swap, part)
+    orb, pot = orbital_rows(pos, fields, (potential, pot1))
 
     def swapped(value):
-        return jnp.concatenate([value[36:], value[:36]], 0)
+        return jnp.concatenate([value[40:], value[:40]], 0)
 
     part = part + swapped(z_xor(part, 1)) + z_xor(part, 2) + swapped(z_xor(part, 3))
     sums = [part] + [y_xor(part, m) for m in (1, 2, 3)]
     orb, pot, sums = lax.optimization_barrier((orb, pot, sums))
-    right, *cut = right_sides(float(ncells), slots, pos, sums, fields, perts)
+    right, *edge = right_sides(float(ncells), slots, pos, sums, fields, pert)
     u = right
     for count in range(1, ITERS):
-        halos = exchange(*cut)
+        halos = exchange(*edge)
         u = inner_step(count, par, weights, u, right, pot, matrix, orb)
         if count < ITERS - 1:
-            u, *cut = add_faces(count, par, weights, pos, u, halos)
+            u, *edge = add_faces(count, par, weights, pos, u, halos)
     keep, send = tile_density(par, weights, pos, u, halos, orb)
 
-    def other_core(value):
-        return lax.ppermute(value, "c", [(0, 1), (1, 0)])
-
-    chip = call(pair_kernel, "pair", (keep, other_core(send)), [TILE])[0]
+    chip = call(pair_kernel, (keep, other_core(send)), [TILE])[0]
     parts = [chip] + [lax.ppermute(chip, "x", [(i, i ^ m) for i in range(4)]) for m in (1, 2, 3)]
-    same, cross = call(split_kernel, "split", (pos, *parts), [(8, CHUNK)] * 2, scalars=1)
+    same, cross = call(split_kernel, (pos, *parts), [(8, CHUNK)] * 2, scalars=1)
     tiles = [same, z_xor(same, 1), z_xor(cross, 2), z_xor(cross, 3)]
-    slab = call(place_kernel, "place", (pos, *tiles), [(8, 4 * CHUNK)], scalars=1)[0]
+    slab = call(place_kernel, (pos, *tiles), [(8, 4 * CHUNK)], scalars=1)[0]
     return both_components(pos, slab, other_core(slab))
 
 
@@ -591,7 +684,7 @@
     fine = Mesh(mesh.devices.reshape(2, 4, 2, 4, 2), ("zl", "x", "c", "y", "zh"))
     ka, grid = ("zl", "x", "c"), ("y", "zh")
     return jax.shard_map(
-        on_device,
+        program,
         mesh=fine,
         in_specs=(
             P(ka, None, None, grid, None),

time: 159 us -> 152 us (0.956)
  other arithmetic: 5.07 us -> 0.22 us
  local copies, waits for them, and re-layouts: 4.83 us -> 0.12 us
  waiting for transfers between devices: 52.5 us -> 54.5 us
    ppermute x9, waiting for transfers between devices: 0.45 us -> 6.12 us  [y_xor(): return lax.ppermute(value, 'y', [(i, i ^ m) for i in range(4)])]
    pallas_call x12 -> x13, Pallas kernels: 50.5 us -> 45.5 us  [call(): pl.pallas_call(kernel, in_specs=specs, out_specs=[pl.BlockSpec(memory_spa...]
    pallas_call x0 -> x2, Pallas kernels: none -> 4.11 us  [the longest x1 2.38 us: cut_near(): pl.pallas_call(cut_near_kernel, in_specs=[pl.BlockSpec(memory_space=pltpu...]
    ppermute x17, waiting for transfers between devices: 43.3 us -> 39.6 us  [z_xor(): return lax.ppermute(value, ZAX, z_perm(lambda z: z ^ m))]
    concatenate x3 -> x1, other arithmetic: 3.4 us -> 0.01 us  [program(): par = jnp.concatenate([mine[:2, :8], got[0, :2, HALF:HALF + 8]], 0)]
    dynamic_slice x4 -> x0, local copies, waits for them, and re-layouts: 3.02 us -> none  [chunk(): lax.dynamic_slice_in_dim(array, q * CHUNK, CHUNK, axis=array.ndim - 1)]
    ppermute x9, starting transfers between devices: 10.3 us -> 7.89 us  [y_xor(): return lax.ppermute(value, 'y', [(i, i ^ m) for i in range(4)])]
    ppermute x2 -> x3, starting transfers between devices: 10.9 us -> 12.5 us  [other_core(): return lax.ppermute(value, 'c', [(0, 1), (1, 0)])]
  transfers between devices with their start and end apart: 31 -> 32, of which waited for: 12 -> 16; matrix products, arithmetic and copies ran while one was open for 4% -> 0% of each run, Pallas kernels for 17% -> 19%
where the time goes in v4:
time: 152 us; the launch traced here: 151 us
  waiting for transfers between devices  54.5 us (36%)
  Pallas kernels  51 us (34%)
  starting transfers between devices  45.2 us (30%)
    pallas_call x13, Pallas kernels, call(): pl.pallas_call(kernel, in_specs=specs, out_specs=[pl.BlockSpec(memory_spa...  45.5 us
    ppermute x17, waiting for transfers between devices, z_xor(): return lax.ppermute(value, ZAX, z_perm(lambda z: z ^ m))  39.6 us
    ppermute x17, starting transfers between devices, z_xor(): return lax.ppermute(value, ZAX, z_perm(lambda z: z ^ m))  21.5 us
    ppermute x3, starting transfers between devices, other_core(): return lax.ppermute(value, 'c', [(0, 1), (1, 0)])  12.5 us
    ppermute x9, starting transfers between devices, y_xor(): return lax.ppermute(value, 'y', [(i, i ^ m) for i in range(4)])  7.89 us
    ppermute x3, waiting for transfers between devices, program(): lax.ppermute(chip, 'x', [(i, i ^ m) for i in range(4)])  6.55 us
    ppermute x9, waiting for transfers between devices, y_xor(): return lax.ppermute(value, 'y', [(i, i ^ m) for i in range(4)])  6.12 us
    ppermute x3, starting transfers between devices, program(): lax.ppermute(chip, 'x', [(i, i ^ m) for i in range(4)])  3.33 us
  transfers between devices with their start and end apart: 32, of which 16 were waited for; matrix products, arithmetic and copies ran while one was open for 0% of the time, Pallas kernels for 19%

profile of v4, /device:TPU:1, one launch (start us, length us, event | category | flops | bytes accessed | tf_op | source)
XLA Modules:
  0.0 151.4 jit_solution(14160824452654280094)
XLA Ops:
  0.0 0.1 stack.23.pos_ref
  0.1 2.4 %cut_near.1 = (f32[2,3,2,8,2304]{4,3,2,1,0:T(8,128)S(1)}, f32[2,3,2,8,2304]{4,3,2,1,0:T(8,128)S(1)}, f32[2,8,1280]{2,1,0:T(8,128)S(1)}, f32[8,128]{1,0:T(8,128)S(1)}) custom-call(s32[5]{0:T(128)S(1)} %stack.23.pos_ref, f32[2,3,2,8,9216]{4,3,2,1,0:T(8,128)} %o0.5, f32[2,8,9216]{2,1,0:T(8,128)} %pert0.1, f32[2,3]{1,0:T(2,128)} %wave.1, f32[2,3]{1,0:T(2,128)} %level.1, ...), custom_call_target="tpu_custom_call" | custom-call | tf_op jit(solution)/shard_map/cut_near/pallas_call | solution.py:126
  2.5 2.5 %collective-permute-start.1 = (f32[2,3,2,8,2304]{4,3,2,1,0:T(8,128)S(1)}, f32[2,3,2,8,2304]{4,3,2,1,0:T(8,128)S(1)}, u32[]{:S(2)}, u32[]{:S(2)}) collective-permute-start(f32[2,3,2,8,2304]{4,3,2,1,0:T(8,128)S(1)} %get-tuple-element.40.after), channel_id=1, source_target_pairs={{0,64},{64,0},{1,65},{65,1},{2,66},{66,2},{3,67},{67,3},{4,68},{68... | collective-permute-start | bytes 2654216 | tf_op jit(solution)/shard_map/ppermute | solution.py:28
  5.0 2.2 %collective-permute-start.3 = (f32[2,3,2,8,2304]{4,3,2,1,0:T(8,128)S(1)}, f32[2,3,2,8,2304]{4,3,2,1,0:T(8,128)S(1)}, u32[]{:S(2)}, u32[]{:S(2)}) collective-permute-start(f32[2,3,2,8,2304]{4,3,2,1,0:T(8,128)S(1)} %get-tuple-element.42), channel_id=1, source_target_pairs={{0,65},{64,1},{1,64},{65,0},{2,67},{66,3},{3,66},{67,2},{4,69},{68... | collective-permute-start | bytes 2654216 | tf_op jit(solution)/shard_map/ppermute | solution.py:28
  7.3 1.7 %cut_far.1 = (f32[2,3,2,8,2304]{4,3,2,1,0:T(8,128)S(1)}, f32[8,2304]{1,0:T(8,128)S(1)}) custom-call(s32[5]{0:T(128)S(1)} %stack.23.pos_ref, f32[2,3,2,8,9216]{4,3,2,1,0:T(8,128)} %o0.5, f32[8,9216]{1,0:T(8,128)} %pot.3, f32[2,3,2,8,2304]{4,3,2,1,0:T(8,128)S(1)} %get-tuple-element.40.after), custom_call_target="tpu_custom_call" | custom-call | tf_op jit(solution)/shard_map/cut_far/pallas_call | solution.py:153
  9.0 1.1 collective-permute-start.2
  10.1 2.1 %collective-permute-start = (f32[2,8,1280]{2,1,0:T(8,128)S(1)}, f32[2,8,1280]{2,1,0:T(8,128)S(1)}, u32[]{:S(2)}, u32[]{:S(2)}) collective-permute-start(f32[2,8,1280]{2,1,0:T(8,128)S(1)} %get-tuple-element.39), channel_id=1, source_target_pairs={{0,65},{64,1},{1,64},{65,0},{2,67},{66,3},{3,66},{67,2},{4,69},{68... | collective-permute-start | bytes 245768 | tf_op jit(solution)/shard_map/ppermute | solution.py:28
  12.2 33.8 %collective-permute-done.refs_0_.got = f32[2,8,1280]{2,1,0:T(8,128)S(1)} collective-permute-done((f32[2,8,1280]{2,1,0:T(8,128)S(1)}, f32[2,8,1280]{2,1,0:T(8,128)S(1)}, u32[]{:S(2)}, u32[]{:S(2)}) %collective-permute-start) | collective-permute-done | bytes 81952 | tf_op jit(solution)/shard_map/ppermute | solution.py:28
  46.0 3.0 %collective-permute-start.5 = (f32[2,8,1280]{2,1,0:T(8,128)S(1)}, f32[2,8,1280]{2,1,0:T(8,128)S(1)}, u32[]{:S(2)}, u32[]{:S(2)}) collective-permute-start(f32[2,8,1280]{2,1,0:T(8,128)S(1)} %collective-permute-done.refs_0_.got), channel_id=1, source_target_pairs={{0,8},{8,0},{1,9},{9,1},{2,10},{10,2},{3,11},{11,3},{4,12},{12,4},... | collective-permute-start | bytes 245768 | tf_op jit(solution)/shard_map/ppermute | solution.py:32
  49.0 0.2 convert_reduce_fusion.slot_ref
  49.2 1.7 %shard_map.83.refs_2_ = f32[80,128]{1,0:T(8,128)S(1)} custom-call(s32[5]{0:T(128)S(1)} %stack.23.pos_ref, s32[4]{0:T(128)S(1)} %convert_reduce_fusion.slot_ref, f32[2,3,2,8,9216]{4,3,2,1,0:T(8,128)S(1)} %copy-done, f32[2,3,2,8,2304]{4,3,2,1,0:T(8,128)S(1)} %collective-permute-done.1.o1, f32[2,8,9216]{2,1,0:T(8,128)S(1)} %copy-done.1), custom_call_target="tpu_custom_call" | custom-call | flops 20000000 | bytes 10000000 | tf_op jit(solution)/shard_map/pallas_call | solution.py:69
  51.0 1.7 %shard_map.84 = f32[80,128]{1,0:T(8,128)S(1)} custom-call(s32[5]{0:T(128)S(1)} %stack.23.pos_ref, s32[4]{0:T(128)S(1)} %convert_reduce_fusion.slot_ref, f32[2,3,2,8,2304]{4,3,2,1,0:T(8,128)S(1)} %collective-permute-done.2.o2.o0, f32[2,3,2,8,2304]{4,3,2,1,0:T(8,128)S(1)} %collective-permute-done.3.o3.o1, f32[2,8,1280]{2,1,0:T(8,128)S(1)} %collective-permute-done.refs_0_.got, ...), custom_call_target="tpu_custom_call" | custom-call | flops 20000000 | bytes 10000000 | tf_op jit(solution)/shard_map/pallas_call | solution.py:69
  52.7 2.3 %collective-permute-start.8 = (f32[80,128]{1,0:T(8,128)S(1)}, f32[80,128]{1,0:T(8,128)S(1)}, u32[]{:S(2)}, u32[]{:S(2)}) collective-permute-start(f32[80,128]{1,0:T(8,128)S(1)} %shard_map.84), channel_id=1, source_target_pairs={{0,65},{64,1},{1,64},{65,0},{2,67},{66,3},{3,66},{67,2},{4,69},{68... | collective-permute-start | bytes 122888 | tf_op jit(solution)/shard_map/ppermute | solution.py:28
  55.0 0.4 collective-permute-start.4
  55.4 0.9 collective-permute-start.7
  56.3 1.9 %collective-permute-start.6 = (f32[80,128]{1,0:T(8,128)S(1)}, f32[80,128]{1,0:T(8,128)S(1)}, u32[]{:S(2)}, u32[]{:S(2)}) collective-permute-start(f32[80,128]{1,0:T(8,128)S(1)} %shard_map.84), channel_id=1, source_target_pairs={{0,64},{64,0},{1,65},{65,1},{2,66},{66,2},{3,67},{67,3},{4,68},{68... | collective-permute-start | bytes 122888 | tf_op jit(solution)/shard_map/ppermute | solution.py:28
  58.3 2.1 %collective-permute-done.6 = f32[80,128]{1,0:T(8,128)S(1)} collective-permute-done((f32[80,128]{1,0:T(8,128)S(1)}, f32[80,128]{1,0:T(8,128)S(1)}, u32[]{:S(2)}, u32[]{:S(2)}) %collective-permute-start.6) | collective-permute-done | bytes 40992 | tf_op jit(solution)/shard_map/ppermute | solution.py:28
  60.4 2.8 %collective-permute-start.11 = (f32[80,128]{1,0:T(8,128)S(1)}, f32[80,128]{1,0:T(8,128)S(1)}, u32[]{:S(2)}, u32[]{:S(2)}) collective-permute-start(f32[80,128]{1,0:T(8,128)S(1)} %fusion.1.s0), channel_id=1, source_target_pairs={{0,6},{2,4},{4,2},{6,0},{1,7},{3,5},{5,3},{7,1},{8,14},{10,12},{12... | collective-permute-start | bytes 122888 | tf_op jit(solution)/shard_map/ppermute | solution.py:36
  63.2 0.3 collective-permute-start.10
  63.6 0.3 collective-permute-start.9
  63.9 2.0 %shard_map.82 = (f32[9216,128]{1,0:T(8,128)S(1)}, f32[384,128]{1,0:T(8,128)S(1)}) custom-call(s32[5]{0:T(128)S(1)} %stack.23.pos_ref, f32[2,3,2,8,9216]{4,3,2,1,0:T(8,128)S(1)} %copy-done, f32[2,3,2,8,2304]{4,3,2,1,0:T(8,128)S(1)} %collective-permute-done.1.o1, f32[2,3,2,8,2304]{4,3,2,1,0:T(8,128)S(1)} %collective-permute-done.2.o2.o0, ...), custom_call_target="tpu_custom_call" | custom-call | flops 10000000 | bytes 10000000 | tf_op jit(solution)/shard_map/pallas_call | solution.py:69
  65.9 1.6 %collective-permute-done.10.s2 = f32[80,128]{1,0:T(8,128)S(1)} collective-permute-done((f32[80,128]{1,0:T(8,128)S(1)}, f32[80,128]{1,0:T(8,128)S(1)}, u32[]{:S(2)}, u32[]{:S(2)}) %collective-permute-start.10) | collective-permute-done | bytes 40992 | tf_op jit(solution)/shard_map/ppermute | solution.py:36
  67.6 6.0 %shard_map.85 = (f32[24,28,32,128]{3,2,1,0:T(8,128)S(1)}, f32[1152,128]{1,0:T(8,128)S(1)}, f32[1152,128]{1,0:T(8,128)S(1)}, f32[768,128]{1,0:T(8,128)S(1)}, f32[768,128]{1,0:T(8,128)S(1)}) custom-call(s32[4]{0:T(128)S(1)} %convert_reduce_fusion.slot_ref, s32[5]{0:T(128)S(1)} %stack.23.pos_ref, f32[80,128]{1,0:T(8,128)S(1)} %fusion.1.s0, ...), custom_call_target="tpu_custom_call" | custom-call | flops 20000000 | bytes 10000000 | tf_op jit(solution)/shard_map/pallas_call | solution.py:69
  73.6 0.1 collective-permute-start.12
  73.7 1.7 %collective-permute-start.13 = (f32[1152,128]{1,0:T(8,128)S(1)}, f32[1152,128]{1,0:T(8,128)S(1)}, u32[]{:S(2)}, u32[]{:S(2)}) collective-permute-start(f32[1152,128]{1,0:T(8,128)S(1)} %get-tuple-element.53), channel_id=1, source_target_pairs={{0,6},{2,4},{4,2},{6,0},{1,7},{3,5},{5,3},{7,1},{8,14},{10,12},{12... | collective-permute-start | bytes 1769480 | tf_op jit(solution)/shard_map/ppermute | solution.py:36
  75.4 0.7 collective-permute-start.14
  76.1 0.9 collective-permute-start.15
  77.1 7.1 %shard_map.86.u_in = f32[9216,128]{1,0:T(8,128)S(1)} custom-call(f32[4,8]{1,0:T(4,128)S(1)} %pad_maximum_fusion.par_ref, f32[4]{0:T(128)S(1)} %convert_multiply_fusion.w_ref, f32[24,28,32,128]{3,2,1,0:T(8,128)S(1)} %get-tuple-element.50.refs_0_.refs_1_, f32[384,128]{1,0:T(8,128)S(1)} %get-tuple-element.51.refs_1_.refs_2_, bf16[256,256]{1,0:T(8,128)(2,1)S(1)} %copy-done.2), custom_call_target="tpu_custom_call" | custom-call | flops 60000000 | bytes 10000000 | tf_op jit(solution)/shard_map/pallas_call | solution.py:69
  84.2 0.1 collective-permute-done.15.yb_in
  84.3 1.4 collective-permute-done.12.za_in
  85.7 1.2 collective-permute-done.13.zb_in
  86.9 3.7 %shard_map.87 = (f32[24,28,32,128]{3,2,1,0:T(8,128)S(1)}, f32[1152,128]{1,0:T(8,128)S(1)}, f32[1152,128]{1,0:T(8,128)S(1)}, f32[768,128]{1,0:T(8,128)S(1)}, f32[768,128]{1,0:T(8,128)S(1)}) custom-call(f32[4,8]{1,0:T(4,128)S(1)} %pad_maximum_fusion.par_ref, f32[4]{0:T(128)S(1)} %convert_multiply_fusion.w_ref, s32[5]{0:T(128)S(1)} %stack.23.pos_ref, ...), custom_call_target="tpu_custom_call" | custom-call | flops 10000000 | bytes 10000000 | tf_op jit(solution)/shard_map/pallas_call | solution.py:69
  90.6 0.1 collective-permute-start.16
  90.7 1.3 collective-permute-start.17
  91.9 0.1 collective-permute-start.18
  92.0 1.5 collective-permute-start.19
  93.5 7.5 %shard_map.88.u_in = f32[9216,128]{1,0:T(8,128)S(1)} custom-call(f32[4,8]{1,0:T(4,128)S(1)} %pad_maximum_fusion.par_ref, f32[4]{0:T(128)S(1)} %convert_multiply_fusion.w_ref, f32[24,28,32,128]{3,2,1,0:T(8,128)S(1)} %get-tuple-element.56.refs_0_, f32[24,28,32,128]{3,2,1,0:T(8,128)S(1)} %get-tuple-element.50.refs_0_.refs_1_, ...), custom_call_target="tpu_custom_call" | custom-call | flops 60000000 | bytes 10000000 | tf_op jit(solution)/shard_map/pallas_call | solution.py:69
  101.0 0.7 collective-permute-done.16.za_in
  101.8 0.9 collective-permute-done.17.zb_in
  102.7 3.7 %shard_map.89 = (f32[24,28,32,128]{3,2,1,0:T(8,128)S(1)}, f32[1152,128]{1,0:T(8,128)S(1)}, f32[1152,128]{1,0:T(8,128)S(1)}, f32[768,128]{1,0:T(8,128)S(1)}, f32[768,128]{1,0:T(8,128)S(1)}) custom-call(f32[4,8]{1,0:T(4,128)S(1)} %pad_maximum_fusion.par_ref, f32[4]{0:T(128)S(1)} %convert_multiply_fusion.w_ref, s32[5]{0:T(128)S(1)} %stack.23.pos_ref, ...), custom_call_target="tpu_custom_call" | custom-call | flops 10000000 | bytes 10000000 | tf_op jit(solution)/shard_map/pallas_call | solution.py:69
  106.4 0.3 collective-permute-start.20
  106.7 0.9 collective-permute-start.21
  107.7 1.5 collective-permute-start.23
  109.1 8.3 %shard_map.90.d_in = f32[768,128]{1,0:T(8,128)S(1)} custom-call(f32[4,8]{1,0:T(4,128)S(1)} %pad_maximum_fusion.par_ref, f32[4]{0:T(128)S(1)} %convert_multiply_fusion.w_ref, f32[24,28,32,128]{3,2,1,0:T(8,128)S(1)} %get-tuple-element.61.refs_0_, f32[24,28,32,128]{3,2,1,0:T(8,128)S(1)} %get-tuple-element.50.refs_0_.refs_1_, ...), custom_call_target="tpu_custom_call" | custom-call | flops 60000000 | bytes 10000000 | tf_op jit(solution)/shard_map/pallas_call | solution.py:69
  117.5 0.1 collective-permute-done.21.zb
  117.6 2.6 %shard_map.91 = (f32[2,8,2304]{2,1,0:T(8,128)S(1)}, f32[2,8,2304]{2,1,0:T(8,128)S(1)}) custom-call(f32[4,8]{1,0:T(4,128)S(1)} %pad_maximum_fusion.par_ref, f32[4]{0:T(128)S(1)} %convert_multiply_fusion.w_ref, s32[5]{0:T(128)S(1)} %stack.23.pos_ref, f32[768,128]{1,0:T(8,128)S(1)} %shard_map.90.d_in, f32[1152,128]{1,0:T(8,128)S(1)} %collective-permute-done.20.za, ...), custom_call_target="tpu_custom_call" | custom-call | flops 10000000 | bytes 10000000 | tf_op jit(solution)/shard_map/pallas_call | solution.py:69
  120.3 6.3 %collective-permute-start.24 = (f32[2,8,2304]{2,1,0:T(8,128)S(1)}, f32[2,8,2304]{2,1,0:T(8,128)S(1)}, u32[]{:S(2)}, u32[]{:S(2)}) collective-permute-start(f32[2,8,2304]{2,1,0:T(8,128)S(1)} %get-tuple-element.68), channel_id=1, source_target_pairs={{0,8},{8,0},{1,9},{9,1},{2,10},{10,2},{3,11},{11,3},{4,12},{12,4},... | collective-permute-start | bytes 442376 | tf_op jit(solution)/shard_map/ppermute | solution.py:32
  126.6 1.0 collective-permute-done.24.b
  127.6 2.6 %collective-permute-start.27 = (f32[2,8,2304]{2,1,0:T(8,128)S(1)}, f32[2,8,2304]{2,1,0:T(8,128)S(1)}, u32[]{:S(2)}, u32[]{:S(2)}) collective-permute-start(f32[2,8,2304]{2,1,0:T(8,128)S(1)} %shard_map.92.s0), channel_id=1, source_target_pairs={{0,48},{16,32},{32,16},{48,0},{1,49},{17,33},{33,17},{49,1},{2,50}... | collective-permute-start | bytes 442376 | tf_op jit(solution)/shard_map/ppermute | solution.py:676
  130.2 0.5 collective-permute-start.26
  130.7 0.3 collective-permute-start.25
  130.9 5.3 %collective-permute-done.27.s3 = f32[2,8,2304]{2,1,0:T(8,128)S(1)} collective-permute-done((f32[2,8,2304]{2,1,0:T(8,128)S(1)}, f32[2,8,2304]{2,1,0:T(8,128)S(1)}, u32[]{:S(2)}, u32[]{:S(2)}) %collective-permute-start.27) | collective-permute-done | bytes 147488 | tf_op jit(solution)/shard_map/ppermute | solution.py:676
  136.3 0.3 collective-permute-done.26.s2
  136.5 1.0 collective-permute-done.25.s1
  137.5 0.6 shard_map.93
  138.1 0.6 collective-permute-start.28
  138.7 1.5 %collective-permute-start.30 = (f32[8,2304]{1,0:T(8,128)S(1)}, f32[8,2304]{1,0:T(8,128)S(1)}, u32[]{:S(2)}, u32[]{:S(2)}) collective-permute-start(f32[8,2304]{1,0:T(8,128)S(1)} %get-tuple-element.70), channel_id=1, source_target_pairs={{0,65},{64,1},{1,64},{65,0},{2,67},{66,3},{3,66},{67,2},{4,69},{68... | collective-permute-start | bytes 221192 | tf_op jit(solution)/shard_map/ppermute | solution.py:28
  140.2 1.2 collective-permute-start.29
  141.4 1.6 %collective-permute-done.30.t3 = f32[8,2304]{1,0:T(8,128)S(1)} collective-permute-done((f32[8,2304]{1,0:T(8,128)S(1)}, f32[8,2304]{1,0:T(8,128)S(1)}, u32[]{:S(2)}, u32[]{:S(2)}) %collective-permute-start.30) | collective-permute-done | bytes 73760 | tf_op jit(solution)/shard_map/ppermute | solution.py:28
  143.1 2.0 %collective-permute-done.29.t2 = f32[8,2304]{1,0:T(8,128)S(1)} collective-permute-done((f32[8,2304]{1,0:T(8,128)S(1)}, f32[8,2304]{1,0:T(8,128)S(1)}, u32[]{:S(2)}, u32[]{:S(2)}) %collective-permute-start.29) | collective-permute-done | bytes 73760 | tf_op jit(solution)/shard_map/ppermute | solution.py:28
  145.0 0.6 shard_map.94.mine
  145.6 3.2 %collective-permute-start.31 = (f32[8,9216]{1,0:T(8,128)S(1)}, f32[8,9216]{1,0:T(8,128)S(1)}, u32[]{:S(2)}, u32[]{:S(2)}) collective-permute-start(f32[8,9216]{1,0:T(8,128)S(1)} %shard_map.94.mine), channel_id=1, source_target_pairs={{0,8},{8,0},{1,9},{9,1},{2,10},{10,2},{3,11},{11,3},{4,12},{12,4},... | collective-permute-start | bytes 884744 | tf_op jit(solution)/shard_map/ppermute | solution.py:32
  148.8 1.2 collective-permute-done.31.other
  150.0 1.4 both_components.1
  (35 shorter events, 0.1 us)
Async XLA Ops:
  0.0 49.2 %copy-start = (f32[2,3,2,8,9216]{4,3,2,1,0:T(8,128)S(1)}, f32[2,3,2,8,9216]{4,3,2,1,0:T(8,128)}, u32[]{:S(2)}) copy-start(f32[2,3,2,8,9216]{4,3,2,1,0:T(8,128)} %o0.5) | copy-start | bytes 10616836
  0.1 49.1 %copy-start.1 = (f32[2,8,9216]{2,1,0:T(8,128)S(1)}, f32[2,8,9216]{2,1,0:T(8,128)}, u32[]{:S(2)}) copy-start(f32[2,8,9216]{2,1,0:T(8,128)} %pert0.1) | copy-start | bytes 1769476
  2.5 46.7 %collective-permute-start.1 = (f32[2,3,2,8,2304]{4,3,2,1,0:T(8,128)S(1)}, f32[2,3,2,8,2304]{4,3,2,1,0:T(8,128)S(1)}, u32[]{:S(2)}, u32[]{:S(2)}) collective-permute-start(f32[2,3,2,8,2304]{4,3,2,1,0:T(8,128)S(1)} %get-tuple-element.40.after), channel_id=1, source_target_pairs={{0,64},{64,0},{1,65},{65,1},{2,66},{66,2},{3,67},{67,3},{4,68},{68... | collective-permute-start | bytes 2654216 | tf_op jit(solution)/shard_map/ppermute | solution.py:28
  5.0 45.9 %collective-permute-start.3 = (f32[2,3,2,8,2304]{4,3,2,1,0:T(8,128)S(1)}, f32[2,3,2,8,2304]{4,3,2,1,0:T(8,128)S(1)}, u32[]{:S(2)}, u32[]{:S(2)}) collective-permute-start(f32[2,3,2,8,2304]{4,3,2,1,0:T(8,128)S(1)} %get-tuple-element.42), channel_id=1, source_target_pairs={{0,65},{64,1},{1,64},{65,0},{2,67},{66,3},{3,66},{67,2},{4,69},{68... | collective-permute-start | bytes 2654216 | tf_op jit(solution)/shard_map/ppermute | solution.py:28
  9.0 54.9 %copy-start.3 = (f32[8,9216]{1,0:T(8,128)S(1)}, f32[8,9216]{1,0:T(8,128)}, u32[]{:S(2)}) copy-start(f32[8,9216]{1,0:T(8,128)} %pot.3) | copy-start | bytes 884740
  9.0 42.0 %collective-permute-start.2 = (f32[2,3,2,8,2304]{4,3,2,1,0:T(8,128)S(1)}, f32[2,3,2,8,2304]{4,3,2,1,0:T(8,128)S(1)}, u32[]{:S(2)}, u32[]{:S(2)}) collective-permute-start(f32[2,3,2,8,2304]{4,3,2,1,0:T(8,128)S(1)} %get-tuple-element.41), channel_id=1, source_target_pairs={{0,1},{64,65},{1,0},{65,64},{2,3},{66,67},{3,2},{67,66},{4,5},{68,... | collective-permute-start | bytes 2654216 | tf_op jit(solution)/shard_map/ppermute | solution.py:28
  10.1 35.9 %collective-permute-start = (f32[2,8,1280]{2,1,0:T(8,128)S(1)}, f32[2,8,1280]{2,1,0:T(8,128)S(1)}, u32[]{:S(2)}, u32[]{:S(2)}) collective-permute-start(f32[2,8,1280]{2,1,0:T(8,128)S(1)} %get-tuple-element.39), channel_id=1, source_target_pairs={{0,65},{64,1},{1,64},{65,0},{2,67},{66,3},{3,66},{67,2},{4,69},{68... | collective-permute-start | bytes 245768 | tf_op jit(solution)/shard_map/ppermute | solution.py:28
  46.0 4.9 %collective-permute-start.5 = (f32[2,8,1280]{2,1,0:T(8,128)S(1)}, f32[2,8,1280]{2,1,0:T(8,128)S(1)}, u32[]{:S(2)}, u32[]{:S(2)}) collective-permute-start(f32[2,8,1280]{2,1,0:T(8,128)S(1)} %collective-permute-done.refs_0_.got), channel_id=1, source_target_pairs={{0,8},{8,0},{1,9},{9,1},{2,10},{10,2},{3,11},{11,3},{4,12},{12,4},... | collective-permute-start | bytes 245768 | tf_op jit(solution)/shard_map/ppermute | solution.py:32
  52.7 5.6 %collective-permute-start.8 = (f32[80,128]{1,0:T(8,128)S(1)}, f32[80,128]{1,0:T(8,128)S(1)}, u32[]{:S(2)}, u32[]{:S(2)}) collective-permute-start(f32[80,128]{1,0:T(8,128)S(1)} %shard_map.84), channel_id=1, source_target_pairs={{0,65},{64,1},{1,64},{65,0},{2,67},{66,3},{3,66},{67,2},{4,69},{68... | collective-permute-start | bytes 122888 | tf_op jit(solution)/shard_map/ppermute | solution.py:28
  55.0 8.9 %collective-permute-start.4 = (f32[8,2304]{1,0:T(8,128)S(1)}, f32[8,2304]{1,0:T(8,128)S(1)}, u32[]{:S(2)}, u32[]{:S(2)}) collective-permute-start(f32[8,2304]{1,0:T(8,128)S(1)} %get-tuple-element.43), channel_id=1, source_target_pairs={{0,65},{64,1},{1,64},{65,0},{2,67},{66,3},{3,66},{67,2},{4,69},{68... | collective-permute-start | bytes 221192 | tf_op jit(solution)/shard_map/ppermute | solution.py:28
  55.4 4.9 %collective-permute-start.7 = (f32[80,128]{1,0:T(8,128)S(1)}, f32[80,128]{1,0:T(8,128)S(1)}, u32[]{:S(2)}, u32[]{:S(2)}) collective-permute-start(f32[80,128]{1,0:T(8,128)S(1)} %shard_map.84), channel_id=1, source_target_pairs={{0,1},{64,65},{1,0},{65,64},{2,3},{66,67},{3,2},{67,66},{4,5},{68,... | collective-permute-start | bytes 122888 | tf_op jit(solution)/shard_map/ppermute | solution.py:28
  56.3 4.1 %collective-permute-start.6 = (f32[80,128]{1,0:T(8,128)S(1)}, f32[80,128]{1,0:T(8,128)S(1)}, u32[]{:S(2)}, u32[]{:S(2)}) collective-permute-start(f32[80,128]{1,0:T(8,128)S(1)} %shard_map.84), channel_id=1, source_target_pairs={{0,64},{64,0},{1,65},{65,1},{2,66},{66,2},{3,67},{67,3},{4,68},{68... | collective-permute-start | bytes 122888 | tf_op jit(solution)/shard_map/ppermute | solution.py:28
  60.4 5.5 %collective-permute-start.11 = (f32[80,128]{1,0:T(8,128)S(1)}, f32[80,128]{1,0:T(8,128)S(1)}, u32[]{:S(2)}, u32[]{:S(2)}) collective-permute-start(f32[80,128]{1,0:T(8,128)S(1)} %fusion.1.s0), channel_id=1, source_target_pairs={{0,6},{2,4},{4,2},{6,0},{1,7},{3,5},{5,3},{7,1},{8,14},{10,12},{12... | collective-permute-start | bytes 122888 | tf_op jit(solution)/shard_map/ppermute | solution.py:36
  63.2 4.4 %collective-permute-start.10 = (f32[80,128]{1,0:T(8,128)S(1)}, f32[80,128]{1,0:T(8,128)S(1)}, u32[]{:S(2)}, u32[]{:S(2)}) collective-permute-start(f32[80,128]{1,0:T(8,128)S(1)} %fusion.1.s0), channel_id=1, source_target_pairs={{0,4},{2,6},{4,0},{6,2},{1,5},{3,7},{5,1},{7,3},{8,12},{10,14},{12... | collective-permute-start | bytes 122888 | tf_op jit(solution)/shard_map/ppermute | solution.py:36
  63.6 4.0 %collective-permute-start.9 = (f32[80,128]{1,0:T(8,128)S(1)}, f32[80,128]{1,0:T(8,128)S(1)}, u32[]{:S(2)}, u32[]{:S(2)}) collective-permute-start(f32[80,128]{1,0:T(8,128)S(1)} %fusion.1.s0), channel_id=1, source_target_pairs={{0,2},{2,0},{4,6},{6,4},{1,3},{3,1},{5,7},{7,5},{8,10},{10,8},{12,... | collective-permute-start | bytes 122888 | tf_op jit(solution)/shard_map/ppermute | solution.py:36
  65.9 11.2 %copy-start.4 = (s32[4]{0:T(128)S(1)}, s32[4]{0:T(128)}, u32[]{:S(2)}) copy-start(s32[4]{0:T(128)} %param.14) | copy-start | bytes 52
  65.9 11.2 %copy-start.2 = (bf16[256,256]{1,0:T(8,128)(2,1)S(1)}, bf16[256,256]{1,0:T(8,128)(2,1)}, u32[]{:S(2)}) copy-start(bf16[256,256]{1,0:T(8,128)(2,1)} %constant.26.clone.refs_2_.refs_3_) | copy-start | bytes 393220
  73.6 12.1 %collective-permute-start.12 = (f32[1152,128]{1,0:T(8,128)S(1)}, f32[1152,128]{1,0:T(8,128)S(1)}, u32[]{:S(2)}, u32[]{:S(2)}) collective-permute-start(f32[1152,128]{1,0:T(8,128)S(1)} %get-tuple-element.52), channel_id=1, source_target_pairs={{0,2},{2,0},{4,6},{6,4},{1,3},{3,1},{5,7},{7,5},{8,10},{10,8},{12,... | collective-permute-start | bytes 1769480 | tf_op jit(solution)/shard_map/ppermute | solution.py:36
  73.7 13.2 %collective-permute-start.13 = (f32[1152,128]{1,0:T(8,128)S(1)}, f32[1152,128]{1,0:T(8,128)S(1)}, u32[]{:S(2)}, u32[]{:S(2)}) collective-permute-start(f32[1152,128]{1,0:T(8,128)S(1)} %get-tuple-element.53), channel_id=1, source_target_pairs={{0,6},{2,4},{4,2},{6,0},{1,7},{3,5},{5,3},{7,1},{8,14},{10,12},{12... | collective-permute-start | bytes 1769480 | tf_op jit(solution)/shard_map/ppermute | solution.py:36
  75.4 8.8 %collective-permute-start.14 = (f32[768,128]{1,0:T(8,128)S(1)}, f32[768,128]{1,0:T(8,128)S(1)}, u32[]{:S(2)}, u32[]{:S(2)}) collective-permute-start(f32[768,128]{1,0:T(8,128)S(1)} %get-tuple-element.54), channel_id=1, source_target_pairs={{0,64},{64,0},{1,65},{65,1},{2,66},{66,2},{3,67},{67,3},{4,68},{68... | collective-permute-start | bytes 1179656 | tf_op jit(solution)/shard_map/ppermute | solution.py:28
  76.1 8.1 %collective-permute-start.15 = (f32[768,128]{1,0:T(8,128)S(1)}, f32[768,128]{1,0:T(8,128)S(1)}, u32[]{:S(2)}, u32[]{:S(2)}) collective-permute-start(f32[768,128]{1,0:T(8,128)S(1)} %get-tuple-element.55), channel_id=1, source_target_pairs={{0,65},{64,1},{1,64},{65,0},{2,67},{66,3},{3,66},{67,2},{4,69},{68... | collective-permute-start | bytes 1179656 | tf_op jit(solution)/shard_map/ppermute | solution.py:28
  90.6 11.2 %collective-permute-start.16 = (f32[1152,128]{1,0:T(8,128)S(1)}, f32[1152,128]{1,0:T(8,128)S(1)}, u32[]{:S(2)}, u32[]{:S(2)}) collective-permute-start(f32[1152,128]{1,0:T(8,128)S(1)} %get-tuple-element.57), channel_id=1, source_target_pairs={{0,2},{2,0},{4,6},{6,4},{1,3},{3,1},{5,7},{7,5},{8,10},{10,8},{12,... | collective-permute-start | bytes 1769480 | tf_op jit(solution)/shard_map/ppermute | solution.py:36
  90.7 12.0 %collective-permute-start.17 = (f32[1152,128]{1,0:T(8,128)S(1)}, f32[1152,128]{1,0:T(8,128)S(1)}, u32[]{:S(2)}, u32[]{:S(2)}) collective-permute-start(f32[1152,128]{1,0:T(8,128)S(1)} %get-tuple-element.58), channel_id=1, source_target_pairs={{0,6},{2,4},{4,2},{6,0},{1,7},{3,5},{5,3},{7,1},{8,14},{10,12},{12... | collective-permute-start | bytes 1769480 | tf_op jit(solution)/shard_map/ppermute | solution.py:36
  91.9 9.1 %collective-permute-start.18 = (f32[768,128]{1,0:T(8,128)S(1)}, f32[768,128]{1,0:T(8,128)S(1)}, u32[]{:S(2)}, u32[]{:S(2)}) collective-permute-start(f32[768,128]{1,0:T(8,128)S(1)} %get-tuple-element.59), channel_id=1, source_target_pairs={{0,64},{64,0},{1,65},{65,1},{2,66},{66,2},{3,67},{67,3},{4,68},{68... | collective-permute-start | bytes 1179656 | tf_op jit(solution)/shard_map/ppermute | solution.py:28
  92.0 9.0 %collective-permute-start.19 = (f32[768,128]{1,0:T(8,128)S(1)}, f32[768,128]{1,0:T(8,128)S(1)}, u32[]{:S(2)}, u32[]{:S(2)}) collective-permute-start(f32[768,128]{1,0:T(8,128)S(1)} %get-tuple-element.60), channel_id=1, source_target_pairs={{0,65},{64,1},{1,64},{65,0},{2,67},{66,3},{3,66},{67,2},{4,69},{68... | collective-permute-start | bytes 1179656 | tf_op jit(solution)/shard_map/ppermute | solution.py:28
  106.4 11.1 %collective-permute-start.20 = (f32[1152,128]{1,0:T(8,128)S(1)}, f32[1152,128]{1,0:T(8,128)S(1)}, u32[]{:S(2)}, u32[]{:S(2)}) collective-permute-start(f32[1152,128]{1,0:T(8,128)S(1)} %get-tuple-element.63), channel_id=1, source_target_pairs={{0,2},{2,0},{4,6},{6,4},{1,3},{3,1},{5,7},{7,5},{8,10},{10,8},{12,... | collective-permute-start | bytes 1769480 | tf_op jit(solution)/shard_map/ppermute | solution.py:36
  106.7 10.9 %collective-permute-start.21 = (f32[1152,128]{1,0:T(8,128)S(1)}, f32[1152,128]{1,0:T(8,128)S(1)}, u32[]{:S(2)}, u32[]{:S(2)}) collective-permute-start(f32[1152,128]{1,0:T(8,128)S(1)} %get-tuple-element.64), channel_id=1, source_target_pairs={{0,6},{2,4},{4,2},{6,0},{1,7},{3,5},{5,3},{7,1},{8,14},{10,12},{12... | collective-permute-start | bytes 1769480 | tf_op jit(solution)/shard_map/ppermute | solution.py:36
  107.7 9.8 %collective-permute-start.22 = (f32[768,128]{1,0:T(8,128)S(1)}, f32[768,128]{1,0:T(8,128)S(1)}, u32[]{:S(2)}, u32[]{:S(2)}) collective-permute-start(f32[768,128]{1,0:T(8,128)S(1)} %get-tuple-element.65), channel_id=1, source_target_pairs={{0,64},{64,0},{1,65},{65,1},{2,66},{66,2},{3,67},{67,3},{4,68},{68... | collective-permute-start | bytes 1179656 | tf_op jit(solution)/shard_map/ppermute | solution.py:28
  107.7 9.8 %collective-permute-start.23 = (f32[768,128]{1,0:T(8,128)S(1)}, f32[768,128]{1,0:T(8,128)S(1)}, u32[]{:S(2)}, u32[]{:S(2)}) collective-permute-start(f32[768,128]{1,0:T(8,128)S(1)} %get-tuple-element.66), channel_id=1, source_target_pairs={{0,65},{64,1},{1,64},{65,0},{2,67},{66,3},{3,66},{67,2},{4,69},{68... | collective-permute-start | bytes 1179656 | tf_op jit(solution)/shard_map/ppermute | solution.py:28
  120.3 7.3 %collective-permute-start.24 = (f32[2,8,2304]{2,1,0:T(8,128)S(1)}, f32[2,8,2304]{2,1,0:T(8,128)S(1)}, u32[]{:S(2)}, u32[]{:S(2)}) collective-permute-start(f32[2,8,2304]{2,1,0:T(8,128)S(1)} %get-tuple-element.68), channel_id=1, source_target_pairs={{0,8},{8,0},{1,9},{9,1},{2,10},{10,2},{3,11},{11,3},{4,12},{12,4},... | collective-permute-start | bytes 442376 | tf_op jit(solution)/shard_map/ppermute | solution.py:32
  127.6 8.7 %collective-permute-start.27 = (f32[2,8,2304]{2,1,0:T(8,128)S(1)}, f32[2,8,2304]{2,1,0:T(8,128)S(1)}, u32[]{:S(2)}, u32[]{:S(2)}) collective-permute-start(f32[2,8,2304]{2,1,0:T(8,128)S(1)} %shard_map.92.s0), channel_id=1, source_target_pairs={{0,48},{16,32},{32,16},{48,0},{1,49},{17,33},{33,17},{49,1},{2,50}... | collective-permute-start | bytes 442376 | tf_op jit(solution)/shard_map/ppermute | solution.py:676
  130.2 6.4 %collective-permute-start.26 = (f32[2,8,2304]{2,1,0:T(8,128)S(1)}, f32[2,8,2304]{2,1,0:T(8,128)S(1)}, u32[]{:S(2)}, u32[]{:S(2)}) collective-permute-start(f32[2,8,2304]{2,1,0:T(8,128)S(1)} %shard_map.92.s0), channel_id=1, source_target_pairs={{0,32},{16,48},{32,0},{48,16},{1,33},{17,49},{33,1},{49,17},{2,34}... | collective-permute-start | bytes 442376 | tf_op jit(solution)/shard_map/ppermute | solution.py:676
  130.7 6.8 %collective-permute-start.25 = (f32[2,8,2304]{2,1,0:T(8,128)S(1)}, f32[2,8,2304]{2,1,0:T(8,128)S(1)}, u32[]{:S(2)}, u32[]{:S(2)}) collective-permute-start(f32[2,8,2304]{2,1,0:T(8,128)S(1)} %shard_map.92.s0), channel_id=1, source_target_pairs={{0,16},{16,0},{32,48},{48,32},{1,17},{17,1},{33,49},{49,33},{2,18}... | collective-permute-start | bytes 442376 | tf_op jit(solution)/shard_map/ppermute | solution.py:676
  138.1 3.3 %collective-permute-start.28 = (f32[8,2304]{1,0:T(8,128)S(1)}, f32[8,2304]{1,0:T(8,128)S(1)}, u32[]{:S(2)}, u32[]{:S(2)}) collective-permute-start(f32[8,2304]{1,0:T(8,128)S(1)} %get-tuple-element.69.t0), channel_id=1, source_target_pairs={{0,64},{64,0},{1,65},{65,1},{2,66},{66,2},{3,67},{67,3},{4,68},{68... | collective-permute-start | bytes 221192 | tf_op jit(solution)/shard_map/ppermute | solution.py:28
  138.7 4.4 %collective-permute-start.30 = (f32[8,2304]{1,0:T(8,128)S(1)}, f32[8,2304]{1,0:T(8,128)S(1)}, u32[]{:S(2)}, u32[]{:S(2)}) collective-permute-start(f32[8,2304]{1,0:T(8,128)S(1)} %get-tuple-element.70), channel_id=1, source_target_pairs={{0,65},{64,1},{1,64},{65,0},{2,67},{66,3},{3,66},{67,2},{4,69},{68... | collective-permute-start | bytes 221192 | tf_op jit(solution)/shard_map/ppermute | solution.py:28
  140.2 4.9 %collective-permute-start.29 = (f32[8,2304]{1,0:T(8,128)S(1)}, f32[8,2304]{1,0:T(8,128)S(1)}, u32[]{:S(2)}, u32[]{:S(2)}) collective-permute-start(f32[8,2304]{1,0:T(8,128)S(1)} %get-tuple-element.70), channel_id=1, source_target_pairs={{0,1},{64,65},{1,0},{65,64},{2,3},{66,67},{3,2},{67,66},{4,5},{68,... | collective-permute-start | bytes 221192 | tf_op jit(solution)/shard_map/ppermute | solution.py:28
  145.6 4.4 %collective-permute-start.31 = (f32[8,9216]{1,0:T(8,128)S(1)}, f32[8,9216]{1,0:T(8,128)S(1)}, u32[]{:S(2)}, u32[]{:S(2)}) collective-permute-start(f32[8,9216]{1,0:T(8,128)S(1)} %shard_map.94.mine), channel_id=1, source_target_pairs={{0,8},{8,0},{1,9},{9,1},{2,10},{10,2},{3,11},{11,3},{4,12},{12,4},... | collective-permute-start | bytes 884744 | tf_op jit(solution)/shard_map/ppermute | solution.py:32

commit v5 on v4

--- a/solution.py
+++ b/solution.py
@@ -91,13 +91,14 @@
     return ref.at[index]
 
 
-def cut_near_kernel(pos_ref, orb, pert, wave, level, partner, send3, send1, small, mine, wave_s, level_s, partner_s, sems):
+def cut_near_kernel(pos_ref, orb, pert, pot, wave, level, partner, send3, send1, small, mine, wave_s, level_s, partner_s, sems):
     z, core = pos_ref[1], pos_ref[3]
     moves = [
         (wave, wave_s),
         (level, level_s),
         (partner, partner_s),
-        (rows_of_chunk(pert, z ^ 3, core * HALF, HALF), small.at[:, :, pl.ds(0, HALF)]),
+        (rows_of_chunk(pert, z ^ 3, core * HALF, HALF), small.at[pl.ds(0, 2), :, pl.ds(0, HALF)]),
+        (rows_of_chunk(pot, z ^ 3, core * HALF, HALF), small.at[2, :, pl.ds(0, HALF)]),
         (rows_of_chunk(orb, z ^ 3), send3),
         (rows_of_chunk(orb, z ^ 1), send1),
     ]
@@ -115,50 +116,46 @@
         for j, value in enumerate(values):
             out = jnp.where((rows == k) & (cols == j), value, out)
     mine[...] = out
-    small[0, :, HALF:] = out
-    small[1, :, HALF:] = out
+    for i in range(3):
+        small[i, :, HALF:] = out
     for copy in copies[3:]:
         copy.wait()
 
 
-def cut_near(pos, orbitals, perturbation, wave, level, partner_map):
+def cut_near(pos, orbitals, perturbation, potential, wave, level, partner_map):
     chunk = orbitals.shape[:-1] + (CHUNK,)
     return pl.pallas_call(
         cut_near_kernel,
-        in_specs=[pl.BlockSpec(memory_space=pltpu.SMEM)] + [IN_HBM] * 5,
+        in_specs=[pl.BlockSpec(memory_space=pltpu.SMEM)] + [IN_HBM] * 6,
         out_specs=[pl.BlockSpec(memory_space=pltpu.VMEM)] * 4,
-        out_shape=[in_vmem(chunk), in_vmem(chunk), in_vmem((2, 8, HALF + 128)), in_vmem((8, 128))],
+        out_shape=[in_vmem(chunk), in_vmem(chunk), in_vmem((3, 8, HALF + 128)), in_vmem((8, 128))],
         scratch_shapes=[
             pltpu.SMEM((2, 3), F32),
             pltpu.SMEM((2, 3), F32),
             pltpu.SMEM((2,), jnp.int32),
-            pltpu.SemaphoreType.DMA((6,)),
+            pltpu.SemaphoreType.DMA((7,)),
         ],
         compiler_params=pltpu.CompilerParams(vmem_limit_bytes=4 * 2**20),
         name="cut_near",
-    )(pos, *[pltpu.with_memory_space_constraint(a, pltpu.HBM) for a in (orbitals, perturbation, wave, level, partner_map)])
-
-
-def cut_far_kernel(pos_ref, orb, pot, after, send2, pot_send, sems):
-    z = pos_ref[1]
-    moves = ((rows_of_chunk(orb, z ^ 2), send2), (rows_of_chunk(pot, z ^ 3), pot_send))
-    copies = [pltpu.make_async_copy(source, target, sems.at[i]) for i, (source, target) in enumerate(moves)]
-    for copy in copies:
-        copy.start()
-    for copy in copies:
-        copy.wait()
-
-
-def cut_far(pos, orbitals, potential, after):
+    )(pos, *[pltpu.with_memory_space_constraint(a, pltpu.HBM) for a in (orbitals, perturbation, potential, wave, level, partner_map)])
+
+
+def cut_far_kernel(pos_ref, orb, after, send2, sem):
+    copy = pltpu.make_async_copy(rows_of_chunk(orb, pos_ref[1] ^ 2), send2, sem)
+    copy.start()
+    copy.wait()
+
+
+def cut_far(pos, orbitals, after):
     return pl.pallas_call(
         cut_far_kernel,
-        in_specs=[pl.BlockSpec(memory_space=pltpu.SMEM), IN_HBM, IN_HBM, pl.BlockSpec(memory_space=pl.ANY)],
-        out_specs=[pl.BlockSpec(memory_space=pltpu.VMEM)] * 2,
-        out_shape=[in_vmem(orbitals.shape[:-1] + (CHUNK,)), in_vmem((8, CHUNK))],
-        scratch_shapes=[pltpu.SemaphoreType.DMA((2,))],
+        in_specs=[pl.BlockSpec(memory_space=pltpu.SMEM), IN_HBM, pl.BlockSpec(memory_space=pl.ANY)],
+        out_specs=pl.BlockSpec(memory_space=pltpu.VMEM),
+        out_shape=in_vmem(orbitals.shape[:-1] + (CHUNK,)),
+        scratch_shapes=[pltpu.SemaphoreType.DMA],
         compiler_params=pltpu.CompilerParams(vmem_limit_bytes=4 * 2**20),
         name="cut_far",
-    )(pos, *[pltpu.with_memory_space_constraint(a, pltpu.HBM) for a in (orbitals, potential)], after)
+    )(pos, pltpu.with_memory_space_constraint(orbitals, pltpu.HBM), after)
 
 
 def perturbed(field, pert_r, pert_i):
@@ -166,10 +163,11 @@
     return pert_r * re - pert_i * im, pert_r * im + pert_i * re
 
 
-def join_halves(pos_ref, got, swap, joined):
+def join_halves(pos_ref, got, swap, joined, fields):
     core = pos_ref[3]
-    joined[:, :, pl.ds(pl.multiple_of(core * HALF, 128), HALF)] = got[:, :, :HALF]
-    joined[:, :, pl.ds(pl.multiple_of((1 - core) * HALF, 128), HALF)] = swap[:, :, :HALF]
+    for to, i in enumerate(fields):
+        joined[to, :, pl.ds(pl.multiple_of(core * HALF, 128), HALF)] = got[i, :, :HALF]
+        joined[to, :, pl.ds(pl.multiple_of((1 - core) * HALF, 128), HALF)] = swap[i, :, :HALF]
 
 
 def products_kernel(near, pos_ref, slot_ref, o0, o1, *refs):
@@ -178,7 +176,7 @@
         base = pos_ref[1] * CHUNK
     else:
         got, swap, near_ref, out_ref, pert = refs
-        join_halves(pos_ref, got, swap, pert)
+        join_halves(pos_ref, got, swap, pert, (0, 1))
         base = 0
     pair, bases = (o0, o1), (base, 0)
     for k in range(4):
@@ -221,7 +219,7 @@
     )[0]
 
 
-TALL, DEEP = ROWS + 4, 32
+TALL, DEEP = ROWS + 4, 24
 FIELD = (24, TALL, DEEP, 128)
 ORBITALS = (24 * ROWS * 16, 128)
 
@@ -230,7 +228,9 @@
     return ((kn * 2 + c) * ROWS + r) * 16
 
 
-def orbital_rows_kernel(pos_ref, o0, o1, o2, o3, pot, pot1, orb_ref, v_ref):
+def orbital_rows_kernel(pos_ref, o0, o1, o2, o3, pot, got, swap, orb_ref, v_ref, joined):
+    join_halves(pos_ref, got, swap, joined, (2,))
+    pot1 = joined.at[0]
     lanes = lane_ids()
     half = pos_ref[0]
 
@@ -254,14 +254,14 @@
 
 
 def orbital_rows(pos, fields, pots):
-    return call(orbital_rows_kernel, (pos, *fields, *pots), [ORBITALS, (ROWS * 16, 128)], scalars=1)
+    return call(orbital_rows_kernel, (pos, *fields, *pots), [ORBITALS, (ROWS * 16, 128)], scratch=[pltpu.VMEM((1, 8, CHUNK), F32)], scalars=1)
 
 
 ZHALO, YHALO = (48 * ROWS, 128), (24 * 32, 128)
 
 
 def field_rows(kn, c, r, plane):
-    return ((kn * 2 + c) * TALL + r + 2) * DEEP + 8 + plane
+    return ((kn * 2 + c) * TALL + r + 2) * DEEP + 4 + plane
 
 
 def clear_margin(u_ref, kn):
@@ -269,8 +269,8 @@
         for r in (0, 1, TALL - 2, TALL - 1):
             u_ref[i, r] = jnp.zeros((DEEP, 128), F32)
         for r in range(2, TALL - 2):
-            u_ref[i, r, 0:8] = jnp.zeros((8, 128), F32)
-            u_ref[i, r, 24:32] = jnp.zeros((8, 128), F32)
+            u_ref[i, r, 0:4] = jnp.zeros((4, 128), F32)
+            u_ref[i, r, 20:24] = jnp.zeros((4, 128), F32)
 
 
 def near_face(parity, size):
@@ -293,7 +293,7 @@
             i = kn * 2 + c
             for p in range(2):
                 to = pl.ds(pl.multiple_of((i * 2 + p) * 16, 8), 16)
-                ref[to, :] = u_ref[i, 2 + first + p, 8:24, :]
+                ref[to, :] = u_ref[i, 2 + first + p, 4:20, :]
 
 
 def exchange(za, zb, ya, yb):
@@ -301,7 +301,7 @@
 
 
 def right_kernel(ncells, slot_ref, pos_ref, s0, s1, s2, s3, o0, o1, o2, o3, pert0, got, swap, r_ref, za, zb, ya, yb, prod_ref, pert1):
-    join_halves(pos_ref, got, swap, pert1)
+    join_halves(pos_ref, got, swap, pert1, (0, 1))
     total = (s0[...] + s1[...]) + (s2[...] + s3[...])
     ones = jnp.full((128, 128), 1.0, F32)
     prod_ref[...] = jnp.dot(total, ones, precision=lax.Precision.HIGHEST, preferred_element_type=F32) / ncells
@@ -337,7 +337,7 @@
                     for c in range(2):
                         rows = unpack_rows(*right[n][c], lanes)
                         for j in range(4):
-                            planes = pl.ds(pl.multiple_of(8 + 8 * z, 8), 8)
+                            planes = pl.ds(4 + 8 * z, 8)
                             r_ref[(k * 3 + n) * 2 + c, 2 + 4 * g + j, planes, :] = rows[j]
             return carry
 
@@ -397,7 +397,7 @@
         out_ref, *flats = refs
 
     def along_x(kn, g, flat):
-        cells = [u_ref[kn * 2 + c, 2 + 8 * g : 10 + 8 * g, 8:24, :].reshape(128, 128) for c in range(2)]
+        cells = [u_ref[kn * 2 + c, 2 + 8 * g : 10 + 8 * g, 4:20, :].reshape(128, 128) for c in range(2)]
         u2 = jnp.concatenate(cells, 0)
         hi = u2.astype(jnp.bfloat16)
         lo = (u2 - hi.astype(F32)).astype(jnp.bfloat16)
@@ -410,11 +410,11 @@
             for c in range(2):
                 i = kn * 2 + c
                 at = slice((c * 8 + r - 8 * g) * 16, (c * 8 + r - 8 * g + 1) * 16)
-                yp1, ym1 = u_ref[i, r + 3, 8:24, :], u_ref[i, r + 1, 8:24, :]
-                yp2, ym2 = u_ref[i, r + 4, 8:24, :], u_ref[i, r, 8:24, :]
-                zp1, zm1 = u_ref[i, r + 2, 9:25, :], u_ref[i, r + 2, 7:23, :]
-                zp2, zm2 = u_ref[i, r + 2, 10:26, :], u_ref[i, r + 2, 6:22, :]
-                cells.append(u_ref[i, r + 2, 8:24, :])
+                yp1, ym1 = u_ref[i, r + 3, 4:20, :], u_ref[i, r + 1, 4:20, :]
+                yp2, ym2 = u_ref[i, r + 4, 4:20, :], u_ref[i, r, 4:20, :]
+                zp1, zm1 = u_ref[i, r + 2, 5:21, :], u_ref[i, r + 2, 3:19, :]
+                zp2, zm2 = u_ref[i, r + 2, 6:22, :], u_ref[i, r + 2, 2:18, :]
+                cells.append(u_ref[i, r + 2, 4:20, :])
                 one = (yp1 + ym1) + (zp1 + zm1)
                 two = (yp2 + ym2) + (zp2 + zm2)
                 second.append(flat[at, 0:128] + (16.0 * one - two))
@@ -427,7 +427,7 @@
                 i = kn * 2 + c
                 value = center * cells[c] + lap * second[c]
                 if not first:
-                    value = value + wt * r_ref[i, r + 2, 8:24, :]
+                    value = value + wt * r_ref[i, r + 2, 4:20, :]
                 new.append(value - grad[1] if c == 0 else value + grad[0])
             if last:
                 orb_r = orb_ref[pl.ds(pl.multiple_of(rows_at(kn, 0, r), 16), 16), :]
@@ -514,7 +514,7 @@
         clear_margin(u_ref, kn)
         for c in range(2):
             for r in range(ROWS):
-                u_ref[kn * 2 + c, r + 2, 8:24, :] = u_in[pl.ds(pl.multiple_of(rows_at(kn, c, r), 16), 16), :]
+                u_ref[kn * 2 + c, r + 2, 4:20, :] = u_in[pl.ds(pl.multiple_of(rows_at(kn, c, r), 16), 16), :]
 
         def add_plane(p, term, which, place):
             for c in range(2):
@@ -526,7 +526,7 @@
 
         def add_row(r, term, which, place):
             for c in range(2):
-                u_ref[kn * 2 + c, r + 2, 8:24, :] = u_ref[kn * 2 + c, r + 2, 8:24, :] + term[c]
+                u_ref[kn * 2 + c, r + 2, 4:20, :] = u_ref[kn * 2 + c, r + 2, 4:20, :] + term[c]
 
         faces(count, par_ref, w_ref, pos_ref, kn, za_in, zb_in, ya_in, yb_in, add_plane, add_row)
         cut_rows(u_ref, pos_ref, kn, ya, yb)
@@ -640,13 +640,12 @@
     ncells = 64 * 4 * CHUNK
     matrix = jnp.asarray(x_matrix(), jnp.bfloat16)
 
-    send3, send1, small, mine = cut_near(pos, orbitals, perturbation, wave_vectors, levels, partner_map)
+    send3, send1, small, mine = cut_near(pos, orbitals, perturbation, potential, wave_vectors, levels, partner_map)
     got = z_xor(small, 3)
     o3 = z_xor(send3, 3)
     o1 = z_xor(send1, 1)
-    send2, pot_send = cut_far(pos, orbitals, potential, send1)
+    send2 = cut_far(pos, orbitals, send1)
     o2 = z_xor(send2, 2)
-    pot1 = z_xor(pot_send, 3)
     swap = other_core(got)
     par = jnp.concatenate([mine[:2, :8], got[0, :2, HALF : HALF + 8]], 0)
     slots = par[:, 6].astype(jnp.int32)
@@ -655,7 +654,7 @@
     fields, pert = [orbitals, o1, o2, o3], (perturbation, got, swap)
     part = products(pos, slots, orbitals, o1, perturbation)
     part = products(pos, slots, o2, o3, got, swap, part)
-    orb, pot = orbital_rows(pos, fields, (potential, pot1))
+    orb, pot = orbital_rows(pos, fields, (potential, got, swap))
 
     def swapped(value):
         return jnp.concatenate([value[40:], value[:40]], 0)

time: 152 us -> 152 us (level)
  waiting for transfers between devices: 54.5 us -> 62.7 us
  starting transfers between devices: 45.2 us -> 41.2 us
  Pallas kernels: 51 us -> 47.7 us
    ppermute x17 -> x16, waiting for transfers between devices: 39.6 us -> 45.8 us  [z_xor(): return lax.ppermute(value, ZAX, z_perm(lambda z: z ^ m))]
    pallas_call x13, Pallas kernels: 45.5 us -> 42.2 us  [call(): pl.pallas_call(kernel, in_specs=specs, out_specs=[pl.BlockSpec(memory_spa...]
    ppermute x17 -> x16, starting transfers between devices: 21.5 us -> 18.9 us  [z_xor(): return lax.ppermute(value, ZAX, z_perm(lambda z: z ^ m))]
    ppermute x9, waiting for transfers between devices: 6.12 us -> 8.13 us  [y_xor(): return lax.ppermute(value, 'y', [(i, i ^ m) for i in range(4)])]
  transfers between devices with their start and end apart: 32 -> 31, of which waited for: 16 -> 16; matrix products, arithmetic and copies ran while one was open for 0% -> 0% of each run, Pallas kernels for 19% -> 19%
where the time goes in v5:
time: 152 us
  waiting for transfers between devices  62.7 us (41%)
  Pallas kernels  47.7 us (31%)
  starting transfers between devices  41.2 us (27%)
    ppermute x16, waiting for transfers between devices, z_xor(): return lax.ppermute(value, ZAX, z_perm(lambda z: z ^ m))  45.8 us
    pallas_call x13, Pallas kernels, call(): pl.pallas_call(kernel, in_specs=specs, out_specs=[pl.BlockSpec(memory_spa...  42.2 us
    ppermute x16, starting transfers between devices, z_xor(): return lax.ppermute(value, ZAX, z_perm(lambda z: z ^ m))  18.9 us
    ppermute x3, starting transfers between devices, other_core(): return lax.ppermute(value, 'c', [(0, 1), (1, 0)])  11.2 us
    ppermute x9, waiting for transfers between devices, y_xor(): return lax.ppermute(value, 'y', [(i, i ^ m) for i in range(4)])  8.13 us
    ppermute x9, starting transfers between devices, y_xor(): return lax.ppermute(value, 'y', [(i, i ^ m) for i in range(4)])  7.82 us
    ppermute x3, waiting for transfers between devices, program(): lax.ppermute(chip, 'x', [(i, i ^ m) for i in range(4)])  6.54 us
    ppermute x3, starting transfers between devices, program(): lax.ppermute(chip, 'x', [(i, i ^ m) for i in range(4)])  3.33 us
  transfers between devices with their start and end apart: 31, of which 16 were waited for; matrix products, arithmetic and copies ran while one was open for 0% of the time, Pallas kernels for 19%

profile of v5, /device:TPU:1, one launch (start us, length us, event | category | flops | bytes accessed | tf_op | source)
XLA Modules:
  0.0 152.2 jit_solution(4777322393972140078)
XLA Ops:
  0.0 0.1 stack.23.pos_ref
  0.1 2.4 %cut_near.1 = (f32[2,3,2,8,2304]{4,3,2,1,0:T(8,128)S(1)}, f32[2,3,2,8,2304]{4,3,2,1,0:T(8,128)S(1)}, f32[3,8,1280]{2,1,0:T(8,128)S(1)}, f32[8,128]{1,0:T(8,128)S(1)}) custom-call(s32[5]{0:T(128)S(1)} %stack.23.pos_ref, f32[2,3,2,8,9216]{4,3,2,1,0:T(8,128)} %o0.5, f32[2,8,9216]{2,1,0:T(8,128)} %pert0.1, f32[8,9216]{1,0:T(8,128)} %pot.3, f32[2,3]{1,0:T(2,128)} %wave.1, ...), custom_call_target="tpu_custom_call" | custom-call | tf_op jit(solution)/shard_map/cut_near/pallas_call | solution.py:127
  2.5 2.5 %collective-permute-start.1 = (f32[2,3,2,8,2304]{4,3,2,1,0:T(8,128)S(1)}, f32[2,3,2,8,2304]{4,3,2,1,0:T(8,128)S(1)}, u32[]{:S(2)}, u32[]{:S(2)}) collective-permute-start(f32[2,3,2,8,2304]{4,3,2,1,0:T(8,128)S(1)} %get-tuple-element.38.after), channel_id=1, source_target_pairs={{0,64},{64,0},{1,65},{65,1},{2,66},{66,2},{3,67},{67,3},{4,68},{68... | collective-permute-start | bytes 2654216 | tf_op jit(solution)/shard_map/ppermute | solution.py:28
  5.0 1.7 %cut_far.1 = f32[2,3,2,8,2304]{4,3,2,1,0:T(8,128)S(1)} custom-call(s32[5]{0:T(128)S(1)} %stack.23.pos_ref, f32[2,3,2,8,9216]{4,3,2,1,0:T(8,128)} %o0.5, f32[2,3,2,8,2304]{4,3,2,1,0:T(8,128)S(1)} %get-tuple-element.38.after), custom_call_target="tpu_custom_call" | custom-call | tf_op jit(solution)/shard_map/cut_far/pallas_call | solution.py:150
  6.7 0.0 copy-start.3
  6.7 3.4 %collective-permute-start.2 = (f32[2,3,2,8,2304]{4,3,2,1,0:T(8,128)S(1)}, f32[2,3,2,8,2304]{4,3,2,1,0:T(8,128)S(1)}, u32[]{:S(2)}, u32[]{:S(2)}) collective-permute-start(f32[2,3,2,8,2304]{4,3,2,1,0:T(8,128)S(1)} %cut_far.1), channel_id=1, source_target_pairs={{0,1},{64,65},{1,0},{65,64},{2,3},{66,67},{3,2},{67,66},{4,5},{68,... | collective-permute-start | bytes 2654216 | tf_op jit(solution)/shard_map/ppermute | solution.py:28
  10.1 2.7 %collective-permute-start = (f32[3,8,1280]{2,1,0:T(8,128)S(1)}, f32[3,8,1280]{2,1,0:T(8,128)S(1)}, u32[]{:S(2)}, u32[]{:S(2)}) collective-permute-start(f32[3,8,1280]{2,1,0:T(8,128)S(1)} %get-tuple-element.37), channel_id=1, source_target_pairs={{0,65},{64,1},{1,64},{65,0},{2,67},{66,3},{3,66},{67,2},{4,69},{68... | collective-permute-start | bytes 368648 | tf_op jit(solution)/shard_map/ppermute | solution.py:28
  12.8 40.1 %collective-permute-done.got.refs_0_ = f32[3,8,1280]{2,1,0:T(8,128)S(1)} collective-permute-done((f32[3,8,1280]{2,1,0:T(8,128)S(1)}, f32[3,8,1280]{2,1,0:T(8,128)S(1)}, u32[]{:S(2)}, u32[]{:S(2)}) %collective-permute-start) | collective-permute-done | bytes 122912 | tf_op jit(solution)/shard_map/ppermute | solution.py:28
  52.9 2.1 %collective-permute-start.4 = (f32[3,8,1280]{2,1,0:T(8,128)S(1)}, f32[3,8,1280]{2,1,0:T(8,128)S(1)}, u32[]{:S(2)}, u32[]{:S(2)}) collective-permute-start(f32[3,8,1280]{2,1,0:T(8,128)S(1)} %collective-permute-done.got.refs_0_), channel_id=1, source_target_pairs={{0,8},{8,0},{1,9},{9,1},{2,10},{10,2},{3,11},{11,3},{4,12},{12,4},... | collective-permute-start | bytes 368648 | tf_op jit(solution)/shard_map/ppermute | solution.py:32
  55.0 0.2 convert_reduce_fusion.slot_ref
  55.2 1.7 %shard_map.83.refs_2_ = f32[80,128]{1,0:T(8,128)S(1)} custom-call(s32[5]{0:T(128)S(1)} %stack.23.pos_ref, s32[4]{0:T(128)S(1)} %convert_reduce_fusion.slot_ref, f32[2,3,2,8,9216]{4,3,2,1,0:T(8,128)S(1)} %copy-done, f32[2,3,2,8,2304]{4,3,2,1,0:T(8,128)S(1)} %collective-permute-done.1.o1, f32[2,8,9216]{2,1,0:T(8,128)S(1)} %copy-done.1), custom_call_target="tpu_custom_call" | custom-call | flops 20000000 | bytes 10000000 | tf_op jit(solution)/shard_map/pallas_call | solution.py:69
  57.0 1.7 %shard_map.84 = f32[80,128]{1,0:T(8,128)S(1)} custom-call(s32[5]{0:T(128)S(1)} %stack.23.pos_ref, s32[4]{0:T(128)S(1)} %convert_reduce_fusion.slot_ref, f32[2,3,2,8,2304]{4,3,2,1,0:T(8,128)S(1)} %collective-permute-done.2.o2.o0, f32[2,3,2,8,2304]{4,3,2,1,0:T(8,128)S(1)} %collective-permute-done.3.o3.o1, f32[3,8,1280]{2,1,0:T(8,128)S(1)} %collective-permute-done.got.refs_0_, ...), custom_call_target="tpu_custom_call" | custom-call | flops 20000000 | bytes 10000000 | tf_op jit(solution)/shard_map/pallas_call | solution.py:69
  58.7 0.1 collective-permute-start.7
  58.8 0.1 collective-permute-start.6
  58.9 3.1 %collective-permute-start.5 = (f32[80,128]{1,0:T(8,128)S(1)}, f32[80,128]{1,0:T(8,128)S(1)}, u32[]{:S(2)}, u32[]{:S(2)}) collective-permute-start(f32[80,128]{1,0:T(8,128)S(1)} %shard_map.84), channel_id=1, source_target_pairs={{0,64},{64,0},{1,65},{65,1},{2,66},{66,2},{3,67},{67,3},{4,68},{68... | collective-permute-start | bytes 122888 | tf_op jit(solution)/shard_map/ppermute | solution.py:28
  62.0 0.8 collective-permute-done.7
  62.8 1.4 collective-permute-done.5
  64.3 2.8 %collective-permute-start.10 = (f32[80,128]{1,0:T(8,128)S(1)}, f32[80,128]{1,0:T(8,128)S(1)}, u32[]{:S(2)}, u32[]{:S(2)}) collective-permute-start(f32[80,128]{1,0:T(8,128)S(1)} %fusion.1.s0), channel_id=1, source_target_pairs={{0,6},{2,4},{4,2},{6,0},{1,7},{3,5},{5,3},{7,1},{8,14},{10,12},{12... | collective-permute-start | bytes 122888 | tf_op jit(solution)/shard_map/ppermute | solution.py:36
  67.1 0.3 collective-permute-start.9
  67.4 0.3 collective-permute-start.8
  67.8 2.0 %shard_map.82 = (f32[9216,128]{1,0:T(8,128)S(1)}, f32[384,128]{1,0:T(8,128)S(1)}) custom-call(s32[5]{0:T(128)S(1)} %stack.23.pos_ref, f32[2,3,2,8,9216]{4,3,2,1,0:T(8,128)S(1)} %copy-done, f32[2,3,2,8,2304]{4,3,2,1,0:T(8,128)S(1)} %collective-permute-done.1.o1, f32[2,3,2,8,2304]{4,3,2,1,0:T(8,128)S(1)} %collective-permute-done.2.o2.o0, ...), custom_call_target="tpu_custom_call" | custom-call | flops 10000000 | bytes 10000000 | tf_op jit(solution)/shard_map/pallas_call | solution.py:69
  69.8 0.0 copy-start.4
  69.8 0.0 copy-start.2
  69.8 1.6 %collective-permute-done.9.s2 = f32[80,128]{1,0:T(8,128)S(1)} collective-permute-done((f32[80,128]{1,0:T(8,128)S(1)}, f32[80,128]{1,0:T(8,128)S(1)}, u32[]{:S(2)}, u32[]{:S(2)}) %collective-permute-start.9) | collective-permute-done | bytes 40992 | tf_op jit(solution)/shard_map/ppermute | solution.py:36
  71.4 5.3 %shard_map.85 = (f32[24,28,24,128]{3,2,1,0:T(8,128)S(1)}, f32[1152,128]{1,0:T(8,128)S(1)}, f32[1152,128]{1,0:T(8,128)S(1)}, f32[768,128]{1,0:T(8,128)S(1)}, f32[768,128]{1,0:T(8,128)S(1)}) custom-call(s32[4]{0:T(128)S(1)} %convert_reduce_fusion.slot_ref, s32[5]{0:T(128)S(1)} %stack.23.pos_ref, f32[80,128]{1,0:T(8,128)S(1)} %fusion.1.s0, ...), custom_call_target="tpu_custom_call" | custom-call | flops 20000000 | bytes 10000000 | tf_op jit(solution)/shard_map/pallas_call | solution.py:69
  76.8 0.1 collective-permute-start.11
  76.9 1.7 %collective-permute-start.12 = (f32[1152,128]{1,0:T(8,128)S(1)}, f32[1152,128]{1,0:T(8,128)S(1)}, u32[]{:S(2)}, u32[]{:S(2)}) collective-permute-start(f32[1152,128]{1,0:T(8,128)S(1)} %get-tuple-element.49), channel_id=1, source_target_pairs={{0,6},{2,4},{4,2},{6,0},{1,7},{3,5},{5,3},{7,1},{8,14},{10,12},{12... | collective-permute-start | bytes 1769480 | tf_op jit(solution)/shard_map/ppermute | solution.py:36
  78.6 0.6 collective-permute-start.13
  79.2 0.9 collective-permute-start.14
  80.1 7.2 %shard_map.86.u_in = f32[9216,128]{1,0:T(8,128)S(1)} custom-call(f32[4,8]{1,0:T(4,128)S(1)} %pad_maximum_fusion.par_ref, f32[4]{0:T(128)S(1)} %convert_multiply_fusion.w_ref, f32[24,28,24,128]{3,2,1,0:T(8,128)S(1)} %get-tuple-element.46.refs_0_.refs_1_, f32[384,128]{1,0:T(8,128)S(1)} %get-tuple-element.47.refs_1_.refs_2_, bf16[256,256]{1,0:T(8,128)(2,1)S(1)} %copy-done.2), custom_call_target="tpu_custom_call" | custom-call | flops 60000000 | bytes 10000000 | tf_op jit(solution)/shard_map/pallas_call | solution.py:69
  87.4 1.8 %collective-permute-done.11.za_in = f32[1152,128]{1,0:T(8,128)S(1)} collective-permute-done((f32[1152,128]{1,0:T(8,128)S(1)}, f32[1152,128]{1,0:T(8,128)S(1)}, u32[]{:S(2)}, u32[]{:S(2)}) %collective-permute-start.11) | collective-permute-done | bytes 589856 | tf_op jit(solution)/shard_map/ppermute | solution.py:36
  89.2 1.3 collective-permute-done.12.zb_in
  90.4 2.3 %shard_map.87 = (f32[24,28,24,128]{3,2,1,0:T(8,128)S(1)}, f32[1152,128]{1,0:T(8,128)S(1)}, f32[1152,128]{1,0:T(8,128)S(1)}, f32[768,128]{1,0:T(8,128)S(1)}, f32[768,128]{1,0:T(8,128)S(1)}) custom-call(f32[4,8]{1,0:T(4,128)S(1)} %pad_maximum_fusion.par_ref, f32[4]{0:T(128)S(1)} %convert_multiply_fusion.w_ref, s32[5]{0:T(128)S(1)} %stack.23.pos_ref, ...), custom_call_target="tpu_custom_call" | custom-call | flops 10000000 | bytes 10000000 | tf_op jit(solution)/shard_map/pallas_call | solution.py:69
  92.8 0.1 collective-permute-start.15
  92.8 1.2 collective-permute-start.16
  94.1 1.0 collective-permute-start.18
  95.1 7.5 %shard_map.88.u_in = f32[9216,128]{1,0:T(8,128)S(1)} custom-call(f32[4,8]{1,0:T(4,128)S(1)} %pad_maximum_fusion.par_ref, f32[4]{0:T(128)S(1)} %convert_multiply_fusion.w_ref, f32[24,28,24,128]{3,2,1,0:T(8,128)S(1)} %get-tuple-element.52.refs_0_, f32[24,28,24,128]{3,2,1,0:T(8,128)S(1)} %get-tuple-element.46.refs_0_.refs_1_, ...), custom_call_target="tpu_custom_call" | custom-call | flops 60000000 | bytes 10000000 | tf_op jit(solution)/shard_map/pallas_call | solution.py:69
  102.6 1.7 %collective-permute-done.15.za_in = f32[1152,128]{1,0:T(8,128)S(1)} collective-permute-done((f32[1152,128]{1,0:T(8,128)S(1)}, f32[1152,128]{1,0:T(8,128)S(1)}, u32[]{:S(2)}, u32[]{:S(2)}) %collective-permute-start.15) | collective-permute-done | bytes 589856 | tf_op jit(solution)/shard_map/ppermute | solution.py:36
  104.2 0.9 collective-permute-done.16.zb_in
  105.2 2.3 %shard_map.89 = (f32[24,28,24,128]{3,2,1,0:T(8,128)S(1)}, f32[1152,128]{1,0:T(8,128)S(1)}, f32[1152,128]{1,0:T(8,128)S(1)}, f32[768,128]{1,0:T(8,128)S(1)}, f32[768,128]{1,0:T(8,128)S(1)}) custom-call(f32[4,8]{1,0:T(4,128)S(1)} %pad_maximum_fusion.par_ref, f32[4]{0:T(128)S(1)} %convert_multiply_fusion.w_ref, s32[5]{0:T(128)S(1)} %stack.23.pos_ref, ...), custom_call_target="tpu_custom_call" | custom-call | flops 10000000 | bytes 10000000 | tf_op jit(solution)/shard_map/pallas_call | solution.py:69
  107.5 0.3 collective-permute-start.19
  107.8 0.8 collective-permute-start.20
  108.7 1.1 collective-permute-start.22
  109.8 8.4 %shard_map.90.d_in = f32[768,128]{1,0:T(8,128)S(1)} custom-call(f32[4,8]{1,0:T(4,128)S(1)} %pad_maximum_fusion.par_ref, f32[4]{0:T(128)S(1)} %convert_multiply_fusion.w_ref, f32[24,28,24,128]{3,2,1,0:T(8,128)S(1)} %get-tuple-element.57.refs_0_, f32[24,28,24,128]{3,2,1,0:T(8,128)S(1)} %get-tuple-element.46.refs_0_.refs_1_, ...), custom_call_target="tpu_custom_call" | custom-call | flops 60000000 | bytes 10000000 | tf_op jit(solution)/shard_map/pallas_call | solution.py:69
  118.3 0.8 collective-permute-done.20.zb
  119.1 2.6 %shard_map.91 = (f32[2,8,2304]{2,1,0:T(8,128)S(1)}, f32[2,8,2304]{2,1,0:T(8,128)S(1)}) custom-call(f32[4,8]{1,0:T(4,128)S(1)} %pad_maximum_fusion.par_ref, f32[4]{0:T(128)S(1)} %convert_multiply_fusion.w_ref, s32[5]{0:T(128)S(1)} %stack.23.pos_ref, f32[768,128]{1,0:T(8,128)S(1)} %shard_map.90.d_in, f32[1152,128]{1,0:T(8,128)S(1)} %collective-permute-done.19.za, ...), custom_call_target="tpu_custom_call" | custom-call | flops 10000000 | bytes 10000000 | tf_op jit(solution)/shard_map/pallas_call | solution.py:69
  121.7 5.8 %collective-permute-start.23 = (f32[2,8,2304]{2,1,0:T(8,128)S(1)}, f32[2,8,2304]{2,1,0:T(8,128)S(1)}, u32[]{:S(2)}, u32[]{:S(2)}) collective-permute-start(f32[2,8,2304]{2,1,0:T(8,128)S(1)} %get-tuple-element.64), channel_id=1, source_target_pairs={{0,8},{8,0},{1,9},{9,1},{2,10},{10,2},{3,11},{11,3},{4,12},{12,4},... | collective-permute-start | bytes 442376 | tf_op jit(solution)/shard_map/ppermute | solution.py:32
  127.5 1.0 collective-permute-done.23.b
  128.5 2.6 %collective-permute-start.26 = (f32[2,8,2304]{2,1,0:T(8,128)S(1)}, f32[2,8,2304]{2,1,0:T(8,128)S(1)}, u32[]{:S(2)}, u32[]{:S(2)}) collective-permute-start(f32[2,8,2304]{2,1,0:T(8,128)S(1)} %shard_map.92.s0), channel_id=1, source_target_pairs={{0,48},{16,32},{32,16},{48,0},{1,49},{17,33},{33,17},{49,1},{2,50}... | collective-permute-start | bytes 442376 | tf_op jit(solution)/shard_map/ppermute | solution.py:675
  131.1 0.5 collective-permute-start.25
  131.6 0.3 collective-permute-start.24
  131.9 5.3 %collective-permute-done.26.s3 = f32[2,8,2304]{2,1,0:T(8,128)S(1)} collective-permute-done((f32[2,8,2304]{2,1,0:T(8,128)S(1)}, f32[2,8,2304]{2,1,0:T(8,128)S(1)}, u32[]{:S(2)}, u32[]{:S(2)}) %collective-permute-start.26) | collective-permute-done | bytes 147488 | tf_op jit(solution)/shard_map/ppermute | solution.py:675
  137.2 0.3 collective-permute-done.25.s2
  137.4 1.0 collective-permute-done.24.s1
  138.4 0.6 shard_map.93
  139.0 0.3 collective-permute-start.27
  139.3 1.8 %collective-permute-start.29 = (f32[8,2304]{1,0:T(8,128)S(1)}, f32[8,2304]{1,0:T(8,128)S(1)}, u32[]{:S(2)}, u32[]{:S(2)}) collective-permute-start(f32[8,2304]{1,0:T(8,128)S(1)} %get-tuple-element.66), channel_id=1, source_target_pairs={{0,65},{64,1},{1,64},{65,0},{2,67},{66,3},{3,66},{67,2},{4,69},{68... | collective-permute-start | bytes 221192 | tf_op jit(solution)/shard_map/ppermute | solution.py:28
  141.0 1.3 collective-permute-start.28
  142.3 1.3 collective-permute-done.29.t3
  143.7 2.1 %collective-permute-done.28.t2 = f32[8,2304]{1,0:T(8,128)S(1)} collective-permute-done((f32[8,2304]{1,0:T(8,128)S(1)}, f32[8,2304]{1,0:T(8,128)S(1)}, u32[]{:S(2)}, u32[]{:S(2)}) %collective-permute-start.28) | collective-permute-done | bytes 73760 | tf_op jit(solution)/shard_map/ppermute | solution.py:28
  145.8 0.6 shard_map.94.mine
  146.4 3.3 %collective-permute-start.30 = (f32[8,9216]{1,0:T(8,128)S(1)}, f32[8,9216]{1,0:T(8,128)S(1)}, u32[]{:S(2)}, u32[]{:S(2)}) collective-permute-start(f32[8,9216]{1,0:T(8,128)S(1)} %shard_map.94.mine), channel_id=1, source_target_pairs={{0,8},{8,0},{1,9},{9,1},{2,10},{10,2},{3,11},{11,3},{4,12},{12,4},... | collective-permute-start | bytes 884744 | tf_op jit(solution)/shard_map/ppermute | solution.py:32
  149.6 1.2 collective-permute-done.30.other
  150.8 1.4 both_components.1
  (33 shorter events, 0.1 us)
Async XLA Ops:
  0.1 55.1 %copy-start = (f32[2,3,2,8,9216]{4,3,2,1,0:T(8,128)S(1)}, f32[2,3,2,8,9216]{4,3,2,1,0:T(8,128)}, u32[]{:S(2)}) copy-start(f32[2,3,2,8,9216]{4,3,2,1,0:T(8,128)} %o0.5) | copy-start | bytes 10616836
  0.1 55.1 %copy-start.1 = (f32[2,8,9216]{2,1,0:T(8,128)S(1)}, f32[2,8,9216]{2,1,0:T(8,128)}, u32[]{:S(2)}) copy-start(f32[2,8,9216]{2,1,0:T(8,128)} %pert0.1) | copy-start | bytes 1769476
  2.5 52.7 %collective-permute-start.1 = (f32[2,3,2,8,2304]{4,3,2,1,0:T(8,128)S(1)}, f32[2,3,2,8,2304]{4,3,2,1,0:T(8,128)S(1)}, u32[]{:S(2)}, u32[]{:S(2)}) collective-permute-start(f32[2,3,2,8,2304]{4,3,2,1,0:T(8,128)S(1)} %get-tuple-element.38.after), channel_id=1, source_target_pairs={{0,64},{64,0},{1,65},{65,1},{2,66},{66,2},{3,67},{67,3},{4,68},{68... | collective-permute-start | bytes 2654216 | tf_op jit(solution)/shard_map/ppermute | solution.py:28
  6.7 61.0 %copy-start.3 = (f32[8,9216]{1,0:T(8,128)S(1)}, f32[8,9216]{1,0:T(8,128)}, u32[]{:S(2)}) copy-start(f32[8,9216]{1,0:T(8,128)} %pot.3) | copy-start | bytes 884740
  6.7 50.2 %collective-permute-start.2 = (f32[2,3,2,8,2304]{4,3,2,1,0:T(8,128)S(1)}, f32[2,3,2,8,2304]{4,3,2,1,0:T(8,128)S(1)}, u32[]{:S(2)}, u32[]{:S(2)}) collective-permute-start(f32[2,3,2,8,2304]{4,3,2,1,0:T(8,128)S(1)} %cut_far.1), channel_id=1, source_target_pairs={{0,1},{64,65},{1,0},{65,64},{2,3},{66,67},{3,2},{67,66},{4,5},{68,... | collective-permute-start | bytes 2654216 | tf_op jit(solution)/shard_map/ppermute | solution.py:28
  10.1 46.8 %collective-permute-start.3 = (f32[2,3,2,8,2304]{4,3,2,1,0:T(8,128)S(1)}, f32[2,3,2,8,2304]{4,3,2,1,0:T(8,128)S(1)}, u32[]{:S(2)}, u32[]{:S(2)}) collective-permute-start(f32[2,3,2,8,2304]{4,3,2,1,0:T(8,128)S(1)} %get-tuple-element.39), channel_id=1, source_target_pairs={{0,65},{64,1},{1,64},{65,0},{2,67},{66,3},{3,66},{67,2},{4,69},{68... | collective-permute-start | bytes 2654216 | tf_op jit(solution)/shard_map/ppermute | solution.py:28
  10.1 42.8 %collective-permute-start = (f32[3,8,1280]{2,1,0:T(8,128)S(1)}, f32[3,8,1280]{2,1,0:T(8,128)S(1)}, u32[]{:S(2)}, u32[]{:S(2)}) collective-permute-start(f32[3,8,1280]{2,1,0:T(8,128)S(1)} %get-tuple-element.37), channel_id=1, source_target_pairs={{0,65},{64,1},{1,64},{65,0},{2,67},{66,3},{3,66},{67,2},{4,69},{68... | collective-permute-start | bytes 368648 | tf_op jit(solution)/shard_map/ppermute | solution.py:28
  52.9 4.0 %collective-permute-start.4 = (f32[3,8,1280]{2,1,0:T(8,128)S(1)}, f32[3,8,1280]{2,1,0:T(8,128)S(1)}, u32[]{:S(2)}, u32[]{:S(2)}) collective-permute-start(f32[3,8,1280]{2,1,0:T(8,128)S(1)} %collective-permute-done.got.refs_0_), channel_id=1, source_target_pairs={{0,8},{8,0},{1,9},{9,1},{2,10},{10,2},{3,11},{11,3},{4,12},{12,4},... | collective-permute-start | bytes 368648 | tf_op jit(solution)/shard_map/ppermute | solution.py:32
  58.7 4.2 %collective-permute-start.7 = (f32[80,128]{1,0:T(8,128)S(1)}, f32[80,128]{1,0:T(8,128)S(1)}, u32[]{:S(2)}, u32[]{:S(2)}) collective-permute-start(f32[80,128]{1,0:T(8,128)S(1)} %shard_map.84), channel_id=1, source_target_pairs={{0,65},{64,1},{1,64},{65,0},{2,67},{66,3},{3,66},{67,2},{4,69},{68... | collective-permute-start | bytes 122888 | tf_op jit(solution)/shard_map/ppermute | solution.py:28
  58.8 5.5 %collective-permute-start.6 = (f32[80,128]{1,0:T(8,128)S(1)}, f32[80,128]{1,0:T(8,128)S(1)}, u32[]{:S(2)}, u32[]{:S(2)}) collective-permute-start(f32[80,128]{1,0:T(8,128)S(1)} %shard_map.84), channel_id=1, source_target_pairs={{0,1},{64,65},{1,0},{65,64},{2,3},{66,67},{3,2},{67,66},{4,5},{68,... | collective-permute-start | bytes 122888 | tf_op jit(solution)/shard_map/ppermute | solution.py:28
  58.9 5.4 %collective-permute-start.5 = (f32[80,128]{1,0:T(8,128)S(1)}, f32[80,128]{1,0:T(8,128)S(1)}, u32[]{:S(2)}, u32[]{:S(2)}) collective-permute-start(f32[80,128]{1,0:T(8,128)S(1)} %shard_map.84), channel_id=1, source_target_pairs={{0,64},{64,0},{1,65},{65,1},{2,66},{66,2},{3,67},{67,3},{4,68},{68... | collective-permute-start | bytes 122888 | tf_op jit(solution)/shard_map/ppermute | solution.py:28
  64.3 5.5 %collective-permute-start.10 = (f32[80,128]{1,0:T(8,128)S(1)}, f32[80,128]{1,0:T(8,128)S(1)}, u32[]{:S(2)}, u32[]{:S(2)}) collective-permute-start(f32[80,128]{1,0:T(8,128)S(1)} %fusion.1.s0), channel_id=1, source_target_pairs={{0,6},{2,4},{4,2},{6,0},{1,7},{3,5},{5,3},{7,1},{8,14},{10,12},{12... | collective-permute-start | bytes 122888 | tf_op jit(solution)/shard_map/ppermute | solution.py:36
  67.1 4.4 %collective-permute-start.9 = (f32[80,128]{1,0:T(8,128)S(1)}, f32[80,128]{1,0:T(8,128)S(1)}, u32[]{:S(2)}, u32[]{:S(2)}) collective-permute-start(f32[80,128]{1,0:T(8,128)S(1)} %fusion.1.s0), channel_id=1, source_target_pairs={{0,4},{2,6},{4,0},{6,2},{1,5},{3,7},{5,1},{7,3},{8,12},{10,14},{12... | collective-permute-start | bytes 122888 | tf_op jit(solution)/shard_map/ppermute | solution.py:36
  67.4 4.0 %collective-permute-start.8 = (f32[80,128]{1,0:T(8,128)S(1)}, f32[80,128]{1,0:T(8,128)S(1)}, u32[]{:S(2)}, u32[]{:S(2)}) collective-permute-start(f32[80,128]{1,0:T(8,128)S(1)} %fusion.1.s0), channel_id=1, source_target_pairs={{0,2},{2,0},{4,6},{6,4},{1,3},{3,1},{5,7},{7,5},{8,10},{10,8},{12,... | collective-permute-start | bytes 122888 | tf_op jit(solution)/shard_map/ppermute | solution.py:36
  69.8 10.4 %copy-start.4 = (s32[4]{0:T(128)S(1)}, s32[4]{0:T(128)}, u32[]{:S(2)}) copy-start(s32[4]{0:T(128)} %param.14) | copy-start | bytes 52
  69.8 10.3 %copy-start.2 = (bf16[256,256]{1,0:T(8,128)(2,1)S(1)}, bf16[256,256]{1,0:T(8,128)(2,1)}, u32[]{:S(2)}) copy-start(bf16[256,256]{1,0:T(8,128)(2,1)} %constant.26.clone.refs_2_.refs_3_) | copy-start | bytes 393220
  76.8 12.4 %collective-permute-start.11 = (f32[1152,128]{1,0:T(8,128)S(1)}, f32[1152,128]{1,0:T(8,128)S(1)}, u32[]{:S(2)}, u32[]{:S(2)}) collective-permute-start(f32[1152,128]{1,0:T(8,128)S(1)} %get-tuple-element.48), channel_id=1, source_target_pairs={{0,2},{2,0},{4,6},{6,4},{1,3},{3,1},{5,7},{7,5},{8,10},{10,8},{12,... | collective-permute-start | bytes 1769480 | tf_op jit(solution)/shard_map/ppermute | solution.py:36
  76.9 13.6 %collective-permute-start.12 = (f32[1152,128]{1,0:T(8,128)S(1)}, f32[1152,128]{1,0:T(8,128)S(1)}, u32[]{:S(2)}, u32[]{:S(2)}) collective-permute-start(f32[1152,128]{1,0:T(8,128)S(1)} %get-tuple-element.49), channel_id=1, source_target_pairs={{0,6},{2,4},{4,2},{6,0},{1,7},{3,5},{5,3},{7,1},{8,14},{10,12},{12... | collective-permute-start | bytes 1769480 | tf_op jit(solution)/shard_map/ppermute | solution.py:36
  78.6 8.7 %collective-permute-start.13 = (f32[768,128]{1,0:T(8,128)S(1)}, f32[768,128]{1,0:T(8,128)S(1)}, u32[]{:S(2)}, u32[]{:S(2)}) collective-permute-start(f32[768,128]{1,0:T(8,128)S(1)} %get-tuple-element.50), channel_id=1, source_target_pairs={{0,64},{64,0},{1,65},{65,1},{2,66},{66,2},{3,67},{67,3},{4,68},{68... | collective-permute-start | bytes 1179656 | tf_op jit(solution)/shard_map/ppermute | solution.py:28
  79.2 8.1 %collective-permute-start.14 = (f32[768,128]{1,0:T(8,128)S(1)}, f32[768,128]{1,0:T(8,128)S(1)}, u32[]{:S(2)}, u32[]{:S(2)}) collective-permute-start(f32[768,128]{1,0:T(8,128)S(1)} %get-tuple-element.51), channel_id=1, source_target_pairs={{0,65},{64,1},{1,64},{65,0},{2,67},{66,3},{3,66},{67,2},{4,69},{68... | collective-permute-start | bytes 1179656 | tf_op jit(solution)/shard_map/ppermute | solution.py:28
  92.8 11.5 %collective-permute-start.15 = (f32[1152,128]{1,0:T(8,128)S(1)}, f32[1152,128]{1,0:T(8,128)S(1)}, u32[]{:S(2)}, u32[]{:S(2)}) collective-permute-start(f32[1152,128]{1,0:T(8,128)S(1)} %get-tuple-element.53), channel_id=1, source_target_pairs={{0,2},{2,0},{4,6},{6,4},{1,3},{3,1},{5,7},{7,5},{8,10},{10,8},{12,... | collective-permute-start | bytes 1769480 | tf_op jit(solution)/shard_map/ppermute | solution.py:36
  92.8 12.3 %collective-permute-start.16 = (f32[1152,128]{1,0:T(8,128)S(1)}, f32[1152,128]{1,0:T(8,128)S(1)}, u32[]{:S(2)}, u32[]{:S(2)}) collective-permute-start(f32[1152,128]{1,0:T(8,128)S(1)} %get-tuple-element.54), channel_id=1, source_target_pairs={{0,6},{2,4},{4,2},{6,0},{1,7},{3,5},{5,3},{7,1},{8,14},{10,12},{12... | collective-permute-start | bytes 1769480 | tf_op jit(solution)/shard_map/ppermute | solution.py:36
  94.1 8.5 %collective-permute-start.17 = (f32[768,128]{1,0:T(8,128)S(1)}, f32[768,128]{1,0:T(8,128)S(1)}, u32[]{:S(2)}, u32[]{:S(2)}) collective-permute-start(f32[768,128]{1,0:T(8,128)S(1)} %get-tuple-element.55), channel_id=1, source_target_pairs={{0,64},{64,0},{1,65},{65,1},{2,66},{66,2},{3,67},{67,3},{4,68},{68... | collective-permute-start | bytes 1179656 | tf_op jit(solution)/shard_map/ppermute | solution.py:28
  94.1 8.5 %collective-permute-start.18 = (f32[768,128]{1,0:T(8,128)S(1)}, f32[768,128]{1,0:T(8,128)S(1)}, u32[]{:S(2)}, u32[]{:S(2)}) collective-permute-start(f32[768,128]{1,0:T(8,128)S(1)} %get-tuple-element.56), channel_id=1, source_target_pairs={{0,65},{64,1},{1,64},{65,0},{2,67},{66,3},{3,66},{67,2},{4,69},{68... | collective-permute-start | bytes 1179656 | tf_op jit(solution)/shard_map/ppermute | solution.py:28
  107.5 10.8 %collective-permute-start.19 = (f32[1152,128]{1,0:T(8,128)S(1)}, f32[1152,128]{1,0:T(8,128)S(1)}, u32[]{:S(2)}, u32[]{:S(2)}) collective-permute-start(f32[1152,128]{1,0:T(8,128)S(1)} %get-tuple-element.59), channel_id=1, source_target_pairs={{0,2},{2,0},{4,6},{6,4},{1,3},{3,1},{5,7},{7,5},{8,10},{10,8},{12,... | collective-permute-start | bytes 1769480 | tf_op jit(solution)/shard_map/ppermute | solution.py:36
  107.8 11.2 %collective-permute-start.20 = (f32[1152,128]{1,0:T(8,128)S(1)}, f32[1152,128]{1,0:T(8,128)S(1)}, u32[]{:S(2)}, u32[]{:S(2)}) collective-permute-start(f32[1152,128]{1,0:T(8,128)S(1)} %get-tuple-element.60), channel_id=1, source_target_pairs={{0,6},{2,4},{4,2},{6,0},{1,7},{3,5},{5,3},{7,1},{8,14},{10,12},{12... | collective-permute-start | bytes 1769480 | tf_op jit(solution)/shard_map/ppermute | solution.py:36
  108.7 9.6 %collective-permute-start.21 = (f32[768,128]{1,0:T(8,128)S(1)}, f32[768,128]{1,0:T(8,128)S(1)}, u32[]{:S(2)}, u32[]{:S(2)}) collective-permute-start(f32[768,128]{1,0:T(8,128)S(1)} %get-tuple-element.61), channel_id=1, source_target_pairs={{0,64},{64,0},{1,65},{65,1},{2,66},{66,2},{3,67},{67,3},{4,68},{68... | collective-permute-start | bytes 1179656 | tf_op jit(solution)/shard_map/ppermute | solution.py:28
  108.7 9.6 %collective-permute-start.22 = (f32[768,128]{1,0:T(8,128)S(1)}, f32[768,128]{1,0:T(8,128)S(1)}, u32[]{:S(2)}, u32[]{:S(2)}) collective-permute-start(f32[768,128]{1,0:T(8,128)S(1)} %get-tuple-element.62), channel_id=1, source_target_pairs={{0,65},{64,1},{1,64},{65,0},{2,67},{66,3},{3,66},{67,2},{4,69},{68... | collective-permute-start | bytes 1179656 | tf_op jit(solution)/shard_map/ppermute | solution.py:28
  121.7 6.8 %collective-permute-start.23 = (f32[2,8,2304]{2,1,0:T(8,128)S(1)}, f32[2,8,2304]{2,1,0:T(8,128)S(1)}, u32[]{:S(2)}, u32[]{:S(2)}) collective-permute-start(f32[2,8,2304]{2,1,0:T(8,128)S(1)} %get-tuple-element.64), channel_id=1, source_target_pairs={{0,8},{8,0},{1,9},{9,1},{2,10},{10,2},{3,11},{11,3},{4,12},{12,4},... | collective-permute-start | bytes 442376 | tf_op jit(solution)/shard_map/ppermute | solution.py:32
  128.5 8.7 %collective-permute-start.26 = (f32[2,8,2304]{2,1,0:T(8,128)S(1)}, f32[2,8,2304]{2,1,0:T(8,128)S(1)}, u32[]{:S(2)}, u32[]{:S(2)}) collective-permute-start(f32[2,8,2304]{2,1,0:T(8,128)S(1)} %shard_map.92.s0), channel_id=1, source_target_pairs={{0,48},{16,32},{32,16},{48,0},{1,49},{17,33},{33,17},{49,1},{2,50}... | collective-permute-start | bytes 442376 | tf_op jit(solution)/shard_map/ppermute | solution.py:675
  131.1 6.4 %collective-permute-start.25 = (f32[2,8,2304]{2,1,0:T(8,128)S(1)}, f32[2,8,2304]{2,1,0:T(8,128)S(1)}, u32[]{:S(2)}, u32[]{:S(2)}) collective-permute-start(f32[2,8,2304]{2,1,0:T(8,128)S(1)} %shard_map.92.s0), channel_id=1, source_target_pairs={{0,32},{16,48},{32,0},{48,16},{1,33},{17,49},{33,1},{49,17},{2,34}... | collective-permute-start | bytes 442376 | tf_op jit(solution)/shard_map/ppermute | solution.py:675
  131.6 6.8 %collective-permute-start.24 = (f32[2,8,2304]{2,1,0:T(8,128)S(1)}, f32[2,8,2304]{2,1,0:T(8,128)S(1)}, u32[]{:S(2)}, u32[]{:S(2)}) collective-permute-start(f32[2,8,2304]{2,1,0:T(8,128)S(1)} %shard_map.92.s0), channel_id=1, source_target_pairs={{0,16},{16,0},{32,48},{48,32},{1,17},{17,1},{33,49},{49,33},{2,18}... | collective-permute-start | bytes 442376 | tf_op jit(solution)/shard_map/ppermute | solution.py:675
  139.0 3.3 %collective-permute-start.27 = (f32[8,2304]{1,0:T(8,128)S(1)}, f32[8,2304]{1,0:T(8,128)S(1)}, u32[]{:S(2)}, u32[]{:S(2)}) collective-permute-start(f32[8,2304]{1,0:T(8,128)S(1)} %get-tuple-element.65.t0), channel_id=1, source_target_pairs={{0,64},{64,0},{1,65},{65,1},{2,66},{66,2},{3,67},{67,3},{4,68},{68... | collective-permute-start | bytes 221192 | tf_op jit(solution)/shard_map/ppermute | solution.py:28
  139.3 4.4 %collective-permute-start.29 = (f32[8,2304]{1,0:T(8,128)S(1)}, f32[8,2304]{1,0:T(8,128)S(1)}, u32[]{:S(2)}, u32[]{:S(2)}) collective-permute-start(f32[8,2304]{1,0:T(8,128)S(1)} %get-tuple-element.66), channel_id=1, source_target_pairs={{0,65},{64,1},{1,64},{65,0},{2,67},{66,3},{3,66},{67,2},{4,69},{68... | collective-permute-start | bytes 221192 | tf_op jit(solution)/shard_map/ppermute | solution.py:28
  141.0 4.8 %collective-permute-start.28 = (f32[8,2304]{1,0:T(8,128)S(1)}, f32[8,2304]{1,0:T(8,128)S(1)}, u32[]{:S(2)}, u32[]{:S(2)}) collective-permute-start(f32[8,2304]{1,0:T(8,128)S(1)} %get-tuple-element.66), channel_id=1, source_target_pairs={{0,1},{64,65},{1,0},{65,64},{2,3},{66,67},{3,2},{67,66},{4,5},{68,... | collective-permute-start | bytes 221192 | tf_op jit(solution)/shard_map/ppermute | solution.py:28
  146.4 4.5 %collective-permute-start.30 = (f32[8,9216]{1,0:T(8,128)S(1)}, f32[8,9216]{1,0:T(8,128)S(1)}, u32[]{:S(2)}, u32[]{:S(2)}) collective-permute-start(f32[8,9216]{1,0:T(8,128)S(1)} %shard_map.94.mine), channel_id=1, source_target_pairs={{0,8},{8,0},{1,9},{9,1},{2,10},{10,2},{3,11},{11,3},{4,12},{12,4},... | collective-permute-start | bytes 884744 | tf_op jit(solution)/shard_map/ppermute | solution.py:32

commit v6 on v5

--- a/solution.py
+++ b/solution.py
@@ -30,6 +30,10 @@
 
 def other_core(value):
     return lax.ppermute(value, "c", [(0, 1), (1, 0)])
+
+
+def x_xor(value, m):
+    return lax.ppermute(value, "x", [(i, i ^ m) for i in range(4)])
 
 
 def y_xor(value, m):
@@ -91,20 +95,25 @@
     return ref.at[index]
 
 
-def cut_near_kernel(pos_ref, orb, pert, pot, wave, level, partner, send3, send1, small, mine, wave_s, level_s, partner_s, sems):
+def cut_kernel(pos_ref, orb, pert, pot, wave, level, partner, send3, send1, send2, small, mine, wave_s, level_s, partner_s, sems):
     z, core = pos_ref[1], pos_ref[3]
     moves = [
         (wave, wave_s),
         (level, level_s),
         (partner, partner_s),
-        (rows_of_chunk(pert, z ^ 3, core * HALF, HALF), small.at[pl.ds(0, 2), :, pl.ds(0, HALF)]),
-        (rows_of_chunk(pot, z ^ 3, core * HALF, HALF), small.at[2, :, pl.ds(0, HALF)]),
         (rows_of_chunk(orb, z ^ 3), send3),
         (rows_of_chunk(orb, z ^ 1), send1),
+        (rows_of_chunk(orb, z ^ 2), send2),
     ]
     copies = [pltpu.make_async_copy(source, target, sems.at[i]) for i, (source, target) in enumerate(moves)]
     for copy in copies:
         copy.start()
+    field = small.at[:, pl.ds(0, HALF)]
+    of_pert = rows_of_chunk(pert, z ^ 3, core * HALF, HALF).at[jnp.minimum(pos_ref[2], 1)]
+    pert_copy = pltpu.make_async_copy(of_pert, field, sems.at[6])
+    pot_copy = pltpu.make_async_copy(rows_of_chunk(pot, z ^ 3, core * HALF, HALF), field, sems.at[6])
+    pl.when(pos_ref[2] < 2)(pert_copy.start)
+    pl.when(pos_ref[2] >= 2)(pot_copy.start)
     rows = lax.broadcasted_iota(jnp.int32, (8, 128), 0)
     cols = lax.broadcasted_iota(jnp.int32, (8, 128), 1)
     out = jnp.zeros((8, 128), F32)
@@ -116,19 +125,19 @@
         for j, value in enumerate(values):
             out = jnp.where((rows == k) & (cols == j), value, out)
     mine[...] = out
-    for i in range(3):
-        small[i, :, HALF:] = out
+    small[:, HALF:] = out
+    pot_copy.wait()
     for copy in copies[3:]:
         copy.wait()
 
 
-def cut_near(pos, orbitals, perturbation, potential, wave, level, partner_map):
+def cut(pos, orbitals, perturbation, potential, wave, level, partner_map):
     chunk = orbitals.shape[:-1] + (CHUNK,)
     return pl.pallas_call(
-        cut_near_kernel,
+        cut_kernel,
         in_specs=[pl.BlockSpec(memory_space=pltpu.SMEM)] + [IN_HBM] * 6,
-        out_specs=[pl.BlockSpec(memory_space=pltpu.VMEM)] * 4,
-        out_shape=[in_vmem(chunk), in_vmem(chunk), in_vmem((3, 8, HALF + 128)), in_vmem((8, 128))],
+        out_specs=[pl.BlockSpec(memory_space=pltpu.VMEM)] * 5,
+        out_shape=[in_vmem(chunk)] * 3 + [in_vmem((8, HALF + 128)), in_vmem((8, 128))],
         scratch_shapes=[
             pltpu.SMEM((2, 3), F32),
             pltpu.SMEM((2, 3), F32),
@@ -136,26 +145,8 @@
             pltpu.SemaphoreType.DMA((7,)),
         ],
         compiler_params=pltpu.CompilerParams(vmem_limit_bytes=4 * 2**20),
-        name="cut_near",
+        name="cut",
     )(pos, *[pltpu.with_memory_space_constraint(a, pltpu.HBM) for a in (orbitals, perturbation, potential, wave, level, partner_map)])
-
-
-def cut_far_kernel(pos_ref, orb, after, send2, sem):
-    copy = pltpu.make_async_copy(rows_of_chunk(orb, pos_ref[1] ^ 2), send2, sem)
-    copy.start()
-    copy.wait()
-
-
-def cut_far(pos, orbitals, after):
-    return pl.pallas_call(
-        cut_far_kernel,
-        in_specs=[pl.BlockSpec(memory_space=pltpu.SMEM), IN_HBM, pl.BlockSpec(memory_space=pl.ANY)],
-        out_specs=pl.BlockSpec(memory_space=pltpu.VMEM),
-        out_shape=in_vmem(orbitals.shape[:-1] + (CHUNK,)),
-        scratch_shapes=[pltpu.SemaphoreType.DMA],
-        compiler_params=pltpu.CompilerParams(vmem_limit_bytes=4 * 2**20),
-        name="cut_far",
-    )(pos, pltpu.with_memory_space_constraint(orbitals, pltpu.HBM), after)
 
 
 def perturbed(field, pert_r, pert_i):
@@ -164,10 +155,21 @@
 
 
 def join_halves(pos_ref, got, swap, joined, fields):
-    core = pos_ref[3]
+    x, core = pos_ref[2], pos_ref[3]
     for to, i in enumerate(fields):
-        joined[to, :, pl.ds(pl.multiple_of(core * HALF, 128), HALF)] = got[i, :, :HALF]
-        joined[to, :, pl.ds(pl.multiple_of((1 - core) * HALF, 128), HALF)] = swap[i, :, :HALF]
+        joined[to, :, pl.ds(pl.multiple_of(core * HALF, 128), HALF)] = got[x ^ i, :, :HALF]
+        joined[to, :, pl.ds(pl.multiple_of((1 - core) * HALF, 128), HALF)] = swap[x ^ i, :, :HALF]
+
+
+def one_lane_each(rows):
+    row = lax.broadcasted_iota(jnp.int32, (40, 128), 0)
+    lane = lax.broadcasted_iota(jnp.int32, (40, 128), 1)
+    return jnp.where(row == lane, rows, 0.0)
+
+
+def over_lanes(rows):
+    ones = jnp.full((128, 128), 1.0, F32)
+    return jnp.dot(rows, ones, precision=lax.Precision.HIGHEST, preferred_element_type=F32)
 
 
 def products_kernel(near, pos_ref, slot_ref, o0, o1, *refs):
@@ -175,7 +177,7 @@
         pert, out_ref = refs
         base = pos_ref[1] * CHUNK
     else:
-        got, swap, near_ref, out_ref, pert = refs
+        got, swap, near_ref, sums_ref, pert, out_ref = refs
         join_halves(pos_ref, got, swap, pert, (0, 1))
         base = 0
     pair, bases = (o0, o1), (base, 0)
@@ -205,6 +207,11 @@
             out_ref[at, :] = value if near else near_ref[at, :] + value
     for block in range(2):
         out_ref[block * 40 + 36 : block * 40 + 40, :] = jnp.zeros((4, 128), F32)
+    if not near:
+        total = over_lanes(out_ref[...])
+        for block in range(2):
+            row = jnp.sum(one_lane_each(total[block * 40 : block * 40 + 40]), axis=0, keepdims=True)
+            sums_ref[block * 8 : block * 8 + 8, :] = jnp.broadcast_to(row, (8, 128))
 
 
 def products(pos, slots, o0, o1, *pert):
@@ -212,8 +219,8 @@
     return call(
         functools.partial(products_kernel, near),
         (pos, slots, o0, o1, *pert),
-        [(80, 128)],
-        scratch=() if near else [pltpu.VMEM((2, 8, CHUNK), F32)],
+        [(80, 128) if near else (16, 128)],
+        scratch=() if near else [pltpu.VMEM((2, 8, CHUNK), F32), pltpu.VMEM((80, 128), F32)],
         scalars=2,
         flops=20_000_000,
     )[0]
@@ -303,8 +310,8 @@
 def right_kernel(ncells, slot_ref, pos_ref, s0, s1, s2, s3, o0, o1, o2, o3, pert0, got, swap, r_ref, za, zb, ya, yb, prod_ref, pert1):
     join_halves(pos_ref, got, swap, pert1, (0, 1))
     total = (s0[...] + s1[...]) + (s2[...] + s3[...])
-    ones = jnp.full((128, 128), 1.0, F32)
-    prod_ref[...] = jnp.dot(total, ones, precision=lax.Precision.HIGHEST, preferred_element_type=F32) / ncells
+    spread = [one_lane_each(jnp.broadcast_to(total[8 * block : 8 * block + 1], (40, 128))) for block in range(2)]
+    prod_ref[...] = over_lanes(jnp.concatenate(spread, 0)) / ncells
     lanes = lane_ids()
     half = pos_ref[0]
     slabs = (((o0, o1), pert0, half, pos_ref[1] * CHUNK), ((o2, o3), pert1, 1 - half, 0))
@@ -610,27 +617,30 @@
     other[...] = (s0[half] + s1[half]) + (s2[half] + s3[half])
 
 
-def place_kernel(pos_ref, t0, t1, t2, t3, out_ref):
-    z = pos_ref[1]
-    for m, tile in enumerate((t0, t1, t2, t3)):
-        out_ref[:, pl.ds(pl.multiple_of((z ^ m) * CHUNK, 128), CHUNK)] = tile[...]
-
-
-def both_kernel(pos_ref, mine, other, out_ref):
-    core = pos_ref[3]
-    out_ref[core] = mine[...]
-    out_ref[1 - core] = other[...]
-
-
-def both_components(pos, mine, other):
+def place_kernel(pos_ref, *refs):
+    tiles, out_ref, sems = refs[:8], refs[8], refs[9]
+    z, core = pos_ref[1], pos_ref[3]
+    copies = []
+    for i, tile in enumerate(tiles):
+        component = core if i < 4 else 1 - core
+        target = out_ref.at[component, :, pl.ds(pl.multiple_of((z ^ (i % 4)) * CHUNK, 128), CHUNK)]
+        copies.append(pltpu.make_async_copy(tile, target, sems.at[i]))
+    for copy in copies:
+        copy.start()
+    for copy in copies:
+        copy.wait()
+
+
+def place(pos, tiles):
     return pl.pallas_call(
-        both_kernel,
-        in_specs=[pl.BlockSpec(memory_space=pltpu.SMEM)] + [pl.BlockSpec(memory_space=pltpu.VMEM)] * 2,
-        out_specs=pl.BlockSpec(memory_space=pltpu.VMEM),
+        place_kernel,
+        in_specs=[pl.BlockSpec(memory_space=pltpu.SMEM)] + [pl.BlockSpec(memory_space=pl.ANY)] * 8,
+        out_specs=IN_HBM,
         out_shape=jax.ShapeDtypeStruct((2, 8, 4 * CHUNK), F32),
-        compiler_params=pltpu.CompilerParams(vmem_limit_bytes=8 * 2**20),
-        name="both_components",
-    )(pos, mine, other)
+        scratch_shapes=[pltpu.SemaphoreType.DMA((8,))],
+        compiler_params=pltpu.CompilerParams(vmem_limit_bytes=4 * 2**20),
+        name="place",
+    )(pos, *[pltpu.with_memory_space_constraint(t, pltpu.VMEM) for t in tiles])
 
 
 def program(orbitals, partner_map, wave_vectors, levels, potential, perturbation, step_weights):
@@ -640,14 +650,17 @@
     ncells = 64 * 4 * CHUNK
     matrix = jnp.asarray(x_matrix(), jnp.bfloat16)
 
-    send3, send1, small, mine = cut_near(pos, orbitals, perturbation, potential, wave_vectors, levels, partner_map)
-    got = z_xor(small, 3)
+    send3, send1, send2, small, mine = cut(pos, orbitals, perturbation, potential, wave_vectors, levels, partner_map)
+    field = z_xor(small, 3)
     o3 = z_xor(send3, 3)
     o1 = z_xor(send1, 1)
-    send2 = cut_far(pos, orbitals, send1)
     o2 = z_xor(send2, 2)
+    shared = [field]
+    for m in (1, 2, 3):
+        shared.append(x_xor(field, m))
+    got = jnp.stack(shared)
     swap = other_core(got)
-    par = jnp.concatenate([mine[:2, :8], got[0, :2, HALF : HALF + 8]], 0)
+    par = jnp.concatenate([mine[:2, :8], field[:2, HALF : HALF + 8]], 0)
     slots = par[:, 6].astype(jnp.int32)
     weights = step_weights.astype(F32) / 100.0
 
@@ -657,7 +670,7 @@
     orb, pot = orbital_rows(pos, fields, (potential, got, swap))
 
     def swapped(value):
-        return jnp.concatenate([value[40:], value[:40]], 0)
+        return jnp.concatenate([value[8:], value[:8]], 0)
 
     part = part + swapped(z_xor(part, 1)) + z_xor(part, 2) + swapped(z_xor(part, 3))
     sums = [part] + [y_xor(part, m) for m in (1, 2, 3)]
@@ -672,11 +685,12 @@
     keep, send = tile_density(par, weights, pos, u, halos, orb)
 
     chip = call(pair_kernel, (keep, other_core(send)), [TILE])[0]
-    parts = [chip] + [lax.ppermute(chip, "x", [(i, i ^ m) for i in range(4)]) for m in (1, 2, 3)]
+    parts = [chip]
+    for m in (1, 2, 3):
+        parts.append(x_xor(chip, m))
     same, cross = call(split_kernel, (pos, *parts), [(8, CHUNK)] * 2, scalars=1)
     tiles = [same, z_xor(same, 1), z_xor(cross, 2), z_xor(cross, 3)]
-    slab = call(place_kernel, (pos, *tiles), [(8, 4 * CHUNK)], scalars=1)[0]
-    return both_components(pos, slab, other_core(slab))
+    return place(pos, tiles + [other_core(tile) for tile in tiles])
 
 
 def solution(mesh):

time: 152 us -> 157 us (1.033)
  starting transfers between devices: 41.2 us -> 51.4 us
  waiting for transfers between devices: 62.7 us -> 58.6 us
  Pallas kernels: 47.7 us -> 45.7 us
    ppermute x16, waiting for transfers between devices: 45.8 us -> 39.9 us  [z_xor(): return lax.ppermute(value, ZAX, z_perm(lambda z: z ^ m))]
    ppermute x3 -> x6, starting transfers between devices: 11.2 us -> 16.3 us  [other_core(): return lax.ppermute(value, 'c', [(0, 1), (1, 0)])]
    ppermute x3 -> x6, waiting for transfers between devices: 6.54 us -> 10.7 us  [x_xor(): return lax.ppermute(value, 'x', [(i, i ^ m) for i in range(4)])]
    ppermute x3 -> x6, starting transfers between devices: 3.33 us -> 6.51 us  [x_xor(): return lax.ppermute(value, 'x', [(i, i ^ m) for i in range(4)])]
    ppermute x9, waiting for transfers between devices: 8.13 us -> 5.72 us  [y_xor(): return lax.ppermute(value, 'y', [(i, i ^ m) for i in range(4)])]
    pallas_call x3 -> x2, Pallas kernels: 5.48 us -> 4.03 us  [the longest x1 2.62 us: cut(): pl.pallas_call(cut_kernel, in_specs=[pl.BlockSpec(memory_space=pltpu.SMEM...]
    pallas_call x13 -> x12, Pallas kernels: 42.2 us -> 41.7 us  [call(): pl.pallas_call(kernel, in_specs=specs, out_specs=[pl.BlockSpec(memory_spa...]
  transfers between devices with their start and end apart: 31 -> 37, of which waited for: 16 -> 19; matrix products, arithmetic and copies ran while one was open for 0% -> 0% of each run, Pallas kernels for 19% -> 17%
where the time goes in v6:
time: 157 us
  waiting for transfers between devices  58.6 us (37%)
  starting transfers between devices  51.4 us (33%)
  Pallas kernels  45.7 us (29%)
    pallas_call x12, Pallas kernels, call(): pl.pallas_call(kernel, in_specs=specs, out_specs=[pl.BlockSpec(memory_spa...  41.7 us
    ppermute x16, waiting for transfers between devices, z_xor(): return lax.ppermute(value, ZAX, z_perm(lambda z: z ^ m))  39.9 us
    ppermute x16, starting transfers between devices, z_xor(): return lax.ppermute(value, ZAX, z_perm(lambda z: z ^ m))  19.9 us
    ppermute x6, starting transfers between devices, other_core(): return lax.ppermute(value, 'c', [(0, 1), (1, 0)])  16.3 us
    ppermute x6, waiting for transfers between devices, x_xor(): return lax.ppermute(value, 'x', [(i, i ^ m) for i in range(4)])  10.7 us
    ppermute x9, starting transfers between devices, y_xor(): return lax.ppermute(value, 'y', [(i, i ^ m) for i in range(4)])  8.77 us
    ppermute x6, starting transfers between devices, x_xor(): return lax.ppermute(value, 'x', [(i, i ^ m) for i in range(4)])  6.51 us
    ppermute x9, waiting for transfers between devices, y_xor(): return lax.ppermute(value, 'y', [(i, i ^ m) for i in range(4)])  5.72 us
  transfers between devices with their start and end apart: 37, of which 19 were waited for; matrix products, arithmetic and copies ran while one was open for 0% of the time, Pallas kernels for 17%

profile of v6, /device:TPU:1, one launch (start us, length us, event | category | flops | bytes accessed | tf_op | source)
XLA Modules:
  0.0 156.5 jit_solution(4113103440345055635)
XLA Ops:
  0.1 2.6 %cut.1 = (f32[2,3,2,8,2304]{4,3,2,1,0:T(8,128)S(1)}, f32[2,3,2,8,2304]{4,3,2,1,0:T(8,128)S(1)}, f32[2,3,2,8,2304]{4,3,2,1,0:T(8,128)S(1)}, f32[8,1280]{1,0:T(8,128)S(1)}, f32[8,128]{1,0:T(8,128)S(1)}) custom-call(s32[5]{0:T(128)S(1)} %stack.38.pos_ref, f32[2,3,2,8,9216]{4,3,2,1,0:T(8,128)} %o0.5, f32[2,8,9216]{2,1,0:T(8,128)} %pert0.1, f32[8,9216]{1,0:T(8,128)} %pot.3, ...), custom_call_target="tpu_custom_call" | custom-call | tf_op jit(solution)/shard_map/cut/pallas_call | solution.py:136
  2.7 2.5 %collective-permute-start.1 = (f32[2,3,2,8,2304]{4,3,2,1,0:T(8,128)S(1)}, f32[2,3,2,8,2304]{4,3,2,1,0:T(8,128)S(1)}, u32[]{:S(2)}, u32[]{:S(2)}) collective-permute-start(f32[2,3,2,8,2304]{4,3,2,1,0:T(8,128)S(1)} %get-tuple-element.39), channel_id=1, source_target_pairs={{0,64},{64,0},{1,65},{65,1},{2,66},{66,2},{3,67},{67,3},{4,68},{68... | collective-permute-start | bytes 2654216 | tf_op jit(solution)/shard_map/ppermute | solution.py:28
  5.3 3.3 %collective-permute-start.2 = (f32[2,3,2,8,2304]{4,3,2,1,0:T(8,128)S(1)}, f32[2,3,2,8,2304]{4,3,2,1,0:T(8,128)S(1)}, u32[]{:S(2)}, u32[]{:S(2)}) collective-permute-start(f32[2,3,2,8,2304]{4,3,2,1,0:T(8,128)S(1)} %get-tuple-element.40), channel_id=1, source_target_pairs={{0,1},{64,65},{1,0},{65,64},{2,3},{66,67},{3,2},{67,66},{4,5},{68,... | collective-permute-start | bytes 2654216 | tf_op jit(solution)/shard_map/ppermute | solution.py:28
  8.6 2.7 %collective-permute-start = (f32[8,1280]{1,0:T(8,128)S(1)}, f32[8,1280]{1,0:T(8,128)S(1)}, u32[]{:S(2)}, u32[]{:S(2)}) collective-permute-start(f32[8,1280]{1,0:T(8,128)S(1)} %get-tuple-element.38), channel_id=1, source_target_pairs={{0,65},{64,1},{1,64},{65,0},{2,67},{66,3},{3,66},{67,2},{4,69},{68... | collective-permute-start | bytes 122888 | tf_op jit(solution)/shard_map/ppermute | solution.py:28
  11.2 38.3 %collective-permute-done = f32[8,1280]{1,0:T(8,128)S(1)} collective-permute-done((f32[8,1280]{1,0:T(8,128)S(1)}, f32[8,1280]{1,0:T(8,128)S(1)}, u32[]{:S(2)}, u32[]{:S(2)}) %collective-permute-start) | collective-permute-done | bytes 40992 | tf_op jit(solution)/shard_map/ppermute | solution.py:28
  49.6 2.5 %collective-permute-start.6 = (f32[8,1280]{1,0:T(8,128)S(1)}, f32[8,1280]{1,0:T(8,128)S(1)}, u32[]{:S(2)}, u32[]{:S(2)}) collective-permute-start(f32[8,1280]{1,0:T(8,128)S(1)} %collective-permute-done), channel_id=1, source_target_pairs={{0,48},{16,32},{32,16},{48,0},{1,49},{17,33},{33,17},{49,1},{2,50}... | collective-permute-start | bytes 122888 | tf_op jit(solution)/shard_map/ppermute | solution.py:36
  52.1 0.5 collective-permute-start.5
  52.6 1.1 collective-permute-done.6
  53.7 2.9 %collective-permute-done.5 = f32[8,1280]{1,0:T(8,128)S(1)} collective-permute-done((f32[8,1280]{1,0:T(8,128)S(1)}, f32[8,1280]{1,0:T(8,128)S(1)}, u32[]{:S(2)}, u32[]{:S(2)}) %collective-permute-start.5) | collective-permute-done | bytes 40992 | tf_op jit(solution)/shard_map/ppermute | solution.py:36
  56.5 0.3 collective-permute-done.4
  56.8 4.6 %collective-permute-start.7 = (f32[4,8,1280]{2,1,0:T(8,128)S(1)}, f32[4,8,1280]{2,1,0:T(8,128)S(1)}, u32[]{:S(2)}, u32[]{:S(2)}) collective-permute-start(f32[4,8,1280]{2,1,0:T(8,128)S(1)} %pad_maximum_fusion.got.refs_0_), channel_id=1, source_target_pairs={{0,8},{8,0},{1,9},{9,1},{2,10},{10,2},{3,11},{11,3},{4,12},{12,4},... | collective-permute-start | bytes 491528 | tf_op jit(solution)/shard_map/ppermute | solution.py:32
  61.4 0.2 convert_reduce_fusion.slot_ref
  61.6 1.7 %shard_map.83.refs_2_ = f32[80,128]{1,0:T(8,128)S(1)} custom-call(s32[5]{0:T(128)S(1)} %stack.38.pos_ref, s32[4]{0:T(128)S(1)} %convert_reduce_fusion.slot_ref, f32[2,3,2,8,9216]{4,3,2,1,0:T(8,128)S(1)} %copy-done, f32[2,3,2,8,2304]{4,3,2,1,0:T(8,128)S(1)} %collective-permute-done.1.o1, f32[2,8,9216]{2,1,0:T(8,128)S(1)} %copy-done.1), custom_call_target="tpu_custom_call" | custom-call | flops 20000000 | bytes 10000000 | tf_op jit(solution)/shard_map/pallas_call | solution.py:73
  63.4 1.9 %shard_map.84 = f32[16,128]{1,0:T(8,128)S(1)} custom-call(s32[5]{0:T(128)S(1)} %stack.38.pos_ref, s32[4]{0:T(128)S(1)} %convert_reduce_fusion.slot_ref, f32[2,3,2,8,2304]{4,3,2,1,0:T(8,128)S(1)} %collective-permute-done.2.o2.o0, f32[2,3,2,8,2304]{4,3,2,1,0:T(8,128)S(1)} %collective-permute-done.3.o3.o1, f32[4,8,1280]{2,1,0:T(8,128)S(1)} %pad_maximum_fusion.got.refs_0_, ...), custom_call_target="tpu_custom_call" | custom-call | flops 20000000 | bytes 10000000 | tf_op jit(solution)/shard_map/pallas_call | solution.py:73
  65.3 0.1 collective-permute-start.10
  65.4 0.1 collective-permute-start.9
  65.5 3.1 %collective-permute-start.8 = (f32[16,128]{1,0:T(8,128)S(1)}, f32[16,128]{1,0:T(8,128)S(1)}, u32[]{:S(2)}, u32[]{:S(2)}) collective-permute-start(f32[16,128]{1,0:T(8,128)S(1)} %shard_map.84), channel_id=1, source_target_pairs={{0,64},{64,0},{1,65},{65,1},{2,66},{66,2},{3,67},{67,3},{4,68},{68... | collective-permute-start | bytes 24584 | tf_op jit(solution)/shard_map/ppermute | solution.py:28
  68.6 0.5 collective-permute-done.10
  69.1 1.0 collective-permute-done.8
  70.0 2.8 %collective-permute-start.13 = (f32[16,128]{1,0:T(8,128)S(1)}, f32[16,128]{1,0:T(8,128)S(1)}, u32[]{:S(2)}, u32[]{:S(2)}) collective-permute-start(f32[16,128]{1,0:T(8,128)S(1)} %fusion.1.s0), channel_id=1, source_target_pairs={{0,6},{2,4},{4,2},{6,0},{1,7},{3,5},{5,3},{7,1},{8,14},{10,12},{12... | collective-permute-start | bytes 24584 | tf_op jit(solution)/shard_map/ppermute | solution.py:40
  72.9 0.3 collective-permute-start.12
  73.2 0.3 collective-permute-start.11
  73.5 2.0 %shard_map.82 = (f32[9216,128]{1,0:T(8,128)S(1)}, f32[384,128]{1,0:T(8,128)S(1)}) custom-call(s32[5]{0:T(128)S(1)} %stack.38.pos_ref, f32[2,3,2,8,9216]{4,3,2,1,0:T(8,128)S(1)} %copy-done, f32[2,3,2,8,2304]{4,3,2,1,0:T(8,128)S(1)} %collective-permute-done.1.o1, f32[2,3,2,8,2304]{4,3,2,1,0:T(8,128)S(1)} %collective-permute-done.2.o2.o0, ...), custom_call_target="tpu_custom_call" | custom-call | flops 10000000 | bytes 10000000 | tf_op jit(solution)/shard_map/pallas_call | solution.py:73
  75.6 1.3 collective-permute-done.12.s2
  76.9 5.3 %shard_map.85 = (f32[24,28,24,128]{3,2,1,0:T(8,128)S(1)}, f32[1152,128]{1,0:T(8,128)S(1)}, f32[1152,128]{1,0:T(8,128)S(1)}, f32[768,128]{1,0:T(8,128)S(1)}, f32[768,128]{1,0:T(8,128)S(1)}) custom-call(s32[4]{0:T(128)S(1)} %convert_reduce_fusion.slot_ref, s32[5]{0:T(128)S(1)} %stack.38.pos_ref, f32[16,128]{1,0:T(8,128)S(1)} %fusion.1.s0, ...), custom_call_target="tpu_custom_call" | custom-call | flops 20000000 | bytes 10000000 | tf_op jit(solution)/shard_map/pallas_call | solution.py:73
  82.2 0.1 collective-permute-start.14
  82.3 1.8 %collective-permute-start.15 = (f32[1152,128]{1,0:T(8,128)S(1)}, f32[1152,128]{1,0:T(8,128)S(1)}, u32[]{:S(2)}, u32[]{:S(2)}) collective-permute-start(f32[1152,128]{1,0:T(8,128)S(1)} %get-tuple-element.51), channel_id=1, source_target_pairs={{0,6},{2,4},{4,2},{6,0},{1,7},{3,5},{5,3},{7,1},{8,14},{10,12},{12... | collective-permute-start | bytes 1769480 | tf_op jit(solution)/shard_map/ppermute | solution.py:40
  84.1 1.1 collective-permute-start.16
  85.1 0.8 collective-permute-start.17
  86.0 7.1 %shard_map.86.u_in = f32[9216,128]{1,0:T(8,128)S(1)} custom-call(f32[4,8]{1,0:T(4,128)S(1)} %pad_maximum_fusion.1.par_ref, f32[4]{0:T(128)S(1)} %convert_multiply_fusion.w_ref, f32[24,28,24,128]{3,2,1,0:T(8,128)S(1)} %get-tuple-element.48.refs_0_.refs_1_, f32[384,128]{1,0:T(8,128)S(1)} %get-tuple-element.49.refs_1_.refs_2_, bf16[256,256]{1,0:T(8,128)(2,1)S(1)} %copy-done.2), custom_call_target="tpu_custom_call" | custom-call | flops 60000000 | bytes 10000000 | tf_op jit(solution)/shard_map/pallas_call | solution.py:73
  93.2 0.1 collective-permute-done.17.yb_in
  93.3 1.3 collective-permute-done.14.za_in
  94.6 1.3 collective-permute-done.15.zb_in
  95.8 2.3 %shard_map.87 = (f32[24,28,24,128]{3,2,1,0:T(8,128)S(1)}, f32[1152,128]{1,0:T(8,128)S(1)}, f32[1152,128]{1,0:T(8,128)S(1)}, f32[768,128]{1,0:T(8,128)S(1)}, f32[768,128]{1,0:T(8,128)S(1)}) custom-call(f32[4,8]{1,0:T(4,128)S(1)} %pad_maximum_fusion.1.par_ref, f32[4]{0:T(128)S(1)} %convert_multiply_fusion.w_ref, s32[5]{0:T(128)S(1)} %stack.38.pos_ref, ...), custom_call_target="tpu_custom_call" | custom-call | flops 10000000 | bytes 10000000 | tf_op jit(solution)/shard_map/pallas_call | solution.py:73
  98.2 1.6 collective-permute-start.19
  99.8 0.4 collective-permute-start.20
  100.2 1.1 collective-permute-start.21
  101.3 7.4 %shard_map.88.u_in = f32[9216,128]{1,0:T(8,128)S(1)} custom-call(f32[4,8]{1,0:T(4,128)S(1)} %pad_maximum_fusion.1.par_ref, f32[4]{0:T(128)S(1)} %convert_multiply_fusion.w_ref, f32[24,28,24,128]{3,2,1,0:T(8,128)S(1)} %get-tuple-element.54.refs_0_, f32[24,28,24,128]{3,2,1,0:T(8,128)S(1)} %get-tuple-element.48.refs_0_.refs_1_, ...), custom_call_target="tpu_custom_call" | custom-call | flops 60000000 | bytes 10000000 | tf_op jit(solution)/shard_map/pallas_call | solution.py:73
  108.8 0.8 collective-permute-done.18.za_in
  109.6 0.9 collective-permute-done.19.zb_in
  110.6 2.3 %shard_map.89 = (f32[24,28,24,128]{3,2,1,0:T(8,128)S(1)}, f32[1152,128]{1,0:T(8,128)S(1)}, f32[1152,128]{1,0:T(8,128)S(1)}, f32[768,128]{1,0:T(8,128)S(1)}, f32[768,128]{1,0:T(8,128)S(1)}) custom-call(f32[4,8]{1,0:T(4,128)S(1)} %pad_maximum_fusion.1.par_ref, f32[4]{0:T(128)S(1)} %convert_multiply_fusion.w_ref, s32[5]{0:T(128)S(1)} %stack.38.pos_ref, ...), custom_call_target="tpu_custom_call" | custom-call | flops 10000000 | bytes 10000000 | tf_op jit(solution)/shard_map/pallas_call | solution.py:73
  112.9 0.3 collective-permute-start.22
  113.2 1.4 collective-permute-start.23
  114.6 1.2 collective-permute-start.25
  115.9 8.4 %shard_map.90.d_in = f32[768,128]{1,0:T(8,128)S(1)} custom-call(f32[4,8]{1,0:T(4,128)S(1)} %pad_maximum_fusion.1.par_ref, f32[4]{0:T(128)S(1)} %convert_multiply_fusion.w_ref, f32[24,28,24,128]{3,2,1,0:T(8,128)S(1)} %get-tuple-element.59.refs_0_, f32[24,28,24,128]{3,2,1,0:T(8,128)S(1)} %get-tuple-element.48.refs_0_.refs_1_, ...), custom_call_target="tpu_custom_call" | custom-call | flops 60000000 | bytes 10000000 | tf_op jit(solution)/shard_map/pallas_call | solution.py:73
  124.3 0.2 collective-permute-done.23.zb
  124.4 2.6 %shard_map.91 = (f32[2,8,2304]{2,1,0:T(8,128)S(1)}, f32[2,8,2304]{2,1,0:T(8,128)S(1)}) custom-call(f32[4,8]{1,0:T(4,128)S(1)} %pad_maximum_fusion.1.par_ref, f32[4]{0:T(128)S(1)} %convert_multiply_fusion.w_ref, s32[5]{0:T(128)S(1)} %stack.38.pos_ref, f32[768,128]{1,0:T(8,128)S(1)} %shard_map.90.d_in, f32[1152,128]{1,0:T(8,128)S(1)} %collective-permute-done.22.za, ...), custom_call_target="tpu_custom_call" | custom-call | flops 10000000 | bytes 10000000 | tf_op jit(solution)/shard_map/pallas_call | solution.py:73
  127.0 5.8 %collective-permute-start.26 = (f32[2,8,2304]{2,1,0:T(8,128)S(1)}, f32[2,8,2304]{2,1,0:T(8,128)S(1)}, u32[]{:S(2)}, u32[]{:S(2)}) collective-permute-start(f32[2,8,2304]{2,1,0:T(8,128)S(1)} %get-tuple-element.66), channel_id=1, source_target_pairs={{0,8},{8,0},{1,9},{9,1},{2,10},{10,2},{3,11},{11,3},{4,12},{12,4},... | collective-permute-start | bytes 442376 | tf_op jit(solution)/shard_map/ppermute | solution.py:32
  132.9 1.0 collective-permute-done.26.b
  133.9 2.3 %collective-permute-start.29 = (f32[2,8,2304]{2,1,0:T(8,128)S(1)}, f32[2,8,2304]{2,1,0:T(8,128)S(1)}, u32[]{:S(2)}, u32[]{:S(2)}) collective-permute-start(f32[2,8,2304]{2,1,0:T(8,128)S(1)} %shard_map.92.s0), channel_id=1, source_target_pairs={{0,48},{16,32},{32,16},{48,0},{1,49},{17,33},{33,17},{49,1},{2,50}... | collective-permute-start | bytes 442376 | tf_op jit(solution)/shard_map/ppermute | solution.py:36
  136.2 1.2 collective-permute-start.27
  137.4 4.6 %collective-permute-done.29.s3 = f32[2,8,2304]{2,1,0:T(8,128)S(1)} collective-permute-done((f32[2,8,2304]{2,1,0:T(8,128)S(1)}, f32[2,8,2304]{2,1,0:T(8,128)S(1)}, u32[]{:S(2)}, u32[]{:S(2)}) %collective-permute-start.29) | collective-permute-done | bytes 147488 | tf_op jit(solution)/shard_map/ppermute | solution.py:36
  142.0 0.6 collective-permute-done.28.s2
  142.6 1.4 collective-permute-done.27.s1
  144.0 0.6 shard_map.93
  144.5 1.6 collective-permute-start.32
  146.1 1.1 collective-permute-start.31
  147.2 0.7 collective-permute-start.30
  147.9 2.3 %collective-permute-start.33 = (f32[8,2304]{1,0:T(8,128)S(1)}, f32[8,2304]{1,0:T(8,128)S(1)}, u32[]{:S(2)}, u32[]{:S(2)}) collective-permute-start(f32[8,2304]{1,0:T(8,128)S(1)} %get-tuple-element.67.refs_0_), channel_id=1, source_target_pairs={{0,8},{8,0},{1,9},{9,1},{2,10},{10,2},{3,11},{11,3},{4,12},{12,4},... | collective-permute-start | bytes 221192 | tf_op jit(solution)/shard_map/ppermute | solution.py:32
  150.2 2.1 %collective-permute-start.36 = (f32[8,2304]{1,0:T(8,128)S(1)}, f32[8,2304]{1,0:T(8,128)S(1)}, u32[]{:S(2)}, u32[]{:S(2)}) collective-permute-start(f32[8,2304]{1,0:T(8,128)S(1)} %collective-permute-done.32.refs_3_), channel_id=1, source_target_pairs={{0,8},{8,0},{1,9},{9,1},{2,10},{10,2},{3,11},{11,3},{4,12},{12,4},... | collective-permute-start | bytes 221192 | tf_op jit(solution)/shard_map/ppermute | solution.py:32
  152.3 1.4 collective-permute-start.35
  153.7 0.9 collective-permute-done.35.refs_6_
  154.6 0.4 collective-permute-done.34.refs_5_
  155.0 1.4 place.1
  (44 shorter events, 0.3 us)
Async XLA Ops:
  0.0 61.6 %copy-start = (f32[2,3,2,8,9216]{4,3,2,1,0:T(8,128)S(1)}, f32[2,3,2,8,9216]{4,3,2,1,0:T(8,128)}, u32[]{:S(2)}) copy-start(f32[2,3,2,8,9216]{4,3,2,1,0:T(8,128)} %o0.5) | copy-start | bytes 10616836
  0.1 61.6 %copy-start.1 = (f32[2,8,9216]{2,1,0:T(8,128)S(1)}, f32[2,8,9216]{2,1,0:T(8,128)}, u32[]{:S(2)}) copy-start(f32[2,8,9216]{2,1,0:T(8,128)} %pert0.1) | copy-start | bytes 1769476
  2.7 70.8 %copy-start.3 = (f32[8,9216]{1,0:T(8,128)S(1)}, f32[8,9216]{1,0:T(8,128)}, u32[]{:S(2)}) copy-start(f32[8,9216]{1,0:T(8,128)} %pot.3) | copy-start | bytes 884740
  2.7 58.9 %collective-permute-start.1 = (f32[2,3,2,8,2304]{4,3,2,1,0:T(8,128)S(1)}, f32[2,3,2,8,2304]{4,3,2,1,0:T(8,128)S(1)}, u32[]{:S(2)}, u32[]{:S(2)}) collective-permute-start(f32[2,3,2,8,2304]{4,3,2,1,0:T(8,128)S(1)} %get-tuple-element.39), channel_id=1, source_target_pairs={{0,64},{64,0},{1,65},{65,1},{2,66},{66,2},{3,67},{67,3},{4,68},{68... | collective-permute-start | bytes 2654216 | tf_op jit(solution)/shard_map/ppermute | solution.py:28
  5.3 58.1 %collective-permute-start.2 = (f32[2,3,2,8,2304]{4,3,2,1,0:T(8,128)S(1)}, f32[2,3,2,8,2304]{4,3,2,1,0:T(8,128)S(1)}, u32[]{:S(2)}, u32[]{:S(2)}) collective-permute-start(f32[2,3,2,8,2304]{4,3,2,1,0:T(8,128)S(1)} %get-tuple-element.40), channel_id=1, source_target_pairs={{0,1},{64,65},{1,0},{65,64},{2,3},{66,67},{3,2},{67,66},{4,5},{68,... | collective-permute-start | bytes 2654216 | tf_op jit(solution)/shard_map/ppermute | solution.py:28
  8.6 54.8 %collective-permute-start.3 = (f32[2,3,2,8,2304]{4,3,2,1,0:T(8,128)S(1)}, f32[2,3,2,8,2304]{4,3,2,1,0:T(8,128)S(1)}, u32[]{:S(2)}, u32[]{:S(2)}) collective-permute-start(f32[2,3,2,8,2304]{4,3,2,1,0:T(8,128)S(1)} %get-tuple-element.41), channel_id=1, source_target_pairs={{0,65},{64,1},{1,64},{65,0},{2,67},{66,3},{3,66},{67,2},{4,69},{68... | collective-permute-start | bytes 2654216 | tf_op jit(solution)/shard_map/ppermute | solution.py:28
  8.6 41.0 %collective-permute-start = (f32[8,1280]{1,0:T(8,128)S(1)}, f32[8,1280]{1,0:T(8,128)S(1)}, u32[]{:S(2)}, u32[]{:S(2)}) collective-permute-start(f32[8,1280]{1,0:T(8,128)S(1)} %get-tuple-element.38), channel_id=1, source_target_pairs={{0,65},{64,1},{1,64},{65,0},{2,67},{66,3},{3,66},{67,2},{4,69},{68... | collective-permute-start | bytes 122888 | tf_op jit(solution)/shard_map/ppermute | solution.py:28
  49.6 4.1 %collective-permute-start.6 = (f32[8,1280]{1,0:T(8,128)S(1)}, f32[8,1280]{1,0:T(8,128)S(1)}, u32[]{:S(2)}, u32[]{:S(2)}) collective-permute-start(f32[8,1280]{1,0:T(8,128)S(1)} %collective-permute-done), channel_id=1, source_target_pairs={{0,48},{16,32},{32,16},{48,0},{1,49},{17,33},{33,17},{49,1},{2,50}... | collective-permute-start | bytes 122888 | tf_op jit(solution)/shard_map/ppermute | solution.py:36
  52.1 4.5 %collective-permute-start.5 = (f32[8,1280]{1,0:T(8,128)S(1)}, f32[8,1280]{1,0:T(8,128)S(1)}, u32[]{:S(2)}, u32[]{:S(2)}) collective-permute-start(f32[8,1280]{1,0:T(8,128)S(1)} %collective-permute-done), channel_id=1, source_target_pairs={{0,32},{16,48},{32,0},{48,16},{1,33},{17,49},{33,1},{49,17},{2,34}... | collective-permute-start | bytes 122888 | tf_op jit(solution)/shard_map/ppermute | solution.py:36
  53.6 3.1 %collective-permute-start.4 = (f32[8,1280]{1,0:T(8,128)S(1)}, f32[8,1280]{1,0:T(8,128)S(1)}, u32[]{:S(2)}, u32[]{:S(2)}) collective-permute-start(f32[8,1280]{1,0:T(8,128)S(1)} %collective-permute-done), channel_id=1, source_target_pairs={{0,16},{16,0},{32,48},{48,32},{1,17},{17,1},{33,49},{49,33},{2,18}... | collective-permute-start | bytes 122888 | tf_op jit(solution)/shard_map/ppermute | solution.py:36
  56.8 6.5 %collective-permute-start.7 = (f32[4,8,1280]{2,1,0:T(8,128)S(1)}, f32[4,8,1280]{2,1,0:T(8,128)S(1)}, u32[]{:S(2)}, u32[]{:S(2)}) collective-permute-start(f32[4,8,1280]{2,1,0:T(8,128)S(1)} %pad_maximum_fusion.got.refs_0_), channel_id=1, source_target_pairs={{0,8},{8,0},{1,9},{9,1},{2,10},{10,2},{3,11},{11,3},{4,12},{12,4},... | collective-permute-start | bytes 491528 | tf_op jit(solution)/shard_map/ppermute | solution.py:32
  65.3 3.8 %collective-permute-start.10 = (f32[16,128]{1,0:T(8,128)S(1)}, f32[16,128]{1,0:T(8,128)S(1)}, u32[]{:S(2)}, u32[]{:S(2)}) collective-permute-start(f32[16,128]{1,0:T(8,128)S(1)} %shard_map.84), channel_id=1, source_target_pairs={{0,65},{64,1},{1,64},{65,0},{2,67},{66,3},{3,66},{67,2},{4,69},{68... | collective-permute-start | bytes 24584 | tf_op jit(solution)/shard_map/ppermute | solution.py:28
  65.4 4.7 %collective-permute-start.9 = (f32[16,128]{1,0:T(8,128)S(1)}, f32[16,128]{1,0:T(8,128)S(1)}, u32[]{:S(2)}, u32[]{:S(2)}) collective-permute-start(f32[16,128]{1,0:T(8,128)S(1)} %shard_map.84), channel_id=1, source_target_pairs={{0,1},{64,65},{1,0},{65,64},{2,3},{66,67},{3,2},{67,66},{4,5},{68,... | collective-permute-start | bytes 24584 | tf_op jit(solution)/shard_map/ppermute | solution.py:28
  65.5 4.6 %collective-permute-start.8 = (f32[16,128]{1,0:T(8,128)S(1)}, f32[16,128]{1,0:T(8,128)S(1)}, u32[]{:S(2)}, u32[]{:S(2)}) collective-permute-start(f32[16,128]{1,0:T(8,128)S(1)} %shard_map.84), channel_id=1, source_target_pairs={{0,64},{64,0},{1,65},{65,1},{2,66},{66,2},{3,67},{67,3},{4,68},{68... | collective-permute-start | bytes 24584 | tf_op jit(solution)/shard_map/ppermute | solution.py:28
  70.0 5.5 %collective-permute-start.13 = (f32[16,128]{1,0:T(8,128)S(1)}, f32[16,128]{1,0:T(8,128)S(1)}, u32[]{:S(2)}, u32[]{:S(2)}) collective-permute-start(f32[16,128]{1,0:T(8,128)S(1)} %fusion.1.s0), channel_id=1, source_target_pairs={{0,6},{2,4},{4,2},{6,0},{1,7},{3,5},{5,3},{7,1},{8,14},{10,12},{12... | collective-permute-start | bytes 24584 | tf_op jit(solution)/shard_map/ppermute | solution.py:40
  72.9 4.0 %collective-permute-start.12 = (f32[16,128]{1,0:T(8,128)S(1)}, f32[16,128]{1,0:T(8,128)S(1)}, u32[]{:S(2)}, u32[]{:S(2)}) collective-permute-start(f32[16,128]{1,0:T(8,128)S(1)} %fusion.1.s0), channel_id=1, source_target_pairs={{0,4},{2,6},{4,0},{6,2},{1,5},{3,7},{5,1},{7,3},{8,12},{10,14},{12... | collective-permute-start | bytes 24584 | tf_op jit(solution)/shard_map/ppermute | solution.py:40
  73.2 3.7 %collective-permute-start.11 = (f32[16,128]{1,0:T(8,128)S(1)}, f32[16,128]{1,0:T(8,128)S(1)}, u32[]{:S(2)}, u32[]{:S(2)}) collective-permute-start(f32[16,128]{1,0:T(8,128)S(1)} %fusion.1.s0), channel_id=1, source_target_pairs={{0,2},{2,0},{4,6},{6,4},{1,3},{3,1},{5,7},{7,5},{8,10},{10,8},{12,... | collective-permute-start | bytes 24584 | tf_op jit(solution)/shard_map/ppermute | solution.py:40
  75.5 10.4 %copy-start.4 = (s32[4]{0:T(128)S(1)}, s32[4]{0:T(128)}, u32[]{:S(2)}) copy-start(s32[4]{0:T(128)} %param.14) | copy-start | bytes 52
  75.6 10.4 %copy-start.2 = (bf16[256,256]{1,0:T(8,128)(2,1)S(1)}, bf16[256,256]{1,0:T(8,128)(2,1)}, u32[]{:S(2)}) copy-start(bf16[256,256]{1,0:T(8,128)(2,1)} %constant.26.clone.refs_2_.refs_3_) | copy-start | bytes 393220
  82.2 12.4 %collective-permute-start.14 = (f32[1152,128]{1,0:T(8,128)S(1)}, f32[1152,128]{1,0:T(8,128)S(1)}, u32[]{:S(2)}, u32[]{:S(2)}) collective-permute-start(f32[1152,128]{1,0:T(8,128)S(1)} %get-tuple-element.50), channel_id=1, source_target_pairs={{0,2},{2,0},{4,6},{6,4},{1,3},{3,1},{5,7},{7,5},{8,10},{10,8},{12,... | collective-permute-start | bytes 1769480 | tf_op jit(solution)/shard_map/ppermute | solution.py:40
  82.3 13.6 %collective-permute-start.15 = (f32[1152,128]{1,0:T(8,128)S(1)}, f32[1152,128]{1,0:T(8,128)S(1)}, u32[]{:S(2)}, u32[]{:S(2)}) collective-permute-start(f32[1152,128]{1,0:T(8,128)S(1)} %get-tuple-element.51), channel_id=1, source_target_pairs={{0,6},{2,4},{4,2},{6,0},{1,7},{3,5},{5,3},{7,1},{8,14},{10,12},{12... | collective-permute-start | bytes 1769480 | tf_op jit(solution)/shard_map/ppermute | solution.py:40
  84.1 9.1 %collective-permute-start.16 = (f32[768,128]{1,0:T(8,128)S(1)}, f32[768,128]{1,0:T(8,128)S(1)}, u32[]{:S(2)}, u32[]{:S(2)}) collective-permute-start(f32[768,128]{1,0:T(8,128)S(1)} %get-tuple-element.52), channel_id=1, source_target_pairs={{0,64},{64,0},{1,65},{65,1},{2,66},{66,2},{3,67},{67,3},{4,68},{68... | collective-permute-start | bytes 1179656 | tf_op jit(solution)/shard_map/ppermute | solution.py:28
  85.1 8.1 %collective-permute-start.17 = (f32[768,128]{1,0:T(8,128)S(1)}, f32[768,128]{1,0:T(8,128)S(1)}, u32[]{:S(2)}, u32[]{:S(2)}) collective-permute-start(f32[768,128]{1,0:T(8,128)S(1)} %get-tuple-element.53), channel_id=1, source_target_pairs={{0,65},{64,1},{1,64},{65,0},{2,67},{66,3},{3,66},{67,2},{4,69},{68... | collective-permute-start | bytes 1179656 | tf_op jit(solution)/shard_map/ppermute | solution.py:28
  98.1 11.5 %collective-permute-start.18 = (f32[1152,128]{1,0:T(8,128)S(1)}, f32[1152,128]{1,0:T(8,128)S(1)}, u32[]{:S(2)}, u32[]{:S(2)}) collective-permute-start(f32[1152,128]{1,0:T(8,128)S(1)} %get-tuple-element.55), channel_id=1, source_target_pairs={{0,2},{2,0},{4,6},{6,4},{1,3},{3,1},{5,7},{7,5},{8,10},{10,8},{12,... | collective-permute-start | bytes 1769480 | tf_op jit(solution)/shard_map/ppermute | solution.py:40
  98.2 12.3 %collective-permute-start.19 = (f32[1152,128]{1,0:T(8,128)S(1)}, f32[1152,128]{1,0:T(8,128)S(1)}, u32[]{:S(2)}, u32[]{:S(2)}) collective-permute-start(f32[1152,128]{1,0:T(8,128)S(1)} %get-tuple-element.56), channel_id=1, source_target_pairs={{0,6},{2,4},{4,2},{6,0},{1,7},{3,5},{5,3},{7,1},{8,14},{10,12},{12... | collective-permute-start | bytes 1769480 | tf_op jit(solution)/shard_map/ppermute | solution.py:40
  99.8 9.0 %collective-permute-start.20 = (f32[768,128]{1,0:T(8,128)S(1)}, f32[768,128]{1,0:T(8,128)S(1)}, u32[]{:S(2)}, u32[]{:S(2)}) collective-permute-start(f32[768,128]{1,0:T(8,128)S(1)} %get-tuple-element.57), channel_id=1, source_target_pairs={{0,64},{64,0},{1,65},{65,1},{2,66},{66,2},{3,67},{67,3},{4,68},{68... | collective-permute-start | bytes 1179656 | tf_op jit(solution)/shard_map/ppermute | solution.py:28
  100.2 8.6 %collective-permute-start.21 = (f32[768,128]{1,0:T(8,128)S(1)}, f32[768,128]{1,0:T(8,128)S(1)}, u32[]{:S(2)}, u32[]{:S(2)}) collective-permute-start(f32[768,128]{1,0:T(8,128)S(1)} %get-tuple-element.58), channel_id=1, source_target_pairs={{0,65},{64,1},{1,64},{65,0},{2,67},{66,3},{3,66},{67,2},{4,69},{68... | collective-permute-start | bytes 1179656 | tf_op jit(solution)/shard_map/ppermute | solution.py:28
  112.9 11.4 %collective-permute-start.22 = (f32[1152,128]{1,0:T(8,128)S(1)}, f32[1152,128]{1,0:T(8,128)S(1)}, u32[]{:S(2)}, u32[]{:S(2)}) collective-permute-start(f32[1152,128]{1,0:T(8,128)S(1)} %get-tuple-element.61), channel_id=1, source_target_pairs={{0,2},{2,0},{4,6},{6,4},{1,3},{3,1},{5,7},{7,5},{8,10},{10,8},{12,... | collective-permute-start | bytes 1769480 | tf_op jit(solution)/shard_map/ppermute | solution.py:40
  113.2 11.2 %collective-permute-start.23 = (f32[1152,128]{1,0:T(8,128)S(1)}, f32[1152,128]{1,0:T(8,128)S(1)}, u32[]{:S(2)}, u32[]{:S(2)}) collective-permute-start(f32[1152,128]{1,0:T(8,128)S(1)} %get-tuple-element.62), channel_id=1, source_target_pairs={{0,6},{2,4},{4,2},{6,0},{1,7},{3,5},{5,3},{7,1},{8,14},{10,12},{12... | collective-permute-start | bytes 1769480 | tf_op jit(solution)/shard_map/ppermute | solution.py:40
  114.6 9.6 %collective-permute-start.24 = (f32[768,128]{1,0:T(8,128)S(1)}, f32[768,128]{1,0:T(8,128)S(1)}, u32[]{:S(2)}, u32[]{:S(2)}) collective-permute-start(f32[768,128]{1,0:T(8,128)S(1)} %get-tuple-element.63), channel_id=1, source_target_pairs={{0,64},{64,0},{1,65},{65,1},{2,66},{66,2},{3,67},{67,3},{4,68},{68... | collective-permute-start | bytes 1179656 | tf_op jit(solution)/shard_map/ppermute | solution.py:28
  114.6 9.6 %collective-permute-start.25 = (f32[768,128]{1,0:T(8,128)S(1)}, f32[768,128]{1,0:T(8,128)S(1)}, u32[]{:S(2)}, u32[]{:S(2)}) collective-permute-start(f32[768,128]{1,0:T(8,128)S(1)} %get-tuple-element.64), channel_id=1, source_target_pairs={{0,65},{64,1},{1,64},{65,0},{2,67},{66,3},{3,66},{67,2},{4,69},{68... | collective-permute-start | bytes 1179656 | tf_op jit(solution)/shard_map/ppermute | solution.py:28
  127.0 6.8 %collective-permute-start.26 = (f32[2,8,2304]{2,1,0:T(8,128)S(1)}, f32[2,8,2304]{2,1,0:T(8,128)S(1)}, u32[]{:S(2)}, u32[]{:S(2)}) collective-permute-start(f32[2,8,2304]{2,1,0:T(8,128)S(1)} %get-tuple-element.66), channel_id=1, source_target_pairs={{0,8},{8,0},{1,9},{9,1},{2,10},{10,2},{3,11},{11,3},{4,12},{12,4},... | collective-permute-start | bytes 442376 | tf_op jit(solution)/shard_map/ppermute | solution.py:32
  133.9 8.1 %collective-permute-start.29 = (f32[2,8,2304]{2,1,0:T(8,128)S(1)}, f32[2,8,2304]{2,1,0:T(8,128)S(1)}, u32[]{:S(2)}, u32[]{:S(2)}) collective-permute-start(f32[2,8,2304]{2,1,0:T(8,128)S(1)} %shard_map.92.s0), channel_id=1, source_target_pairs={{0,48},{16,32},{32,16},{48,0},{1,49},{17,33},{33,17},{49,1},{2,50}... | collective-permute-start | bytes 442376 | tf_op jit(solution)/shard_map/ppermute | solution.py:36
  136.2 6.4 %collective-permute-start.28 = (f32[2,8,2304]{2,1,0:T(8,128)S(1)}, f32[2,8,2304]{2,1,0:T(8,128)S(1)}, u32[]{:S(2)}, u32[]{:S(2)}) collective-permute-start(f32[2,8,2304]{2,1,0:T(8,128)S(1)} %shard_map.92.s0), channel_id=1, source_target_pairs={{0,32},{16,48},{32,0},{48,16},{1,33},{17,49},{33,1},{49,17},{2,34}... | collective-permute-start | bytes 442376 | tf_op jit(solution)/shard_map/ppermute | solution.py:36
  136.2 7.8 %collective-permute-start.27 = (f32[2,8,2304]{2,1,0:T(8,128)S(1)}, f32[2,8,2304]{2,1,0:T(8,128)S(1)}, u32[]{:S(2)}, u32[]{:S(2)}) collective-permute-start(f32[2,8,2304]{2,1,0:T(8,128)S(1)} %shard_map.92.s0), channel_id=1, source_target_pairs={{0,16},{16,0},{32,48},{48,32},{1,17},{17,1},{33,49},{49,33},{2,18}... | collective-permute-start | bytes 442376 | tf_op jit(solution)/shard_map/ppermute | solution.py:36
  144.5 5.6 %collective-permute-start.32 = (f32[8,2304]{1,0:T(8,128)S(1)}, f32[8,2304]{1,0:T(8,128)S(1)}, u32[]{:S(2)}, u32[]{:S(2)}) collective-permute-start(f32[8,2304]{1,0:T(8,128)S(1)} %get-tuple-element.68), channel_id=1, source_target_pairs={{0,65},{64,1},{1,64},{65,0},{2,67},{66,3},{3,66},{67,2},{4,69},{68... | collective-permute-start | bytes 221192 | tf_op jit(solution)/shard_map/ppermute | solution.py:28
  146.1 6.2 %collective-permute-start.31 = (f32[8,2304]{1,0:T(8,128)S(1)}, f32[8,2304]{1,0:T(8,128)S(1)}, u32[]{:S(2)}, u32[]{:S(2)}) collective-permute-start(f32[8,2304]{1,0:T(8,128)S(1)} %get-tuple-element.68), channel_id=1, source_target_pairs={{0,1},{64,65},{1,0},{65,64},{2,3},{66,67},{3,2},{67,66},{4,5},{68,... | collective-permute-start | bytes 221192 | tf_op jit(solution)/shard_map/ppermute | solution.py:28
  147.2 6.5 %collective-permute-start.30 = (f32[8,2304]{1,0:T(8,128)S(1)}, f32[8,2304]{1,0:T(8,128)S(1)}, u32[]{:S(2)}, u32[]{:S(2)}) collective-permute-start(f32[8,2304]{1,0:T(8,128)S(1)} %get-tuple-element.67.refs_0_), channel_id=1, source_target_pairs={{0,64},{64,0},{1,65},{65,1},{2,66},{66,2},{3,67},{67,3},{4,68},{68... | collective-permute-start | bytes 221192 | tf_op jit(solution)/shard_map/ppermute | solution.py:28
  147.9 5.8 %collective-permute-start.33 = (f32[8,2304]{1,0:T(8,128)S(1)}, f32[8,2304]{1,0:T(8,128)S(1)}, u32[]{:S(2)}, u32[]{:S(2)}) collective-permute-start(f32[8,2304]{1,0:T(8,128)S(1)} %get-tuple-element.67.refs_0_), channel_id=1, source_target_pairs={{0,8},{8,0},{1,9},{9,1},{2,10},{10,2},{3,11},{11,3},{4,12},{12,4},... | collective-permute-start | bytes 221192 | tf_op jit(solution)/shard_map/ppermute | solution.py:32
  150.2 3.5 %collective-permute-start.36 = (f32[8,2304]{1,0:T(8,128)S(1)}, f32[8,2304]{1,0:T(8,128)S(1)}, u32[]{:S(2)}, u32[]{:S(2)}) collective-permute-start(f32[8,2304]{1,0:T(8,128)S(1)} %collective-permute-done.32.refs_3_), channel_id=1, source_target_pairs={{0,8},{8,0},{1,9},{9,1},{2,10},{10,2},{3,11},{11,3},{4,12},{12,4},... | collective-permute-start | bytes 221192 | tf_op jit(solution)/shard_map/ppermute | solution.py:32
  152.3 2.3 %collective-permute-start.35 = (f32[8,2304]{1,0:T(8,128)S(1)}, f32[8,2304]{1,0:T(8,128)S(1)}, u32[]{:S(2)}, u32[]{:S(2)}) collective-permute-start(f32[8,2304]{1,0:T(8,128)S(1)} %collective-permute-done.31.refs_2_), channel_id=1, source_target_pairs={{0,8},{8,0},{1,9},{9,1},{2,10},{10,2},{3,11},{11,3},{4,12},{12,4},... | collective-permute-start | bytes 221192 | tf_op jit(solution)/shard_map/ppermute | solution.py:32
  153.7 1.3 collective-permute-start.34

commit v7 on v6

--- a/solution.py
+++ b/solution.py
@@ -235,33 +235,45 @@
     return ((kn * 2 + c) * ROWS + r) * 16
 
 
-def orbital_rows_kernel(pos_ref, o0, o1, o2, o3, pot, got, swap, orb_ref, v_ref, joined):
-    join_halves(pos_ref, got, swap, joined, (2,))
-    pot1 = joined.at[0]
+def orbital_rows_kernel(pos_ref, o0, o1, o2, o3, pot, pert, got, swap, orb_ref, w_ref, v_ref, joined):
+    join_halves(pos_ref, got, swap, joined, (0, 1, 2))
     lanes = lane_ids()
     half = pos_ref[0]
 
+    def rows_of(ref, index, g, base):
+        return unpack_rows(*[ref[index + (slice(None), lanes_at(g, v, base))] for v in range(3)], lanes)
+
     def body(g, carry):
-        for pair, pot_ref, z, base in (((o0, o1), pot, half, pos_ref[1] * CHUNK), ((o2, o3), pot1, 1 - half, 0)):
-            rows = unpack_rows(*[pot_ref[:, lanes_at(g, v, base)] for v in range(3)], lanes)
+        near = pos_ref[1] * CHUNK
+        fields = ((pert, (0,)), (pert, (1,)), (pot, ())), tuple((joined, (i,)) for i in range(3))
+        for pair, local, z, base in (((o0, o1), fields[0], half, near), ((o2, o3), fields[1], 1 - half, 0)):
+            pert_r, pert_i, rows = (rows_of(ref, index, g, base) for ref, index in local)
             for j in range(4):
                 v_ref[pl.ds(pl.multiple_of((4 * g + j) * 16 + 8 * z, 8), 8), :] = rows[j]
             for k in range(4):
                 start = base if k < 2 else 0
                 for n in range(3):
-                    for c in range(2):
-                        cells = [pair[k // 2][k % 2, n, c, :, lanes_at(g, v, start)] for v in range(3)]
-                        rows = unpack_rows(*cells, lanes)
-                        for j in range(4):
-                            at = pl.multiple_of(rows_at(k * 3 + n, c, 4 * g + j) + 8 * z, 8)
-                            orb_ref[pl.ds(at, 8), :] = rows[j]
+                    field = [rows_of(pair[k // 2], (k % 2, n, c), g, start) for c in range(2)]
+                    for j in range(4):
+                        orb = field[0][j], field[1][j]
+                        w = perturbed(orb, pert_r[j], pert_i[j])
+                        for c in range(2):
+                            at = pl.ds(pl.multiple_of(rows_at(k * 3 + n, c, 4 * g + j) + 8 * z, 8), 8)
+                            orb_ref[at, :] = orb[c]
+                            w_ref[at, :] = w[c]
         return carry
 
     lax.fori_loop(0, CHUNK // GROUP, body, 0)
 
 
-def orbital_rows(pos, fields, pots):
-    return call(orbital_rows_kernel, (pos, *fields, *pots), [ORBITALS, (ROWS * 16, 128)], scratch=[pltpu.VMEM((1, 8, CHUNK), F32)], scalars=1)
+def orbital_rows(pos, fields, *local):
+    return call(
+        orbital_rows_kernel,
+        (pos, *fields, *local),
+        [ORBITALS, ORBITALS, (ROWS * 16, 128)],
+        scratch=[pltpu.VMEM((3, 8, CHUNK), F32)],
+        scalars=1,
+    )
 
 
 ZHALO, YHALO = (48 * ROWS, 128), (24 * 32, 128)
@@ -271,13 +283,14 @@
     return ((kn * 2 + c) * TALL + r + 2) * DEEP + 4 + plane
 
 
-def clear_margin(u_ref, kn):
-    for i in (kn * 2, kn * 2 + 1):
-        for r in (0, 1, TALL - 2, TALL - 1):
-            u_ref[i, r] = jnp.zeros((DEEP, 128), F32)
-        for r in range(2, TALL - 2):
-            u_ref[i, r, 0:4] = jnp.zeros((4, 128), F32)
-            u_ref[i, r, 20:24] = jnp.zeros((4, 128), F32)
+def clear_rows(u_ref, i):
+    for r in (0, 1, TALL - 2, TALL - 1):
+        u_ref[i, r] = jnp.zeros((DEEP, 128), F32)
+
+
+def clear_sides(u_ref, i, r):
+    u_ref[i, r, 0:4] = jnp.zeros((4, 128), F32)
+    u_ref[i, r, 20:24] = jnp.zeros((4, 128), F32)
 
 
 def near_face(parity, size):
@@ -307,53 +320,38 @@
     return y_xor(za, 1), y_xor(zb, 3), z_xor(ya, 1), z_xor(yb, 3)
 
 
-def right_kernel(ncells, slot_ref, pos_ref, s0, s1, s2, s3, o0, o1, o2, o3, pert0, got, swap, r_ref, za, zb, ya, yb, prod_ref, pert1):
-    join_halves(pos_ref, got, swap, pert1, (0, 1))
+def right_kernel(ncells, slot_ref, pos_ref, s0, s1, s2, s3, orb_ref, w_ref, r_ref, za, zb, ya, yb, prod_ref):
     total = (s0[...] + s1[...]) + (s2[...] + s3[...])
     spread = [one_lane_each(jnp.broadcast_to(total[8 * block : 8 * block + 1], (40, 128))) for block in range(2)]
     prod_ref[...] = over_lanes(jnp.concatenate(spread, 0)) / ncells
-    lanes = lane_ids()
-    half = pos_ref[0]
-    slabs = (((o0, o1), pert0, half, pos_ref[1] * CHUNK), ((o2, o3), pert1, 1 - half, 0))
     for k in range(4):
         block, kk = k // 2, k % 2
-        slot = slot_ref[k]
-
-        def body(g, carry, k=k, block=block, kk=kk, slot=slot):
-            for pair, pert, z, base in slabs:
-                own, mate = pair[block], pair[1 - block]
-                own_base, mate_base = (base, 0) if block == 0 else (0, base)
-                right = [[[], []] for _ in range(3)]
-                for v in range(3):
-                    at, mate_at, pert_at = (lanes_at(g, v, start) for start in (own_base, mate_base, base))
-                    pr, pi = pert[0, :, pert_at], pert[1, :, pert_at]
-                    mates = [(mate[slot, m, 0, :, mate_at], mate[slot, m, 1, :, mate_at]) for m in range(3)]
-                    for n in range(3):
-                        wr, wi = perturbed((own[kk, n, 0, :, at], own[kk, n, 1, :, at]), pr, pi)
-                        gr, gi = -wr, -wi
-                        for m in range(3):
-                            row = block * 40 + kk * 18 + (m * 3 + n) * 2
-                            qr = prod_ref[pl.ds(row, 1), :]
-                            qi = prod_ref[pl.ds(row + 1, 1), :]
-                            mr, mi = mates[m]
-                            gr = gr + (qr * mr - qi * mi)
-                            gi = gi + (qi * mr + qr * mi)
-                        right[n][0].append(gr)
-                        right[n][1].append(gi)
-                for n in range(3):
-                    for c in range(2):
-                        rows = unpack_rows(*right[n][c], lanes)
-                        for j in range(4):
-                            planes = pl.ds(4 + 8 * z, 8)
-                            r_ref[(k * 3 + n) * 2 + c, 2 + 4 * g + j, planes, :] = rows[j]
+        mate = (2 - 2 * block + slot_ref[k]) * 3
+
+        def body(r, carry, k=k, block=block, kk=kk, mate=mate):
+            def cells(ref, kn, c):
+                return ref[pl.ds(pl.multiple_of(rows_at(kn, c, r), 16), 16), :]
+
+            mates = [(cells(orb_ref, mate + m, 0), cells(orb_ref, mate + m, 1)) for m in range(3)]
+            for n in range(3):
+                gr, gi = -cells(w_ref, k * 3 + n, 0), -cells(w_ref, k * 3 + n, 1)
+                for m, (mr, mi) in enumerate(mates):
+                    row = block * 40 + kk * 18 + (m * 3 + n) * 2
+                    qr, qi = prod_ref[pl.ds(row, 1), :], prod_ref[pl.ds(row + 1, 1), :]
+                    gr = gr + (qr * mr - qi * mi)
+                    gi = gi + (qi * mr + qr * mi)
+                for c, value in enumerate((gr, gi)):
+                    i = (k * 3 + n) * 2 + c
+                    clear_sides(r_ref, i, r + 2)
+                    r_ref[i, r + 2, 4:20, :] = value
             return carry
 
-        lax.fori_loop(0, CHUNK // GROUP, body, 0)
-
+        lax.fori_loop(0, ROWS, body, 0, unroll=4)
     flat = r_ref.reshape(24 * TALL * DEEP, 128)
 
     def cut(kn, carry):
-        clear_margin(r_ref, kn)
+        for c in range(2):
+            clear_rows(r_ref, kn * 2 + c)
         cut_planes(flat, pos_ref, kn, za, zb)
         cut_rows(r_ref, pos_ref, kn, ya, yb)
         return carry
@@ -361,12 +359,12 @@
     lax.fori_loop(0, 12, cut, 0)
 
 
-def right_sides(ncells, slots, pos, sums, fields, perts):
+def right_sides(ncells, slots, pos, sums, orb, w):
     return call(
         functools.partial(right_kernel, ncells),
-        (slots, pos, *sums, *fields, *perts),
+        (slots, pos, *sums, orb, w),
         [FIELD, ZHALO, ZHALO, YHALO, YHALO],
-        scratch=[pltpu.VMEM((80, 128), F32), pltpu.VMEM((2, 8, CHUNK), F32)],
+        scratch=[pltpu.VMEM((80, 128), F32)],
         scalars=2,
         flops=20_000_000,
     )
@@ -518,9 +516,10 @@
     flat = u_ref.reshape(24 * TALL * DEEP, 128)
 
     def orbital(kn, carry):
-        clear_margin(u_ref, kn)
         for c in range(2):
+            clear_rows(u_ref, kn * 2 + c)
             for r in range(ROWS):
+                clear_sides(u_ref, kn * 2 + c, r + 2)
                 u_ref[kn * 2 + c, r + 2, 4:20, :] = u_in[pl.ds(pl.multiple_of(rows_at(kn, c, r), 16), 16), :]
 
         def add_plane(p, term, which, place):
@@ -664,18 +663,17 @@
     slots = par[:, 6].astype(jnp.int32)
     weights = step_weights.astype(F32) / 100.0
 
-    fields, pert = [orbitals, o1, o2, o3], (perturbation, got, swap)
     part = products(pos, slots, orbitals, o1, perturbation)
     part = products(pos, slots, o2, o3, got, swap, part)
-    orb, pot = orbital_rows(pos, fields, (potential, got, swap))
+    orb, w, pot = orbital_rows(pos, [orbitals, o1, o2, o3], potential, perturbation, got, swap)
 
     def swapped(value):
         return jnp.concatenate([value[8:], value[:8]], 0)
 
     part = part + swapped(z_xor(part, 1)) + z_xor(part, 2) + swapped(z_xor(part, 3))
     sums = [part] + [y_xor(part, m) for m in (1, 2, 3)]
-    orb, pot, sums = lax.optimization_barrier((orb, pot, sums))
-    right, *edge = right_sides(float(ncells), slots, pos, sums, fields, pert)
+    orb, w, pot, sums = lax.optimization_barrier((orb, w, pot, sums))
+    right, *edge = right_sides(float(ncells), slots, pos, sums, orb, w)
     u = right
     for count in range(1, ITERS):
         halos = exchange(*edge)

time: 157 us -> 155 us (0.987)
  transfers between devices with their start and end apart: 37 -> 37, of which waited for: 19 -> 18; matrix products, arithmetic and copies ran while one was open for 0% -> 0% of each run, Pallas kernels for 17% -> 17%
where the time goes in v7:
time: 155 us
  waiting for transfers between devices  57.7 us (37%)
  starting transfers between devices  52.3 us (34%)
  Pallas kernels  44.2 us (29%)
    pallas_call x12, Pallas kernels, call(): pl.pallas_call(kernel, in_specs=specs, out_specs=[pl.BlockSpec(memory_spa...  40.1 us
    ppermute x16, waiting for transfers between devices, z_xor(): return lax.ppermute(value, ZAX, z_perm(lambda z: z ^ m))  39.9 us
    ppermute x16, starting transfers between devices, z_xor(): return lax.ppermute(value, ZAX, z_perm(lambda z: z ^ m))  19.9 us
    ppermute x6, starting transfers between devices, other_core(): return lax.ppermute(value, 'c', [(0, 1), (1, 0)])  16.2 us
    ppermute x6, waiting for transfers between devices, x_xor(): return lax.ppermute(value, 'x', [(i, i ^ m) for i in range(4)])  10.8 us
    ppermute x9, starting transfers between devices, y_xor(): return lax.ppermute(value, 'y', [(i, i ^ m) for i in range(4)])  9.98 us
    ppermute x6, starting transfers between devices, x_xor(): return lax.ppermute(value, 'x', [(i, i ^ m) for i in range(4)])  6.33 us
    ppermute x9, waiting for transfers between devices, y_xor(): return lax.ppermute(value, 'y', [(i, i ^ m) for i in range(4)])  4.83 us
  transfers between devices with their start and end apart: 37, of which 18 were waited for; matrix products, arithmetic and copies ran while one was open for 0% of the time, Pallas kernels for 17%

profile of v7, /device:TPU:1, one launch (start us, length us, event | category | flops | bytes accessed | tf_op | source)
XLA Modules:
  0.0 154.9 jit_solution(13246963503805076348)
XLA Ops:
  0.0 0.1 stack.38.pos_ref
  0.1 2.6 %cut.1 = (f32[2,3,2,8,2304]{4,3,2,1,0:T(8,128)S(1)}, f32[2,3,2,8,2304]{4,3,2,1,0:T(8,128)S(1)}, f32[2,3,2,8,2304]{4,3,2,1,0:T(8,128)S(1)}, f32[8,1280]{1,0:T(8,128)S(1)}, f32[8,128]{1,0:T(8,128)S(1)}) custom-call(s32[5]{0:T(128)S(1)} %stack.38.pos_ref, f32[2,3,2,8,9216]{4,3,2,1,0:T(8,128)} %o0.3, f32[2,8,9216]{2,1,0:T(8,128)} %refs_0_.1, f32[8,9216]{1,0:T(8,128)} %pot.3, ...), custom_call_target="tpu_custom_call" | custom-call | tf_op jit(solution)/shard_map/cut/pallas_call | solution.py:136
  2.7 2.5 %collective-permute-start.1 = (f32[2,3,2,8,2304]{4,3,2,1,0:T(8,128)S(1)}, f32[2,3,2,8,2304]{4,3,2,1,0:T(8,128)S(1)}, u32[]{:S(2)}, u32[]{:S(2)}) collective-permute-start(f32[2,3,2,8,2304]{4,3,2,1,0:T(8,128)S(1)} %get-tuple-element.41), channel_id=1, source_target_pairs={{0,64},{64,0},{1,65},{65,1},{2,66},{66,2},{3,67},{67,3},{4,68},{68... | collective-permute-start | bytes 2654216 | tf_op jit(solution)/shard_map/ppermute | solution.py:28
  5.3 3.3 %collective-permute-start.2 = (f32[2,3,2,8,2304]{4,3,2,1,0:T(8,128)S(1)}, f32[2,3,2,8,2304]{4,3,2,1,0:T(8,128)S(1)}, u32[]{:S(2)}, u32[]{:S(2)}) collective-permute-start(f32[2,3,2,8,2304]{4,3,2,1,0:T(8,128)S(1)} %get-tuple-element.42), channel_id=1, source_target_pairs={{0,1},{64,65},{1,0},{65,64},{2,3},{66,67},{3,2},{67,66},{4,5},{68,... | collective-permute-start | bytes 2654216 | tf_op jit(solution)/shard_map/ppermute | solution.py:28
  8.6 2.7 %collective-permute-start = (f32[8,1280]{1,0:T(8,128)S(1)}, f32[8,1280]{1,0:T(8,128)S(1)}, u32[]{:S(2)}, u32[]{:S(2)}) collective-permute-start(f32[8,1280]{1,0:T(8,128)S(1)} %get-tuple-element.40), channel_id=1, source_target_pairs={{0,65},{64,1},{1,64},{65,0},{2,67},{66,3},{3,66},{67,2},{4,69},{68... | collective-permute-start | bytes 122888 | tf_op jit(solution)/shard_map/ppermute | solution.py:28
  11.2 38.3 %collective-permute-done = f32[8,1280]{1,0:T(8,128)S(1)} collective-permute-done((f32[8,1280]{1,0:T(8,128)S(1)}, f32[8,1280]{1,0:T(8,128)S(1)}, u32[]{:S(2)}, u32[]{:S(2)}) %collective-permute-start) | collective-permute-done | bytes 40992 | tf_op jit(solution)/shard_map/ppermute | solution.py:28
  49.6 2.5 %collective-permute-start.6 = (f32[8,1280]{1,0:T(8,128)S(1)}, f32[8,1280]{1,0:T(8,128)S(1)}, u32[]{:S(2)}, u32[]{:S(2)}) collective-permute-start(f32[8,1280]{1,0:T(8,128)S(1)} %collective-permute-done), channel_id=1, source_target_pairs={{0,48},{16,32},{32,16},{48,0},{1,49},{17,33},{33,17},{49,1},{2,50}... | collective-permute-start | bytes 122888 | tf_op jit(solution)/shard_map/ppermute | solution.py:36
  52.1 0.5 collective-permute-start.5
  52.6 1.1 collective-permute-done.6
  53.7 2.9 %collective-permute-done.5 = f32[8,1280]{1,0:T(8,128)S(1)} collective-permute-done((f32[8,1280]{1,0:T(8,128)S(1)}, f32[8,1280]{1,0:T(8,128)S(1)}, u32[]{:S(2)}, u32[]{:S(2)}) %collective-permute-start.5) | collective-permute-done | bytes 40992 | tf_op jit(solution)/shard_map/ppermute | solution.py:36
  56.5 0.3 collective-permute-done.4
  56.8 4.6 %collective-permute-start.7 = (f32[4,8,1280]{2,1,0:T(8,128)S(1)}, f32[4,8,1280]{2,1,0:T(8,128)S(1)}, u32[]{:S(2)}, u32[]{:S(2)}) collective-permute-start(f32[4,8,1280]{2,1,0:T(8,128)S(1)} %pad_maximum_fusion.got.refs_0_), channel_id=1, source_target_pairs={{0,8},{8,0},{1,9},{9,1},{2,10},{10,2},{3,11},{11,3},{4,12},{12,4},... | collective-permute-start | bytes 491528 | tf_op jit(solution)/shard_map/ppermute | solution.py:32
  61.4 0.2 convert_reduce_fusion.slot_ref
  61.6 1.7 %shard_map.83.refs_2_ = f32[80,128]{1,0:T(8,128)S(1)} custom-call(s32[5]{0:T(128)S(1)} %stack.38.pos_ref, s32[4]{0:T(128)S(1)} %convert_reduce_fusion.slot_ref, f32[2,3,2,8,9216]{4,3,2,1,0:T(8,128)S(1)} %copy-done, f32[2,3,2,8,2304]{4,3,2,1,0:T(8,128)S(1)} %collective-permute-done.1.o1, f32[2,8,9216]{2,1,0:T(8,128)S(1)} %copy-done.1), custom_call_target="tpu_custom_call" | custom-call | flops 20000000 | bytes 10000000 | tf_op jit(solution)/shard_map/pallas_call | solution.py:73
  63.4 1.9 %shard_map.84 = f32[16,128]{1,0:T(8,128)S(1)} custom-call(s32[5]{0:T(128)S(1)} %stack.38.pos_ref, s32[4]{0:T(128)S(1)} %convert_reduce_fusion.slot_ref, f32[2,3,2,8,2304]{4,3,2,1,0:T(8,128)S(1)} %collective-permute-done.2.o2.o0, f32[2,3,2,8,2304]{4,3,2,1,0:T(8,128)S(1)} %collective-permute-done.3.o3.o1, f32[4,8,1280]{2,1,0:T(8,128)S(1)} %pad_maximum_fusion.got.refs_0_, ...), custom_call_target="tpu_custom_call" | custom-call | flops 20000000 | bytes 10000000 | tf_op jit(solution)/shard_map/pallas_call | solution.py:73
  65.3 0.1 collective-permute-start.10
  65.4 0.1 collective-permute-start.9
  65.5 3.1 %collective-permute-start.8 = (f32[16,128]{1,0:T(8,128)S(1)}, f32[16,128]{1,0:T(8,128)S(1)}, u32[]{:S(2)}, u32[]{:S(2)}) collective-permute-start(f32[16,128]{1,0:T(8,128)S(1)} %shard_map.84), channel_id=1, source_target_pairs={{0,64},{64,0},{1,65},{65,1},{2,66},{66,2},{3,67},{67,3},{4,68},{68... | collective-permute-start | bytes 24584 | tf_op jit(solution)/shard_map/ppermute | solution.py:28
  68.6 0.5 collective-permute-done.10
  69.1 1.0 collective-permute-done.8
  70.0 2.8 %collective-permute-start.13 = (f32[16,128]{1,0:T(8,128)S(1)}, f32[16,128]{1,0:T(8,128)S(1)}, u32[]{:S(2)}, u32[]{:S(2)}) collective-permute-start(f32[16,128]{1,0:T(8,128)S(1)} %fusion.1.s0), channel_id=1, source_target_pairs={{0,6},{2,4},{4,2},{6,0},{1,7},{3,5},{5,3},{7,1},{8,14},{10,12},{12... | collective-permute-start | bytes 24584 | tf_op jit(solution)/shard_map/ppermute | solution.py:40
  72.9 0.3 collective-permute-start.12
  73.2 0.3 collective-permute-start.11
  73.5 2.3 %shard_map.82 = (f32[9216,128]{1,0:T(8,128)S(1)}, f32[9216,128]{1,0:T(8,128)S(1)}, f32[384,128]{1,0:T(8,128)S(1)}) custom-call(s32[5]{0:T(128)S(1)} %stack.38.pos_ref, f32[2,3,2,8,9216]{4,3,2,1,0:T(8,128)S(1)} %copy-done, f32[2,3,2,8,2304]{4,3,2,1,0:T(8,128)S(1)} %collective-permute-done.1.o1, f32[2,3,2,8,2304]{4,3,2,1,0:T(8,128)S(1)} %collective-permute-done.2.o2.o0, ...), custom_call_target="tpu_custom_call" | custom-call | flops 10000000 | bytes 10000000 | tf_op jit(solution)/shard_map/pallas_call | solution.py:73
  75.8 1.1 collective-permute-done.12.s2
  76.9 3.3 %shard_map.85 = (f32[24,28,24,128]{3,2,1,0:T(8,128)S(1)}, f32[1152,128]{1,0:T(8,128)S(1)}, f32[1152,128]{1,0:T(8,128)S(1)}, f32[768,128]{1,0:T(8,128)S(1)}, f32[768,128]{1,0:T(8,128)S(1)}) custom-call(s32[4]{0:T(128)S(1)} %convert_reduce_fusion.slot_ref, s32[5]{0:T(128)S(1)} %stack.38.pos_ref, f32[16,128]{1,0:T(8,128)S(1)} %fusion.1.s0, ...), custom_call_target="tpu_custom_call" | custom-call | flops 20000000 | bytes 10000000 | tf_op jit(solution)/shard_map/pallas_call | solution.py:73
  80.2 0.2 collective-permute-start.14
  80.4 1.9 %collective-permute-start.15 = (f32[1152,128]{1,0:T(8,128)S(1)}, f32[1152,128]{1,0:T(8,128)S(1)}, u32[]{:S(2)}, u32[]{:S(2)}) collective-permute-start(f32[1152,128]{1,0:T(8,128)S(1)} %get-tuple-element.56), channel_id=1, source_target_pairs={{0,6},{2,4},{4,2},{6,0},{1,7},{3,5},{5,3},{7,1},{8,14},{10,12},{12... | collective-permute-start | bytes 1769480 | tf_op jit(solution)/shard_map/ppermute | solution.py:40
  82.3 1.1 collective-permute-start.16
  83.4 0.8 collective-permute-start.17
  84.3 7.2 %shard_map.86.u_in = f32[9216,128]{1,0:T(8,128)S(1)} custom-call(f32[4,8]{1,0:T(4,128)S(1)} %pad_maximum_fusion.1.par_ref, f32[4]{0:T(128)S(1)} %convert_multiply_fusion.w_ref, f32[24,28,24,128]{3,2,1,0:T(8,128)S(1)} %get-tuple-element.53.refs_0_.refs_1_, f32[384,128]{1,0:T(8,128)S(1)} %get-tuple-element.54.refs_1_.refs_2_, bf16[256,256]{1,0:T(8,128)(2,1)S(1)} %copy-done.2), custom_call_target="tpu_custom_call" | custom-call | flops 60000000 | bytes 10000000 | tf_op jit(solution)/shard_map/pallas_call | solution.py:73
  91.5 1.1 collective-permute-done.14.za_in
  92.6 1.3 collective-permute-done.15.zb_in
  93.9 2.3 %shard_map.87 = (f32[24,28,24,128]{3,2,1,0:T(8,128)S(1)}, f32[1152,128]{1,0:T(8,128)S(1)}, f32[1152,128]{1,0:T(8,128)S(1)}, f32[768,128]{1,0:T(8,128)S(1)}, f32[768,128]{1,0:T(8,128)S(1)}) custom-call(f32[4,8]{1,0:T(4,128)S(1)} %pad_maximum_fusion.1.par_ref, f32[4]{0:T(128)S(1)} %convert_multiply_fusion.w_ref, s32[5]{0:T(128)S(1)} %stack.38.pos_ref, ...), custom_call_target="tpu_custom_call" | custom-call | flops 10000000 | bytes 10000000 | tf_op jit(solution)/shard_map/pallas_call | solution.py:73
  96.2 0.1 collective-permute-start.18
  96.3 2.0 %collective-permute-start.19 = (f32[1152,128]{1,0:T(8,128)S(1)}, f32[1152,128]{1,0:T(8,128)S(1)}, u32[]{:S(2)}, u32[]{:S(2)}) collective-permute-start(f32[1152,128]{1,0:T(8,128)S(1)} %get-tuple-element.61), channel_id=1, source_target_pairs={{0,6},{2,4},{4,2},{6,0},{1,7},{3,5},{5,3},{7,1},{8,14},{10,12},{12... | collective-permute-start | bytes 1769480 | tf_op jit(solution)/shard_map/ppermute | solution.py:40
  98.3 0.4 collective-permute-start.20
  98.7 1.1 collective-permute-start.21
  99.9 7.5 %shard_map.88.u_in = f32[9216,128]{1,0:T(8,128)S(1)} custom-call(f32[4,8]{1,0:T(4,128)S(1)} %pad_maximum_fusion.1.par_ref, f32[4]{0:T(128)S(1)} %convert_multiply_fusion.w_ref, f32[24,28,24,128]{3,2,1,0:T(8,128)S(1)} %get-tuple-element.59.refs_0_, f32[24,28,24,128]{3,2,1,0:T(8,128)S(1)} %get-tuple-element.53.refs_0_.refs_1_, ...), custom_call_target="tpu_custom_call" | custom-call | flops 60000000 | bytes 10000000 | tf_op jit(solution)/shard_map/pallas_call | solution.py:73
  107.3 0.4 collective-permute-done.18.za_in
  107.8 1.0 collective-permute-done.19.zb_in
  108.7 2.3 %shard_map.89 = (f32[24,28,24,128]{3,2,1,0:T(8,128)S(1)}, f32[1152,128]{1,0:T(8,128)S(1)}, f32[1152,128]{1,0:T(8,128)S(1)}, f32[768,128]{1,0:T(8,128)S(1)}, f32[768,128]{1,0:T(8,128)S(1)}) custom-call(f32[4,8]{1,0:T(4,128)S(1)} %pad_maximum_fusion.1.par_ref, f32[4]{0:T(128)S(1)} %convert_multiply_fusion.w_ref, s32[5]{0:T(128)S(1)} %stack.38.pos_ref, ...), custom_call_target="tpu_custom_call" | custom-call | flops 10000000 | bytes 10000000 | tf_op jit(solution)/shard_map/pallas_call | solution.py:73
  111.0 0.3 collective-permute-start.22
  111.4 2.0 %collective-permute-start.23 = (f32[1152,128]{1,0:T(8,128)S(1)}, f32[1152,128]{1,0:T(8,128)S(1)}, u32[]{:S(2)}, u32[]{:S(2)}) collective-permute-start(f32[1152,128]{1,0:T(8,128)S(1)} %get-tuple-element.66), channel_id=1, source_target_pairs={{0,6},{2,4},{4,2},{6,0},{1,7},{3,5},{5,3},{7,1},{8,14},{10,12},{12... | collective-permute-start | bytes 1769480 | tf_op jit(solution)/shard_map/ppermute | solution.py:40
  113.4 1.2 collective-permute-start.25
  114.6 8.4 %shard_map.90.d_in = f32[768,128]{1,0:T(8,128)S(1)} custom-call(f32[4,8]{1,0:T(4,128)S(1)} %pad_maximum_fusion.1.par_ref, f32[4]{0:T(128)S(1)} %convert_multiply_fusion.w_ref, f32[24,28,24,128]{3,2,1,0:T(8,128)S(1)} %get-tuple-element.64.refs_0_, f32[24,28,24,128]{3,2,1,0:T(8,128)S(1)} %get-tuple-element.53.refs_0_.refs_1_, ...), custom_call_target="tpu_custom_call" | custom-call | flops 60000000 | bytes 10000000 | tf_op jit(solution)/shard_map/pallas_call | solution.py:73
  123.1 2.6 %shard_map.91 = (f32[2,8,2304]{2,1,0:T(8,128)S(1)}, f32[2,8,2304]{2,1,0:T(8,128)S(1)}) custom-call(f32[4,8]{1,0:T(4,128)S(1)} %pad_maximum_fusion.1.par_ref, f32[4]{0:T(128)S(1)} %convert_multiply_fusion.w_ref, s32[5]{0:T(128)S(1)} %stack.38.pos_ref, f32[768,128]{1,0:T(8,128)S(1)} %shard_map.90.d_in, f32[1152,128]{1,0:T(8,128)S(1)} %collective-permute-done.22.za, ...), custom_call_target="tpu_custom_call" | custom-call | flops 10000000 | bytes 10000000 | tf_op jit(solution)/shard_map/pallas_call | solution.py:73
  125.7 5.4 %collective-permute-start.26 = (f32[2,8,2304]{2,1,0:T(8,128)S(1)}, f32[2,8,2304]{2,1,0:T(8,128)S(1)}, u32[]{:S(2)}, u32[]{:S(2)}) collective-permute-start(f32[2,8,2304]{2,1,0:T(8,128)S(1)} %get-tuple-element.70), channel_id=1, source_target_pairs={{0,8},{8,0},{1,9},{9,1},{2,10},{10,2},{3,11},{11,3},{4,12},{12,4},... | collective-permute-start | bytes 442376 | tf_op jit(solution)/shard_map/ppermute | solution.py:32
  131.1 1.0 collective-permute-done.26.b
  132.1 2.1 %collective-permute-start.29 = (f32[2,8,2304]{2,1,0:T(8,128)S(1)}, f32[2,8,2304]{2,1,0:T(8,128)S(1)}, u32[]{:S(2)}, u32[]{:S(2)}) collective-permute-start(f32[2,8,2304]{2,1,0:T(8,128)S(1)} %shard_map.92.s0), channel_id=1, source_target_pairs={{0,48},{16,32},{32,16},{48,0},{1,49},{17,33},{33,17},{49,1},{2,50}... | collective-permute-start | bytes 442376 | tf_op jit(solution)/shard_map/ppermute | solution.py:36
  134.3 1.2 collective-permute-start.27
  135.5 4.6 %collective-permute-done.29.s3 = f32[2,8,2304]{2,1,0:T(8,128)S(1)} collective-permute-done((f32[2,8,2304]{2,1,0:T(8,128)S(1)}, f32[2,8,2304]{2,1,0:T(8,128)S(1)}, u32[]{:S(2)}, u32[]{:S(2)}) %collective-permute-start.29) | collective-permute-done | bytes 147488 | tf_op jit(solution)/shard_map/ppermute | solution.py:36
  140.1 0.6 collective-permute-done.28.s2
  140.6 1.4 collective-permute-done.27.s1
  142.0 0.6 shard_map.93
  142.6 1.9 %collective-permute-start.32 = (f32[8,2304]{1,0:T(8,128)S(1)}, f32[8,2304]{1,0:T(8,128)S(1)}, u32[]{:S(2)}, u32[]{:S(2)}) collective-permute-start(f32[8,2304]{1,0:T(8,128)S(1)} %get-tuple-element.72), channel_id=1, source_target_pairs={{0,65},{64,1},{1,64},{65,0},{2,67},{66,3},{3,66},{67,2},{4,69},{68... | collective-permute-start | bytes 221192 | tf_op jit(solution)/shard_map/ppermute | solution.py:28
  144.5 1.1 collective-permute-start.31
  145.6 0.3 collective-permute-start.30
  145.9 2.3 %collective-permute-start.33 = (f32[8,2304]{1,0:T(8,128)S(1)}, f32[8,2304]{1,0:T(8,128)S(1)}, u32[]{:S(2)}, u32[]{:S(2)}) collective-permute-start(f32[8,2304]{1,0:T(8,128)S(1)} %get-tuple-element.71.refs_0_), channel_id=1, source_target_pairs={{0,8},{8,0},{1,9},{9,1},{2,10},{10,2},{3,11},{11,3},{4,12},{12,4},... | collective-permute-start | bytes 221192 | tf_op jit(solution)/shard_map/ppermute | solution.py:32
  148.2 2.3 %collective-permute-start.36 = (f32[8,2304]{1,0:T(8,128)S(1)}, f32[8,2304]{1,0:T(8,128)S(1)}, u32[]{:S(2)}, u32[]{:S(2)}) collective-permute-start(f32[8,2304]{1,0:T(8,128)S(1)} %collective-permute-done.32.refs_3_), channel_id=1, source_target_pairs={{0,8},{8,0},{1,9},{9,1},{2,10},{10,2},{3,11},{11,3},{4,12},{12,4},... | collective-permute-start | bytes 221192 | tf_op jit(solution)/shard_map/ppermute | solution.py:32
  150.5 1.6 %collective-permute-start.35 = (f32[8,2304]{1,0:T(8,128)S(1)}, f32[8,2304]{1,0:T(8,128)S(1)}, u32[]{:S(2)}, u32[]{:S(2)}) collective-permute-start(f32[8,2304]{1,0:T(8,128)S(1)} %collective-permute-done.31.refs_2_), channel_id=1, source_target_pairs={{0,8},{8,0},{1,9},{9,1},{2,10},{10,2},{3,11},{11,3},{4,12},{12,4},... | collective-permute-start | bytes 221192 | tf_op jit(solution)/shard_map/ppermute | solution.py:32
  152.1 0.9 collective-permute-done.35.refs_6_
  153.0 0.4 collective-permute-done.34.refs_5_
  153.4 1.4 place.1
  (44 shorter events, 0.2 us)
Async XLA Ops:
  0.0 61.6 %copy-start = (f32[2,3,2,8,9216]{4,3,2,1,0:T(8,128)S(1)}, f32[2,3,2,8,9216]{4,3,2,1,0:T(8,128)}, u32[]{:S(2)}) copy-start(f32[2,3,2,8,9216]{4,3,2,1,0:T(8,128)} %o0.3) | copy-start | bytes 10616836
  0.1 61.6 %copy-start.1 = (f32[2,8,9216]{2,1,0:T(8,128)S(1)}, f32[2,8,9216]{2,1,0:T(8,128)}, u32[]{:S(2)}) copy-start(f32[2,8,9216]{2,1,0:T(8,128)} %refs_0_.1) | copy-start | bytes 1769476
  2.7 70.8 %copy-start.3 = (f32[8,9216]{1,0:T(8,128)S(1)}, f32[8,9216]{1,0:T(8,128)}, u32[]{:S(2)}) copy-start(f32[8,9216]{1,0:T(8,128)} %pot.3) | copy-start | bytes 884740
  2.7 58.9 %collective-permute-start.1 = (f32[2,3,2,8,2304]{4,3,2,1,0:T(8,128)S(1)}, f32[2,3,2,8,2304]{4,3,2,1,0:T(8,128)S(1)}, u32[]{:S(2)}, u32[]{:S(2)}) collective-permute-start(f32[2,3,2,8,2304]{4,3,2,1,0:T(8,128)S(1)} %get-tuple-element.41), channel_id=1, source_target_pairs={{0,64},{64,0},{1,65},{65,1},{2,66},{66,2},{3,67},{67,3},{4,68},{68... | collective-permute-start | bytes 2654216 | tf_op jit(solution)/shard_map/ppermute | solution.py:28
  5.3 58.1 %collective-permute-start.2 = (f32[2,3,2,8,2304]{4,3,2,1,0:T(8,128)S(1)}, f32[2,3,2,8,2304]{4,3,2,1,0:T(8,128)S(1)}, u32[]{:S(2)}, u32[]{:S(2)}) collective-permute-start(f32[2,3,2,8,2304]{4,3,2,1,0:T(8,128)S(1)} %get-tuple-element.42), channel_id=1, source_target_pairs={{0,1},{64,65},{1,0},{65,64},{2,3},{66,67},{3,2},{67,66},{4,5},{68,... | collective-permute-start | bytes 2654216 | tf_op jit(solution)/shard_map/ppermute | solution.py:28
  8.6 54.8 %collective-permute-start.3 = (f32[2,3,2,8,2304]{4,3,2,1,0:T(8,128)S(1)}, f32[2,3,2,8,2304]{4,3,2,1,0:T(8,128)S(1)}, u32[]{:S(2)}, u32[]{:S(2)}) collective-permute-start(f32[2,3,2,8,2304]{4,3,2,1,0:T(8,128)S(1)} %get-tuple-element.43), channel_id=1, source_target_pairs={{0,65},{64,1},{1,64},{65,0},{2,67},{66,3},{3,66},{67,2},{4,69},{68... | collective-permute-start | bytes 2654216 | tf_op jit(solution)/shard_map/ppermute | solution.py:28
  8.6 41.0 %collective-permute-start = (f32[8,1280]{1,0:T(8,128)S(1)}, f32[8,1280]{1,0:T(8,128)S(1)}, u32[]{:S(2)}, u32[]{:S(2)}) collective-permute-start(f32[8,1280]{1,0:T(8,128)S(1)} %get-tuple-element.40), channel_id=1, source_target_pairs={{0,65},{64,1},{1,64},{65,0},{2,67},{66,3},{3,66},{67,2},{4,69},{68... | collective-permute-start | bytes 122888 | tf_op jit(solution)/shard_map/ppermute | solution.py:28
  49.6 4.1 %collective-permute-start.6 = (f32[8,1280]{1,0:T(8,128)S(1)}, f32[8,1280]{1,0:T(8,128)S(1)}, u32[]{:S(2)}, u32[]{:S(2)}) collective-permute-start(f32[8,1280]{1,0:T(8,128)S(1)} %collective-permute-done), channel_id=1, source_target_pairs={{0,48},{16,32},{32,16},{48,0},{1,49},{17,33},{33,17},{49,1},{2,50}... | collective-permute-start | bytes 122888 | tf_op jit(solution)/shard_map/ppermute | solution.py:36
  52.1 4.5 %collective-permute-start.5 = (f32[8,1280]{1,0:T(8,128)S(1)}, f32[8,1280]{1,0:T(8,128)S(1)}, u32[]{:S(2)}, u32[]{:S(2)}) collective-permute-start(f32[8,1280]{1,0:T(8,128)S(1)} %collective-permute-done), channel_id=1, source_target_pairs={{0,32},{16,48},{32,0},{48,16},{1,33},{17,49},{33,1},{49,17},{2,34}... | collective-permute-start | bytes 122888 | tf_op jit(solution)/shard_map/ppermute | solution.py:36
  53.6 3.1 %collective-permute-start.4 = (f32[8,1280]{1,0:T(8,128)S(1)}, f32[8,1280]{1,0:T(8,128)S(1)}, u32[]{:S(2)}, u32[]{:S(2)}) collective-permute-start(f32[8,1280]{1,0:T(8,128)S(1)} %collective-permute-done), channel_id=1, source_target_pairs={{0,16},{16,0},{32,48},{48,32},{1,17},{17,1},{33,49},{49,33},{2,18}... | collective-permute-start | bytes 122888 | tf_op jit(solution)/shard_map/ppermute | solution.py:36
  56.8 6.5 %collective-permute-start.7 = (f32[4,8,1280]{2,1,0:T(8,128)S(1)}, f32[4,8,1280]{2,1,0:T(8,128)S(1)}, u32[]{:S(2)}, u32[]{:S(2)}) collective-permute-start(f32[4,8,1280]{2,1,0:T(8,128)S(1)} %pad_maximum_fusion.got.refs_0_), channel_id=1, source_target_pairs={{0,8},{8,0},{1,9},{9,1},{2,10},{10,2},{3,11},{11,3},{4,12},{12,4},... | collective-permute-start | bytes 491528 | tf_op jit(solution)/shard_map/ppermute | solution.py:32
  65.3 3.8 %collective-permute-start.10 = (f32[16,128]{1,0:T(8,128)S(1)}, f32[16,128]{1,0:T(8,128)S(1)}, u32[]{:S(2)}, u32[]{:S(2)}) collective-permute-start(f32[16,128]{1,0:T(8,128)S(1)} %shard_map.84), channel_id=1, source_target_pairs={{0,65},{64,1},{1,64},{65,0},{2,67},{66,3},{3,66},{67,2},{4,69},{68... | collective-permute-start | bytes 24584 | tf_op jit(solution)/shard_map/ppermute | solution.py:28
  65.4 4.7 %collective-permute-start.9 = (f32[16,128]{1,0:T(8,128)S(1)}, f32[16,128]{1,0:T(8,128)S(1)}, u32[]{:S(2)}, u32[]{:S(2)}) collective-permute-start(f32[16,128]{1,0:T(8,128)S(1)} %shard_map.84), channel_id=1, source_target_pairs={{0,1},{64,65},{1,0},{65,64},{2,3},{66,67},{3,2},{67,66},{4,5},{68,... | collective-permute-start | bytes 24584 | tf_op jit(solution)/shard_map/ppermute | solution.py:28
  65.5 4.6 %collective-permute-start.8 = (f32[16,128]{1,0:T(8,128)S(1)}, f32[16,128]{1,0:T(8,128)S(1)}, u32[]{:S(2)}, u32[]{:S(2)}) collective-permute-start(f32[16,128]{1,0:T(8,128)S(1)} %shard_map.84), channel_id=1, source_target_pairs={{0,64},{64,0},{1,65},{65,1},{2,66},{66,2},{3,67},{67,3},{4,68},{68... | collective-permute-start | bytes 24584 | tf_op jit(solution)/shard_map/ppermute | solution.py:28
  70.0 5.8 %collective-permute-start.13 = (f32[16,128]{1,0:T(8,128)S(1)}, f32[16,128]{1,0:T(8,128)S(1)}, u32[]{:S(2)}, u32[]{:S(2)}) collective-permute-start(f32[16,128]{1,0:T(8,128)S(1)} %fusion.1.s0), channel_id=1, source_target_pairs={{0,6},{2,4},{4,2},{6,0},{1,7},{3,5},{5,3},{7,1},{8,14},{10,12},{12... | collective-permute-start | bytes 24584 | tf_op jit(solution)/shard_map/ppermute | solution.py:40
  72.9 4.0 %collective-permute-start.12 = (f32[16,128]{1,0:T(8,128)S(1)}, f32[16,128]{1,0:T(8,128)S(1)}, u32[]{:S(2)}, u32[]{:S(2)}) collective-permute-start(f32[16,128]{1,0:T(8,128)S(1)} %fusion.1.s0), channel_id=1, source_target_pairs={{0,4},{2,6},{4,0},{6,2},{1,5},{3,7},{5,1},{7,3},{8,12},{10,14},{12... | collective-permute-start | bytes 24584 | tf_op jit(solution)/shard_map/ppermute | solution.py:40
  73.2 3.7 %collective-permute-start.11 = (f32[16,128]{1,0:T(8,128)S(1)}, f32[16,128]{1,0:T(8,128)S(1)}, u32[]{:S(2)}, u32[]{:S(2)}) collective-permute-start(f32[16,128]{1,0:T(8,128)S(1)} %fusion.1.s0), channel_id=1, source_target_pairs={{0,2},{2,0},{4,6},{6,4},{1,3},{3,1},{5,7},{7,5},{8,10},{10,8},{12,... | collective-permute-start | bytes 24584 | tf_op jit(solution)/shard_map/ppermute | solution.py:40
  76.9 7.4 %copy-start.4 = (s32[4]{0:T(128)S(1)}, s32[4]{0:T(128)}, u32[]{:S(2)}) copy-start(s32[4]{0:T(128)} %param.14) | copy-start | bytes 52
  76.9 7.4 %copy-start.2 = (bf16[256,256]{1,0:T(8,128)(2,1)S(1)}, bf16[256,256]{1,0:T(8,128)(2,1)}, u32[]{:S(2)}) copy-start(bf16[256,256]{1,0:T(8,128)(2,1)} %constant.26.clone.refs_2_.refs_3_) | copy-start | bytes 393220
  80.2 12.4 %collective-permute-start.14 = (f32[1152,128]{1,0:T(8,128)S(1)}, f32[1152,128]{1,0:T(8,128)S(1)}, u32[]{:S(2)}, u32[]{:S(2)}) collective-permute-start(f32[1152,128]{1,0:T(8,128)S(1)} %get-tuple-element.55), channel_id=1, source_target_pairs={{0,2},{2,0},{4,6},{6,4},{1,3},{3,1},{5,7},{7,5},{8,10},{10,8},{12,... | collective-permute-start | bytes 1769480 | tf_op jit(solution)/shard_map/ppermute | solution.py:40
  80.4 13.5 %collective-permute-start.15 = (f32[1152,128]{1,0:T(8,128)S(1)}, f32[1152,128]{1,0:T(8,128)S(1)}, u32[]{:S(2)}, u32[]{:S(2)}) collective-permute-start(f32[1152,128]{1,0:T(8,128)S(1)} %get-tuple-element.56), channel_id=1, source_target_pairs={{0,6},{2,4},{4,2},{6,0},{1,7},{3,5},{5,3},{7,1},{8,14},{10,12},{12... | collective-permute-start | bytes 1769480 | tf_op jit(solution)/shard_map/ppermute | solution.py:40
  82.3 9.1 %collective-permute-start.16 = (f32[768,128]{1,0:T(8,128)S(1)}, f32[768,128]{1,0:T(8,128)S(1)}, u32[]{:S(2)}, u32[]{:S(2)}) collective-permute-start(f32[768,128]{1,0:T(8,128)S(1)} %get-tuple-element.57), channel_id=1, source_target_pairs={{0,64},{64,0},{1,65},{65,1},{2,66},{66,2},{3,67},{67,3},{4,68},{68... | collective-permute-start | bytes 1179656 | tf_op jit(solution)/shard_map/ppermute | solution.py:28
  83.4 8.1 %collective-permute-start.17 = (f32[768,128]{1,0:T(8,128)S(1)}, f32[768,128]{1,0:T(8,128)S(1)}, u32[]{:S(2)}, u32[]{:S(2)}) collective-permute-start(f32[768,128]{1,0:T(8,128)S(1)} %get-tuple-element.58), channel_id=1, source_target_pairs={{0,65},{64,1},{1,64},{65,0},{2,67},{66,3},{3,66},{67,2},{4,69},{68... | collective-permute-start | bytes 1179656 | tf_op jit(solution)/shard_map/ppermute | solution.py:28
  96.2 11.5 %collective-permute-start.18 = (f32[1152,128]{1,0:T(8,128)S(1)}, f32[1152,128]{1,0:T(8,128)S(1)}, u32[]{:S(2)}, u32[]{:S(2)}) collective-permute-start(f32[1152,128]{1,0:T(8,128)S(1)} %get-tuple-element.60), channel_id=1, source_target_pairs={{0,2},{2,0},{4,6},{6,4},{1,3},{3,1},{5,7},{7,5},{8,10},{10,8},{12,... | collective-permute-start | bytes 1769480 | tf_op jit(solution)/shard_map/ppermute | solution.py:40
  96.3 12.4 %collective-permute-start.19 = (f32[1152,128]{1,0:T(8,128)S(1)}, f32[1152,128]{1,0:T(8,128)S(1)}, u32[]{:S(2)}, u32[]{:S(2)}) collective-permute-start(f32[1152,128]{1,0:T(8,128)S(1)} %get-tuple-element.61), channel_id=1, source_target_pairs={{0,6},{2,4},{4,2},{6,0},{1,7},{3,5},{5,3},{7,1},{8,14},{10,12},{12... | collective-permute-start | bytes 1769480 | tf_op jit(solution)/shard_map/ppermute | solution.py:40
  98.3 9.0 %collective-permute-start.20 = (f32[768,128]{1,0:T(8,128)S(1)}, f32[768,128]{1,0:T(8,128)S(1)}, u32[]{:S(2)}, u32[]{:S(2)}) collective-permute-start(f32[768,128]{1,0:T(8,128)S(1)} %get-tuple-element.62), channel_id=1, source_target_pairs={{0,64},{64,0},{1,65},{65,1},{2,66},{66,2},{3,67},{67,3},{4,68},{68... | collective-permute-start | bytes 1179656 | tf_op jit(solution)/shard_map/ppermute | solution.py:28
  98.7 8.6 %collective-permute-start.21 = (f32[768,128]{1,0:T(8,128)S(1)}, f32[768,128]{1,0:T(8,128)S(1)}, u32[]{:S(2)}, u32[]{:S(2)}) collective-permute-start(f32[768,128]{1,0:T(8,128)S(1)} %get-tuple-element.63), channel_id=1, source_target_pairs={{0,65},{64,1},{1,64},{65,0},{2,67},{66,3},{3,66},{67,2},{4,69},{68... | collective-permute-start | bytes 1179656 | tf_op jit(solution)/shard_map/ppermute | solution.py:28
  111.0 12.0 %collective-permute-start.22 = (f32[1152,128]{1,0:T(8,128)S(1)}, f32[1152,128]{1,0:T(8,128)S(1)}, u32[]{:S(2)}, u32[]{:S(2)}) collective-permute-start(f32[1152,128]{1,0:T(8,128)S(1)} %get-tuple-element.65), channel_id=1, source_target_pairs={{0,2},{2,0},{4,6},{6,4},{1,3},{3,1},{5,7},{7,5},{8,10},{10,8},{12,... | collective-permute-start | bytes 1769480 | tf_op jit(solution)/shard_map/ppermute | solution.py:40
  111.4 11.7 %collective-permute-start.23 = (f32[1152,128]{1,0:T(8,128)S(1)}, f32[1152,128]{1,0:T(8,128)S(1)}, u32[]{:S(2)}, u32[]{:S(2)}) collective-permute-start(f32[1152,128]{1,0:T(8,128)S(1)} %get-tuple-element.66), channel_id=1, source_target_pairs={{0,6},{2,4},{4,2},{6,0},{1,7},{3,5},{5,3},{7,1},{8,14},{10,12},{12... | collective-permute-start | bytes 1769480 | tf_op jit(solution)/shard_map/ppermute | solution.py:40
  113.4 9.7 %collective-permute-start.24 = (f32[768,128]{1,0:T(8,128)S(1)}, f32[768,128]{1,0:T(8,128)S(1)}, u32[]{:S(2)}, u32[]{:S(2)}) collective-permute-start(f32[768,128]{1,0:T(8,128)S(1)} %get-tuple-element.67), channel_id=1, source_target_pairs={{0,64},{64,0},{1,65},{65,1},{2,66},{66,2},{3,67},{67,3},{4,68},{68... | collective-permute-start | bytes 1179656 | tf_op jit(solution)/shard_map/ppermute | solution.py:28
  113.4 9.7 %collective-permute-start.25 = (f32[768,128]{1,0:T(8,128)S(1)}, f32[768,128]{1,0:T(8,128)S(1)}, u32[]{:S(2)}, u32[]{:S(2)}) collective-permute-start(f32[768,128]{1,0:T(8,128)S(1)} %get-tuple-element.68), channel_id=1, source_target_pairs={{0,65},{64,1},{1,64},{65,0},{2,67},{66,3},{3,66},{67,2},{4,69},{68... | collective-permute-start | bytes 1179656 | tf_op jit(solution)/shard_map/ppermute | solution.py:28
  125.7 6.4 %collective-permute-start.26 = (f32[2,8,2304]{2,1,0:T(8,128)S(1)}, f32[2,8,2304]{2,1,0:T(8,128)S(1)}, u32[]{:S(2)}, u32[]{:S(2)}) collective-permute-start(f32[2,8,2304]{2,1,0:T(8,128)S(1)} %get-tuple-element.70), channel_id=1, source_target_pairs={{0,8},{8,0},{1,9},{9,1},{2,10},{10,2},{3,11},{11,3},{4,12},{12,4},... | collective-permute-start | bytes 442376 | tf_op jit(solution)/shard_map/ppermute | solution.py:32
  132.1 7.9 %collective-permute-start.29 = (f32[2,8,2304]{2,1,0:T(8,128)S(1)}, f32[2,8,2304]{2,1,0:T(8,128)S(1)}, u32[]{:S(2)}, u32[]{:S(2)}) collective-permute-start(f32[2,8,2304]{2,1,0:T(8,128)S(1)} %shard_map.92.s0), channel_id=1, source_target_pairs={{0,48},{16,32},{32,16},{48,0},{1,49},{17,33},{33,17},{49,1},{2,50}... | collective-permute-start | bytes 442376 | tf_op jit(solution)/shard_map/ppermute | solution.py:36
  134.3 6.4 %collective-permute-start.28 = (f32[2,8,2304]{2,1,0:T(8,128)S(1)}, f32[2,8,2304]{2,1,0:T(8,128)S(1)}, u32[]{:S(2)}, u32[]{:S(2)}) collective-permute-start(f32[2,8,2304]{2,1,0:T(8,128)S(1)} %shard_map.92.s0), channel_id=1, source_target_pairs={{0,32},{16,48},{32,0},{48,16},{1,33},{17,49},{33,1},{49,17},{2,34}... | collective-permute-start | bytes 442376 | tf_op jit(solution)/shard_map/ppermute | solution.py:36
  134.3 7.8 %collective-permute-start.27 = (f32[2,8,2304]{2,1,0:T(8,128)S(1)}, f32[2,8,2304]{2,1,0:T(8,128)S(1)}, u32[]{:S(2)}, u32[]{:S(2)}) collective-permute-start(f32[2,8,2304]{2,1,0:T(8,128)S(1)} %shard_map.92.s0), channel_id=1, source_target_pairs={{0,16},{16,0},{32,48},{48,32},{1,17},{17,1},{33,49},{49,33},{2,18}... | collective-permute-start | bytes 442376 | tf_op jit(solution)/shard_map/ppermute | solution.py:36
  142.6 5.6 %collective-permute-start.32 = (f32[8,2304]{1,0:T(8,128)S(1)}, f32[8,2304]{1,0:T(8,128)S(1)}, u32[]{:S(2)}, u32[]{:S(2)}) collective-permute-start(f32[8,2304]{1,0:T(8,128)S(1)} %get-tuple-element.72), channel_id=1, source_target_pairs={{0,65},{64,1},{1,64},{65,0},{2,67},{66,3},{3,66},{67,2},{4,69},{68... | collective-permute-start | bytes 221192 | tf_op jit(solution)/shard_map/ppermute | solution.py:28
  144.5 6.0 %collective-permute-start.31 = (f32[8,2304]{1,0:T(8,128)S(1)}, f32[8,2304]{1,0:T(8,128)S(1)}, u32[]{:S(2)}, u32[]{:S(2)}) collective-permute-start(f32[8,2304]{1,0:T(8,128)S(1)} %get-tuple-element.72), channel_id=1, source_target_pairs={{0,1},{64,65},{1,0},{65,64},{2,3},{66,67},{3,2},{67,66},{4,5},{68,... | collective-permute-start | bytes 221192 | tf_op jit(solution)/shard_map/ppermute | solution.py:28
  145.6 6.5 %collective-permute-start.30 = (f32[8,2304]{1,0:T(8,128)S(1)}, f32[8,2304]{1,0:T(8,128)S(1)}, u32[]{:S(2)}, u32[]{:S(2)}) collective-permute-start(f32[8,2304]{1,0:T(8,128)S(1)} %get-tuple-element.71.refs_0_), channel_id=1, source_target_pairs={{0,64},{64,0},{1,65},{65,1},{2,66},{66,2},{3,67},{67,3},{4,68},{68... | collective-permute-start | bytes 221192 | tf_op jit(solution)/shard_map/ppermute | solution.py:28
  145.9 6.2 %collective-permute-start.33 = (f32[8,2304]{1,0:T(8,128)S(1)}, f32[8,2304]{1,0:T(8,128)S(1)}, u32[]{:S(2)}, u32[]{:S(2)}) collective-permute-start(f32[8,2304]{1,0:T(8,128)S(1)} %get-tuple-element.71.refs_0_), channel_id=1, source_target_pairs={{0,8},{8,0},{1,9},{9,1},{2,10},{10,2},{3,11},{11,3},{4,12},{12,4},... | collective-permute-start | bytes 221192 | tf_op jit(solution)/shard_map/ppermute | solution.py:32
  148.2 3.9 %collective-permute-start.36 = (f32[8,2304]{1,0:T(8,128)S(1)}, f32[8,2304]{1,0:T(8,128)S(1)}, u32[]{:S(2)}, u32[]{:S(2)}) collective-permute-start(f32[8,2304]{1,0:T(8,128)S(1)} %collective-permute-done.32.refs_3_), channel_id=1, source_target_pairs={{0,8},{8,0},{1,9},{9,1},{2,10},{10,2},{3,11},{11,3},{4,12},{12,4},... | collective-permute-start | bytes 221192 | tf_op jit(solution)/shard_map/ppermute | solution.py:32
  150.5 2.5 %collective-permute-start.35 = (f32[8,2304]{1,0:T(8,128)S(1)}, f32[8,2304]{1,0:T(8,128)S(1)}, u32[]{:S(2)}, u32[]{:S(2)}) collective-permute-start(f32[8,2304]{1,0:T(8,128)S(1)} %collective-permute-done.31.refs_2_), channel_id=1, source_target_pairs={{0,8},{8,0},{1,9},{9,1},{2,10},{10,2},{3,11},{11,3},{4,12},{12,4},... | collective-permute-start | bytes 221192 | tf_op jit(solution)/shard_map/ppermute | solution.py:32
  152.1 1.3 collective-permute-start.34

commit v8 on v7

--- a/solution.py
+++ b/solution.py
@@ -317,7 +317,10 @@
 
 
 def exchange(za, zb, ya, yb):
-    return y_xor(za, 1), y_xor(zb, 3), z_xor(ya, 1), z_xor(yb, 3)
+    got = []
+    for move, value, m in ((y_xor, za, 1), (y_xor, zb, 3), (z_xor, ya, 1), (z_xor, yb, 3)):
+        got.append(move(value, m))
+    return got
 
 
 def right_kernel(ncells, slot_ref, pos_ref, s0, s1, s2, s3, orb_ref, w_ref, r_ref, za, zb, ya, yb, prod_ref):
@@ -356,7 +359,7 @@
         cut_rows(r_ref, pos_ref, kn, ya, yb)
         return carry
 
-    lax.fori_loop(0, 12, cut, 0)
+    lax.fori_loop(0, 12, cut, 0, unroll=4)
 
 
 def right_sides(ncells, slots, pos, sums, orb, w):
@@ -576,7 +579,7 @@
         faces(ITERS - 1, par_ref, w_ref, pos_ref, kn, za, zb, ya, yb, add_plane, add_row)
         return carry
 
-    lax.fori_loop(0, 12, orbital, 0)
+    lax.fori_loop(0, 12, orbital, 0, unroll=4)
     ids = lane_ids()
     core = pos_ref[3]
     for ref, c in ((send_ref, 1 - core), (keep_ref, core)):

time: 155 us -> 155 us (level)
  no operation moved by 1% of the time
where the time goes in v8:
time: 155 us
  waiting for transfers between devices  57.7 us (37%)
  starting transfers between devices  52.5 us (34%)
  Pallas kernels  44.1 us (28%)
    pallas_call x12, Pallas kernels, call(): pl.pallas_call(kernel, in_specs=specs, out_specs=[pl.BlockSpec(memory_spa...  40 us
    ppermute x16, waiting for transfers between devices, z_xor(): return lax.ppermute(value, ZAX, z_perm(lambda z: z ^ m))  39.9 us
    ppermute x16, starting transfers between devices, z_xor(): return lax.ppermute(value, ZAX, z_perm(lambda z: z ^ m))  19.9 us
    ppermute x6, starting transfers between devices, other_core(): return lax.ppermute(value, 'c', [(0, 1), (1, 0)])  16.3 us
    ppermute x6, waiting for transfers between devices, x_xor(): return lax.ppermute(value, 'x', [(i, i ^ m) for i in range(4)])  10.8 us
    ppermute x9, starting transfers between devices, y_xor(): return lax.ppermute(value, 'y', [(i, i ^ m) for i in range(4)])  9.98 us
    ppermute x6, starting transfers between devices, x_xor(): return lax.ppermute(value, 'x', [(i, i ^ m) for i in range(4)])  6.33 us
    ppermute x9, waiting for transfers between devices, y_xor(): return lax.ppermute(value, 'y', [(i, i ^ m) for i in range(4)])  4.83 us
  transfers between devices with their start and end apart: 37, of which 18 were waited for; matrix products, arithmetic and copies ran while one was open for 0% of the time, Pallas kernels for 17%

profile of v8, /device:TPU:1, one launch (start us, length us, event | category | flops | bytes accessed | tf_op | source)
XLA Modules:
  0.0 155.0 jit_solution(1694945470740293170)
XLA Ops:
  0.0 0.1 stack.38.pos_ref
  0.1 2.6 %cut.1 = (f32[2,3,2,8,2304]{4,3,2,1,0:T(8,128)S(1)}, f32[2,3,2,8,2304]{4,3,2,1,0:T(8,128)S(1)}, f32[2,3,2,8,2304]{4,3,2,1,0:T(8,128)S(1)}, f32[8,1280]{1,0:T(8,128)S(1)}, f32[8,128]{1,0:T(8,128)S(1)}) custom-call(s32[5]{0:T(128)S(1)} %stack.38.pos_ref, f32[2,3,2,8,9216]{4,3,2,1,0:T(8,128)} %o0.3, f32[2,8,9216]{2,1,0:T(8,128)} %refs_0_.1, f32[8,9216]{1,0:T(8,128)} %pot.3, ...), custom_call_target="tpu_custom_call" | custom-call | tf_op jit(solution)/shard_map/cut/pallas_call | solution.py:136
  2.7 2.5 %collective-permute-start.1 = (f32[2,3,2,8,2304]{4,3,2,1,0:T(8,128)S(1)}, f32[2,3,2,8,2304]{4,3,2,1,0:T(8,128)S(1)}, u32[]{:S(2)}, u32[]{:S(2)}) collective-permute-start(f32[2,3,2,8,2304]{4,3,2,1,0:T(8,128)S(1)} %get-tuple-element.41), channel_id=1, source_target_pairs={{0,64},{64,0},{1,65},{65,1},{2,66},{66,2},{3,67},{67,3},{4,68},{68... | collective-permute-start | bytes 2654216 | tf_op jit(solution)/shard_map/ppermute | solution.py:28
  5.3 3.3 %collective-permute-start.2 = (f32[2,3,2,8,2304]{4,3,2,1,0:T(8,128)S(1)}, f32[2,3,2,8,2304]{4,3,2,1,0:T(8,128)S(1)}, u32[]{:S(2)}, u32[]{:S(2)}) collective-permute-start(f32[2,3,2,8,2304]{4,3,2,1,0:T(8,128)S(1)} %get-tuple-element.42), channel_id=1, source_target_pairs={{0,1},{64,65},{1,0},{65,64},{2,3},{66,67},{3,2},{67,66},{4,5},{68,... | collective-permute-start | bytes 2654216 | tf_op jit(solution)/shard_map/ppermute | solution.py:28
  8.6 2.7 %collective-permute-start = (f32[8,1280]{1,0:T(8,128)S(1)}, f32[8,1280]{1,0:T(8,128)S(1)}, u32[]{:S(2)}, u32[]{:S(2)}) collective-permute-start(f32[8,1280]{1,0:T(8,128)S(1)} %get-tuple-element.40), channel_id=1, source_target_pairs={{0,65},{64,1},{1,64},{65,0},{2,67},{66,3},{3,66},{67,2},{4,69},{68... | collective-permute-start | bytes 122888 | tf_op jit(solution)/shard_map/ppermute | solution.py:28
  11.2 38.3 %collective-permute-done = f32[8,1280]{1,0:T(8,128)S(1)} collective-permute-done((f32[8,1280]{1,0:T(8,128)S(1)}, f32[8,1280]{1,0:T(8,128)S(1)}, u32[]{:S(2)}, u32[]{:S(2)}) %collective-permute-start) | collective-permute-done | bytes 40992 | tf_op jit(solution)/shard_map/ppermute | solution.py:28
  49.6 2.5 %collective-permute-start.6 = (f32[8,1280]{1,0:T(8,128)S(1)}, f32[8,1280]{1,0:T(8,128)S(1)}, u32[]{:S(2)}, u32[]{:S(2)}) collective-permute-start(f32[8,1280]{1,0:T(8,128)S(1)} %collective-permute-done), channel_id=1, source_target_pairs={{0,48},{16,32},{32,16},{48,0},{1,49},{17,33},{33,17},{49,1},{2,50}... | collective-permute-start | bytes 122888 | tf_op jit(solution)/shard_map/ppermute | solution.py:36
  52.1 0.5 collective-permute-start.5
  52.6 1.1 collective-permute-done.6
  53.7 2.9 %collective-permute-done.5 = f32[8,1280]{1,0:T(8,128)S(1)} collective-permute-done((f32[8,1280]{1,0:T(8,128)S(1)}, f32[8,1280]{1,0:T(8,128)S(1)}, u32[]{:S(2)}, u32[]{:S(2)}) %collective-permute-start.5) | collective-permute-done | bytes 40992 | tf_op jit(solution)/shard_map/ppermute | solution.py:36
  56.5 0.3 collective-permute-done.4
  56.8 4.6 %collective-permute-start.7 = (f32[4,8,1280]{2,1,0:T(8,128)S(1)}, f32[4,8,1280]{2,1,0:T(8,128)S(1)}, u32[]{:S(2)}, u32[]{:S(2)}) collective-permute-start(f32[4,8,1280]{2,1,0:T(8,128)S(1)} %pad_maximum_fusion.got.refs_0_), channel_id=1, source_target_pairs={{0,8},{8,0},{1,9},{9,1},{2,10},{10,2},{3,11},{11,3},{4,12},{12,4},... | collective-permute-start | bytes 491528 | tf_op jit(solution)/shard_map/ppermute | solution.py:32
  61.4 0.2 convert_reduce_fusion.slot_ref
  61.6 1.7 %shard_map.83.refs_2_ = f32[80,128]{1,0:T(8,128)S(1)} custom-call(s32[5]{0:T(128)S(1)} %stack.38.pos_ref, s32[4]{0:T(128)S(1)} %convert_reduce_fusion.slot_ref, f32[2,3,2,8,9216]{4,3,2,1,0:T(8,128)S(1)} %copy-done, f32[2,3,2,8,2304]{4,3,2,1,0:T(8,128)S(1)} %collective-permute-done.1.o1, f32[2,8,9216]{2,1,0:T(8,128)S(1)} %copy-done.1), custom_call_target="tpu_custom_call" | custom-call | flops 20000000 | bytes 10000000 | tf_op jit(solution)/shard_map/pallas_call | solution.py:73
  63.4 1.9 %shard_map.84 = f32[16,128]{1,0:T(8,128)S(1)} custom-call(s32[5]{0:T(128)S(1)} %stack.38.pos_ref, s32[4]{0:T(128)S(1)} %convert_reduce_fusion.slot_ref, f32[2,3,2,8,2304]{4,3,2,1,0:T(8,128)S(1)} %collective-permute-done.2.o2.o0, f32[2,3,2,8,2304]{4,3,2,1,0:T(8,128)S(1)} %collective-permute-done.3.o3.o1, f32[4,8,1280]{2,1,0:T(8,128)S(1)} %pad_maximum_fusion.got.refs_0_, ...), custom_call_target="tpu_custom_call" | custom-call | flops 20000000 | bytes 10000000 | tf_op jit(solution)/shard_map/pallas_call | solution.py:73
  65.3 0.1 collective-permute-start.10
  65.4 0.1 collective-permute-start.9
  65.5 3.1 %collective-permute-start.8 = (f32[16,128]{1,0:T(8,128)S(1)}, f32[16,128]{1,0:T(8,128)S(1)}, u32[]{:S(2)}, u32[]{:S(2)}) collective-permute-start(f32[16,128]{1,0:T(8,128)S(1)} %shard_map.84), channel_id=1, source_target_pairs={{0,64},{64,0},{1,65},{65,1},{2,66},{66,2},{3,67},{67,3},{4,68},{68... | collective-permute-start | bytes 24584 | tf_op jit(solution)/shard_map/ppermute | solution.py:28
  68.6 0.5 collective-permute-done.10
  69.1 1.0 collective-permute-done.8
  70.0 2.8 %collective-permute-start.13 = (f32[16,128]{1,0:T(8,128)S(1)}, f32[16,128]{1,0:T(8,128)S(1)}, u32[]{:S(2)}, u32[]{:S(2)}) collective-permute-start(f32[16,128]{1,0:T(8,128)S(1)} %fusion.1.s0), channel_id=1, source_target_pairs={{0,6},{2,4},{4,2},{6,0},{1,7},{3,5},{5,3},{7,1},{8,14},{10,12},{12... | collective-permute-start | bytes 24584 | tf_op jit(solution)/shard_map/ppermute | solution.py:40
  72.9 0.3 collective-permute-start.12
  73.2 0.3 collective-permute-start.11
  73.5 2.3 %shard_map.82 = (f32[9216,128]{1,0:T(8,128)S(1)}, f32[9216,128]{1,0:T(8,128)S(1)}, f32[384,128]{1,0:T(8,128)S(1)}) custom-call(s32[5]{0:T(128)S(1)} %stack.38.pos_ref, f32[2,3,2,8,9216]{4,3,2,1,0:T(8,128)S(1)} %copy-done, f32[2,3,2,8,2304]{4,3,2,1,0:T(8,128)S(1)} %collective-permute-done.1.o1, f32[2,3,2,8,2304]{4,3,2,1,0:T(8,128)S(1)} %collective-permute-done.2.o2.o0, ...), custom_call_target="tpu_custom_call" | custom-call | flops 10000000 | bytes 10000000 | tf_op jit(solution)/shard_map/pallas_call | solution.py:73
  75.8 1.1 collective-permute-done.12.s2
  76.9 3.3 %shard_map.85 = (f32[24,28,24,128]{3,2,1,0:T(8,128)S(1)}, f32[1152,128]{1,0:T(8,128)S(1)}, f32[1152,128]{1,0:T(8,128)S(1)}, f32[768,128]{1,0:T(8,128)S(1)}, f32[768,128]{1,0:T(8,128)S(1)}) custom-call(s32[4]{0:T(128)S(1)} %convert_reduce_fusion.slot_ref, s32[5]{0:T(128)S(1)} %stack.38.pos_ref, f32[16,128]{1,0:T(8,128)S(1)} %fusion.1.s0, ...), custom_call_target="tpu_custom_call" | custom-call | flops 20000000 | bytes 10000000 | tf_op jit(solution)/shard_map/pallas_call | solution.py:73
  80.2 0.2 collective-permute-start.14
  80.4 1.9 %collective-permute-start.15 = (f32[1152,128]{1,0:T(8,128)S(1)}, f32[1152,128]{1,0:T(8,128)S(1)}, u32[]{:S(2)}, u32[]{:S(2)}) collective-permute-start(f32[1152,128]{1,0:T(8,128)S(1)} %get-tuple-element.56), channel_id=1, source_target_pairs={{0,6},{2,4},{4,2},{6,0},{1,7},{3,5},{5,3},{7,1},{8,14},{10,12},{12... | collective-permute-start | bytes 1769480 | tf_op jit(solution)/shard_map/ppermute | solution.py:40
  82.3 1.1 collective-permute-start.16
  83.4 0.8 collective-permute-start.17
  84.2 7.2 %shard_map.86.u_in = f32[9216,128]{1,0:T(8,128)S(1)} custom-call(f32[4,8]{1,0:T(4,128)S(1)} %pad_maximum_fusion.1.par_ref, f32[4]{0:T(128)S(1)} %convert_multiply_fusion.w_ref, f32[24,28,24,128]{3,2,1,0:T(8,128)S(1)} %get-tuple-element.53.refs_0_.refs_1_, f32[384,128]{1,0:T(8,128)S(1)} %get-tuple-element.54.refs_1_.refs_2_, bf16[256,256]{1,0:T(8,128)(2,1)S(1)} %copy-done.2), custom_call_target="tpu_custom_call" | custom-call | flops 60000000 | bytes 10000000 | tf_op jit(solution)/shard_map/pallas_call | solution.py:73
  91.5 1.1 collective-permute-done.14.za_in
  92.6 1.3 collective-permute-done.15.zb_in
  93.9 2.3 %shard_map.87 = (f32[24,28,24,128]{3,2,1,0:T(8,128)S(1)}, f32[1152,128]{1,0:T(8,128)S(1)}, f32[1152,128]{1,0:T(8,128)S(1)}, f32[768,128]{1,0:T(8,128)S(1)}, f32[768,128]{1,0:T(8,128)S(1)}) custom-call(f32[4,8]{1,0:T(4,128)S(1)} %pad_maximum_fusion.1.par_ref, f32[4]{0:T(128)S(1)} %convert_multiply_fusion.w_ref, s32[5]{0:T(128)S(1)} %stack.38.pos_ref, ...), custom_call_target="tpu_custom_call" | custom-call | flops 10000000 | bytes 10000000 | tf_op jit(solution)/shard_map/pallas_call | solution.py:73
  96.2 0.1 collective-permute-start.18
  96.3 2.0 %collective-permute-start.19 = (f32[1152,128]{1,0:T(8,128)S(1)}, f32[1152,128]{1,0:T(8,128)S(1)}, u32[]{:S(2)}, u32[]{:S(2)}) collective-permute-start(f32[1152,128]{1,0:T(8,128)S(1)} %get-tuple-element.61), channel_id=1, source_target_pairs={{0,6},{2,4},{4,2},{6,0},{1,7},{3,5},{5,3},{7,1},{8,14},{10,12},{12... | collective-permute-start | bytes 1769480 | tf_op jit(solution)/shard_map/ppermute | solution.py:40
  98.3 0.4 collective-permute-start.20
  98.7 1.1 collective-permute-start.21
  99.8 7.5 %shard_map.88.u_in = f32[9216,128]{1,0:T(8,128)S(1)} custom-call(f32[4,8]{1,0:T(4,128)S(1)} %pad_maximum_fusion.1.par_ref, f32[4]{0:T(128)S(1)} %convert_multiply_fusion.w_ref, f32[24,28,24,128]{3,2,1,0:T(8,128)S(1)} %get-tuple-element.59.refs_0_, f32[24,28,24,128]{3,2,1,0:T(8,128)S(1)} %get-tuple-element.53.refs_0_.refs_1_, ...), custom_call_target="tpu_custom_call" | custom-call | flops 60000000 | bytes 10000000 | tf_op jit(solution)/shard_map/pallas_call | solution.py:73
  107.3 0.4 collective-permute-done.18.za_in
  107.7 1.0 collective-permute-done.19.zb_in
  108.7 2.3 %shard_map.89 = (f32[24,28,24,128]{3,2,1,0:T(8,128)S(1)}, f32[1152,128]{1,0:T(8,128)S(1)}, f32[1152,128]{1,0:T(8,128)S(1)}, f32[768,128]{1,0:T(8,128)S(1)}, f32[768,128]{1,0:T(8,128)S(1)}) custom-call(f32[4,8]{1,0:T(4,128)S(1)} %pad_maximum_fusion.1.par_ref, f32[4]{0:T(128)S(1)} %convert_multiply_fusion.w_ref, s32[5]{0:T(128)S(1)} %stack.38.pos_ref, ...), custom_call_target="tpu_custom_call" | custom-call | flops 10000000 | bytes 10000000 | tf_op jit(solution)/shard_map/pallas_call | solution.py:73
  111.0 0.3 collective-permute-start.22
  111.3 2.0 %collective-permute-start.23 = (f32[1152,128]{1,0:T(8,128)S(1)}, f32[1152,128]{1,0:T(8,128)S(1)}, u32[]{:S(2)}, u32[]{:S(2)}) collective-permute-start(f32[1152,128]{1,0:T(8,128)S(1)} %get-tuple-element.66), channel_id=1, source_target_pairs={{0,6},{2,4},{4,2},{6,0},{1,7},{3,5},{5,3},{7,1},{8,14},{10,12},{12... | collective-permute-start | bytes 1769480 | tf_op jit(solution)/shard_map/ppermute | solution.py:40
  113.4 1.2 collective-permute-start.25
  114.6 8.4 %shard_map.90.d_in = f32[768,128]{1,0:T(8,128)S(1)} custom-call(f32[4,8]{1,0:T(4,128)S(1)} %pad_maximum_fusion.1.par_ref, f32[4]{0:T(128)S(1)} %convert_multiply_fusion.w_ref, f32[24,28,24,128]{3,2,1,0:T(8,128)S(1)} %get-tuple-element.64.refs_0_, f32[24,28,24,128]{3,2,1,0:T(8,128)S(1)} %get-tuple-element.53.refs_0_.refs_1_, ...), custom_call_target="tpu_custom_call" | custom-call | flops 60000000 | bytes 10000000 | tf_op jit(solution)/shard_map/pallas_call | solution.py:73
  123.1 2.5 %shard_map.91 = (f32[2,8,2304]{2,1,0:T(8,128)S(1)}, f32[2,8,2304]{2,1,0:T(8,128)S(1)}) custom-call(f32[4,8]{1,0:T(4,128)S(1)} %pad_maximum_fusion.1.par_ref, f32[4]{0:T(128)S(1)} %convert_multiply_fusion.w_ref, s32[5]{0:T(128)S(1)} %stack.38.pos_ref, f32[768,128]{1,0:T(8,128)S(1)} %shard_map.90.d_in, f32[1152,128]{1,0:T(8,128)S(1)} %collective-permute-done.22.za, ...), custom_call_target="tpu_custom_call" | custom-call | flops 10000000 | bytes 10000000 | tf_op jit(solution)/shard_map/pallas_call | solution.py:73
  125.6 5.6 %collective-permute-start.26 = (f32[2,8,2304]{2,1,0:T(8,128)S(1)}, f32[2,8,2304]{2,1,0:T(8,128)S(1)}, u32[]{:S(2)}, u32[]{:S(2)}) collective-permute-start(f32[2,8,2304]{2,1,0:T(8,128)S(1)} %get-tuple-element.70), channel_id=1, source_target_pairs={{0,8},{8,0},{1,9},{9,1},{2,10},{10,2},{3,11},{11,3},{4,12},{12,4},... | collective-permute-start | bytes 442376 | tf_op jit(solution)/shard_map/ppermute | solution.py:32
  131.2 1.0 collective-permute-done.26.b
  132.2 2.1 %collective-permute-start.29 = (f32[2,8,2304]{2,1,0:T(8,128)S(1)}, f32[2,8,2304]{2,1,0:T(8,128)S(1)}, u32[]{:S(2)}, u32[]{:S(2)}) collective-permute-start(f32[2,8,2304]{2,1,0:T(8,128)S(1)} %shard_map.92.s0), channel_id=1, source_target_pairs={{0,48},{16,32},{32,16},{48,0},{1,49},{17,33},{33,17},{49,1},{2,50}... | collective-permute-start | bytes 442376 | tf_op jit(solution)/shard_map/ppermute | solution.py:36
  134.3 1.2 collective-permute-start.27
  135.5 4.6 %collective-permute-done.29.s3 = f32[2,8,2304]{2,1,0:T(8,128)S(1)} collective-permute-done((f32[2,8,2304]{2,1,0:T(8,128)S(1)}, f32[2,8,2304]{2,1,0:T(8,128)S(1)}, u32[]{:S(2)}, u32[]{:S(2)}) %collective-permute-start.29) | collective-permute-done | bytes 147488 | tf_op jit(solution)/shard_map/ppermute | solution.py:36
  140.1 0.6 collective-permute-done.28.s2
  140.7 1.4 collective-permute-done.27.s1
  142.1 0.6 shard_map.93
  142.7 1.9 %collective-permute-start.32 = (f32[8,2304]{1,0:T(8,128)S(1)}, f32[8,2304]{1,0:T(8,128)S(1)}, u32[]{:S(2)}, u32[]{:S(2)}) collective-permute-start(f32[8,2304]{1,0:T(8,128)S(1)} %get-tuple-element.72), channel_id=1, source_target_pairs={{0,65},{64,1},{1,64},{65,0},{2,67},{66,3},{3,66},{67,2},{4,69},{68... | collective-permute-start | bytes 221192 | tf_op jit(solution)/shard_map/ppermute | solution.py:28
  144.6 1.1 collective-permute-start.31
  145.7 0.4 collective-permute-start.30
  146.0 2.3 %collective-permute-start.33 = (f32[8,2304]{1,0:T(8,128)S(1)}, f32[8,2304]{1,0:T(8,128)S(1)}, u32[]{:S(2)}, u32[]{:S(2)}) collective-permute-start(f32[8,2304]{1,0:T(8,128)S(1)} %get-tuple-element.71.refs_0_), channel_id=1, source_target_pairs={{0,8},{8,0},{1,9},{9,1},{2,10},{10,2},{3,11},{11,3},{4,12},{12,4},... | collective-permute-start | bytes 221192 | tf_op jit(solution)/shard_map/ppermute | solution.py:32
  148.3 2.3 %collective-permute-start.36 = (f32[8,2304]{1,0:T(8,128)S(1)}, f32[8,2304]{1,0:T(8,128)S(1)}, u32[]{:S(2)}, u32[]{:S(2)}) collective-permute-start(f32[8,2304]{1,0:T(8,128)S(1)} %collective-permute-done.32.refs_3_), channel_id=1, source_target_pairs={{0,8},{8,0},{1,9},{9,1},{2,10},{10,2},{3,11},{11,3},{4,12},{12,4},... | collective-permute-start | bytes 221192 | tf_op jit(solution)/shard_map/ppermute | solution.py:32
  150.6 1.6 %collective-permute-start.35 = (f32[8,2304]{1,0:T(8,128)S(1)}, f32[8,2304]{1,0:T(8,128)S(1)}, u32[]{:S(2)}, u32[]{:S(2)}) collective-permute-start(f32[8,2304]{1,0:T(8,128)S(1)} %collective-permute-done.31.refs_2_), channel_id=1, source_target_pairs={{0,8},{8,0},{1,9},{9,1},{2,10},{10,2},{3,11},{11,3},{4,12},{12,4},... | collective-permute-start | bytes 221192 | tf_op jit(solution)/shard_map/ppermute | solution.py:32
  152.2 0.9 collective-permute-done.35.refs_6_
  153.1 0.4 collective-permute-done.34.refs_5_
  153.4 1.4 place.1
  (44 shorter events, 0.2 us)
Async XLA Ops:
  0.0 61.6 %copy-start = (f32[2,3,2,8,9216]{4,3,2,1,0:T(8,128)S(1)}, f32[2,3,2,8,9216]{4,3,2,1,0:T(8,128)}, u32[]{:S(2)}) copy-start(f32[2,3,2,8,9216]{4,3,2,1,0:T(8,128)} %o0.3) | copy-start | bytes 10616836
  0.1 61.6 %copy-start.1 = (f32[2,8,9216]{2,1,0:T(8,128)S(1)}, f32[2,8,9216]{2,1,0:T(8,128)}, u32[]{:S(2)}) copy-start(f32[2,8,9216]{2,1,0:T(8,128)} %refs_0_.1) | copy-start | bytes 1769476
  2.7 70.8 %copy-start.3 = (f32[8,9216]{1,0:T(8,128)S(1)}, f32[8,9216]{1,0:T(8,128)}, u32[]{:S(2)}) copy-start(f32[8,9216]{1,0:T(8,128)} %pot.3) | copy-start | bytes 884740
  2.7 58.9 %collective-permute-start.1 = (f32[2,3,2,8,2304]{4,3,2,1,0:T(8,128)S(1)}, f32[2,3,2,8,2304]{4,3,2,1,0:T(8,128)S(1)}, u32[]{:S(2)}, u32[]{:S(2)}) collective-permute-start(f32[2,3,2,8,2304]{4,3,2,1,0:T(8,128)S(1)} %get-tuple-element.41), channel_id=1, source_target_pairs={{0,64},{64,0},{1,65},{65,1},{2,66},{66,2},{3,67},{67,3},{4,68},{68... | collective-permute-start | bytes 2654216 | tf_op jit(solution)/shard_map/ppermute | solution.py:28
  5.3 58.1 %collective-permute-start.2 = (f32[2,3,2,8,2304]{4,3,2,1,0:T(8,128)S(1)}, f32[2,3,2,8,2304]{4,3,2,1,0:T(8,128)S(1)}, u32[]{:S(2)}, u32[]{:S(2)}) collective-permute-start(f32[2,3,2,8,2304]{4,3,2,1,0:T(8,128)S(1)} %get-tuple-element.42), channel_id=1, source_target_pairs={{0,1},{64,65},{1,0},{65,64},{2,3},{66,67},{3,2},{67,66},{4,5},{68,... | collective-permute-start | bytes 2654216 | tf_op jit(solution)/shard_map/ppermute | solution.py:28
  8.6 54.8 %collective-permute-start.3 = (f32[2,3,2,8,2304]{4,3,2,1,0:T(8,128)S(1)}, f32[2,3,2,8,2304]{4,3,2,1,0:T(8,128)S(1)}, u32[]{:S(2)}, u32[]{:S(2)}) collective-permute-start(f32[2,3,2,8,2304]{4,3,2,1,0:T(8,128)S(1)} %get-tuple-element.43), channel_id=1, source_target_pairs={{0,65},{64,1},{1,64},{65,0},{2,67},{66,3},{3,66},{67,2},{4,69},{68... | collective-permute-start | bytes 2654216 | tf_op jit(solution)/shard_map/ppermute | solution.py:28
  8.6 41.0 %collective-permute-start = (f32[8,1280]{1,0:T(8,128)S(1)}, f32[8,1280]{1,0:T(8,128)S(1)}, u32[]{:S(2)}, u32[]{:S(2)}) collective-permute-start(f32[8,1280]{1,0:T(8,128)S(1)} %get-tuple-element.40), channel_id=1, source_target_pairs={{0,65},{64,1},{1,64},{65,0},{2,67},{66,3},{3,66},{67,2},{4,69},{68... | collective-permute-start | bytes 122888 | tf_op jit(solution)/shard_map/ppermute | solution.py:28
  49.6 4.1 %collective-permute-start.6 = (f32[8,1280]{1,0:T(8,128)S(1)}, f32[8,1280]{1,0:T(8,128)S(1)}, u32[]{:S(2)}, u32[]{:S(2)}) collective-permute-start(f32[8,1280]{1,0:T(8,128)S(1)} %collective-permute-done), channel_id=1, source_target_pairs={{0,48},{16,32},{32,16},{48,0},{1,49},{17,33},{33,17},{49,1},{2,50}... | collective-permute-start | bytes 122888 | tf_op jit(solution)/shard_map/ppermute | solution.py:36
  52.1 4.5 %collective-permute-start.5 = (f32[8,1280]{1,0:T(8,128)S(1)}, f32[8,1280]{1,0:T(8,128)S(1)}, u32[]{:S(2)}, u32[]{:S(2)}) collective-permute-start(f32[8,1280]{1,0:T(8,128)S(1)} %collective-permute-done), channel_id=1, source_target_pairs={{0,32},{16,48},{32,0},{48,16},{1,33},{17,49},{33,1},{49,17},{2,34}... | collective-permute-start | bytes 122888 | tf_op jit(solution)/shard_map/ppermute | solution.py:36
  53.6 3.1 %collective-permute-start.4 = (f32[8,1280]{1,0:T(8,128)S(1)}, f32[8,1280]{1,0:T(8,128)S(1)}, u32[]{:S(2)}, u32[]{:S(2)}) collective-permute-start(f32[8,1280]{1,0:T(8,128)S(1)} %collective-permute-done), channel_id=1, source_target_pairs={{0,16},{16,0},{32,48},{48,32},{1,17},{17,1},{33,49},{49,33},{2,18}... | collective-permute-start | bytes 122888 | tf_op jit(solution)/shard_map/ppermute | solution.py:36
  56.8 6.5 %collective-permute-start.7 = (f32[4,8,1280]{2,1,0:T(8,128)S(1)}, f32[4,8,1280]{2,1,0:T(8,128)S(1)}, u32[]{:S(2)}, u32[]{:S(2)}) collective-permute-start(f32[4,8,1280]{2,1,0:T(8,128)S(1)} %pad_maximum_fusion.got.refs_0_), channel_id=1, source_target_pairs={{0,8},{8,0},{1,9},{9,1},{2,10},{10,2},{3,11},{11,3},{4,12},{12,4},... | collective-permute-start | bytes 491528 | tf_op jit(solution)/shard_map/ppermute | solution.py:32
  65.3 3.8 %collective-permute-start.10 = (f32[16,128]{1,0:T(8,128)S(1)}, f32[16,128]{1,0:T(8,128)S(1)}, u32[]{:S(2)}, u32[]{:S(2)}) collective-permute-start(f32[16,128]{1,0:T(8,128)S(1)} %shard_map.84), channel_id=1, source_target_pairs={{0,65},{64,1},{1,64},{65,0},{2,67},{66,3},{3,66},{67,2},{4,69},{68... | collective-permute-start | bytes 24584 | tf_op jit(solution)/shard_map/ppermute | solution.py:28
  65.4 4.7 %collective-permute-start.9 = (f32[16,128]{1,0:T(8,128)S(1)}, f32[16,128]{1,0:T(8,128)S(1)}, u32[]{:S(2)}, u32[]{:S(2)}) collective-permute-start(f32[16,128]{1,0:T(8,128)S(1)} %shard_map.84), channel_id=1, source_target_pairs={{0,1},{64,65},{1,0},{65,64},{2,3},{66,67},{3,2},{67,66},{4,5},{68,... | collective-permute-start | bytes 24584 | tf_op jit(solution)/shard_map/ppermute | solution.py:28
  65.5 4.6 %collective-permute-start.8 = (f32[16,128]{1,0:T(8,128)S(1)}, f32[16,128]{1,0:T(8,128)S(1)}, u32[]{:S(2)}, u32[]{:S(2)}) collective-permute-start(f32[16,128]{1,0:T(8,128)S(1)} %shard_map.84), channel_id=1, source_target_pairs={{0,64},{64,0},{1,65},{65,1},{2,66},{66,2},{3,67},{67,3},{4,68},{68... | collective-permute-start | bytes 24584 | tf_op jit(solution)/shard_map/ppermute | solution.py:28
  70.0 5.8 %collective-permute-start.13 = (f32[16,128]{1,0:T(8,128)S(1)}, f32[16,128]{1,0:T(8,128)S(1)}, u32[]{:S(2)}, u32[]{:S(2)}) collective-permute-start(f32[16,128]{1,0:T(8,128)S(1)} %fusion.1.s0), channel_id=1, source_target_pairs={{0,6},{2,4},{4,2},{6,0},{1,7},{3,5},{5,3},{7,1},{8,14},{10,12},{12... | collective-permute-start | bytes 24584 | tf_op jit(solution)/shard_map/ppermute | solution.py:40
  72.9 4.0 %collective-permute-start.12 = (f32[16,128]{1,0:T(8,128)S(1)}, f32[16,128]{1,0:T(8,128)S(1)}, u32[]{:S(2)}, u32[]{:S(2)}) collective-permute-start(f32[16,128]{1,0:T(8,128)S(1)} %fusion.1.s0), channel_id=1, source_target_pairs={{0,4},{2,6},{4,0},{6,2},{1,5},{3,7},{5,1},{7,3},{8,12},{10,14},{12... | collective-permute-start | bytes 24584 | tf_op jit(solution)/shard_map/ppermute | solution.py:40
  73.2 3.7 %collective-permute-start.11 = (f32[16,128]{1,0:T(8,128)S(1)}, f32[16,128]{1,0:T(8,128)S(1)}, u32[]{:S(2)}, u32[]{:S(2)}) collective-permute-start(f32[16,128]{1,0:T(8,128)S(1)} %fusion.1.s0), channel_id=1, source_target_pairs={{0,2},{2,0},{4,6},{6,4},{1,3},{3,1},{5,7},{7,5},{8,10},{10,8},{12,... | collective-permute-start | bytes 24584 | tf_op jit(solution)/shard_map/ppermute | solution.py:40
  76.9 7.4 %copy-start.4 = (s32[4]{0:T(128)S(1)}, s32[4]{0:T(128)}, u32[]{:S(2)}) copy-start(s32[4]{0:T(128)} %param.14) | copy-start | bytes 52
  76.9 7.4 %copy-start.2 = (bf16[256,256]{1,0:T(8,128)(2,1)S(1)}, bf16[256,256]{1,0:T(8,128)(2,1)}, u32[]{:S(2)}) copy-start(bf16[256,256]{1,0:T(8,128)(2,1)} %constant.26.clone.refs_2_.refs_3_) | copy-start | bytes 393220
  80.2 12.4 %collective-permute-start.14 = (f32[1152,128]{1,0:T(8,128)S(1)}, f32[1152,128]{1,0:T(8,128)S(1)}, u32[]{:S(2)}, u32[]{:S(2)}) collective-permute-start(f32[1152,128]{1,0:T(8,128)S(1)} %get-tuple-element.55), channel_id=1, source_target_pairs={{0,2},{2,0},{4,6},{6,4},{1,3},{3,1},{5,7},{7,5},{8,10},{10,8},{12,... | collective-permute-start | bytes 1769480 | tf_op jit(solution)/shard_map/ppermute | solution.py:40
  80.4 13.5 %collective-permute-start.15 = (f32[1152,128]{1,0:T(8,128)S(1)}, f32[1152,128]{1,0:T(8,128)S(1)}, u32[]{:S(2)}, u32[]{:S(2)}) collective-permute-start(f32[1152,128]{1,0:T(8,128)S(1)} %get-tuple-element.56), channel_id=1, source_target_pairs={{0,6},{2,4},{4,2},{6,0},{1,7},{3,5},{5,3},{7,1},{8,14},{10,12},{12... | collective-permute-start | bytes 1769480 | tf_op jit(solution)/shard_map/ppermute | solution.py:40
  82.3 9.1 %collective-permute-start.16 = (f32[768,128]{1,0:T(8,128)S(1)}, f32[768,128]{1,0:T(8,128)S(1)}, u32[]{:S(2)}, u32[]{:S(2)}) collective-permute-start(f32[768,128]{1,0:T(8,128)S(1)} %get-tuple-element.57), channel_id=1, source_target_pairs={{0,64},{64,0},{1,65},{65,1},{2,66},{66,2},{3,67},{67,3},{4,68},{68... | collective-permute-start | bytes 1179656 | tf_op jit(solution)/shard_map/ppermute | solution.py:28
  83.4 8.1 %collective-permute-start.17 = (f32[768,128]{1,0:T(8,128)S(1)}, f32[768,128]{1,0:T(8,128)S(1)}, u32[]{:S(2)}, u32[]{:S(2)}) collective-permute-start(f32[768,128]{1,0:T(8,128)S(1)} %get-tuple-element.58), channel_id=1, source_target_pairs={{0,65},{64,1},{1,64},{65,0},{2,67},{66,3},{3,66},{67,2},{4,69},{68... | collective-permute-start | bytes 1179656 | tf_op jit(solution)/shard_map/ppermute | solution.py:28
  96.2 11.5 %collective-permute-start.18 = (f32[1152,128]{1,0:T(8,128)S(1)}, f32[1152,128]{1,0:T(8,128)S(1)}, u32[]{:S(2)}, u32[]{:S(2)}) collective-permute-start(f32[1152,128]{1,0:T(8,128)S(1)} %get-tuple-element.60), channel_id=1, source_target_pairs={{0,2},{2,0},{4,6},{6,4},{1,3},{3,1},{5,7},{7,5},{8,10},{10,8},{12,... | collective-permute-start | bytes 1769480 | tf_op jit(solution)/shard_map/ppermute | solution.py:40
  96.3 12.4 %collective-permute-start.19 = (f32[1152,128]{1,0:T(8,128)S(1)}, f32[1152,128]{1,0:T(8,128)S(1)}, u32[]{:S(2)}, u32[]{:S(2)}) collective-permute-start(f32[1152,128]{1,0:T(8,128)S(1)} %get-tuple-element.61), channel_id=1, source_target_pairs={{0,6},{2,4},{4,2},{6,0},{1,7},{3,5},{5,3},{7,1},{8,14},{10,12},{12... | collective-permute-start | bytes 1769480 | tf_op jit(solution)/shard_map/ppermute | solution.py:40
  98.3 9.0 %collective-permute-start.20 = (f32[768,128]{1,0:T(8,128)S(1)}, f32[768,128]{1,0:T(8,128)S(1)}, u32[]{:S(2)}, u32[]{:S(2)}) collective-permute-start(f32[768,128]{1,0:T(8,128)S(1)} %get-tuple-element.62), channel_id=1, source_target_pairs={{0,64},{64,0},{1,65},{65,1},{2,66},{66,2},{3,67},{67,3},{4,68},{68... | collective-permute-start | bytes 1179656 | tf_op jit(solution)/shard_map/ppermute | solution.py:28
  98.7 8.6 %collective-permute-start.21 = (f32[768,128]{1,0:T(8,128)S(1)}, f32[768,128]{1,0:T(8,128)S(1)}, u32[]{:S(2)}, u32[]{:S(2)}) collective-permute-start(f32[768,128]{1,0:T(8,128)S(1)} %get-tuple-element.63), channel_id=1, source_target_pairs={{0,65},{64,1},{1,64},{65,0},{2,67},{66,3},{3,66},{67,2},{4,69},{68... | collective-permute-start | bytes 1179656 | tf_op jit(solution)/shard_map/ppermute | solution.py:28
  111.0 12.0 %collective-permute-start.22 = (f32[1152,128]{1,0:T(8,128)S(1)}, f32[1152,128]{1,0:T(8,128)S(1)}, u32[]{:S(2)}, u32[]{:S(2)}) collective-permute-start(f32[1152,128]{1,0:T(8,128)S(1)} %get-tuple-element.65), channel_id=1, source_target_pairs={{0,2},{2,0},{4,6},{6,4},{1,3},{3,1},{5,7},{7,5},{8,10},{10,8},{12,... | collective-permute-start | bytes 1769480 | tf_op jit(solution)/shard_map/ppermute | solution.py:40
  111.3 11.7 %collective-permute-start.23 = (f32[1152,128]{1,0:T(8,128)S(1)}, f32[1152,128]{1,0:T(8,128)S(1)}, u32[]{:S(2)}, u32[]{:S(2)}) collective-permute-start(f32[1152,128]{1,0:T(8,128)S(1)} %get-tuple-element.66), channel_id=1, source_target_pairs={{0,6},{2,4},{4,2},{6,0},{1,7},{3,5},{5,3},{7,1},{8,14},{10,12},{12... | collective-permute-start | bytes 1769480 | tf_op jit(solution)/shard_map/ppermute | solution.py:40
  113.4 9.7 %collective-permute-start.24 = (f32[768,128]{1,0:T(8,128)S(1)}, f32[768,128]{1,0:T(8,128)S(1)}, u32[]{:S(2)}, u32[]{:S(2)}) collective-permute-start(f32[768,128]{1,0:T(8,128)S(1)} %get-tuple-element.67), channel_id=1, source_target_pairs={{0,64},{64,0},{1,65},{65,1},{2,66},{66,2},{3,67},{67,3},{4,68},{68... | collective-permute-start | bytes 1179656 | tf_op jit(solution)/shard_map/ppermute | solution.py:28
  113.4 9.7 %collective-permute-start.25 = (f32[768,128]{1,0:T(8,128)S(1)}, f32[768,128]{1,0:T(8,128)S(1)}, u32[]{:S(2)}, u32[]{:S(2)}) collective-permute-start(f32[768,128]{1,0:T(8,128)S(1)} %get-tuple-element.68), channel_id=1, source_target_pairs={{0,65},{64,1},{1,64},{65,0},{2,67},{66,3},{3,66},{67,2},{4,69},{68... | collective-permute-start | bytes 1179656 | tf_op jit(solution)/shard_map/ppermute | solution.py:28
  125.6 6.6 %collective-permute-start.26 = (f32[2,8,2304]{2,1,0:T(8,128)S(1)}, f32[2,8,2304]{2,1,0:T(8,128)S(1)}, u32[]{:S(2)}, u32[]{:S(2)}) collective-permute-start(f32[2,8,2304]{2,1,0:T(8,128)S(1)} %get-tuple-element.70), channel_id=1, source_target_pairs={{0,8},{8,0},{1,9},{9,1},{2,10},{10,2},{3,11},{11,3},{4,12},{12,4},... | collective-permute-start | bytes 442376 | tf_op jit(solution)/shard_map/ppermute | solution.py:32
  132.2 7.9 %collective-permute-start.29 = (f32[2,8,2304]{2,1,0:T(8,128)S(1)}, f32[2,8,2304]{2,1,0:T(8,128)S(1)}, u32[]{:S(2)}, u32[]{:S(2)}) collective-permute-start(f32[2,8,2304]{2,1,0:T(8,128)S(1)} %shard_map.92.s0), channel_id=1, source_target_pairs={{0,48},{16,32},{32,16},{48,0},{1,49},{17,33},{33,17},{49,1},{2,50}... | collective-permute-start | bytes 442376 | tf_op jit(solution)/shard_map/ppermute | solution.py:36
  134.3 6.4 %collective-permute-start.28 = (f32[2,8,2304]{2,1,0:T(8,128)S(1)}, f32[2,8,2304]{2,1,0:T(8,128)S(1)}, u32[]{:S(2)}, u32[]{:S(2)}) collective-permute-start(f32[2,8,2304]{2,1,0:T(8,128)S(1)} %shard_map.92.s0), channel_id=1, source_target_pairs={{0,32},{16,48},{32,0},{48,16},{1,33},{17,49},{33,1},{49,17},{2,34}... | collective-permute-start | bytes 442376 | tf_op jit(solution)/shard_map/ppermute | solution.py:36
  134.3 7.8 %collective-permute-start.27 = (f32[2,8,2304]{2,1,0:T(8,128)S(1)}, f32[2,8,2304]{2,1,0:T(8,128)S(1)}, u32[]{:S(2)}, u32[]{:S(2)}) collective-permute-start(f32[2,8,2304]{2,1,0:T(8,128)S(1)} %shard_map.92.s0), channel_id=1, source_target_pairs={{0,16},{16,0},{32,48},{48,32},{1,17},{17,1},{33,49},{49,33},{2,18}... | collective-permute-start | bytes 442376 | tf_op jit(solution)/shard_map/ppermute | solution.py:36
  142.7 5.6 %collective-permute-start.32 = (f32[8,2304]{1,0:T(8,128)S(1)}, f32[8,2304]{1,0:T(8,128)S(1)}, u32[]{:S(2)}, u32[]{:S(2)}) collective-permute-start(f32[8,2304]{1,0:T(8,128)S(1)} %get-tuple-element.72), channel_id=1, source_target_pairs={{0,65},{64,1},{1,64},{65,0},{2,67},{66,3},{3,66},{67,2},{4,69},{68... | collective-permute-start | bytes 221192 | tf_op jit(solution)/shard_map/ppermute | solution.py:28
  144.6 6.0 %collective-permute-start.31 = (f32[8,2304]{1,0:T(8,128)S(1)}, f32[8,2304]{1,0:T(8,128)S(1)}, u32[]{:S(2)}, u32[]{:S(2)}) collective-permute-start(f32[8,2304]{1,0:T(8,128)S(1)} %get-tuple-element.72), channel_id=1, source_target_pairs={{0,1},{64,65},{1,0},{65,64},{2,3},{66,67},{3,2},{67,66},{4,5},{68,... | collective-permute-start | bytes 221192 | tf_op jit(solution)/shard_map/ppermute | solution.py:28
  145.7 6.5 %collective-permute-start.30 = (f32[8,2304]{1,0:T(8,128)S(1)}, f32[8,2304]{1,0:T(8,128)S(1)}, u32[]{:S(2)}, u32[]{:S(2)}) collective-permute-start(f32[8,2304]{1,0:T(8,128)S(1)} %get-tuple-element.71.refs_0_), channel_id=1, source_target_pairs={{0,64},{64,0},{1,65},{65,1},{2,66},{66,2},{3,67},{67,3},{4,68},{68... | collective-permute-start | bytes 221192 | tf_op jit(solution)/shard_map/ppermute | solution.py:28
  146.0 6.2 %collective-permute-start.33 = (f32[8,2304]{1,0:T(8,128)S(1)}, f32[8,2304]{1,0:T(8,128)S(1)}, u32[]{:S(2)}, u32[]{:S(2)}) collective-permute-start(f32[8,2304]{1,0:T(8,128)S(1)} %get-tuple-element.71.refs_0_), channel_id=1, source_target_pairs={{0,8},{8,0},{1,9},{9,1},{2,10},{10,2},{3,11},{11,3},{4,12},{12,4},... | collective-permute-start | bytes 221192 | tf_op jit(solution)/shard_map/ppermute | solution.py:32
  148.3 3.9 %collective-permute-start.36 = (f32[8,2304]{1,0:T(8,128)S(1)}, f32[8,2304]{1,0:T(8,128)S(1)}, u32[]{:S(2)}, u32[]{:S(2)}) collective-permute-start(f32[8,2304]{1,0:T(8,128)S(1)} %collective-permute-done.32.refs_3_), channel_id=1, source_target_pairs={{0,8},{8,0},{1,9},{9,1},{2,10},{10,2},{3,11},{11,3},{4,12},{12,4},... | collective-permute-start | bytes 221192 | tf_op jit(solution)/shard_map/ppermute | solution.py:32
  150.6 2.5 %collective-permute-start.35 = (f32[8,2304]{1,0:T(8,128)S(1)}, f32[8,2304]{1,0:T(8,128)S(1)}, u32[]{:S(2)}, u32[]{:S(2)}) collective-permute-start(f32[8,2304]{1,0:T(8,128)S(1)} %collective-permute-done.31.refs_2_), channel_id=1, source_target_pairs={{0,8},{8,0},{1,9},{9,1},{2,10},{10,2},{3,11},{11,3},{4,12},{12,4},... | collective-permute-start | bytes 221192 | tf_op jit(solution)/shard_map/ppermute | solution.py:32
  152.2 1.3 collective-permute-start.34
